TPU v7x, 256 devices: a whole 4x4x8 slice. The times are simulated.
256 devices in a mesh: req: 32 (over y, z_lo, core), tp: 8 (over x, z_hi).
Axes of the slice: x: 4, y: 4, z: 8 (z_hi: 2, z_lo: 4; z = z_hi * 4 + z_lo), core: 2. Of those that a mesh axis runs over, the one named last changes fastest.
Arguments:
- stream: bfloat16 [4096, 1792], P('req', 'tp'), may hold values from -6 to 6
- token_req: int32 [4096], P('req'), may hold values from 0 to 64, as said below
- request_leaf: int32 [64], replicated, may hold values from 10 to 31
- parent: int32 [32], replicated, may hold values from 0 to 9, as said below
- owner_map: int32 [32], replicated, may hold values from 0 to 31, each once
- node_state: bfloat16 [32, 16, 273, 112], P('req', 'tp')
- node_norm: bfloat16 [32, 16, 273], P('req', 'tp'), as said below
- node_tail: bfloat16 [32, 2, 1792], P('req', None, 'tp'), may hold values from -16 to 16
- mixer_gain: float32 [1792], replicated, may hold values from 0.5 to 1.5
- ffn_gain: float32 [1792], replicated, may hold values from 0.5 to 1.5
- query_weight: bfloat16 [1792, 256], P(None, 'tp'), may hold values from -0.125 to 0.125
- key_weight: bfloat16 [1792, 256], P(None, 'tp'), may hold values from -0.125 to 0.125
- value_weight: bfloat16 [1792, 1792], P(None, 'tp'), may hold values from -0.125 to 0.125
- conv_gate_weight: bfloat16 [1792, 1792], P(None, 'tp'), may hold values from -0.125 to 0.125
- conv_kernel: float32 [3, 1792], P(None, 'tp'), may hold values from -3 to 3
- out_weight: bfloat16 [1792, 1792], P('tp'), may hold values from -0.125 to 0.125
- ffn_gate: bfloat16 [1792, 4864], P(None, 'tp'), may hold values from -0.125 to 0.125
- ffn_up: bfloat16 [1792, 4864], P(None, 'tp'), may hold values from -0.125 to 0.125
- ffn_down: bfloat16 [4864, 1792], P('tp'), may hold values from -0.078125 to 0.078125
Outputs:
- layer_out: bfloat16 [4096, 1792], P('req', 'tp')
Inputs may be any that keep to these rules, and one draw needn't show every extreme that they name: `token_req`: on the device at index d of req the slots hold, in order, the tokens of requests d * 2 to d * 2 + 1, each request 1 to 64 contiguous tokens, some request exactly that many, then padding slots with value 64; some device has padding. Nodes below 2 are roots and their own parents; nodes 2 to 9 have a root as parent; every other node has one of those as parent. `node_norm`: every row is a sum with positive weights of feature maps phi of key vectors.
All inputs are finite; a program needn't handle non-finite values.
Results may differ from a plain program's by a relative error of at most 0.019.
Values may be sent and summed in bfloat16 or wider, within the bound.
No kernel may reach another device: no remote copies, remote signals or barrier semaphores. Data moves between devices by JAX's collectives and lax.ppermute only.
A program may use at most 128 MiB of HBM per device.

v0:
```python
import jax
import jax.numpy as jnp
from jax import lax
from jax.sharding import PartitionSpec as P

EPSILON = 1e-05


def rms_scale(rows_in, gain_row):
    rows_in = rows_in.astype(jnp.float32)
    return (
        rows_in
        * lax.rsqrt(jnp.mean(rows_in * rows_in, axis=-1, keepdims=True) + EPSILON)
        * gain_row
    )


def taylor_map(projected, head_count):
    row_count = projected.shape[0]
    feature_dim = projected.shape[1] // head_count
    head_parts = projected.reshape(row_count, head_count, feature_dim)
    unit_column = jnp.ones((row_count, head_count, 1), jnp.float32)
    linear = head_parts * feature_dim ** (-0.25)
    square = (head_parts[:, :, :, None] * head_parts[:, :, None, :]).reshape(
        row_count, head_count, feature_dim * feature_dim
    ) * (2.0 * feature_dim) ** (-0.5)
    return jnp.concatenate([unit_column, linear, square], axis=-1)


def token_layout(token_ids, first_request, per_device, total_req):
    row_count = token_ids.shape[0]
    slot_of_token = jnp.where(token_ids >= total_req, per_device, token_ids - first_request)
    slot_ids = jnp.arange(per_device + 1, dtype=jnp.int32)
    matches = slot_of_token[:, None] == slot_ids[None, :]
    amounts = jnp.sum(matches.astype(jnp.int32), axis=0)
    starts = jnp.cumsum(amounts) - amounts
    offset = jnp.sum(jnp.where(matches, starts[None, :], 0), axis=1)
    position = jnp.arange(row_count, dtype=jnp.int32) - offset
    return (slot_of_token, matches, position)


def path_rows(request_leaf, parent, owner_map):
    middle_nodes = parent[request_leaf]
    root_nodes = parent[middle_nodes]
    return (owner_map[request_leaf], owner_map[middle_nodes], owner_map[root_nodes])


def membership(row_sets, node_ids):
    indicator = jnp.zeros((row_sets[0].shape[0], node_ids.shape[0]), jnp.float32)
    for row_set in row_sets:
        indicator = indicator + (row_set[:, None] == node_ids[None, :]).astype(jnp.float32)
    return indicator.astype(jnp.bfloat16)


def short_conv(values, conv_gates, tail_rows, conv_kernel, slot_of_token, position, per_device):
    row_count, row_width = values.shape
    kernel_len = conv_kernel.shape[0]
    tail_ids = jnp.arange((per_device + 1) * (kernel_len - 1), dtype=jnp.int32)
    result = jnp.zeros((row_count, row_width), jnp.float32)
    for lag_index in range(kernel_len):
        if lag_index == 0:
            shifted = values
        else:
            shifted = jnp.concatenate(
                [jnp.zeros((lag_index, row_width), values.dtype), values[: row_count - lag_index]],
                axis=0,
            )
        back_pos = position - lag_index
        inside = back_pos >= 0
        tail_slot = slot_of_token * (kernel_len - 1) + (kernel_len - 1) + back_pos
        picker = (
            (tail_slot[:, None] == tail_ids[None, :]) & jnp.logical_not(inside)[:, None]
        ).astype(jnp.bfloat16)
        from_tail = jnp.dot(picker, tail_rows, preferred_element_type=jnp.float32)
        tapped = jnp.where(inside[:, None], shifted.astype(jnp.float32), from_tail)
        result = result + conv_kernel[lag_index][None, :] * tapped
    return (result * jax.nn.silu(conv_gates)).astype(jnp.bfloat16)


def linear_attention(
    queries, keys_proj, mixed, prefix_state, prefix_norm, slot_of_token, matches, head_count
):
    row_count = queries.shape[0]
    head_dim = mixed.shape[1] // head_count
    query_feat = taylor_map(queries, head_count).astype(jnp.bfloat16)
    key_feat = taylor_map(keys_proj, head_count).astype(jnp.bfloat16)
    scores = jnp.einsum("thf,shf->hts", query_feat, key_feat, preferred_element_type=jnp.float32)
    row_ids = jnp.arange(row_count, dtype=jnp.int32)
    allowed = (slot_of_token[:, None] == slot_of_token[None, :]) & (
        row_ids[None, :] <= row_ids[:, None]
    )
    masked = jnp.where(allowed[None, :, :], scores, 0.0)
    local_den = jnp.transpose(jnp.sum(masked, axis=2))
    value_heads = mixed.reshape(row_count, head_count, head_dim)
    local_num = jnp.einsum(
        "hts,she->the", masked.astype(jnp.bfloat16), value_heads, preferred_element_type=jnp.float32
    )
    selector = matches.astype(jnp.float32)
    prefix_all = jnp.einsum(
        "thf,rhfe->thre", query_feat, prefix_state, preferred_element_type=jnp.float32
    )
    prefix_num = jnp.einsum("thre,tr->the", prefix_all, selector, precision=lax.Precision.HIGHEST)
    norm_all = jnp.einsum(
        "thf,rhf->thr", query_feat.astype(jnp.float32), prefix_norm, precision=lax.Precision.HIGHEST
    )
    prefix_den = jnp.einsum("thr,tr->th", norm_all, selector, precision=lax.Precision.HIGHEST)
    ratio = (local_num + prefix_num) / (local_den + prefix_den)[:, :, None]
    return ratio.astype(jnp.bfloat16).reshape(row_count, head_count * head_dim)


def shards(
    stream,
    token_req,
    request_leaf,
    parent,
    owner_map,
    node_state,
    node_norm,
    node_tail,
    mixer_gain,
    ffn_gain,
    query_weight,
    key_weight,
    value_weight,
    conv_gate_weight,
    conv_kernel,
    out_weight,
    ffn_gate,
    ffn_up,
    ffn_down,
):
    node_here = node_state.shape[0]
    head_count = node_state.shape[1]
    feat_count = node_state.shape[2]
    head_dim = node_state.shape[3]
    value_width = value_weight.shape[1]
    kernel_len = conv_kernel.shape[0]
    total_req = request_leaf.shape[0]
    per_device = total_req // lax.axis_size("req")
    device = lax.axis_index("req")
    first_request = device * per_device
    full_rows = lax.all_gather(stream, "tp", axis=1, tiled=True)
    normed = rms_scale(full_rows, mixer_gain).astype(jnp.bfloat16)
    queries = jnp.dot(normed, query_weight, preferred_element_type=jnp.float32)
    keys_proj = jnp.dot(normed, key_weight, preferred_element_type=jnp.float32)
    values = jnp.dot(normed, value_weight, preferred_element_type=jnp.float32).astype(jnp.bfloat16)
    conv_gates = jnp.dot(normed, conv_gate_weight, preferred_element_type=jnp.float32)
    slot_of_token, matches, position = token_layout(token_req, first_request, per_device, total_req)
    state_width = head_count * feat_count * head_dim
    norm_width = head_count * feat_count
    tail_width = (kernel_len - 1) * value_width
    held_ids = device * node_here + jnp.arange(node_here, dtype=jnp.int32)
    held_state = node_state.reshape(node_here, state_width)
    held_norm = node_norm.reshape(node_here, norm_width)
    held_tail = node_tail.reshape(node_here, tail_width)
    leaf_rows, middle_rows, root_rows = path_rows(request_leaf, parent, owner_map)
    on_path = membership((leaf_rows, middle_rows, root_rows), held_ids)
    on_leaf = membership((leaf_rows,), held_ids)
    state_term = jnp.dot(on_path, held_state, preferred_element_type=jnp.float32)
    norm_term = jnp.dot(on_path, held_norm, preferred_element_type=jnp.float32)
    tail_term = jnp.dot(on_leaf, held_tail, preferred_element_type=jnp.float32)
    joined = lax.psum_scatter(
        jnp.concatenate([state_term, norm_term, tail_term], axis=1).astype(jnp.bfloat16),
        "req",
        scatter_dimension=0,
        tiled=True,
    ).astype(jnp.float32)
    state_sum = joined[:, :state_width]
    norm_sum = joined[:, state_width : state_width + norm_width]
    tail_sum = joined[:, state_width + norm_width :]
    prefix_state = jnp.concatenate(
        [
            state_sum.astype(jnp.bfloat16).reshape(per_device, head_count, feat_count, head_dim),
            jnp.zeros((1, head_count, feat_count, head_dim), jnp.bfloat16),
        ],
        axis=0,
    )
    prefix_norm = jnp.concatenate(
        [
            norm_sum.reshape(per_device, head_count, feat_count),
            jnp.zeros((1, head_count, feat_count), jnp.float32),
        ],
        axis=0,
    )
    tail_rows = jnp.concatenate(
        [
            tail_sum.astype(jnp.bfloat16).reshape(per_device, kernel_len - 1, value_width),
            jnp.zeros((1, kernel_len - 1, value_width), jnp.bfloat16),
        ],
        axis=0,
    ).reshape((per_device + 1) * (kernel_len - 1), value_width)
    mixed = short_conv(
        values, conv_gates, tail_rows, conv_kernel, slot_of_token, position, per_device
    )
    attended = linear_attention(
        queries, keys_proj, mixed, prefix_state, prefix_norm, slot_of_token, matches, head_count
    )
    partial_value = jnp.dot(attended, out_weight, preferred_element_type=jnp.float32)
    share = lax.psum_scatter(
        partial_value.astype(jnp.bfloat16), "tp", scatter_dimension=1, tiled=True
    ).astype(jnp.float32)
    own_rows = (stream.astype(jnp.float32) + share).astype(jnp.bfloat16)
    wide_rows = lax.all_gather(own_rows, "tp", axis=1, tiled=True)
    normed_two = rms_scale(wide_rows, ffn_gain).astype(jnp.bfloat16)
    gate_part = jnp.dot(normed_two, ffn_gate, preferred_element_type=jnp.float32)
    up_part = jnp.dot(normed_two, ffn_up, preferred_element_type=jnp.float32)
    activated = (jax.nn.silu(gate_part) * up_part).astype(jnp.bfloat16)
    down_part = jnp.dot(activated, ffn_down, preferred_element_type=jnp.float32)
    down_share = lax.psum_scatter(
        down_part.astype(jnp.bfloat16), "tp", scatter_dimension=1, tiled=True
    ).astype(jnp.float32)
    return (own_rows.astype(jnp.float32) + down_share).astype(jnp.bfloat16)


def solution(mesh):
    in_specs = (
        P("req", "tp"),
        P("req"),
        P(),
        P(),
        P(),
        P("req", "tp", None, None),
        P("req", "tp", None),
        P("req", None, "tp"),
        P(),
        P(),
        P(None, "tp"),
        P(None, "tp"),
        P(None, "tp"),
        P(None, "tp"),
        P(None, "tp"),
        P("tp", None),
        P(None, "tp"),
        P(None, "tp"),
        P("tp", None),
    )
    out_specs = P("req", "tp")
    return jax.shard_map(shards, mesh=mesh, in_specs=in_specs, out_specs=out_specs, check_vma=False)
```

profile of v0, /device:TPU:8, one launch (start us, length us, event | category | flops | bytes accessed | tf_op | source)
XLA Modules:
  0.0 616.6 jit_solution(2828549122061909118)
XLA Ops:
  6.6 0.8 compare_select_fusion.2
  7.4 1.4 gather_fusion.1
  8.8 1.4 gather_fusion.3
  10.3 1.4 gather_fusion.2
  11.7 1.4 gather_fusion
  13.2 0.8 gather_fusion.4
  14.4 4.0 multiply_convert_fusion
  18.6 38.9 %dynamic-update-slice = bf16[64,62146]{1,0:T(8,128)(2,1)} dynamic-update-slice(bf16[64,62146]{1,0:T(8,128)(2,1)} %custom-call, bf16[64,61152]{1,0:T(8,128)(2,1)} %multiply_convert_fusion, s32[]{} %constant.73, s32[]{} %constant.73) | dynamic-update-slice | bytes 15654916
  57.5 1.9 dynamic-update-slice.1
  59.4 1.6 dynamic-update-slice.2
  63.4 51.1 %all_gather.6 = bf16[128,1792]{0,1:T(8,128)(2,1)S(1)} all-gather(bf16[128,224]{0,1:T(8,128)(2,1)S(1)} %copy-done.3), channel_id=1, replica_groups=mesh['req'=32,'tp'=8] {'tp'}, dimensions={1}, use_global_device_ids=true | all-gather | bytes 516096 | tf_op jit(solution)/shard_map/all_gather | solution.py:142
  117.1 1.0 fusion.73
  118.1 1.2 convolution_convert_fusion.2
  119.2 1.2 fusion.66
  120.4 242.8 %all-reduce.8.cloned.1.call-done = bf16[64,62146]{1,0:T(8,128)(2,1)} async-done(((bf16[64,62146]{1,0:T(8,128)(2,1)}), bf16[64,62146]{1,0:T(8,128)(2,1)}) %all-reduce.8.cloned.1.call-update) | async-done | bytes 7954704
  363.2 0.8 dynamic-slice.2
  364.1 0.8 dynamic-slice.4
  365.0 1.5 constant_dynamic-slice_fusion
  366.4 0.8 reshape.244
  367.2 1.2 fusion.14
  368.4 1.4 fusion.2
  369.8 1.1 fusion.5
  371.0 1.1 fusion.6
  372.1 1.2 fusion.11
  373.5 1.3 convolution_convert_fusion.1
  374.8 99.0 %reduce-scatter.3.cloned.1.call-done = bf16[128,224]{0,1:T(8,128)(2,1)} async-done(((bf16[128,1792]{0,1:T(8,128)(2,1)}), bf16[128,224]{0,1:T(8,128)(2,1)}) %reduce-scatter.3.cloned.1.call-update) | async-done | bytes 57360 | tf_op jit(solution)/shard_map/reduce_scatter | solution.py:199
  473.9 0.8 add_convert_fusion.1
  474.7 46.6 %all_gather.7 = bf16[128,1792]{0,1:T(8,128)(2,1)S(1)} all-gather(bf16[128,224]{0,1:T(8,128)(2,1)S(1)} %add_convert_fusion.1), channel_id=1, replica_groups=mesh['req'=32,'tp'=8] {'tp'}, dimensions={1}, use_global_device_ids=true | all-gather | bytes 516096 | tf_op jit(solution)/shard_map/all_gather | solution.py:203
  521.6 2.5 fusion.33
  524.1 4.9 convolution_convert_fusion
  529.0 79.6 %reduce-scatter.5.cloned.1.call-done = bf16[128,224]{0,1:T(8,128)(2,1)} async-done(((bf16[128,1792]{0,1:T(8,128)(2,1)}), bf16[128,224]{0,1:T(8,128)(2,1)}) %reduce-scatter.5.cloned.1.call-update) | async-done | bytes 57360 | tf_op jit(solution)/shard_map/reduce_scatter | solution.py:209
  608.6 1.5 add_convert_fusion
  (87 shorter events, 5.5 us)
Async XLA Ops:
  6.5 517.5 %copy-start = (bf16[608,1792]{1,0:T(8,128)(2,1)S(1)}, bf16[608,1792]{1,0:T(8,128)(2,1)}, u32[]{:S(2)}) copy-start(bf16[608,1792]{1,0:T(8,128)(2,1)} %param.37) | copy-start | bytes 6537220
  6.5 6.6 %copy-start.1 = (s32[32]{0:T(128)S(1)}, s32[32]{0:T(128)}, u32[]{:S(2)}) copy-start(s32[32]{0:T(128)} %param.23) | copy-start | bytes 388
  6.5 7.4 %copy-start.5 = (bf16[1,2,273,112]{3,1,2,0:T(2,128)(2,1)S(1)}, bf16[1,2,273,112]{3,1,2,0:T(2,128)(2,1)}, u32[]{:S(2)}) copy-start(bf16[1,2,273,112]{3,1,2,0:T(2,128)(2,1)} %param.24) | copy-start | bytes 366916
  6.5 7.7 %copy-start.8 = (bf16[1,2,273]{2,1,0:T(2,128)(2,1)S(1)}, bf16[1,2,273]{2,1,0:T(2,128)(2,1)}, u32[]{:S(2)}) copy-start(bf16[1,2,273]{2,1,0:T(2,128)(2,1)} %param.25) | copy-start | bytes 3280
  6.5 356.7 %all-reduce.8.cloned.1.call-start = ((), (), s32[]{:S(2)}) async-start(), calls=%async_computation.4 | async-start | bytes 15925248
  14.3 4.1 copy-start.9
  61.0 0.7 copy-start.17
  61.1 1.9 copy-start.10
  61.1 2.3 copy-start.3
  61.1 54.9 %copy-start.7 = (f32[3,224]{1,0:T(4,128)S(1)}, f32[3,224]{1,0:T(4,128)}, u32[]{:S(2)}) copy-start(f32[3,224]{1,0:T(4,128)} %param.33) | copy-start | bytes 8068
  61.1 54.9 %copy-start.13 = (bf16[1792,32]{0,1:T(8,128)(2,1)S(1)}, bf16[1792,32]{0,1:T(8,128)(2,1)}, u32[]{:S(2)}) copy-start(bf16[1792,32]{0,1:T(8,128)(2,1)} %param.29) | copy-start | bytes 344068
  61.1 54.9 %copy-start.15 = (f32[1792]{0:T(1024)S(1)}, f32[1792]{0:T(1024)}, u32[]{:S(2)}) copy-start(f32[1792]{0:T(1024)} %param.27) | copy-start | bytes 21508
  61.1 55.4 %copy-start.14 = (bf16[1792,32]{0,1:T(8,128)(2,1)S(1)}, bf16[1792,32]{0,1:T(8,128)(2,1)}, u32[]{:S(2)}) copy-start(bf16[1792,32]{0,1:T(8,128)(2,1)} %param.30) | copy-start | bytes 344068
  61.1 56.9 %copy-start.11 = (bf16[1792,224]{0,1:T(8,128)(2,1)S(1)}, bf16[1792,224]{0,1:T(8,128)(2,1)}, u32[]{:S(2)}) copy-start(bf16[1792,224]{0,1:T(8,128)(2,1)} %param.31) | copy-start | bytes 2408452
  61.1 412.7 %reduce-scatter.3.cloned.1.call-start = ((), (), s32[]{:S(2)}) async-start(), calls=%async_computation.2 | async-start | bytes 516096 | tf_op jit(solution)/shard_map/reduce_scatter | solution.py:199
  116.0 3.2 copy-start.12
  117.0 2.2 copy-start.6
  120.4 253.1 %copy-start.2 = (bf16[224,1792]{1,0:T(8,128)(2,1)S(1)}, bf16[224,1792]{1,0:T(8,128)(2,1)}, u32[]{:S(2)}) copy-start(bf16[224,1792]{1,0:T(8,128)(2,1)} %param.34) | copy-start | bytes 2408452
  367.2 6.1 copy-start.18
  368.4 105.5 %copy-start.4 = (bf16[128,224]{0,1:T(8,128)(2,1)S(1)}, bf16[128,224]{0,1:T(8,128)(2,1)}, u32[]{:S(2)}) copy-start(bf16[128,224]{0,1:T(8,128)(2,1)} %param.19) | copy-start | bytes 172036
  370.9 150.6 %copy-start.16 = (f32[1792]{0:T(1024)S(1)}, f32[1792]{0:T(1024)}, u32[]{:S(2)}) copy-start(f32[1792]{0:T(1024)} %param.28) | copy-start | bytes 21508
  374.8 233.8 %reduce-scatter.5.cloned.1.call-start = ((), (), s32[]{:S(2)}) async-start(), calls=%async_computation.3 | async-start | bytes 516096 | tf_op jit(solution)/shard_map/reduce_scatter | solution.py:209
Sparse Core Ops, SparseCore 0:
  61.3 301.9 all-reduce.7
  374.9 98.8 reduce-scatter.2
  529.1 79.4 reduce-scatter.4
where the time goes:
time: 618 us; the launch traced here: 617 us
  waiting for transfers between devices  421 us (68%)
  blocking collectives  97.7 us (16%)
  local copies, waits for them, and re-layouts  54.5 us (9%)
  matrix products  19.1 us (3%)
  between operations  14.1 us (2%)
  other arithmetic  9.57 us (2%)
    unnamed x4, waiting for transfers between devices  243 us
    reduce_scatter x1, waiting for transfers between devices, shards(): lax.psum_scatter(partial_value.astype(jnp.bfloat16), 'tp', scatter_dimens...  99 us
    reduce_scatter x1, waiting for transfers between devices, shards(): lax.psum_scatter(down_part.astype(jnp.bfloat16), 'tp', scatter_dimension=...  79.6 us
    all_gather x1, blocking collectives, shards(): full_rows = lax.all_gather(stream, 'tp', axis=1, tiled=True)  51.1 us
    all_gather x1, blocking collectives, shards(): wide_rows = lax.all_gather(own_rows, 'tp', axis=1, tiled=True)  46.6 us
    unnamed x41, local copies, waits for them, and re-layouts  42 us
  transfers between devices with their start and end apart: 3, of which 3 were waited for; matrix products, arithmetic and copies ran while one was open for 1% of the time, Pallas kernels for 0%

commit v1 on v0

v1 whole, which is shorter than its diff:
```python
import functools

import jax
import jax.numpy as jnp
import numpy as np
from jax import lax
from jax.experimental import pallas as pl
from jax.experimental.pallas import tpu as pltpu
from jax.sharding import PartitionSpec as P

EPSILON = 1e-05
ROWS = 160
LANES = 128
TAIL_ROW = 153
F32 = jnp.float32
BF16 = jnp.bfloat16

VMEM = pl.BlockSpec(memory_space=pltpu.VMEM)
SMEM = pl.BlockSpec(memory_space=pltpu.SMEM)
PARAMS = pltpu.CompilerParams(vmem_limit_bytes=48 * 1024 * 1024)


def call(kernel, out_shape, specs, args, scratch=(), name=None):
    single = not isinstance(out_shape, (list, tuple))
    return pl.pallas_call(
        kernel,
        out_shape=out_shape,
        in_specs=specs,
        out_specs=VMEM if single else [VMEM] * len(out_shape),
        scratch_shapes=list(scratch),
        compiler_params=PARAMS,
        name=name,
    )(*args)


def sds(shape, dtype):
    return jax.ShapeDtypeStruct(shape, dtype)


def fold_matrix(feat_dim, feat_count):
    fold = np.zeros((ROWS, feat_count), np.float32)
    row = 0
    for i in range(feat_dim):
        fold[row, 1 + i] = 1
        row += 1
    for gap in range(feat_dim // 2 + 1):
        for i in range(feat_dim if gap < feat_dim // 2 else feat_dim // 2):
            j = (i + gap) % feat_dim
            fold[row, 1 + feat_dim + feat_dim * i + j] = 1
            fold[row, 1 + feat_dim + feat_dim * j + i] = 1
            row += 1
    fold[row, 0] = 1
    return fold


def split_norm(total, head_dim):
    rounded = total.astype(BF16).astype(F32)
    lost = pltpu.roll(total - rounded, 1, axis=1)
    lane = lax.broadcasted_iota(jnp.int32, total.shape, 1)
    return jnp.where(lane == head_dim + 1, total + lost, total).astype(BF16)


def fold_kernel(fold_ref, state_ref, norm_ref, tail_ref, out_ref):
    heads, feats, head_dim = state_ref.shape
    fold = fold_ref[...]
    norms = lax.dot_general(fold, norm_ref[...], (((1,), (1,)), ((), ())), preferred_element_type=F32)
    lane = lax.broadcasted_iota(jnp.int32, (ROWS, LANES), 1)
    for h in range(heads):
        state = jnp.dot(fold, state_ref[h], preferred_element_type=F32)
        norm = jnp.broadcast_to(norms[:, h : h + 1], (ROWS, LANES))
        hi = norm.astype(BF16).astype(F32)
        cols = jnp.where(lane == head_dim, hi, jnp.where(lane == head_dim + 1, norm - hi, 0.0))
        out_ref[h] = cols.astype(BF16)
        out_ref[h, :, :head_dim] = state.astype(BF16)
        out_ref[h, TAIL_ROW : TAIL_ROW + 2, :head_dim] = tail_ref[h]


def select_kernel(groups, leaf_ref, parent_ref, owner_ref, dev_ref, mine_ref, other_ref, *rest):
    outs, pool = rest[:groups], rest[groups]
    held = mine_ref.shape[0]
    heads = mine_ref.shape[1]
    count = 2 * held
    for n in range(held):
        pool[n] = mine_ref[n]
        pool[held + n] = other_ref[n]
    pool[count] = jnp.zeros(pool.shape[1:], BF16)
    dev = dev_ref[0]
    total_dev = groups * count
    column = dev // count
    place = (dev % count) // 2
    core = dev % 2

    def slot(row):
        here = (row // count) == column
        at = (row % count) // 2
        k = lax.rem(place - at + held, held)
        k = k + jnp.where((row % 2) == core, 0, held)
        return jnp.where(here, k, count)

    per = leaf_ref.shape[0] // total_dev
    rows = lax.broadcasted_iota(jnp.int32, (ROWS, LANES), 0)
    is_tail = (rows >= TAIL_ROW) & (rows < TAIL_ROW + 2)
    for k in range(groups):
        target = lax.rem(dev + k * count, total_dev)
        for s in range(per):
            leaf = leaf_ref[target * per + s]
            middle = parent_ref[leaf]
            root = parent_ref[middle]
            at = [slot(owner_ref[n]) for n in (leaf, middle, root)]
            for h in range(heads):
                first, second, third = [pool[a, h].astype(F32) for a in at]
                total = first + jnp.where(is_tail, 0.0, second + third)
                outs[k][s, h] = split_norm(total, 112)


def place_blocks(scratch, blocks, half_ref):
    x = half_ref[0]
    z = half_ref[1]
    n = len(blocks)
    rows = blocks[0].shape[1]
    for k, block in enumerate(blocks):
        source = lax.rem(x - k + n, n)
        scratch[pl.ds(pl.multiple_of((2 * source + z) * rows, 32), rows), :] = block[0]
        scratch[pl.ds(pl.multiple_of((2 * source + 1 - z) * rows, 32), rows), :] = block[1]


def row_scale(scratch):
    rows = scratch[...].astype(F32)
    return lax.rsqrt(jnp.mean(rows * rows, axis=0, keepdims=True) + EPSILON)


def project_kernel(half_ref, own_ref, r1_ref, r2_ref, r3_ref, weight_ref, out_ref, scratch):
    place_blocks(scratch, [own_ref, r1_ref, r2_ref, r3_ref], half_ref)
    scale = row_scale(scratch)
    out_ref[...] = jnp.dot(weight_ref[...], scratch[...], preferred_element_type=F32) * scale


def silu(v):
    return v / (1.0 + jnp.exp(-v))


def mix_kernel(
    half_ref, first_ref, token_ref, proj_ref, taps_ref, p0_ref, p1_ref, p2_ref, p3_ref, out_weight_ref, *rest
):
    outs, attended_ref = rest[:4], rest[4]
    per, heads = p0_ref.shape[:2]
    head_dim = attended_ref.shape[0] // heads
    feat_dim = 16
    tokens = token_ref.shape[1]
    ids = token_ref[...]
    slot = jnp.where(ids >= first_ref[1], per, ids - first_ref[0])
    lane = lax.broadcasted_iota(jnp.int32, (1, tokens), 1)
    start = jnp.zeros((1, tokens), jnp.int32)
    for s in range(per):
        amount = jnp.sum((slot == s).astype(jnp.int32), axis=1, keepdims=True)
        start = start + jnp.where(slot > s, amount, 0)
    position = lane - start
    source = lax.broadcasted_iota(jnp.int32, (tokens, tokens), 0)
    target = lax.broadcasted_iota(jnp.int32, (tokens, tokens), 1)
    allowed = (source >= start) & (source <= target)
    width = heads * feat_dim
    payload_row = lax.broadcasted_iota(jnp.int32, (ROWS, tokens), 0)
    values_at = 2 * width
    gates_at = values_at + heads * head_dim
    for h in range(heads):
        query = proj_ref[h * feat_dim : (h + 1) * feat_dim, :]
        key = proj_ref[width + h * feat_dim : width + (h + 1) * feat_dim, :]
        value = proj_ref[values_at + h * head_dim : values_at + (h + 1) * head_dim, :].astype(BF16).astype(F32)
        gate = proj_ref[gates_at + h * head_dim : gates_at + (h + 1) * head_dim, :]
        linear = query * feat_dim ** (-0.25)
        blocks = [linear]
        for gap in range(feat_dim // 2):
            other = query if gap == 0 else pltpu.roll(query, feat_dim - gap, axis=0)
            blocks.append(query * other * (2.0 * feat_dim) ** (-0.5))
        half = feat_dim // 2
        blocks.append(query[:half] * query[half:] * (2.0 * feat_dim) ** (-0.5))
        one = (lax.broadcasted_iota(jnp.int32, (half, tokens), 0) == 0).astype(F32)
        blocks.append(one)
        feature = jnp.concatenate(blocks, axis=0)
        right = []
        states = []
        for s in range(per):
            total = (
                p0_ref[s, h].astype(F32) + p1_ref[s, h].astype(F32) + p2_ref[s, h].astype(F32) + p3_ref[s, h].astype(F32)
            )
            states.append(split_norm(total, head_dim))
            member = slot == s
            lag_one = (member & (position == 0) & (payload_row == TAIL_ROW + 1)).astype(F32)
            lag_two = (
                member
                & (
                    ((position == 0) & (payload_row == TAIL_ROW))
                    | ((position == 1) & (payload_row == TAIL_ROW + 1))
                )
            ).astype(F32)
            keep = jnp.where(member, feature, 0.0)
            right.append(jnp.concatenate([keep, lag_one, lag_two], axis=1).astype(BF16))
        state = jnp.concatenate(states, axis=0)
        reached = lax.dot_general(
            state, jnp.concatenate(right, axis=0), (((0,), (0,)), ((), ())), preferred_element_type=F32
        )
        prefix_num = reached[:head_dim, :tokens]
        prefix_den = reached[head_dim : head_dim + 1, :tokens] + reached[head_dim + 1 : head_dim + 2, :tokens]
        taps = taps_ref[h * head_dim : (h + 1) * head_dim, :]
        lagged_one = jnp.where(position >= 1, pltpu.roll(value, 1, axis=1), reached[:head_dim, tokens : 2 * tokens])
        lagged_two = jnp.where(
            position >= 2, pltpu.roll(value, 2, axis=1), reached[:head_dim, 2 * tokens : 3 * tokens]
        )
        conv = taps[:, 0:1] * value + taps[:, 1:2] * lagged_one + taps[:, 2:3] * lagged_two
        mixed = (conv * silu(gate)).astype(BF16)
        dots = lax.dot_general(
            key, query, (((0,), (0,)), ((), ())), preferred_element_type=F32, precision=lax.Precision.HIGHEST
        )
        scores = jnp.where(allowed, 1.0 + dots * feat_dim ** (-0.5) + dots * dots * (1.0 / (2.0 * feat_dim)), 0.0)
        local_den = jnp.sum(scores, axis=0, keepdims=True)
        local_num = jnp.dot(mixed, scores.astype(BF16), preferred_element_type=F32)
        attended_ref[h * head_dim : (h + 1) * head_dim, :] = (
            (local_num + prefix_num) / (local_den + prefix_den)
        ).astype(BF16)
    spread_blocks(outs, out_weight_ref, attended_ref[...], half_ref)


def spread_blocks(outs, weight_ref, right, half_ref):
    x = half_ref[0]
    z = half_ref[1]
    n = len(outs)
    rows = outs[0].shape[1]
    for k, out in enumerate(outs):
        to = lax.rem(x + k, n)
        for half, at in ((0, 2 * to + z), (1, 2 * to + 1 - z)):
            block = weight_ref[pl.ds(pl.multiple_of(at * rows, 32), rows), :]
            out[half] = jnp.dot(block, right, preferred_element_type=F32).astype(out.dtype)


def ffn_kernel(half_ref, own_ref, r1_ref, r2_ref, r3_ref, gate_ref, up_ref, down_ref, *rest):
    outs, scratch = rest[:4], rest[4]
    place_blocks(scratch, [own_ref, r1_ref, r2_ref, r3_ref], half_ref)
    scale = row_scale(scratch)
    gate = jnp.dot(gate_ref[...], scratch[...], preferred_element_type=F32) * scale
    up = jnp.dot(up_ref[...], scratch[...], preferred_element_type=F32) * scale
    spread_blocks(outs, down_ref, (silu(gate) * up).astype(BF16), half_ref)


def shards(
    stream, token_req, request_leaf, parent, owner_map, node_state, node_norm, node_tail, mixer_gain, ffn_gain,
    query_weight, key_weight, value_weight, conv_gate_weight, conv_kernel, out_weight, ffn_gate, ffn_up, ffn_down,
):
    tokens, width = stream.shape
    heads, feats, head_dim = node_state.shape[1:]
    feat_dim = query_weight.shape[1] // heads
    model = value_weight.shape[0]
    req_size = lax.axis_size("req")
    tp_size = lax.axis_size("tp")
    x_size = tp_size // 2
    y_size, z_size = 4, req_size // 8
    per = request_leaf.shape[0] // req_size
    dev = lax.axis_index("req")
    tp = lax.axis_index("tp")
    halves = jnp.stack([tp // 2, tp % 2]).astype(jnp.int32)

    def along_x(array, k):
        return lax.ppermute(array, "tp", [(i, ((i // 2 + k) % x_size) * 2 + i % 2) for i in range(tp_size)])

    def across_z(array):
        return lax.ppermute(array, "tp", [(i, i ^ 1) for i in range(tp_size)])

    def along_z(array, k):
        count = 2 * z_size
        return lax.ppermute(
            array, "req", [(i, (i // count) * count + (((i % count) // 2 + k) % z_size) * 2 + i % 2) for i in range(req_size)]
        )

    def across_core(array):
        return lax.ppermute(array, "req", [(i, i ^ 1) for i in range(req_size)])

    def along_y(array, k):
        return lax.ppermute(array, "req", [(i, (i + 2 * z_size * k) % req_size) for i in range(req_size)])

    order = (1, 3, 2)

    fold = jnp.asarray(fold_matrix(feat_dim, feats), BF16)
    tails = jnp.transpose(node_tail[0].reshape(2, heads, head_dim), (1, 0, 2))
    payload = call(
        fold_kernel, sds((heads, ROWS, LANES), BF16), [VMEM] * 4, (fold, node_state[0], node_norm[0], tails), name="fold"
    )
    from_z = {k: along_z(payload, k) for k in order}

    own = stream.T
    pair = jnp.stack([own, across_z(own)])

    mine = jnp.stack([payload, from_z[1], from_z[2], from_z[3]])
    other = across_core(mine)
    shares = call(
        functools.partial(select_kernel, y_size),
        [sds((per, heads, ROWS, LANES), BF16)] * y_size,
        [SMEM] * 4 + [VMEM] * 2,
        (request_leaf, parent, owner_map, dev.reshape(1), mine, other),
        scratch=[pltpu.VMEM((2 * z_size + 1, heads, ROWS, LANES), BF16)],
        name="select",
    )
    from_y = {k: along_y(shares[k], k) for k in order}

    rows = {k: along_x(pair, k) for k in order}
    weights = (
        jnp.concatenate([query_weight.T, key_weight.T, value_weight.T, conv_gate_weight.T], axis=0).astype(F32)
        * mixer_gain[None, :]
    ).astype(BF16)
    proj = call(
        project_kernel,
        sds((weights.shape[0], tokens), F32),
        [SMEM] + [VMEM] * 5,
        (halves, pair, rows[1], rows[2], rows[3], weights),
        scratch=[pltpu.VMEM((model, tokens), BF16)],
        name="project",
    )
    first = jnp.stack([dev * per, jnp.int32(request_leaf.shape[0])]).astype(jnp.int32)
    parts = call(
        mix_kernel,
        [sds((2, width, tokens), F32)] + [sds((2, width, tokens), BF16)] * (x_size - 1),
        [SMEM] * 2 + [VMEM] * 8,
        (
            halves, first, token_req.reshape(1, tokens), proj, conv_kernel.T,
            shares[0], from_y[1], from_y[2], from_y[3], out_weight.T,
        ),
        scratch=[pltpu.VMEM((width, tokens), BF16)],
        name="mix",
    )
    got = {k: along_x(parts[k], k) for k in order}
    share = parts[0] + got[1].astype(F32) + got[2].astype(F32) + got[3].astype(F32)
    share_peer = across_z(jnp.stack([share[1], share[0]]).astype(BF16))
    updated = (pair.astype(F32) + share + share_peer.astype(F32)).astype(BF16)

    wide = {k: along_x(updated, k) for k in order}
    gate_scaled = (ffn_gate.T.astype(F32) * ffn_gain[None, :]).astype(BF16)
    up_scaled = (ffn_up.T.astype(F32) * ffn_gain[None, :]).astype(BF16)
    downs = call(
        ffn_kernel,
        [sds((2, width, tokens), F32)] + [sds((2, width, tokens), BF16)] * (x_size - 1),
        [SMEM] + [VMEM] * 7,
        (halves, updated, wide[1], wide[2], wide[3], gate_scaled, up_scaled, ffn_down.T),
        scratch=[pltpu.VMEM((model, tokens), BF16)],
        name="ffn",
    )
    back = {k: along_x(downs[k], k) for k in order}
    down_share = downs[0] + back[1].astype(F32) + back[2].astype(F32) + back[3].astype(F32)
    down_peer = across_z(down_share[1].astype(BF16))
    result = updated[0].astype(F32) + down_share[0] + down_peer.astype(F32)
    return result.astype(BF16).T


def solution(mesh):
    in_specs = (
        P("req", "tp"), P("req"), P(), P(), P(), P("req", "tp", None, None), P("req", "tp", None), P("req", None, "tp"),
        P(), P(), P(None, "tp"), P(None, "tp"), P(None, "tp"), P(None, "tp"), P(None, "tp"), P("tp", None),
        P(None, "tp"), P(None, "tp"), P("tp", None),
    )
    return jax.shard_map(shards, mesh=mesh, in_specs=in_specs, out_specs=P("req", "tp"), check_vma=False)
```

time: 618 us -> 96.6 us (0.16)
  waiting for transfers between devices: 421 us -> 30.1 us
  blocking collectives: 97.7 us -> 0 us
  local copies, waits for them, and re-layouts: 54.5 us -> 12.2 us
  starting transfers between devices: 0.12 us -> 37.6 us
  matrix products: 19.1 us -> 0 us
  between operations: 14.1 us -> 0.21 us
  Pallas kernels: 0 us -> 9.98 us
    unnamed x4 -> x0, waiting for transfers between devices: 243 us -> none
    reduce_scatter x2 -> x0, waiting for transfers between devices: 179 us -> none  [the longest x1 99 us: shards(): lax.psum_scatter(partial_value.astype(jnp.bfloat16), 'tp', scatter_dimens...]
    all_gather x2 -> x0, blocking collectives: 97.7 us -> none  [the longest x1 51.1 us: shards(): full_rows = lax.all_gather(stream, 'tp', axis=1, tiled=True)]
    ppermute x0 -> x22, starting transfers between devices: none -> 37.6 us  [the longest x12 19.9 us: along_x(): lax.ppermute(array, 'tp', [(i, (i // 2 + k) % x_size * 2 + i % 2) for i i...]
    unnamed x41 -> x32, local copies, waits for them, and re-layouts: 42 us -> 11.4 us
    ppermute x0 -> x22, waiting for transfers between devices: none -> 30.1 us  [the longest x3 15.9 us: across_z(): return lax.ppermute(array, 'tp', [(i, i ^ 1) for i in range(tp_size)])]
    dot_general x14 -> x0, matrix products: 19.1 us -> none  [the longest x1 4.93 us: shards(): down_part = jnp.dot(activated, ffn_down, preferred_element_type=jnp.float32)]
    pallas_call x0 -> x5, Pallas kernels: none -> 9.98 us  [call(): pl.pallas_call(kernel, out_shape=out_shape, in_specs=specs, out_specs=VME...]
  transfers between devices with their start and end apart: 3 -> 22, of which waited for: 3 -> 11; matrix products, arithmetic and copies ran while one was open for 1% -> 13% of each run, Pallas kernels for 0% -> 4%
where the time goes in v1:
time: 96.6 us; the launch traced here: 96 us
  starting transfers between devices  37.6 us (39%)
  waiting for transfers between devices  30.1 us (31%)
  local copies, waits for them, and re-layouts  12.2 us (13%)
  Pallas kernels  9.98 us (10%)
  other arithmetic  5.87 us (6%)
    ppermute x12, starting transfers between devices, along_x(): lax.ppermute(array, 'tp', [(i, (i // 2 + k) % x_size * 2 + i % 2) for i i...  19.9 us
    ppermute x3, waiting for transfers between devices, across_z(): return lax.ppermute(array, 'tp', [(i, i ^ 1) for i in range(tp_size)])  15.9 us
    unnamed x32, local copies, waits for them, and re-layouts  11.4 us
    pallas_call x5, Pallas kernels, call(): pl.pallas_call(kernel, out_shape=out_shape, in_specs=specs, out_specs=VME...  9.98 us
    ppermute x3, starting transfers between devices, across_z(): return lax.ppermute(array, 'tp', [(i, i ^ 1) for i in range(tp_size)])  9.11 us
    ppermute x12, waiting for transfers between devices, along_x(): lax.ppermute(array, 'tp', [(i, (i // 2 + k) % x_size * 2 + i % 2) for i i...  8.79 us
    ppermute x3, starting transfers between devices, along_y(): lax.ppermute(array, 'req', [(i, (i + 2 * z_size * k) % req_size) for i in...  4.93 us
    ppermute x3, starting transfers between devices, along_z(): lax.ppermute(array, 'req', [(i, i // count * count + (i % count // 2 + k)...  3.58 us
  transfers between devices with their start and end apart: 22, of which 11 were waited for; matrix products, arithmetic and copies ran while one was open for 13% of the time, Pallas kernels for 4%

profile of v1, /device:TPU:8, one launch (start us, length us, event | category | flops | bytes accessed | tf_op | source)
XLA Modules:
  0.0 96.0 jit_solution(1894297116877340000)
XLA Ops:
  0.0 7.2 %collective-permute-start = (bf16[224,128]{1,0:T(8,128)(2,1)}, bf16[224,128]{1,0:T(8,128)(2,1)S(1)}, u32[]{:S(2)}, u32[]{:S(2)}) collective-permute-start(bf16[224,128]{1,0:T(8,128)(2,1)} %bitcast.53), channel_id=1, source_target_pairs={{0,1},{1,0},{2,3},{3,2},{4,5},{5,4},{6,7},{7,6},{8,9},{9,8},{10,11... | collective-permute-start | bytes 172040 | tf_op jit(solution)/shard_map/ppermute | solution.py:265
  8.0 0.9 copy.32
  10.8 2.0 %collective-permute-start.6 = (bf16[2,160,128]{2,1,0:T(8,128)(2,1)S(1)}, bf16[2,160,128]{2,1,0:T(8,128)(2,1)S(1)}, u32[]{:S(2)}, u32[]{:S(2)}) collective-permute-start(bf16[2,160,128]{2,1,0:T(8,128)(2,1)S(1)} %fold.1), channel_id=1, source_target_pairs={{0,48},{8,56},{16,0},{24,8},{32,16},{40,24},{48,32},{56,40},{64,11... | collective-permute-start | bytes 245768 | tf_op jit(solution)/shard_map/ppermute | solution.py:269
  13.3 1.0 %collective-permute-start.4 = (bf16[2,160,128]{2,1,0:T(8,128)(2,1)S(1)}, bf16[2,160,128]{2,1,0:T(8,128)(2,1)S(1)}, u32[]{:S(2)}, u32[]{:S(2)}) collective-permute-start(bf16[2,160,128]{2,1,0:T(8,128)(2,1)S(1)} %fold.1), channel_id=1, source_target_pairs={{0,16},{8,24},{16,32},{24,40},{32,48},{40,56},{48,0},{56,8},{64,80... | collective-permute-start | bytes 245768 | tf_op jit(solution)/shard_map/ppermute | solution.py:269
  15.2 2.8 %collective-permute-start.3 = (bf16[2,224,128]{2,1,0:T(8,128)(2,1)S(1)}, bf16[2,224,128]{2,1,0:T(8,128)(2,1)S(1)}, u32[]{:S(2)}, u32[]{:S(2)}) collective-permute-start(bf16[2,224,128]{2,1,0:T(8,128)(2,1)S(1)} %pad_maximum_fusion.1.own_ref), channel_id=1, source_target_pairs={{0,6},{1,7},{2,0},{3,1},{4,2},{5,3},{6,4},{7,5},{8,14},{9,15},{10,... | collective-permute-start | bytes 344072 | tf_op jit(solution)/shard_map/ppermute | solution.py:262
  18.1 2.9 %collective-permute-done.5 = bf16[2,160,128]{2,1,0:T(8,128)(2,1)S(1)} collective-permute-done((bf16[2,160,128]{2,1,0:T(8,128)(2,1)S(1)}, bf16[2,160,128]{2,1,0:T(8,128)(2,1)S(1)}, u32[]{:S(2)}, u32[]{:S(2)}) %collective-permute-start.5) | collective-permute-done | bytes 81952 | tf_op jit(solution)/shard_map/ppermute | solution.py:269
  21.2 1.7 %multiply_convert_fusion.2.weight_ref = bf16[512,1792]{1,0:T(8,128)(2,1)S(1)} fusion(bf16[224,1792]{1,0:T(8,128)(2,1)} %bitcast.51, bf16[224,1792]{1,0:T(8,128)(2,1)} %bitcast.52, bf16[32,1792]{1,0:T(8,128)(2,1)} %bitcast.58, bf16[32,1792]{1,0:T(8,128)(2,1)} %bitcast.59, f32[1792]{0:T(1024)} %param.28), kind=kLoop, calls=%fused_computation.2 | loop fusion | flops 9175040 | bytes 3677184 | tf_op jit(solution)/shard_map/convert_element_type | solution.py:307
  22.9 3.1 %collective-permute-start.2 = (bf16[2,224,128]{2,1,0:T(8,128)(2,1)S(1)}, bf16[2,224,128]{2,1,0:T(8,128)(2,1)}, u32[]{:S(2)}, u32[]{:S(2)}) collective-permute-start(bf16[2,224,128]{2,1,0:T(8,128)(2,1)S(1)} %pad_maximum_fusion.1.own_ref), channel_id=1, source_target_pairs={{0,4},{1,5},{2,6},{3,7},{4,0},{5,1},{6,2},{7,3},{8,12},{9,13},{10,... | collective-permute-start | bytes 344072 | tf_op jit(solution)/shard_map/ppermute | solution.py:262
  26.6 1.8 %select.7 = (bf16[2,2,160,128]{3,2,1,0:T(8,128)(2,1)S(1)}, bf16[2,2,160,128]{3,2,1,0:T(8,128)(2,1)}, bf16[2,2,160,128]{3,2,1,0:T(8,128)(2,1)}, bf16[2,2,160,128]{3,2,1,0:T(8,128)(2,1)}) custom-call(s32[64]{0:T(128)S(1)} %copy-done.5, s32[32]{0:T(128)S(1)} %copy-done.6, s32[32]{0:T(128)S(1)} %copy-done.7, s32[1]{0:T(128)} %bitcast.12.dev_ref, ...), custom_call_target="tpu_custom_call" | custom-call | tf_op jit(solution)/shard_map/select/pallas_call | solution.py:25
  28.5 1.6 %collective-permute-start.8 = (bf16[2,2,160,128]{3,2,1,0:T(8,128)(2,1)}, bf16[2,2,160,128]{3,2,1,0:T(8,128)(2,1)S(1)}, u32[]{:S(2)}, u32[]{:S(2)}) collective-permute-start(bf16[2,2,160,128]{3,2,1,0:T(8,128)(2,1)} %get-tuple-element.18), channel_id=1, source_target_pairs={{0,64},{8,72},{16,80},{24,88},{32,96},{40,104},{48,112},{56,120},{... | collective-permute-start | bytes 491528 | tf_op jit(solution)/shard_map/ppermute | solution.py:277
  30.1 0.9 collective-permute-start.9
  31.6 2.4 %collective-permute-start.10 = (bf16[2,2,160,128]{3,2,1,0:T(8,128)(2,1)}, bf16[2,2,160,128]{3,2,1,0:T(8,128)(2,1)}, u32[]{:S(2)}, u32[]{:S(2)}) collective-permute-start(bf16[2,2,160,128]{3,2,1,0:T(8,128)(2,1)} %get-tuple-element.20), channel_id=1, source_target_pairs={{0,192},{8,200},{16,208},{24,216},{32,224},{40,232},{48,240},{56,2... | collective-permute-start | bytes 491528 | tf_op jit(solution)/shard_map/ppermute | solution.py:277
  34.2 1.4 %copy.28 = bf16[224,1792]{0,1:T(8,128)(2,1)S(1)} copy(bf16[224,1792]{1,0:T(8,128)(2,1)} %param.35) | data formatting | bytes 1605632 | tf_op args[15]
  36.7 1.8 %project.1.proj_ref = f32[512,128]{1,0:T(8,128)S(1)} custom-call(s32[2]{0:T(128)S(1)} %pad_add_fusion.half_ref, bf16[2,224,128]{2,1,0:T(8,128)(2,1)S(1)} %pad_maximum_fusion.1.own_ref, bf16[2,224,128]{2,1,0:T(8,128)(2,1)} %collective-permute-done.1.r1_ref, bf16[2,224,128]{2,1,0:T(8,128)(2,1)} %collective-permute-done.2.r2_ref, ...), custom_call_target="tpu_custom_call" | custom-call | tf_op jit(solution)/shard_map/project/pallas_call | solution.py:25
  38.9 2.2 %collective-permute-done.10.p3_ref = bf16[2,2,160,128]{3,2,1,0:T(8,128)(2,1)} collective-permute-done((bf16[2,2,160,128]{3,2,1,0:T(8,128)(2,1)}, bf16[2,2,160,128]{3,2,1,0:T(8,128)(2,1)}, u32[]{:S(2)}, u32[]{:S(2)}) %collective-permute-start.10) | collective-permute-done | bytes 163872 | tf_op jit(solution)/shard_map/ppermute | solution.py:277
  41.1 2.3 %mix.1 = (f32[2,224,128]{2,1,0:T(8,128)S(1)}, bf16[2,224,128]{2,1,0:T(8,128)(2,1)S(1)}, bf16[2,224,128]{2,1,0:T(8,128)(2,1)S(1)}, bf16[2,224,128]{2,1,0:T(8,128)(2,1)S(1)}) custom-call(s32[2]{0:T(128)S(1)} %pad_add_fusion.half_ref, s32[2]{0:T(128)S(1)} %pad_add_fusion.1.first_ref, s32[1,128]{1,0:T(1,128)S(1)} %bitcast.49, f32[512,128]{1,0:T(8,128)S(1)} %project.1.proj_ref, ...), custom_call_target="tpu_custom_call" | custom-call | tf_op jit(solution)/shard_map/mix/pallas_call | solution.py:25
  43.8 3.8 %collective-permute-start.12 = (bf16[2,224,128]{2,1,0:T(8,128)(2,1)S(1)}, bf16[2,224,128]{2,1,0:T(8,128)(2,1)S(1)}, u32[]{:S(2)}, u32[]{:S(2)}) collective-permute-start(bf16[2,224,128]{2,1,0:T(8,128)(2,1)S(1)} %get-tuple-element.23), channel_id=1, source_target_pairs={{0,4},{1,5},{2,6},{3,7},{4,0},{5,1},{6,2},{7,3},{8,12},{9,13},{10,... | collective-permute-start | bytes 344072 | tf_op jit(solution)/shard_map/ppermute | solution.py:262
  48.1 1.7 %collective-permute-done.11 = bf16[2,224,128]{2,1,0:T(8,128)(2,1)S(1)} collective-permute-done((bf16[2,224,128]{2,1,0:T(8,128)(2,1)S(1)}, bf16[2,224,128]{2,1,0:T(8,128)(2,1)S(1)}, u32[]{:S(2)}, u32[]{:S(2)}) %collective-permute-start.11) | collective-permute-done | bytes 114720 | tf_op jit(solution)/shard_map/ppermute | solution.py:262
  49.8 3.2 %collective-permute-done.12 = bf16[2,224,128]{2,1,0:T(8,128)(2,1)S(1)} collective-permute-done((bf16[2,224,128]{2,1,0:T(8,128)(2,1)S(1)}, bf16[2,224,128]{2,1,0:T(8,128)(2,1)S(1)}, u32[]{:S(2)}, u32[]{:S(2)}) %collective-permute-start.12) | collective-permute-done | bytes 114720 | tf_op jit(solution)/shard_map/ppermute | solution.py:262
  53.1 1.1 %collective-permute-start.14 = (bf16[2,224,128]{2,1,0:T(8,128)(2,1)S(1)}, bf16[2,224,128]{2,1,0:T(8,128)(2,1)S(1)}, u32[]{:S(2)}, u32[]{:S(2)}) collective-permute-start(bf16[2,224,128]{2,1,0:T(8,128)(2,1)S(1)} %pad_maximum_fusion.2), channel_id=1, source_target_pairs={{0,1},{1,0},{2,3},{3,2},{4,5},{5,4},{6,7},{7,6},{8,9},{9,8},{10,11... | collective-permute-start | bytes 344072 | tf_op jit(solution)/shard_map/ppermute | solution.py:265
  54.2 8.2 %collective-permute-done.14 = bf16[2,224,128]{2,1,0:T(8,128)(2,1)S(1)} collective-permute-done((bf16[2,224,128]{2,1,0:T(8,128)(2,1)S(1)}, bf16[2,224,128]{2,1,0:T(8,128)(2,1)S(1)}, u32[]{:S(2)}, u32[]{:S(2)}) %collective-permute-start.14) | collective-permute-done | bytes 114720 | tf_op jit(solution)/shard_map/ppermute | solution.py:265
  62.6 2.2 %collective-permute-start.17 = (bf16[2,224,128]{2,1,0:T(8,128)(2,1)S(1)}, bf16[2,224,128]{2,1,0:T(8,128)(2,1)S(1)}, u32[]{:S(2)}, u32[]{:S(2)}) collective-permute-start(bf16[2,224,128]{2,1,0:T(8,128)(2,1)S(1)} %add_convert_fusion.own_ref), channel_id=1, source_target_pairs={{0,6},{1,7},{2,0},{3,1},{4,2},{5,3},{6,4},{7,5},{8,14},{9,15},{10,... | collective-permute-start | bytes 344072 | tf_op jit(solution)/shard_map/ppermute | solution.py:262
  65.9 2.2 %fusion.1 = (bf16[608,1792]{1,0:T(8,128)(2,1)S(1)}, bf16[608,1792]{1,0:T(8,128)(2,1)}) fusion(bf16[1792,608]{0,1:T(8,128)(2,1)S(1)} %copy-done.9, f32[1792]{0:T(1024)S(1)} %copy-done.12, bf16[1792,608]{0,1:T(8,128)(2,1)S(1)} %copy-done.10), kind=kLoop, calls=%fused_computation.4 | loop fusion | flops 6537216 | bytes 8723456 | tf_op jit(solution)/shard_map/convert_element_type | solution.py:335
  68.1 4.1 %copy.29 = bf16[608,1792]{0,1:T(8,128)(2,1)} copy(bf16[608,1792]{1,0:T(8,128)(2,1)} %param.38) | data formatting | bytes 4358144 | tf_op args[18]
  72.5 1.6 %copy-done = bf16[608,1792]{1,0:T(8,128)(2,1)S(1)} copy-done((bf16[608,1792]{1,0:T(8,128)(2,1)S(1)}, bf16[608,1792]{1,0:T(8,128)(2,1)}, u32[]{:S(2)}) %copy-start) | copy-done | bytes 2179096
  74.1 3.7 %ffn.1 = (f32[2,224,128]{2,1,0:T(8,128)S(1)}, bf16[2,224,128]{2,1,0:T(8,128)(2,1)S(1)}, bf16[2,224,128]{2,1,0:T(8,128)(2,1)S(1)}, bf16[2,224,128]{2,1,0:T(8,128)(2,1)S(1)}) custom-call(s32[2]{0:T(128)S(1)} %pad_add_fusion.half_ref, bf16[2,224,128]{2,1,0:T(8,128)(2,1)S(1)} %add_convert_fusion.own_ref, ...), custom_call_target="tpu_custom_call" | custom-call | tf_op jit(solution)/shard_map/ffn/pallas_call | solution.py:25
  77.8 2.2 %collective-permute-start.18 = (bf16[2,224,128]{2,1,0:T(8,128)(2,1)S(1)}, bf16[2,224,128]{2,1,0:T(8,128)(2,1)S(1)}, u32[]{:S(2)}, u32[]{:S(2)}) collective-permute-start(bf16[2,224,128]{2,1,0:T(8,128)(2,1)S(1)} %get-tuple-element.26), channel_id=1, source_target_pairs={{0,2},{1,3},{2,4},{3,5},{4,6},{5,7},{6,0},{7,1},{8,10},{9,11},{10,... | collective-permute-start | bytes 344072 | tf_op jit(solution)/shard_map/ppermute | solution.py:262
  80.0 2.0 %collective-permute-start.19 = (bf16[2,224,128]{2,1,0:T(8,128)(2,1)S(1)}, bf16[2,224,128]{2,1,0:T(8,128)(2,1)S(1)}, u32[]{:S(2)}, u32[]{:S(2)}) collective-permute-start(bf16[2,224,128]{2,1,0:T(8,128)(2,1)S(1)} %get-tuple-element.27), channel_id=1, source_target_pairs={{0,4},{1,5},{2,6},{3,7},{4,0},{5,1},{6,2},{7,3},{8,12},{9,13},{10,... | collective-permute-start | bytes 344072 | tf_op jit(solution)/shard_map/ppermute | solution.py:262
  82.1 1.2 %collective-permute-start.20 = (bf16[2,224,128]{2,1,0:T(8,128)(2,1)S(1)}, bf16[2,224,128]{2,1,0:T(8,128)(2,1)S(1)}, u32[]{:S(2)}, u32[]{:S(2)}) collective-permute-start(bf16[2,224,128]{2,1,0:T(8,128)(2,1)S(1)} %get-tuple-element.28), channel_id=1, source_target_pairs={{0,6},{1,7},{2,0},{3,1},{4,2},{5,3},{6,4},{7,5},{8,14},{9,15},{10,... | collective-permute-start | bytes 344072 | tf_op jit(solution)/shard_map/ppermute | solution.py:262
  83.2 1.4 %collective-permute-done.18 = bf16[2,224,128]{2,1,0:T(8,128)(2,1)S(1)} collective-permute-done((bf16[2,224,128]{2,1,0:T(8,128)(2,1)S(1)}, bf16[2,224,128]{2,1,0:T(8,128)(2,1)S(1)}, u32[]{:S(2)}, u32[]{:S(2)}) %collective-permute-start.18) | collective-permute-done | bytes 114720 | tf_op jit(solution)/shard_map/ppermute | solution.py:262
  84.6 1.7 %collective-permute-done.19 = bf16[2,224,128]{2,1,0:T(8,128)(2,1)S(1)} collective-permute-done((bf16[2,224,128]{2,1,0:T(8,128)(2,1)S(1)}, bf16[2,224,128]{2,1,0:T(8,128)(2,1)S(1)}, u32[]{:S(2)}, u32[]{:S(2)}) %collective-permute-start.19) | collective-permute-done | bytes 114720 | tf_op jit(solution)/shard_map/ppermute | solution.py:262
  87.7 7.6 %collective-permute-done.21 = bf16[224,128]{1,0:T(8,128)(2,1)S(1)} collective-permute-done((bf16[224,128]{1,0:T(8,128)(2,1)S(1)}, bf16[224,128]{1,0:T(8,128)(2,1)S(1)}, u32[]{:S(2)}, u32[]{:S(2)}) %collective-permute-start.21) | collective-permute-done | bytes 57376 | tf_op jit(solution)/shard_map/ppermute | solution.py:265
  (64 shorter events, 11.5 us)
Async XLA Ops:
  0.0 14.3 %collective-permute-start = (bf16[224,128]{1,0:T(8,128)(2,1)}, bf16[224,128]{1,0:T(8,128)(2,1)S(1)}, u32[]{:S(2)}, u32[]{:S(2)}) collective-permute-start(bf16[224,128]{1,0:T(8,128)(2,1)} %bitcast.53), channel_id=1, source_target_pairs={{0,1},{1,0},{2,3},{3,2},{4,5},{5,4},{6,7},{7,6},{8,9},{9,8},{10,11... | collective-permute-start | bytes 172040 | tf_op jit(solution)/shard_map/ppermute | solution.py:265
  10.8 7.3 %collective-permute-start.6 = (bf16[2,160,128]{2,1,0:T(8,128)(2,1)S(1)}, bf16[2,160,128]{2,1,0:T(8,128)(2,1)S(1)}, u32[]{:S(2)}, u32[]{:S(2)}) collective-permute-start(bf16[2,160,128]{2,1,0:T(8,128)(2,1)S(1)} %fold.1), channel_id=1, source_target_pairs={{0,48},{8,56},{16,0},{24,8},{32,16},{40,24},{48,32},{56,40},{64,11... | collective-permute-start | bytes 245768 | tf_op jit(solution)/shard_map/ppermute | solution.py:269
  12.8 8.2 %collective-permute-start.5 = (bf16[2,160,128]{2,1,0:T(8,128)(2,1)S(1)}, bf16[2,160,128]{2,1,0:T(8,128)(2,1)S(1)}, u32[]{:S(2)}, u32[]{:S(2)}) collective-permute-start(bf16[2,160,128]{2,1,0:T(8,128)(2,1)S(1)} %fold.1), channel_id=1, source_target_pairs={{0,32},{8,40},{16,48},{24,56},{32,0},{40,8},{48,16},{56,24},{64,96... | collective-permute-start | bytes 245768 | tf_op jit(solution)/shard_map/ppermute | solution.py:269
  13.3 7.7 %collective-permute-start.4 = (bf16[2,160,128]{2,1,0:T(8,128)(2,1)S(1)}, bf16[2,160,128]{2,1,0:T(8,128)(2,1)S(1)}, u32[]{:S(2)}, u32[]{:S(2)}) collective-permute-start(bf16[2,160,128]{2,1,0:T(8,128)(2,1)S(1)} %fold.1), channel_id=1, source_target_pairs={{0,16},{8,24},{16,32},{24,40},{32,48},{40,56},{48,0},{56,8},{64,80... | collective-permute-start | bytes 245768 | tf_op jit(solution)/shard_map/ppermute | solution.py:269
  14.3 12.3 %copy-start.5 = (s32[64]{0:T(128)S(1)}, s32[64]{0:T(128)}, u32[]{:S(2)}) copy-start(s32[64]{0:T(128)} %leaf_ref.1) | copy-start | bytes 772
  14.3 12.3 %copy-start.6 = (s32[32]{0:T(128)S(1)}, s32[32]{0:T(128)}, u32[]{:S(2)}) copy-start(s32[32]{0:T(128)} %parent_ref.1) | copy-start | bytes 388
  14.3 12.3 %copy-start.7 = (s32[32]{0:T(128)S(1)}, s32[32]{0:T(128)}, u32[]{:S(2)}) copy-start(s32[32]{0:T(128)} %owner_ref.1) | copy-start | bytes 388
  15.2 15.8 %collective-permute-start.3 = (bf16[2,224,128]{2,1,0:T(8,128)(2,1)S(1)}, bf16[2,224,128]{2,1,0:T(8,128)(2,1)S(1)}, u32[]{:S(2)}, u32[]{:S(2)}) collective-permute-start(bf16[2,224,128]{2,1,0:T(8,128)(2,1)S(1)} %pad_maximum_fusion.1.own_ref), channel_id=1, source_target_pairs={{0,6},{1,7},{2,0},{3,1},{4,2},{5,3},{6,4},{7,5},{8,14},{9,15},{10,... | collective-permute-start | bytes 344072 | tf_op jit(solution)/shard_map/ppermute | solution.py:262
  21.1 13.1 %copy-start.13 = (f32[3,224]{1,0:T(4,128)S(1)}, f32[3,224]{1,0:T(4,128)}, u32[]{:S(2)}) copy-start(f32[3,224]{1,0:T(4,128)} %param.34) | copy-start | bytes 8068
  21.1 5.6 %collective-permute-start.7 = (bf16[4,2,160,128]{3,2,1,0:T(8,128)(2,1)S(1)}, bf16[4,2,160,128]{3,2,1,0:T(8,128)(2,1)S(1)}, u32[]{:S(2)}, u32[]{:S(2)}) collective-permute-start(bf16[4,2,160,128]{3,2,1,0:T(8,128)(2,1)S(1)} %pad_maximum_fusion.mine_ref), channel_id=1, source_target_pairs={{0,8},{8,0},{16,24},{24,16},{32,40},{40,32},{48,56},{56,48},{64,72... | collective-permute-start | bytes 983048 | tf_op jit(solution)/shard_map/ppermute | solution.py:274
  22.9 12.9 %collective-permute-start.2 = (bf16[2,224,128]{2,1,0:T(8,128)(2,1)S(1)}, bf16[2,224,128]{2,1,0:T(8,128)(2,1)}, u32[]{:S(2)}, u32[]{:S(2)}) collective-permute-start(bf16[2,224,128]{2,1,0:T(8,128)(2,1)S(1)} %pad_maximum_fusion.1.own_ref), channel_id=1, source_target_pairs={{0,4},{1,5},{2,6},{3,7},{4,0},{5,1},{6,2},{7,3},{8,12},{9,13},{10,... | collective-permute-start | bytes 344072 | tf_op jit(solution)/shard_map/ppermute | solution.py:262
  26.0 9.8 %collective-permute-start.1 = (bf16[2,224,128]{2,1,0:T(8,128)(2,1)S(1)}, bf16[2,224,128]{2,1,0:T(8,128)(2,1)}, u32[]{:S(2)}, u32[]{:S(2)}) collective-permute-start(bf16[2,224,128]{2,1,0:T(8,128)(2,1)S(1)} %pad_maximum_fusion.1.own_ref), channel_id=1, source_target_pairs={{0,2},{1,3},{2,4},{3,5},{4,6},{5,7},{6,0},{7,1},{8,10},{9,11},{10,... | collective-permute-start | bytes 344072 | tf_op jit(solution)/shard_map/ppermute | solution.py:262
  28.5 12.6 %copy-start.8 = (s32[128]{0:T(128)S(1)}, s32[128]{0:T(128)}, u32[]{:S(2)}) copy-start(s32[128]{0:T(128)} %param.21) | copy-start | bytes 1540
  28.5 10.0 %collective-permute-start.8 = (bf16[2,2,160,128]{3,2,1,0:T(8,128)(2,1)}, bf16[2,2,160,128]{3,2,1,0:T(8,128)(2,1)S(1)}, u32[]{:S(2)}, u32[]{:S(2)}) collective-permute-start(bf16[2,2,160,128]{3,2,1,0:T(8,128)(2,1)} %get-tuple-element.18), channel_id=1, source_target_pairs={{0,64},{8,72},{16,80},{24,88},{32,96},{40,104},{48,112},{56,120},{... | collective-permute-start | bytes 491528 | tf_op jit(solution)/shard_map/ppermute | solution.py:277
  30.1 8.8 %collective-permute-start.9 = (bf16[2,2,160,128]{3,2,1,0:T(8,128)(2,1)}, bf16[2,2,160,128]{3,2,1,0:T(8,128)(2,1)S(1)}, u32[]{:S(2)}, u32[]{:S(2)}) collective-permute-start(bf16[2,2,160,128]{3,2,1,0:T(8,128)(2,1)} %get-tuple-element.19), channel_id=1, source_target_pairs={{0,128},{8,136},{16,144},{24,152},{32,160},{40,168},{48,176},{56,1... | collective-permute-start | bytes 491528 | tf_op jit(solution)/shard_map/ppermute | solution.py:277
  31.6 9.4 %collective-permute-start.10 = (bf16[2,2,160,128]{3,2,1,0:T(8,128)(2,1)}, bf16[2,2,160,128]{3,2,1,0:T(8,128)(2,1)}, u32[]{:S(2)}, u32[]{:S(2)}) collective-permute-start(bf16[2,2,160,128]{3,2,1,0:T(8,128)(2,1)} %get-tuple-element.20), channel_id=1, source_target_pairs={{0,192},{8,200},{16,208},{24,216},{32,224},{40,232},{48,240},{56,2... | collective-permute-start | bytes 491528 | tf_op jit(solution)/shard_map/ppermute | solution.py:277
  36.7 25.8 %copy-start.11 = (bf16[128,224]{0,1:T(8,128)(2,1)S(1)}, bf16[128,224]{0,1:T(8,128)(2,1)}, u32[]{:S(2)}) copy-start(bf16[128,224]{0,1:T(8,128)(2,1)} %param.20) | copy-start | bytes 172036
  36.7 29.2 %copy-start.10 = (bf16[1792,608]{0,1:T(8,128)(2,1)S(1)}, bf16[1792,608]{0,1:T(8,128)(2,1)}, u32[]{:S(2)}) copy-start(bf16[1792,608]{0,1:T(8,128)(2,1)} %param.36) | copy-start | bytes 6537220
  38.5 27.4 %copy-start.9 = (bf16[1792,608]{0,1:T(8,128)(2,1)S(1)}, bf16[1792,608]{0,1:T(8,128)(2,1)}, u32[]{:S(2)}) copy-start(bf16[1792,608]{0,1:T(8,128)(2,1)} %param.37) | copy-start | bytes 6537220
  38.5 27.4 %copy-start.12 = (f32[1792]{0:T(1024)S(1)}, f32[1792]{0:T(1024)}, u32[]{:S(2)}) copy-start(f32[1792]{0:T(1024)} %param.29) | copy-start | bytes 21508
  43.4 6.4 %collective-permute-start.11 = (bf16[2,224,128]{2,1,0:T(8,128)(2,1)S(1)}, bf16[2,224,128]{2,1,0:T(8,128)(2,1)S(1)}, u32[]{:S(2)}, u32[]{:S(2)}) collective-permute-start(bf16[2,224,128]{2,1,0:T(8,128)(2,1)S(1)} %get-tuple-element.22), channel_id=1, source_target_pairs={{0,2},{1,3},{2,4},{3,5},{4,6},{5,7},{6,0},{7,1},{8,10},{9,11},{10,... | collective-permute-start | bytes 344072 | tf_op jit(solution)/shard_map/ppermute | solution.py:262
  43.8 9.2 %collective-permute-start.12 = (bf16[2,224,128]{2,1,0:T(8,128)(2,1)S(1)}, bf16[2,224,128]{2,1,0:T(8,128)(2,1)S(1)}, u32[]{:S(2)}, u32[]{:S(2)}) collective-permute-start(bf16[2,224,128]{2,1,0:T(8,128)(2,1)S(1)} %get-tuple-element.23), channel_id=1, source_target_pairs={{0,4},{1,5},{2,6},{3,7},{4,0},{5,1},{6,2},{7,3},{8,12},{9,13},{10,... | collective-permute-start | bytes 344072 | tf_op jit(solution)/shard_map/ppermute | solution.py:262
  47.6 5.4 %collective-permute-start.13 = (bf16[2,224,128]{2,1,0:T(8,128)(2,1)S(1)}, bf16[2,224,128]{2,1,0:T(8,128)(2,1)S(1)}, u32[]{:S(2)}, u32[]{:S(2)}) collective-permute-start(bf16[2,224,128]{2,1,0:T(8,128)(2,1)S(1)} %get-tuple-element.24), channel_id=1, source_target_pairs={{0,6},{1,7},{2,0},{3,1},{4,2},{5,3},{6,4},{7,5},{8,14},{9,15},{10,... | collective-permute-start | bytes 344072 | tf_op jit(solution)/shard_map/ppermute | solution.py:262
  53.1 9.4 %collective-permute-start.14 = (bf16[2,224,128]{2,1,0:T(8,128)(2,1)S(1)}, bf16[2,224,128]{2,1,0:T(8,128)(2,1)S(1)}, u32[]{:S(2)}, u32[]{:S(2)}) collective-permute-start(bf16[2,224,128]{2,1,0:T(8,128)(2,1)S(1)} %pad_maximum_fusion.2), channel_id=1, source_target_pairs={{0,1},{1,0},{2,3},{3,2},{4,5},{5,4},{6,7},{7,6},{8,9},{9,8},{10,11... | collective-permute-start | bytes 344072 | tf_op jit(solution)/shard_map/ppermute | solution.py:265
  62.6 9.7 %collective-permute-start.17 = (bf16[2,224,128]{2,1,0:T(8,128)(2,1)S(1)}, bf16[2,224,128]{2,1,0:T(8,128)(2,1)S(1)}, u32[]{:S(2)}, u32[]{:S(2)}) collective-permute-start(bf16[2,224,128]{2,1,0:T(8,128)(2,1)S(1)} %add_convert_fusion.own_ref), channel_id=1, source_target_pairs={{0,6},{1,7},{2,0},{3,1},{4,2},{5,3},{6,4},{7,5},{8,14},{9,15},{10,... | collective-permute-start | bytes 344072 | tf_op jit(solution)/shard_map/ppermute | solution.py:262
  64.8 7.5 %collective-permute-start.16 = (bf16[2,224,128]{2,1,0:T(8,128)(2,1)S(1)}, bf16[2,224,128]{2,1,0:T(8,128)(2,1)S(1)}, u32[]{:S(2)}, u32[]{:S(2)}) collective-permute-start(bf16[2,224,128]{2,1,0:T(8,128)(2,1)S(1)} %add_convert_fusion.own_ref), channel_id=1, source_target_pairs={{0,4},{1,5},{2,6},{3,7},{4,0},{5,1},{6,2},{7,3},{8,12},{9,13},{10,... | collective-permute-start | bytes 344072 | tf_op jit(solution)/shard_map/ppermute | solution.py:262
  65.6 6.9 %collective-permute-start.15 = (bf16[2,224,128]{2,1,0:T(8,128)(2,1)S(1)}, bf16[2,224,128]{2,1,0:T(8,128)(2,1)S(1)}, u32[]{:S(2)}, u32[]{:S(2)}) collective-permute-start(bf16[2,224,128]{2,1,0:T(8,128)(2,1)S(1)} %add_convert_fusion.own_ref), channel_id=1, source_target_pairs={{0,2},{1,3},{2,4},{3,5},{4,6},{5,7},{6,0},{7,1},{8,10},{9,11},{10,... | collective-permute-start | bytes 344072 | tf_op jit(solution)/shard_map/ppermute | solution.py:262
  72.5 1.6 %copy-start = (bf16[608,1792]{1,0:T(8,128)(2,1)S(1)}, bf16[608,1792]{1,0:T(8,128)(2,1)}, u32[]{:S(2)}) copy-start(bf16[608,1792]{1,0:T(8,128)(2,1)} %get-tuple-element.32.gate_ref) | copy-start | bytes 6537220
  77.8 6.7 %collective-permute-start.18 = (bf16[2,224,128]{2,1,0:T(8,128)(2,1)S(1)}, bf16[2,224,128]{2,1,0:T(8,128)(2,1)S(1)}, u32[]{:S(2)}, u32[]{:S(2)}) collective-permute-start(bf16[2,224,128]{2,1,0:T(8,128)(2,1)S(1)} %get-tuple-element.26), channel_id=1, source_target_pairs={{0,2},{1,3},{2,4},{3,5},{4,6},{5,7},{6,0},{7,1},{8,10},{9,11},{10,... | collective-permute-start | bytes 344072 | tf_op jit(solution)/shard_map/ppermute | solution.py:262
  80.0 6.3 %collective-permute-start.19 = (bf16[2,224,128]{2,1,0:T(8,128)(2,1)S(1)}, bf16[2,224,128]{2,1,0:T(8,128)(2,1)S(1)}, u32[]{:S(2)}, u32[]{:S(2)}) collective-permute-start(bf16[2,224,128]{2,1,0:T(8,128)(2,1)S(1)} %get-tuple-element.27), channel_id=1, source_target_pairs={{0,4},{1,5},{2,6},{3,7},{4,0},{5,1},{6,2},{7,3},{8,12},{9,13},{10,... | collective-permute-start | bytes 344072 | tf_op jit(solution)/shard_map/ppermute | solution.py:262
  82.1 4.8 %collective-permute-start.20 = (bf16[2,224,128]{2,1,0:T(8,128)(2,1)S(1)}, bf16[2,224,128]{2,1,0:T(8,128)(2,1)S(1)}, u32[]{:S(2)}, u32[]{:S(2)}) collective-permute-start(bf16[2,224,128]{2,1,0:T(8,128)(2,1)S(1)} %get-tuple-element.28), channel_id=1, source_target_pairs={{0,6},{1,7},{2,0},{3,1},{4,2},{5,3},{6,4},{7,5},{8,14},{9,15},{10,... | collective-permute-start | bytes 344072 | tf_op jit(solution)/shard_map/ppermute | solution.py:262
  86.9 8.4 %collective-permute-start.21 = (bf16[224,128]{1,0:T(8,128)(2,1)S(1)}, bf16[224,128]{1,0:T(8,128)(2,1)S(1)}, u32[]{:S(2)}, u32[]{:S(2)}) collective-permute-start(bf16[224,128]{1,0:T(8,128)(2,1)S(1)} %fusion.6), channel_id=1, source_target_pairs={{0,1},{1,0},{2,3},{3,2},{4,5},{5,4},{6,7},{7,6},{8,9},{9,8},{10,11... | collective-permute-start | bytes 172040 | tf_op jit(solution)/shard_map/ppermute | solution.py:265
  (4 other events, 3.1 us)

commit v2 on v1

--- a/solution.py
+++ b/solution.py
@@ -17,7 +17,7 @@
 
 VMEM = pl.BlockSpec(memory_space=pltpu.VMEM)
 SMEM = pl.BlockSpec(memory_space=pltpu.SMEM)
-PARAMS = pltpu.CompilerParams(vmem_limit_bytes=48 * 1024 * 1024)
+PARAMS = pltpu.CompilerParams(vmem_limit_bytes=12 * 1024 * 1024)
 
 
 def call(kernel, out_shape, specs, args, scratch=(), name=None):
@@ -61,18 +61,18 @@
 
 
 def fold_kernel(fold_ref, state_ref, norm_ref, tail_ref, out_ref):
-    heads, feats, head_dim = state_ref.shape
+    feats, heads, head_dim = state_ref.shape
     fold = fold_ref[...]
     norms = lax.dot_general(fold, norm_ref[...], (((1,), (1,)), ((), ())), preferred_element_type=F32)
     lane = lax.broadcasted_iota(jnp.int32, (ROWS, LANES), 1)
     for h in range(heads):
-        state = jnp.dot(fold, state_ref[h], preferred_element_type=F32)
+        state = jnp.dot(fold, state_ref[:, h, :], preferred_element_type=F32)
         norm = jnp.broadcast_to(norms[:, h : h + 1], (ROWS, LANES))
         hi = norm.astype(BF16).astype(F32)
         cols = jnp.where(lane == head_dim, hi, jnp.where(lane == head_dim + 1, norm - hi, 0.0))
         out_ref[h] = cols.astype(BF16)
         out_ref[h, :, :head_dim] = state.astype(BF16)
-        out_ref[h, TAIL_ROW : TAIL_ROW + 2, :head_dim] = tail_ref[h]
+        out_ref[h, TAIL_ROW : TAIL_ROW + 2, :head_dim] = tail_ref[:, h * head_dim : (h + 1) * head_dim]
 
 
 def select_kernel(groups, leaf_ref, parent_ref, owner_ref, dev_ref, mine_ref, other_ref, *rest):
@@ -279,13 +279,17 @@
     order = (1, 3, 2)
 
     fold = jnp.asarray(fold_matrix(feat_dim, feats), BF16)
-    tails = jnp.transpose(node_tail[0].reshape(2, heads, head_dim), (1, 0, 2))
+    whole = pl.BlockSpec()
     payload = call(
-        fold_kernel, sds((heads, ROWS, LANES), BF16), [VMEM] * 4, (fold, node_state[0], node_norm[0], tails), name="fold"
-    )
+        fold_kernel,
+        sds((heads, ROWS, LANES), BF16),
+        [whole] * 4,
+        (fold, jnp.transpose(node_state[0], (1, 0, 2)), node_norm[0], node_tail[0]),
+        name="fold",
+    )
+    payload, own = lax.optimization_barrier((payload, stream.T))
     from_z = {k: along_z(payload, k) for k in order}
 
-    own = stream.T
     pair = jnp.stack([own, across_z(own)])
 
     mine = jnp.stack([payload, from_z[1], from_z[2], from_z[3]])
@@ -327,17 +331,23 @@
     )
     got = {k: along_x(parts[k], k) for k in order}
     share = parts[0] + got[1].astype(F32) + got[2].astype(F32) + got[3].astype(F32)
-    share_peer = across_z(jnp.stack([share[1], share[0]]).astype(BF16))
+    crossing, gate_in, up_in, down_in = lax.optimization_barrier(
+        (jnp.stack([share[1], share[0]]).astype(BF16), ffn_gate, ffn_up, ffn_down)
+    )
+    share_peer = across_z(crossing)
+    gate_scaled = (gate_in.T.astype(F32) * ffn_gain[None, :]).astype(BF16)
+    up_scaled = (up_in.T.astype(F32) * ffn_gain[None, :]).astype(BF16)
     updated = (pair.astype(F32) + share + share_peer.astype(F32)).astype(BF16)
+    updated, gate_scaled, up_scaled, down_turned = lax.optimization_barrier(
+        (updated, gate_scaled, up_scaled, down_in.T)
+    )
 
     wide = {k: along_x(updated, k) for k in order}
-    gate_scaled = (ffn_gate.T.astype(F32) * ffn_gain[None, :]).astype(BF16)
-    up_scaled = (ffn_up.T.astype(F32) * ffn_gain[None, :]).astype(BF16)
     downs = call(
         ffn_kernel,
         [sds((2, width, tokens), F32)] + [sds((2, width, tokens), BF16)] * (x_size - 1),
         [SMEM] + [VMEM] * 7,
-        (halves, updated, wide[1], wide[2], wide[3], gate_scaled, up_scaled, ffn_down.T),
+        (halves, updated, wide[1], wide[2], wide[3], gate_scaled, up_scaled, down_turned),
         scratch=[pltpu.VMEM((model, tokens), BF16)],
         name="ffn",
     )

time: 96.6 us -> 96.4 us (level)
    ppermute x3, waiting for transfers between devices: 15.9 us -> 7.62 us  [across_z(): return lax.ppermute(array, 'tp', [(i, i ^ 1) for i in range(tp_size)])]
    ppermute x12, waiting for transfers between devices: 8.79 us -> 15.7 us  [along_x(): lax.ppermute(array, 'tp', [(i, (i // 2 + k) % x_size * 2 + i % 2) for i i...]
    optimization_barrier x0 -> x1, local copies, waits for them, and re-layouts: none -> 3.28 us  [shards(): lax.optimization_barrier((jnp.stack([share[1], share[0]]).astype(BF16), f...]
    unnamed x32 -> x36, local copies, waits for them, and re-layouts: 11.4 us -> 8.62 us
    ppermute x3, starting transfers between devices: 9.11 us -> 11.3 us  [across_z(): return lax.ppermute(array, 'tp', [(i, i ^ 1) for i in range(tp_size)])]
    ppermute x12, starting transfers between devices: 19.9 us -> 18.1 us  [along_x(): lax.ppermute(array, 'tp', [(i, (i // 2 + k) % x_size * 2 + i % 2) for i i...]
    ppermute x3, waiting for transfers between devices: 2.53 us -> 3.49 us  [along_y(): lax.ppermute(array, 'req', [(i, (i + 2 * z_size * k) % req_size) for i in...]
  transfers between devices with their start and end apart: 22 -> 22, of which waited for: 11 -> 13; matrix products, arithmetic and copies ran while one was open for 13% -> 11% of each run, Pallas kernels for 4% -> 4%
where the time goes in v2:
time: 96.4 us; the launch traced here: 95.9 us
  starting transfers between devices  37.9 us (39%)
  waiting for transfers between devices  30.2 us (31%)
  local copies, waits for them, and re-layouts  11.9 us (12%)
  Pallas kernels  9.17 us (10%)
  other arithmetic  6.49 us (7%)
    ppermute x12, starting transfers between devices, along_x(): lax.ppermute(array, 'tp', [(i, (i // 2 + k) % x_size * 2 + i % 2) for i i...  18.1 us
    ppermute x12, waiting for transfers between devices, along_x(): lax.ppermute(array, 'tp', [(i, (i // 2 + k) % x_size * 2 + i % 2) for i i...  15.7 us
    ppermute x3, starting transfers between devices, across_z(): return lax.ppermute(array, 'tp', [(i, i ^ 1) for i in range(tp_size)])  11.3 us
    pallas_call x5, Pallas kernels, call(): pl.pallas_call(kernel, out_shape=out_shape, in_specs=specs, out_specs=VME...  9.17 us
    unnamed x36, local copies, waits for them, and re-layouts  8.62 us
    ppermute x3, waiting for transfers between devices, across_z(): return lax.ppermute(array, 'tp', [(i, i ^ 1) for i in range(tp_size)])  7.62 us
    ppermute x3, starting transfers between devices, along_y(): lax.ppermute(array, 'req', [(i, (i + 2 * z_size * k) % req_size) for i in...  4.93 us
    ppermute x3, starting transfers between devices, along_z(): lax.ppermute(array, 'req', [(i, i // count * count + (i % count // 2 + k)...  3.5 us
  transfers between devices with their start and end apart: 22, of which 13 were waited for; matrix products, arithmetic and copies ran while one was open for 11% of the time, Pallas kernels for 4%

profile of v2, /device:TPU:8, one launch (start us, length us, event | category | flops | bytes accessed | tf_op | source)
XLA Modules:
  0.0 95.9 jit_solution(14766526501647089695)
XLA Ops:
  3.8 7.3 %collective-permute-start = (bf16[224,128]{1,0:T(8,128)(2,1)}, bf16[224,128]{1,0:T(8,128)(2,1)S(1)}, u32[]{:S(2)}, u32[]{:S(2)}) collective-permute-start(bf16[224,128]{1,0:T(8,128)(2,1)} %bitcast.50), channel_id=1, source_target_pairs={{0,1},{1,0},{2,3},{3,2},{4,5},{5,4},{6,7},{7,6},{8,9},{9,8},{10,11... | collective-permute-start | bytes 172040 | tf_op jit(solution)/shard_map/ppermute | solution.py:265
  11.0 1.9 %collective-permute-start.6 = (bf16[2,160,128]{2,1,0:T(8,128)(2,1)S(1)}, bf16[2,160,128]{2,1,0:T(8,128)(2,1)S(1)}, u32[]{:S(2)}, u32[]{:S(2)}) collective-permute-start(bf16[2,160,128]{2,1,0:T(8,128)(2,1)S(1)} %fold.1), channel_id=1, source_target_pairs={{0,48},{8,56},{16,0},{24,8},{32,16},{40,24},{48,32},{56,40},{64,11... | collective-permute-start | bytes 245768 | tf_op jit(solution)/shard_map/ppermute | solution.py:269
  16.0 2.8 %collective-permute-start.3 = (bf16[2,224,128]{2,1,0:T(8,128)(2,1)S(1)}, bf16[2,224,128]{2,1,0:T(8,128)(2,1)S(1)}, u32[]{:S(2)}, u32[]{:S(2)}) collective-permute-start(bf16[2,224,128]{2,1,0:T(8,128)(2,1)S(1)} %pad_maximum_fusion.1.own_ref), channel_id=1, source_target_pairs={{0,6},{1,7},{2,0},{3,1},{4,2},{5,3},{6,4},{7,5},{8,14},{9,15},{10,... | collective-permute-start | bytes 344072 | tf_op jit(solution)/shard_map/ppermute | solution.py:262
  18.9 3.4 %collective-permute-done.5 = bf16[2,160,128]{2,1,0:T(8,128)(2,1)S(1)} collective-permute-done((bf16[2,160,128]{2,1,0:T(8,128)(2,1)S(1)}, bf16[2,160,128]{2,1,0:T(8,128)(2,1)S(1)}, u32[]{:S(2)}, u32[]{:S(2)}) %collective-permute-start.5) | collective-permute-done | bytes 81952 | tf_op jit(solution)/shard_map/ppermute | solution.py:269
  22.4 1.7 %multiply_convert_fusion.2.weight_ref = bf16[512,1792]{1,0:T(8,128)(2,1)S(1)} fusion(bf16[224,1792]{1,0:T(8,128)(2,1)} %bitcast.48, bf16[224,1792]{1,0:T(8,128)(2,1)} %bitcast.49, bf16[32,1792]{1,0:T(8,128)(2,1)} %bitcast.55, bf16[32,1792]{1,0:T(8,128)(2,1)} %bitcast.56, f32[1792]{0:T(1024)} %param.28), kind=kLoop, calls=%fused_computation.2 | loop fusion | flops 9175040 | bytes 3677184 | tf_op jit(solution)/shard_map/convert_element_type | solution.py:311
  24.2 3.1 %collective-permute-start.2 = (bf16[2,224,128]{2,1,0:T(8,128)(2,1)S(1)}, bf16[2,224,128]{2,1,0:T(8,128)(2,1)S(1)}, u32[]{:S(2)}, u32[]{:S(2)}) collective-permute-start(bf16[2,224,128]{2,1,0:T(8,128)(2,1)S(1)} %pad_maximum_fusion.1.own_ref), channel_id=1, source_target_pairs={{0,4},{1,5},{2,6},{3,7},{4,0},{5,1},{6,2},{7,3},{8,12},{9,13},{10,... | collective-permute-start | bytes 344072 | tf_op jit(solution)/shard_map/ppermute | solution.py:262
  27.9 1.8 %select.7 = (bf16[2,2,160,128]{3,2,1,0:T(8,128)(2,1)S(1)}, bf16[2,2,160,128]{3,2,1,0:T(8,128)(2,1)}, bf16[2,2,160,128]{3,2,1,0:T(8,128)(2,1)}, bf16[2,2,160,128]{3,2,1,0:T(8,128)(2,1)}) custom-call(s32[64]{0:T(128)S(1)} %copy-done.6, s32[32]{0:T(128)S(1)} %copy-done.7, s32[32]{0:T(128)S(1)} %copy-done.8, s32[1]{0:T(128)} %bitcast.16.dev_ref, ...), custom_call_target="tpu_custom_call" | custom-call | tf_op jit(solution)/shard_map/select/pallas_call | solution.py:25
  29.7 1.6 %collective-permute-start.8 = (bf16[2,2,160,128]{3,2,1,0:T(8,128)(2,1)}, bf16[2,2,160,128]{3,2,1,0:T(8,128)(2,1)S(1)}, u32[]{:S(2)}, u32[]{:S(2)}) collective-permute-start(bf16[2,2,160,128]{3,2,1,0:T(8,128)(2,1)} %get-tuple-element.30), channel_id=1, source_target_pairs={{0,64},{8,72},{16,80},{24,88},{32,96},{40,104},{48,112},{56,120},{... | collective-permute-start | bytes 491528 | tf_op jit(solution)/shard_map/ppermute | solution.py:277
  32.3 2.4 %collective-permute-start.10 = (bf16[2,2,160,128]{3,2,1,0:T(8,128)(2,1)}, bf16[2,2,160,128]{3,2,1,0:T(8,128)(2,1)}, u32[]{:S(2)}, u32[]{:S(2)}) collective-permute-start(bf16[2,2,160,128]{3,2,1,0:T(8,128)(2,1)} %get-tuple-element.32), channel_id=1, source_target_pairs={{0,192},{8,200},{16,208},{24,216},{32,224},{40,232},{48,240},{56,2... | collective-permute-start | bytes 491528 | tf_op jit(solution)/shard_map/ppermute | solution.py:277
  34.9 1.4 %copy.22 = bf16[224,1792]{0,1:T(8,128)(2,1)S(1)} copy(bf16[224,1792]{1,0:T(8,128)(2,1)} %param.35) | data formatting | bytes 1605632 | tf_op args[15]
  36.4 1.8 %project.1.proj_ref = f32[512,128]{1,0:T(8,128)S(1)} custom-call(s32[2]{0:T(128)S(1)} %pad_add_fusion.half_ref, bf16[2,224,128]{2,1,0:T(8,128)(2,1)S(1)} %pad_maximum_fusion.1.own_ref, bf16[2,224,128]{2,1,0:T(8,128)(2,1)} %collective-permute-done.1.r1_ref, bf16[2,224,128]{2,1,0:T(8,128)(2,1)S(1)} %collective-permute-done.2.r2_ref, ...), custom_call_target="tpu_custom_call" | custom-call | tf_op jit(solution)/shard_map/project/pallas_call | solution.py:25
  38.2 2.1 %collective-permute-done.9.p2_ref = bf16[2,2,160,128]{3,2,1,0:T(8,128)(2,1)} collective-permute-done((bf16[2,2,160,128]{3,2,1,0:T(8,128)(2,1)}, bf16[2,2,160,128]{3,2,1,0:T(8,128)(2,1)}, u32[]{:S(2)}, u32[]{:S(2)}) %collective-permute-start.9) | collective-permute-done | bytes 163872 | tf_op jit(solution)/shard_map/ppermute | solution.py:277
  40.2 1.4 %collective-permute-done.10.p3_ref = bf16[2,2,160,128]{3,2,1,0:T(8,128)(2,1)} collective-permute-done((bf16[2,2,160,128]{3,2,1,0:T(8,128)(2,1)}, bf16[2,2,160,128]{3,2,1,0:T(8,128)(2,1)}, u32[]{:S(2)}, u32[]{:S(2)}) %collective-permute-start.10) | collective-permute-done | bytes 163872 | tf_op jit(solution)/shard_map/ppermute | solution.py:277
  41.7 2.4 %mix.1 = (f32[2,224,128]{2,1,0:T(8,128)S(1)}, bf16[2,224,128]{2,1,0:T(8,128)(2,1)S(1)}, bf16[2,224,128]{2,1,0:T(8,128)(2,1)S(1)}, bf16[2,224,128]{2,1,0:T(8,128)(2,1)S(1)}) custom-call(s32[2]{0:T(128)S(1)} %pad_add_fusion.half_ref, s32[2]{0:T(128)S(1)} %pad_add_fusion.1.first_ref, s32[1,128]{1,0:T(1,128)S(1)} %bitcast.47, f32[512,128]{1,0:T(8,128)S(1)} %project.1.proj_ref, ...), custom_call_target="tpu_custom_call" | custom-call | tf_op jit(solution)/shard_map/mix/pallas_call | solution.py:25
  44.5 3.8 %collective-permute-start.12 = (bf16[2,224,128]{2,1,0:T(8,128)(2,1)S(1)}, bf16[2,224,128]{2,1,0:T(8,128)(2,1)S(1)}, u32[]{:S(2)}, u32[]{:S(2)}) collective-permute-start(bf16[2,224,128]{2,1,0:T(8,128)(2,1)S(1)} %get-tuple-element.35), channel_id=1, source_target_pairs={{0,4},{1,5},{2,6},{3,7},{4,0},{5,1},{6,2},{7,3},{8,12},{9,13},{10,... | collective-permute-start | bytes 344072 | tf_op jit(solution)/shard_map/ppermute | solution.py:262
  48.8 2.6 %collective-permute-done.11 = bf16[2,224,128]{2,1,0:T(8,128)(2,1)S(1)} collective-permute-done((bf16[2,224,128]{2,1,0:T(8,128)(2,1)S(1)}, bf16[2,224,128]{2,1,0:T(8,128)(2,1)S(1)}, u32[]{:S(2)}, u32[]{:S(2)}) %collective-permute-start.11) | collective-permute-done | bytes 114720 | tf_op jit(solution)/shard_map/ppermute | solution.py:262
  51.4 1.6 %collective-permute-done.12 = bf16[2,224,128]{2,1,0:T(8,128)(2,1)S(1)} collective-permute-done((bf16[2,224,128]{2,1,0:T(8,128)(2,1)S(1)}, bf16[2,224,128]{2,1,0:T(8,128)(2,1)S(1)}, u32[]{:S(2)}, u32[]{:S(2)}) %collective-permute-start.12) | collective-permute-done | bytes 114720 | tf_op jit(solution)/shard_map/ppermute | solution.py:262
  53.3 1.4 %collective-permute-start.14 = (bf16[2,224,128]{2,1,0:T(8,128)(2,1)S(1)}, bf16[2,224,128]{2,1,0:T(8,128)(2,1)S(1)}, u32[]{:S(2)}, u32[]{:S(2)}) collective-permute-start(bf16[2,224,128]{2,1,0:T(8,128)(2,1)S(1)} %pad_maximum_fusion.2), channel_id=1, source_target_pairs={{0,1},{1,0},{2,3},{3,2},{4,5},{5,4},{6,7},{7,6},{8,9},{9,8},{10,11... | collective-permute-start | bytes 344072 | tf_op jit(solution)/shard_map/ppermute | solution.py:265
  54.8 2.8 %fusion.1 = (bf16[608,1792]{1,0:T(8,128)(2,1)}, bf16[608,1792]{1,0:T(8,128)(2,1)}) fusion(bf16[1792,608]{0,1:T(8,128)(2,1)S(1)} %copy-done.10, f32[1792]{0:T(1024)S(1)} %copy-done.15, bf16[1792,608]{0,1:T(8,128)(2,1)S(1)} %copy-done.11), kind=kLoop, calls=%fused_computation.4 | loop fusion | flops 6537216 | bytes 8723456 | tf_op jit(solution)/shard_map/convert_element_type | solution.py:339
  57.6 3.3 %copy.23 = bf16[608,1792]{0,1:T(8,128)(2,1)S(1)} copy(bf16[608,1792]{1,0:T(8,128)(2,1)} %param.38) | data formatting | bytes 4358144 | tf_op jit(solution)/shard_map/optimization_barrier | solution.py:334
  60.9 2.1 %collective-permute-done.14 = bf16[2,224,128]{2,1,0:T(8,128)(2,1)S(1)} collective-permute-done((bf16[2,224,128]{2,1,0:T(8,128)(2,1)S(1)}, bf16[2,224,128]{2,1,0:T(8,128)(2,1)S(1)}, u32[]{:S(2)}, u32[]{:S(2)}) %collective-permute-start.14) | collective-permute-done | bytes 114720 | tf_op jit(solution)/shard_map/ppermute | solution.py:265
  63.1 2.3 %collective-permute-start.17 = (bf16[2,224,128]{2,1,0:T(8,128)(2,1)S(1)}, bf16[2,224,128]{2,1,0:T(8,128)(2,1)S(1)}, u32[]{:S(2)}, u32[]{:S(2)}) collective-permute-start(bf16[2,224,128]{2,1,0:T(8,128)(2,1)S(1)} %add_convert_fusion.own_ref), channel_id=1, source_target_pairs={{0,6},{1,7},{2,0},{3,1},{4,2},{5,3},{6,4},{7,5},{8,14},{9,15},{10,... | collective-permute-start | bytes 344072 | tf_op jit(solution)/shard_map/ppermute | solution.py:262
  66.4 2.6 %collective-permute-done.17.r3_ref = bf16[2,224,128]{2,1,0:T(8,128)(2,1)S(1)} collective-permute-done((bf16[2,224,128]{2,1,0:T(8,128)(2,1)S(1)}, bf16[2,224,128]{2,1,0:T(8,128)(2,1)S(1)}, u32[]{:S(2)}, u32[]{:S(2)}) %collective-permute-start.17) | collective-permute-done | bytes 114720 | tf_op jit(solution)/shard_map/ppermute | solution.py:262
  69.0 2.8 %collective-permute-done.16.r2_ref = bf16[2,224,128]{2,1,0:T(8,128)(2,1)S(1)} collective-permute-done((bf16[2,224,128]{2,1,0:T(8,128)(2,1)S(1)}, bf16[2,224,128]{2,1,0:T(8,128)(2,1)S(1)}, u32[]{:S(2)}, u32[]{:S(2)}) %collective-permute-start.16) | collective-permute-done | bytes 114720 | tf_op jit(solution)/shard_map/ppermute | solution.py:262
  73.0 1.6 %copy-done = bf16[608,1792]{1,0:T(8,128)(2,1)S(1)} copy-done((bf16[608,1792]{1,0:T(8,128)(2,1)S(1)}, bf16[608,1792]{1,0:T(8,128)(2,1)}, u32[]{:S(2)}) %copy-start) | copy-done | bytes 2179096
  74.6 1.6 %copy-done.1 = bf16[608,1792]{1,0:T(8,128)(2,1)S(1)} copy-done((bf16[608,1792]{1,0:T(8,128)(2,1)S(1)}, bf16[608,1792]{1,0:T(8,128)(2,1)}, u32[]{:S(2)}) %copy-start.1) | copy-done | bytes 2179096
  76.2 2.6 %ffn.1 = (f32[2,224,128]{2,1,0:T(8,128)S(1)}, bf16[2,224,128]{2,1,0:T(8,128)(2,1)S(1)}, bf16[2,224,128]{2,1,0:T(8,128)(2,1)S(1)}, bf16[2,224,128]{2,1,0:T(8,128)(2,1)S(1)}) custom-call(s32[2]{0:T(128)S(1)} %pad_add_fusion.half_ref, bf16[2,224,128]{2,1,0:T(8,128)(2,1)S(1)} %add_convert_fusion.own_ref, ...), custom_call_target="tpu_custom_call" | custom-call | tf_op jit(solution)/shard_map/ffn/pallas_call | solution.py:25
  78.9 2.0 %collective-permute-start.19 = (bf16[2,224,128]{2,1,0:T(8,128)(2,1)S(1)}, bf16[2,224,128]{2,1,0:T(8,128)(2,1)S(1)}, u32[]{:S(2)}, u32[]{:S(2)}) collective-permute-start(bf16[2,224,128]{2,1,0:T(8,128)(2,1)S(1)} %get-tuple-element.47), channel_id=1, source_target_pairs={{0,4},{1,5},{2,6},{3,7},{4,0},{5,1},{6,2},{7,3},{8,12},{9,13},{10,... | collective-permute-start | bytes 344072 | tf_op jit(solution)/shard_map/ppermute | solution.py:262
  80.9 1.4 %collective-permute-start.20 = (bf16[2,224,128]{2,1,0:T(8,128)(2,1)S(1)}, bf16[2,224,128]{2,1,0:T(8,128)(2,1)S(1)}, u32[]{:S(2)}, u32[]{:S(2)}) collective-permute-start(bf16[2,224,128]{2,1,0:T(8,128)(2,1)S(1)} %get-tuple-element.48), channel_id=1, source_target_pairs={{0,6},{1,7},{2,0},{3,1},{4,2},{5,3},{6,4},{7,5},{8,14},{9,15},{10,... | collective-permute-start | bytes 344072 | tf_op jit(solution)/shard_map/ppermute | solution.py:262
  82.3 3.8 %collective-permute-done.18 = bf16[2,224,128]{2,1,0:T(8,128)(2,1)S(1)} collective-permute-done((bf16[2,224,128]{2,1,0:T(8,128)(2,1)S(1)}, bf16[2,224,128]{2,1,0:T(8,128)(2,1)S(1)}, u32[]{:S(2)}, u32[]{:S(2)}) %collective-permute-start.18) | collective-permute-done | bytes 114720 | tf_op jit(solution)/shard_map/ppermute | solution.py:262
  87.1 2.6 %collective-permute-start.21 = (bf16[224,128]{1,0:T(8,128)(2,1)S(1)}, bf16[224,128]{1,0:T(8,128)(2,1)S(1)}, u32[]{:S(2)}, u32[]{:S(2)}) collective-permute-start(bf16[224,128]{1,0:T(8,128)(2,1)S(1)} %fusion.6), channel_id=1, source_target_pairs={{0,1},{1,0},{2,3},{3,2},{4,5},{5,4},{6,7},{7,6},{8,9},{9,8},{10,11... | collective-permute-start | bytes 172040 | tf_op jit(solution)/shard_map/ppermute | solution.py:265
  89.7 5.5 %collective-permute-done.21 = bf16[224,128]{1,0:T(8,128)(2,1)S(1)} collective-permute-done((bf16[224,128]{1,0:T(8,128)(2,1)S(1)}, bf16[224,128]{1,0:T(8,128)(2,1)S(1)}, u32[]{:S(2)}, u32[]{:S(2)}) %collective-permute-start.21) | collective-permute-done | bytes 57376 | tf_op jit(solution)/shard_map/ppermute | solution.py:265
  (67 shorter events, 13.9 us)
Async XLA Ops:
  3.8 10.8 %collective-permute-start = (bf16[224,128]{1,0:T(8,128)(2,1)}, bf16[224,128]{1,0:T(8,128)(2,1)S(1)}, u32[]{:S(2)}, u32[]{:S(2)}) collective-permute-start(bf16[224,128]{1,0:T(8,128)(2,1)} %bitcast.50), channel_id=1, source_target_pairs={{0,1},{1,0},{2,3},{3,2},{4,5},{5,4},{6,7},{7,6},{8,9},{9,8},{10,11... | collective-permute-start | bytes 172040 | tf_op jit(solution)/shard_map/ppermute | solution.py:265
  11.0 7.8 %collective-permute-start.6 = (bf16[2,160,128]{2,1,0:T(8,128)(2,1)S(1)}, bf16[2,160,128]{2,1,0:T(8,128)(2,1)S(1)}, u32[]{:S(2)}, u32[]{:S(2)}) collective-permute-start(bf16[2,160,128]{2,1,0:T(8,128)(2,1)S(1)} %fold.1), channel_id=1, source_target_pairs={{0,48},{8,56},{16,0},{24,8},{32,16},{40,24},{48,32},{56,40},{64,11... | collective-permute-start | bytes 245768 | tf_op jit(solution)/shard_map/ppermute | solution.py:269
  13.0 9.3 %collective-permute-start.5 = (bf16[2,160,128]{2,1,0:T(8,128)(2,1)S(1)}, bf16[2,160,128]{2,1,0:T(8,128)(2,1)S(1)}, u32[]{:S(2)}, u32[]{:S(2)}) collective-permute-start(bf16[2,160,128]{2,1,0:T(8,128)(2,1)S(1)} %fold.1), channel_id=1, source_target_pairs={{0,32},{8,40},{16,48},{24,56},{32,0},{40,8},{48,16},{56,24},{64,96... | collective-permute-start | bytes 245768 | tf_op jit(solution)/shard_map/ppermute | solution.py:269
  13.5 8.8 %collective-permute-start.4 = (bf16[2,160,128]{2,1,0:T(8,128)(2,1)S(1)}, bf16[2,160,128]{2,1,0:T(8,128)(2,1)S(1)}, u32[]{:S(2)}, u32[]{:S(2)}) collective-permute-start(bf16[2,160,128]{2,1,0:T(8,128)(2,1)S(1)} %fold.1), channel_id=1, source_target_pairs={{0,16},{8,24},{16,32},{24,40},{32,48},{40,56},{48,0},{56,8},{64,80... | collective-permute-start | bytes 245768 | tf_op jit(solution)/shard_map/ppermute | solution.py:269
  15.2 12.7 %copy-start.6 = (s32[64]{0:T(128)S(1)}, s32[64]{0:T(128)}, u32[]{:S(2)}) copy-start(s32[64]{0:T(128)} %leaf_ref.1) | copy-start | bytes 772
  15.2 12.7 %copy-start.7 = (s32[32]{0:T(128)S(1)}, s32[32]{0:T(128)}, u32[]{:S(2)}) copy-start(s32[32]{0:T(128)} %parent_ref.1) | copy-start | bytes 388
  15.2 12.7 %copy-start.8 = (s32[32]{0:T(128)S(1)}, s32[32]{0:T(128)}, u32[]{:S(2)}) copy-start(s32[32]{0:T(128)} %owner_ref.1) | copy-start | bytes 388
  16.0 16.2 %collective-permute-start.3 = (bf16[2,224,128]{2,1,0:T(8,128)(2,1)S(1)}, bf16[2,224,128]{2,1,0:T(8,128)(2,1)S(1)}, u32[]{:S(2)}, u32[]{:S(2)}) collective-permute-start(bf16[2,224,128]{2,1,0:T(8,128)(2,1)S(1)} %pad_maximum_fusion.1.own_ref), channel_id=1, source_target_pairs={{0,6},{1,7},{2,0},{3,1},{4,2},{5,3},{6,4},{7,5},{8,14},{9,15},{10,... | collective-permute-start | bytes 344072 | tf_op jit(solution)/shard_map/ppermute | solution.py:262
  22.3 12.4 %copy-start.16 = (f32[3,224]{1,0:T(4,128)S(1)}, f32[3,224]{1,0:T(4,128)}, u32[]{:S(2)}) copy-start(f32[3,224]{1,0:T(4,128)} %param.34) | copy-start | bytes 8068
  22.3 5.6 %collective-permute-start.7 = (bf16[4,2,160,128]{3,2,1,0:T(8,128)(2,1)S(1)}, bf16[4,2,160,128]{3,2,1,0:T(8,128)(2,1)S(1)}, u32[]{:S(2)}, u32[]{:S(2)}) collective-permute-start(bf16[4,2,160,128]{3,2,1,0:T(8,128)(2,1)S(1)} %pad_maximum_fusion.mine_ref), channel_id=1, source_target_pairs={{0,8},{8,0},{16,24},{24,16},{32,40},{40,32},{48,56},{56,48},{64,72... | collective-permute-start | bytes 983048 | tf_op jit(solution)/shard_map/ppermute | solution.py:274
  24.2 12.2 %collective-permute-start.2 = (bf16[2,224,128]{2,1,0:T(8,128)(2,1)S(1)}, bf16[2,224,128]{2,1,0:T(8,128)(2,1)S(1)}, u32[]{:S(2)}, u32[]{:S(2)}) collective-permute-start(bf16[2,224,128]{2,1,0:T(8,128)(2,1)S(1)} %pad_maximum_fusion.1.own_ref), channel_id=1, source_target_pairs={{0,4},{1,5},{2,6},{3,7},{4,0},{5,1},{6,2},{7,3},{8,12},{9,13},{10,... | collective-permute-start | bytes 344072 | tf_op jit(solution)/shard_map/ppermute | solution.py:262
  27.3 9.1 %collective-permute-start.1 = (bf16[2,224,128]{2,1,0:T(8,128)(2,1)S(1)}, bf16[2,224,128]{2,1,0:T(8,128)(2,1)}, u32[]{:S(2)}, u32[]{:S(2)}) collective-permute-start(bf16[2,224,128]{2,1,0:T(8,128)(2,1)S(1)} %pad_maximum_fusion.1.own_ref), channel_id=1, source_target_pairs={{0,2},{1,3},{2,4},{3,5},{4,6},{5,7},{6,0},{7,1},{8,10},{9,11},{10,... | collective-permute-start | bytes 344072 | tf_op jit(solution)/shard_map/ppermute | solution.py:262
  29.7 11.9 %copy-start.9 = (s32[128]{0:T(128)S(1)}, s32[128]{0:T(128)}, u32[]{:S(2)}) copy-start(s32[128]{0:T(128)} %param.21) | copy-start | bytes 1540
  29.7 8.4 %collective-permute-start.8 = (bf16[2,2,160,128]{3,2,1,0:T(8,128)(2,1)}, bf16[2,2,160,128]{3,2,1,0:T(8,128)(2,1)S(1)}, u32[]{:S(2)}, u32[]{:S(2)}) collective-permute-start(bf16[2,2,160,128]{3,2,1,0:T(8,128)(2,1)} %get-tuple-element.30), channel_id=1, source_target_pairs={{0,64},{8,72},{16,80},{24,88},{32,96},{40,104},{48,112},{56,120},{... | collective-permute-start | bytes 491528 | tf_op jit(solution)/shard_map/ppermute | solution.py:277
  31.3 8.9 %collective-permute-start.9 = (bf16[2,2,160,128]{3,2,1,0:T(8,128)(2,1)}, bf16[2,2,160,128]{3,2,1,0:T(8,128)(2,1)}, u32[]{:S(2)}, u32[]{:S(2)}) collective-permute-start(bf16[2,2,160,128]{3,2,1,0:T(8,128)(2,1)} %get-tuple-element.31), channel_id=1, source_target_pairs={{0,128},{8,136},{16,144},{24,152},{32,160},{40,168},{48,176},{56,1... | collective-permute-start | bytes 491528 | tf_op jit(solution)/shard_map/ppermute | solution.py:277
  32.3 9.4 %collective-permute-start.10 = (bf16[2,2,160,128]{3,2,1,0:T(8,128)(2,1)}, bf16[2,2,160,128]{3,2,1,0:T(8,128)(2,1)}, u32[]{:S(2)}, u32[]{:S(2)}) collective-permute-start(bf16[2,2,160,128]{3,2,1,0:T(8,128)(2,1)} %get-tuple-element.32), channel_id=1, source_target_pairs={{0,192},{8,200},{16,208},{24,216},{32,224},{40,232},{48,240},{56,2... | collective-permute-start | bytes 491528 | tf_op jit(solution)/shard_map/ppermute | solution.py:277
  36.4 18.4 %copy-start.10 = (bf16[1792,608]{0,1:T(8,128)(2,1)S(1)}, bf16[1792,608]{0,1:T(8,128)(2,1)}, u32[]{:S(2)}) copy-start(bf16[1792,608]{0,1:T(8,128)(2,1)} %param.37) | copy-start | bytes 6537220
  36.4 18.4 %copy-start.11 = (bf16[1792,608]{0,1:T(8,128)(2,1)S(1)}, bf16[1792,608]{0,1:T(8,128)(2,1)}, u32[]{:S(2)}) copy-start(bf16[1792,608]{0,1:T(8,128)(2,1)} %param.36) | copy-start | bytes 6537220
  36.4 18.4 %copy-start.15 = (f32[1792]{0:T(1024)S(1)}, f32[1792]{0:T(1024)}, u32[]{:S(2)}) copy-start(f32[1792]{0:T(1024)} %param.29) | copy-start | bytes 21508
  44.1 7.3 %collective-permute-start.11 = (bf16[2,224,128]{2,1,0:T(8,128)(2,1)S(1)}, bf16[2,224,128]{2,1,0:T(8,128)(2,1)S(1)}, u32[]{:S(2)}, u32[]{:S(2)}) collective-permute-start(bf16[2,224,128]{2,1,0:T(8,128)(2,1)S(1)} %get-tuple-element.34), channel_id=1, source_target_pairs={{0,2},{1,3},{2,4},{3,5},{4,6},{5,7},{6,0},{7,1},{8,10},{9,11},{10,... | collective-permute-start | bytes 344072 | tf_op jit(solution)/shard_map/ppermute | solution.py:262
  44.5 8.5 %collective-permute-start.12 = (bf16[2,224,128]{2,1,0:T(8,128)(2,1)S(1)}, bf16[2,224,128]{2,1,0:T(8,128)(2,1)S(1)}, u32[]{:S(2)}, u32[]{:S(2)}) collective-permute-start(bf16[2,224,128]{2,1,0:T(8,128)(2,1)S(1)} %get-tuple-element.35), channel_id=1, source_target_pairs={{0,4},{1,5},{2,6},{3,7},{4,0},{5,1},{6,2},{7,3},{8,12},{9,13},{10,... | collective-permute-start | bytes 344072 | tf_op jit(solution)/shard_map/ppermute | solution.py:262
  48.3 4.9 %collective-permute-start.13 = (bf16[2,224,128]{2,1,0:T(8,128)(2,1)S(1)}, bf16[2,224,128]{2,1,0:T(8,128)(2,1)S(1)}, u32[]{:S(2)}, u32[]{:S(2)}) collective-permute-start(bf16[2,224,128]{2,1,0:T(8,128)(2,1)S(1)} %get-tuple-element.36), channel_id=1, source_target_pairs={{0,6},{1,7},{2,0},{3,1},{4,2},{5,3},{6,4},{7,5},{8,14},{9,15},{10,... | collective-permute-start | bytes 344072 | tf_op jit(solution)/shard_map/ppermute | solution.py:262
  53.3 9.7 %collective-permute-start.14 = (bf16[2,224,128]{2,1,0:T(8,128)(2,1)S(1)}, bf16[2,224,128]{2,1,0:T(8,128)(2,1)S(1)}, u32[]{:S(2)}, u32[]{:S(2)}) collective-permute-start(bf16[2,224,128]{2,1,0:T(8,128)(2,1)S(1)} %pad_maximum_fusion.2), channel_id=1, source_target_pairs={{0,1},{1,0},{2,3},{3,2},{4,5},{5,4},{6,7},{7,6},{8,9},{9,8},{10,11... | collective-permute-start | bytes 344072 | tf_op jit(solution)/shard_map/ppermute | solution.py:265
  57.6 5.4 %copy-start.12 = (bf16[128,224]{0,1:T(8,128)(2,1)S(1)}, bf16[128,224]{0,1:T(8,128)(2,1)}, u32[]{:S(2)}) copy-start(bf16[128,224]{0,1:T(8,128)(2,1)} %param.20) | copy-start | bytes 172036
  57.6 5.4 %copy-start.14 = (bf16[224,128]{1,0:T(8,128)(2,1)S(1)}, bf16[224,128]{1,0:T(8,128)(2,1)}, u32[]{:S(2)}) copy-start(bf16[224,128]{1,0:T(8,128)(2,1)} %copy-done.13) | copy-start | bytes 172036
  63.1 5.9 %collective-permute-start.17 = (bf16[2,224,128]{2,1,0:T(8,128)(2,1)S(1)}, bf16[2,224,128]{2,1,0:T(8,128)(2,1)S(1)}, u32[]{:S(2)}, u32[]{:S(2)}) collective-permute-start(bf16[2,224,128]{2,1,0:T(8,128)(2,1)S(1)} %add_convert_fusion.own_ref), channel_id=1, source_target_pairs={{0,6},{1,7},{2,0},{3,1},{4,2},{5,3},{6,4},{7,5},{8,14},{9,15},{10,... | collective-permute-start | bytes 344072 | tf_op jit(solution)/shard_map/ppermute | solution.py:262
  65.4 6.4 %collective-permute-start.16 = (bf16[2,224,128]{2,1,0:T(8,128)(2,1)S(1)}, bf16[2,224,128]{2,1,0:T(8,128)(2,1)S(1)}, u32[]{:S(2)}, u32[]{:S(2)}) collective-permute-start(bf16[2,224,128]{2,1,0:T(8,128)(2,1)S(1)} %add_convert_fusion.own_ref), channel_id=1, source_target_pairs={{0,4},{1,5},{2,6},{3,7},{4,0},{5,1},{6,2},{7,3},{8,12},{9,13},{10,... | collective-permute-start | bytes 344072 | tf_op jit(solution)/shard_map/ppermute | solution.py:262
  66.1 6.8 %collective-permute-start.15 = (bf16[2,224,128]{2,1,0:T(8,128)(2,1)S(1)}, bf16[2,224,128]{2,1,0:T(8,128)(2,1)S(1)}, u32[]{:S(2)}, u32[]{:S(2)}) collective-permute-start(bf16[2,224,128]{2,1,0:T(8,128)(2,1)S(1)} %add_convert_fusion.own_ref), channel_id=1, source_target_pairs={{0,2},{1,3},{2,4},{3,5},{4,6},{5,7},{6,0},{7,1},{8,10},{9,11},{10,... | collective-permute-start | bytes 344072 | tf_op jit(solution)/shard_map/ppermute | solution.py:262
  78.8 7.3 %collective-permute-start.18 = (bf16[2,224,128]{2,1,0:T(8,128)(2,1)S(1)}, bf16[2,224,128]{2,1,0:T(8,128)(2,1)S(1)}, u32[]{:S(2)}, u32[]{:S(2)}) collective-permute-start(bf16[2,224,128]{2,1,0:T(8,128)(2,1)S(1)} %get-tuple-element.46), channel_id=1, source_target_pairs={{0,2},{1,3},{2,4},{3,5},{4,6},{5,7},{6,0},{7,1},{8,10},{9,11},{10,... | collective-permute-start | bytes 344072 | tf_op jit(solution)/shard_map/ppermute | solution.py:262
  78.9 7.2 %collective-permute-start.19 = (bf16[2,224,128]{2,1,0:T(8,128)(2,1)S(1)}, bf16[2,224,128]{2,1,0:T(8,128)(2,1)S(1)}, u32[]{:S(2)}, u32[]{:S(2)}) collective-permute-start(bf16[2,224,128]{2,1,0:T(8,128)(2,1)S(1)} %get-tuple-element.47), channel_id=1, source_target_pairs={{0,4},{1,5},{2,6},{3,7},{4,0},{5,1},{6,2},{7,3},{8,12},{9,13},{10,... | collective-permute-start | bytes 344072 | tf_op jit(solution)/shard_map/ppermute | solution.py:262
  80.9 6.1 %collective-permute-start.20 = (bf16[2,224,128]{2,1,0:T(8,128)(2,1)S(1)}, bf16[2,224,128]{2,1,0:T(8,128)(2,1)S(1)}, u32[]{:S(2)}, u32[]{:S(2)}) collective-permute-start(bf16[2,224,128]{2,1,0:T(8,128)(2,1)S(1)} %get-tuple-element.48), channel_id=1, source_target_pairs={{0,6},{1,7},{2,0},{3,1},{4,2},{5,3},{6,4},{7,5},{8,14},{9,15},{10,... | collective-permute-start | bytes 344072 | tf_op jit(solution)/shard_map/ppermute | solution.py:262
  87.1 8.2 %collective-permute-start.21 = (bf16[224,128]{1,0:T(8,128)(2,1)S(1)}, bf16[224,128]{1,0:T(8,128)(2,1)S(1)}, u32[]{:S(2)}, u32[]{:S(2)}) collective-permute-start(bf16[224,128]{1,0:T(8,128)(2,1)S(1)} %fusion.6), channel_id=1, source_target_pairs={{0,1},{1,0},{2,3},{3,2},{4,5},{5,4},{6,7},{7,6},{8,9},{9,8},{10,11... | collective-permute-start | bytes 172040 | tf_op jit(solution)/shard_map/ppermute | solution.py:265
  (7 other events, 7.0 us)

commit v3 on v2

v3 whole, which is shorter than its diff:
```python
import functools

import jax
import jax.numpy as jnp
import numpy as np
from jax import lax
from jax.experimental import pallas as pl
from jax.experimental.pallas import tpu as pltpu
from jax.sharding import PartitionSpec as P

EPSILON = 1e-05
ROWS = 160
LANES = 128
TAIL_ROW = 153
F32 = jnp.float32
BF16 = jnp.bfloat16

VMEM = pl.BlockSpec(memory_space=pltpu.VMEM)
SMEM = pl.BlockSpec(memory_space=pltpu.SMEM)
PARAMS = pltpu.CompilerParams(vmem_limit_bytes=12 * 1024 * 1024)


def call(kernel, out_shape, specs, args, scratch=(), name=None):
    single = not isinstance(out_shape, (list, tuple))
    return pl.pallas_call(
        kernel,
        out_shape=out_shape,
        in_specs=specs,
        out_specs=VMEM if single else [VMEM] * len(out_shape),
        scratch_shapes=list(scratch),
        compiler_params=PARAMS,
        name=name,
    )(*args)


def sds(shape, dtype):
    return jax.ShapeDtypeStruct(shape, dtype)


def fold_matrix(feat_dim, feat_count):
    fold = np.zeros((ROWS, feat_count), np.float32)
    row = 0
    for i in range(feat_dim):
        fold[row, 1 + i] = 1
        row += 1
    for gap in range(feat_dim // 2 + 1):
        for i in range(feat_dim if gap < feat_dim // 2 else feat_dim // 2):
            j = (i + gap) % feat_dim
            fold[row, 1 + feat_dim + feat_dim * i + j] = 1
            fold[row, 1 + feat_dim + feat_dim * j + i] = 1
            row += 1
    fold[row, 0] = 1
    return fold


def split_norm(total, head_dim):
    rounded = total.astype(BF16).astype(F32)
    lost = pltpu.roll(total - rounded, 1, axis=1)
    lane = lax.broadcasted_iota(jnp.int32, total.shape, 1)
    return jnp.where(lane == head_dim + 1, total + lost, total).astype(BF16)


def fold_kernel(fold_hbm, state_hbm, norm_hbm, tail_hbm, out_ref, fold_ref, state_ref, norm_ref, tail_ref, sems):
    pairs = ((state_hbm, state_ref), (fold_hbm, fold_ref), (norm_hbm, norm_ref), (tail_hbm, tail_ref))
    copies = [pltpu.make_async_copy(a, b, sems.at[i]) for i, (a, b) in enumerate(pairs)]
    for copy in copies:
        copy.start()
    for copy in copies:
        copy.wait()
    feats, heads, head_dim = state_ref.shape
    fold = fold_ref[...]
    norms = lax.dot_general(fold, norm_ref[...], (((1,), (1,)), ((), ())), preferred_element_type=F32)
    lane = lax.broadcasted_iota(jnp.int32, (ROWS, LANES), 1)
    for h in range(heads):
        state = jnp.dot(fold, state_ref[:, h, :], preferred_element_type=F32)
        norm = jnp.broadcast_to(norms[:, h : h + 1], (ROWS, LANES))
        hi = norm.astype(BF16).astype(F32)
        cols = jnp.where(lane == head_dim, hi, jnp.where(lane == head_dim + 1, norm - hi, 0.0))
        out_ref[h] = cols.astype(BF16)
        out_ref[h, :, :head_dim] = state.astype(BF16)
        out_ref[h, TAIL_ROW : TAIL_ROW + 2, :head_dim] = tail_ref[:, h * head_dim : (h + 1) * head_dim]


def select_kernel(groups, shifts, leaf_ref, parent_ref, owner_ref, mine_ref, other_ref, *rest):
    outs, pool = rest[:-1], rest[-1]
    held = mine_ref.shape[0]
    heads = mine_ref.shape[1]
    count = 2 * held
    for n in range(held):
        pool[n] = mine_ref[n]
        pool[held + n] = other_ref[n]
    pool[count] = jnp.zeros(pool.shape[1:], BF16)
    dev = lax.axis_index("req")
    total_dev = groups * count
    column = dev // count
    place = (dev % count) // 2
    core = dev % 2

    def slot(row):
        here = (row // count) == column
        at = (row % count) // 2
        k = lax.rem(place - at + held, held)
        k = k + jnp.where((row % 2) == core, 0, held)
        return jnp.where(here, k, count)

    per = leaf_ref.shape[0] // total_dev
    rows = lax.broadcasted_iota(jnp.int32, (ROWS, LANES), 0)
    is_tail = (rows >= TAIL_ROW) & (rows < TAIL_ROW + 2)
    for out, k in zip(outs, shifts):
        target = lax.rem(dev + k * count, total_dev)
        for s in range(per):
            leaf = leaf_ref[target * per + s]
            middle = parent_ref[leaf]
            root = parent_ref[middle]
            at = [slot(owner_ref[n]) for n in (leaf, middle, root)]
            for h in range(heads):
                first, second, third = [pool[a, h].astype(F32) for a in at]
                total = first + jnp.where(is_tail, 0.0, second + third)
                out[s, h] = split_norm(total, 112)


def tp_place():
    index = lax.axis_index("tp")
    return index >> 1, index & 1


def place_blocks(scratch, blocks):
    x, z = tp_place()
    n = len(blocks)
    rows = blocks[0].shape[1]
    for k, block in enumerate(blocks):
        source = lax.rem(x - k + n, n)
        scratch[pl.ds(pl.multiple_of((2 * source + z) * rows, 32), rows), :] = block[0]
        scratch[pl.ds(pl.multiple_of((2 * source + 1 - z) * rows, 32), rows), :] = block[1]


def scaled_rows(scratch, gain_ref):
    gain = gain_ref[...].T
    squares = jnp.zeros((LANES, scratch.shape[1]), F32)
    for j in range(scratch.shape[0] // LANES):
        rows = scratch[j * LANES : (j + 1) * LANES, :].astype(F32)
        squares = squares + rows * rows
        scratch[j * LANES : (j + 1) * LANES, :] = (rows * gain[:, j : j + 1]).astype(BF16)
    mean = jnp.sum(squares, axis=0, keepdims=True) / scratch.shape[0]
    return lax.rsqrt(mean + EPSILON)


def silu(v):
    return v / (1.0 + jnp.exp(-v))


def local_kernel(
    total_req, own_ref, r1_ref, r2_ref, r3_ref, gain_ref, token_ref, query_ref, key_ref, value_ref, gate_ref,
    taps_ref, conv_ref, silu_ref, scores_ref, den_ref, right_ref, turned_ref, scratch,
):
    place_blocks(scratch, [own_ref, r1_ref, r2_ref, r3_ref])
    scale = scaled_rows(scratch, gain_ref)
    rows = scratch[...]
    queries = jnp.dot(query_ref[...], rows, preferred_element_type=F32) * scale
    keys = jnp.dot(key_ref[...], rows, preferred_element_type=F32) * scale
    values = (jnp.dot(value_ref[...], rows, preferred_element_type=F32) * scale).astype(BF16).astype(F32)
    gates = jnp.dot(gate_ref[...], rows, preferred_element_type=F32) * scale
    heads = scores_ref.shape[0]
    per = right_ref.shape[1] // ROWS
    feat_dim = queries.shape[0] // heads
    tokens = token_ref.shape[1]
    ids = token_ref[...]
    slot = jnp.where(ids >= total_req, per, ids - lax.axis_index("req") * per)
    lane = lax.broadcasted_iota(jnp.int32, (1, tokens), 1)
    start = jnp.zeros((1, tokens), jnp.int32)
    for s in range(per):
        amount = jnp.sum((slot == s).astype(jnp.int32), axis=1, keepdims=True)
        start = start + jnp.where(slot > s, amount, 0)
    position = lane - start
    source = lax.broadcasted_iota(jnp.int32, (tokens, tokens), 0)
    target = lax.broadcasted_iota(jnp.int32, (tokens, tokens), 1)
    allowed = (source >= start) & (source <= target)
    turned = jnp.concatenate([taps_ref[...], jnp.zeros((5, taps_ref.shape[1]), F32)], axis=0).T
    turned_ref[...] = turned
    taps = turned
    conv_ref[...] = (
        taps[:, 0:1] * values
        + taps[:, 1:2] * jnp.where(position >= 1, pltpu.roll(values, 1, axis=1), 0.0)
        + taps[:, 2:3] * jnp.where(position >= 2, pltpu.roll(values, 2, axis=1), 0.0)
    )
    silu_ref[...] = silu(gates)
    payload_row = lax.broadcasted_iota(jnp.int32, (ROWS, tokens), 0)
    lag_one = (position == 0) & (payload_row == TAIL_ROW + 1)
    lag_two = ((position == 0) & (payload_row == TAIL_ROW)) | ((position == 1) & (payload_row == TAIL_ROW + 1))
    half = feat_dim // 2
    one = (lax.broadcasted_iota(jnp.int32, (half, tokens), 0) == 0).astype(F32)
    for h in range(heads):
        query = queries[h * feat_dim : (h + 1) * feat_dim]
        key = keys[h * feat_dim : (h + 1) * feat_dim]
        blocks = [query * feat_dim ** (-0.25)]
        for gap in range(half):
            other = query if gap == 0 else pltpu.roll(query, feat_dim - gap, axis=0)
            blocks.append(query * other * (2.0 * feat_dim) ** (-0.5))
        blocks.append(query[:half] * query[half:] * (2.0 * feat_dim) ** (-0.5))
        blocks.append(one)
        feature = jnp.concatenate(blocks, axis=0)
        for s in range(per):
            member = slot == s
            at = slice(s * ROWS, (s + 1) * ROWS)
            right_ref[h, at, :tokens] = jnp.where(member, feature, 0.0).astype(BF16)
            right_ref[h, at, tokens : 2 * tokens] = (member & lag_one).astype(F32).astype(BF16)
            right_ref[h, at, 2 * tokens :] = (member & lag_two).astype(F32).astype(BF16)
        dots = lax.dot_general(
            key, query, (((0,), (0,)), ((), ())), preferred_element_type=F32, precision=lax.Precision.HIGHEST
        )
        scores = jnp.where(allowed, 1.0 + dots * feat_dim ** (-0.5) + dots * dots * (1.0 / (2.0 * feat_dim)), 0.0)
        den_ref[h] = jnp.sum(scores, axis=0, keepdims=True)
        scores_ref[h] = scores.astype(BF16)


def turn_kernel(in_ref, out_ref):
    for j in range(out_ref.shape[0] // LANES):
        at = slice(j * LANES, (j + 1) * LANES)
        out_ref[at, :] = in_ref[:, at].T


def turn(weight, name):
    return call(turn_kernel, sds(weight.shape[::-1], weight.dtype), [VMEM], (weight,), name=name)


def mix_kernel(
    conv_ref, silu_ref, scores_ref, den_ref, right_ref, taps_ref, p0_ref, p1_ref, p2_ref, p3_ref,
    out_weight_ref, *rest,
):
    outs, attended_ref = rest[:4], rest[4]
    per, heads = p0_ref.shape[:2]
    head_dim = attended_ref.shape[0] // heads
    tokens = attended_ref.shape[1]
    for h in range(heads):
        states = []
        for s in range(per):
            total = (
                p0_ref[s, h].astype(F32) + p1_ref[s, h].astype(F32) + p2_ref[s, h].astype(F32) + p3_ref[s, h].astype(F32)
            )
            states.append(split_norm(total, head_dim))
        reached = lax.dot_general(
            jnp.concatenate(states, axis=0), right_ref[h], (((0,), (0,)), ((), ())), preferred_element_type=F32
        )
        prefix_num = reached[:head_dim, :tokens]
        prefix_den = reached[head_dim : head_dim + 1, :tokens] + reached[head_dim + 1 : head_dim + 2, :tokens]
        at = slice(h * head_dim, (h + 1) * head_dim)
        taps = taps_ref[at, :]
        conv = (
            conv_ref[at, :]
            + taps[:, 1:2] * reached[:head_dim, tokens : 2 * tokens]
            + taps[:, 2:3] * reached[:head_dim, 2 * tokens :]
        )
        mixed = (conv * silu_ref[at, :]).astype(BF16)
        local_num = jnp.dot(mixed, scores_ref[h], preferred_element_type=F32)
        attended_ref[at, :] = ((local_num + prefix_num) / (den_ref[h] + prefix_den)).astype(BF16)
    spread_blocks(outs, out_weight_ref, attended_ref[...])


def spread_blocks(outs, weight_ref, right):
    x, z = tp_place()
    n = len(outs)
    rows = outs[0].shape[1]
    for k, out in enumerate(outs):
        to = lax.rem(x + k, n)
        for half, at in ((0, 2 * to + z), (1, 2 * to + 1 - z)):
            block = weight_ref[pl.ds(pl.multiple_of(at * rows, 32), rows), :]
            out[half] = jnp.dot(block, right, preferred_element_type=F32).astype(out.dtype)


def ffn_kernel(own_ref, r1_ref, r2_ref, r3_ref, gain_ref, gate_ref, up_ref, down_ref, *rest):
    outs, scratch = rest[:4], rest[4]
    place_blocks(scratch, [own_ref, r1_ref, r2_ref, r3_ref])
    scale = scaled_rows(scratch, gain_ref)
    gate = jnp.dot(gate_ref[...], scratch[...], preferred_element_type=F32) * scale
    up = jnp.dot(up_ref[...], scratch[...], preferred_element_type=F32) * scale
    spread_blocks(outs, down_ref, (silu(gate) * up).astype(BF16))


def shards(
    stream, token_req, request_leaf, parent, owner_map, node_state, node_norm, node_tail, mixer_gain, ffn_gain,
    query_weight, key_weight, value_weight, conv_gate_weight, conv_kernel, out_weight, ffn_gate, ffn_up, ffn_down,
):
    tokens, width = stream.shape
    heads, feats, head_dim = node_state.shape[1:]
    feat_dim = query_weight.shape[1] // heads
    model = value_weight.shape[0]
    req_size = lax.axis_size("req")
    tp_size = lax.axis_size("tp")
    x_size = tp_size // 2
    y_size, z_size = 4, req_size // 8
    per = request_leaf.shape[0] // req_size

    def along_x(array, k):
        return lax.ppermute(array, "tp", [(i, ((i // 2 + k) % x_size) * 2 + i % 2) for i in range(tp_size)])

    def across_z(array):
        return lax.ppermute(array, "tp", [(i, i ^ 1) for i in range(tp_size)])

    def along_z(array, k):
        count = 2 * z_size
        return lax.ppermute(
            array, "req", [(i, (i // count) * count + (((i % count) // 2 + k) % z_size) * 2 + i % 2) for i in range(req_size)]
        )

    def across_core(array):
        return lax.ppermute(array, "req", [(i, i ^ 1) for i in range(req_size)])

    def along_y(array, k):
        return lax.ppermute(array, "req", [(i, (i + 2 * z_size * k) % req_size) for i in range(req_size)])

    order = (1, 3, 2)

    fold = jnp.asarray(fold_matrix(feat_dim, feats), BF16)
    hbm = pl.BlockSpec(memory_space=pltpu.MemorySpace.HBM)
    state_in = jnp.transpose(node_state[0], (1, 0, 2))
    payload = call(
        fold_kernel,
        sds((heads, ROWS, LANES), BF16),
        [hbm] * 4,
        (fold, state_in, node_norm[0], node_tail[0]),
        scratch=[
            pltpu.VMEM(fold.shape, BF16),
            pltpu.VMEM(state_in.shape, BF16),
            pltpu.VMEM(node_norm[0].shape, BF16),
            pltpu.VMEM(node_tail[0].shape, BF16),
            pltpu.SemaphoreType.DMA((4,)),
        ],
        name="fold",
    )
    payload, own = lax.optimization_barrier((payload, stream.T))
    from_z = {k: along_z(payload, k) for k in order}

    pair = jnp.stack([own, across_z(own)])

    mine = jnp.stack([payload, from_z[1], from_z[2], from_z[3]])
    other = across_core(mine)
    def select(shifts, held, name):
        return call(
            functools.partial(select_kernel, y_size, shifts),
            [sds((per, heads, ROWS, LANES), BF16)] * len(shifts),
            [SMEM] * 3 + [VMEM] * 2,
            (request_leaf, parent, owner_map, *held),
            scratch=[pltpu.VMEM((2 * z_size + 1, heads, ROWS, LANES), BF16)],
            name=name,
        )

    sent = dict(zip(order, select(order, (mine, other), "select_sent")))
    mine, other, sent = lax.optimization_barrier((mine, other, sent))
    [kept] = select((0,), (mine, other), "select_kept")
    from_y = {k: along_y(sent[k], k) for k in order}

    rows = {k: along_x(pair, k) for k in order}
    gain_rows = model // LANES

    def gain_block(gain):
        return jnp.pad(gain.reshape(gain_rows, LANES), ((0, -gain_rows % 8), (0, 0)))

    local = call(
        functools.partial(local_kernel, request_leaf.shape[0]),
        [
            sds((width, tokens), F32),
            sds((width, tokens), F32),
            sds((heads, tokens, tokens), BF16),
            sds((heads, 1, tokens), F32),
            sds((heads, per * ROWS, 3 * tokens), BF16),
            sds((width, 8), F32),
        ],
        [VMEM] * 11,
        (
            pair, rows[1], rows[2], rows[3], gain_block(mixer_gain), token_req.reshape(1, tokens),
            query_weight.T, key_weight.T, value_weight.T, conv_gate_weight.T, conv_kernel,
        ),
        scratch=[pltpu.VMEM((model, tokens), BF16)],
        name="local",
    )
    parts = call(
        mix_kernel,
        [sds((2, width, tokens), F32)] + [sds((2, width, tokens), BF16)] * (x_size - 1),
        [VMEM] * 11,
        (*local, kept, from_y[1], from_y[2], from_y[3], turn(out_weight, "turn_out")),
        scratch=[pltpu.VMEM((width, tokens), BF16)],
        name="mix",
    )
    got = {k: along_x(parts[k], k) for k in order}
    share = parts[0] + got[1].astype(F32) + got[2].astype(F32) + got[3].astype(F32)
    crossing, down_in = lax.optimization_barrier((jnp.stack([share[1], share[0]]).astype(BF16), ffn_down))
    share_peer = across_z(crossing)
    updated = (pair.astype(F32) + share + share_peer.astype(F32)).astype(BF16)
    updated, down_turned = lax.optimization_barrier((updated, turn(down_in, "turn_down")))

    wide = {k: along_x(updated, k) for k in order}
    downs = call(
        ffn_kernel,
        [sds((2, width, tokens), F32)] + [sds((2, width, tokens), BF16)] * (x_size - 1),
        [VMEM] * 8,
        (updated, wide[1], wide[2], wide[3], gain_block(ffn_gain), ffn_gate.T, ffn_up.T, down_turned),
        scratch=[pltpu.VMEM((model, tokens), BF16)],
        name="ffn",
    )
    back = {k: along_x(downs[k], k) for k in order}
    down_share = downs[0] + back[1].astype(F32) + back[2].astype(F32) + back[3].astype(F32)
    down_peer = across_z(down_share[1].astype(BF16))
    result = updated[0].astype(F32) + down_share[0] + down_peer.astype(F32)
    return result.astype(BF16).T


def solution(mesh):
    in_specs = (
        P("req", "tp"), P("req"), P(), P(), P(), P("req", "tp", None, None), P("req", "tp", None), P("req", None, "tp"),
        P(), P(), P(None, "tp"), P(None, "tp"), P(None, "tp"), P(None, "tp"), P(None, "tp"), P("tp", None),
        P(None, "tp"), P(None, "tp"), P("tp", None),
    )
    return jax.shard_map(shards, mesh=mesh, in_specs=in_specs, out_specs=P("req", "tp"), check_vma=False)
```

time: 96.4 us -> 97.9 us (1.016); the launches traced: 95.9 us -> 96.1 us
  waiting for transfers between devices: 30.2 us -> 39.4 us
  local copies, waits for them, and re-layouts: 11.9 us -> 5.39 us
  other arithmetic: 6.49 us -> 1.73 us
  starting transfers between devices: 37.9 us -> 40.7 us
    ppermute x12, waiting for transfers between devices: 15.7 us -> 22.5 us  [along_x(): lax.ppermute(array, 'tp', [(i, (i // 2 + k) % x_size * 2 + i % 2) for i i...]
    convert_element_type x2 -> x0, other arithmetic: 4.56 us -> none  [the longest x1 2.84 us: shards(): up_scaled = (up_in.T.astype(F32) * ffn_gain[None, :]).astype(BF16)]
    ppermute x3, starting transfers between devices: 11.3 us -> 15.4 us  [across_z(): return lax.ppermute(array, 'tp', [(i, i ^ 1) for i in range(tp_size)])]
    ppermute x3, waiting for transfers between devices: 3.49 us -> 0.01 us  [along_y(): lax.ppermute(array, 'req', [(i, (i + 2 * z_size * k) % req_size) for i in...]
    ppermute x3, waiting for transfers between devices: 3.39 us -> 6.86 us  [along_z(): lax.ppermute(array, 'req', [(i, i // count * count + (i % count // 2 + k)...]
    optimization_barrier x1 -> x0, local copies, waits for them, and re-layouts: 3.28 us -> none  [shards(): lax.optimization_barrier((jnp.stack([share[1], share[0]]).astype(BF16), f...]
    unnamed x36 -> x46, local copies, waits for them, and re-layouts: 8.62 us -> 5.36 us
    ppermute x12, starting transfers between devices: 18.1 us -> 14.8 us  [along_x(): lax.ppermute(array, 'tp', [(i, (i // 2 + k) % x_size * 2 + i % 2) for i i...]
  transfers between devices with their start and end apart: 22 -> 22, of which waited for: 13 -> 14; matrix products, arithmetic and copies ran while one was open for 11% -> 1% of each run, Pallas kernels for 4% -> 5%
where the time goes in v3:
time: 97.9 us; the launch traced here: 96.1 us
  starting transfers between devices  40.7 us (42%)
  waiting for transfers between devices  39.4 us (40%)
  Pallas kernels  8.63 us (9%)
  local copies, waits for them, and re-layouts  5.39 us (6%)
  other arithmetic  1.73 us (2%)
    ppermute x12, waiting for transfers between devices, along_x(): lax.ppermute(array, 'tp', [(i, (i // 2 + k) % x_size * 2 + i % 2) for i i...  22.5 us
    ppermute x3, starting transfers between devices, across_z(): return lax.ppermute(array, 'tp', [(i, i ^ 1) for i in range(tp_size)])  15.4 us
    ppermute x12, starting transfers between devices, along_x(): lax.ppermute(array, 'tp', [(i, (i // 2 + k) % x_size * 2 + i % 2) for i i...  14.8 us
    ppermute x3, waiting for transfers between devices, across_z(): return lax.ppermute(array, 'tp', [(i, i ^ 1) for i in range(tp_size)])  10 us
    pallas_call x8, Pallas kernels, call(): pl.pallas_call(kernel, out_shape=out_shape, in_specs=specs, out_specs=VME...  8.63 us
    ppermute x3, waiting for transfers between devices, along_z(): lax.ppermute(array, 'req', [(i, i // count * count + (i % count // 2 + k)...  6.86 us
    ppermute x3, starting transfers between devices, along_z(): lax.ppermute(array, 'req', [(i, i // count * count + (i % count // 2 + k)...  5.37 us
    unnamed x46, local copies, waits for them, and re-layouts  5.36 us
  transfers between devices with their start and end apart: 22, of which 14 were waited for; matrix products, arithmetic and copies ran while one was open for 1% of the time, Pallas kernels for 5%

profile of v3, /device:TPU:8, one launch (start us, length us, event | category | flops | bytes accessed | tf_op | source)
XLA Modules:
  0.0 96.1 jit_solution(2389626016975245118)
XLA Ops:
  0.0 1.0 %copy-done.6 = bf16[1,2,273,112]{3,1,2,0:T(2,128)(2,1)S(1)} copy-done((bf16[1,2,273,112]{3,1,2,0:T(2,128)(2,1)S(1)}, bf16[1,2,273,112]{3,1,2,0:T(2,128)(2,1)}, u32[]{:S(2)}) %copy-start.6) | copy-done | bytes 122328
  3.3 1.0 %fold.1 = bf16[2,160,128]{2,1,0:T(8,128)(2,1)S(1)} custom-call(bf16[160,273]{1,0:T(8,128)(2,1)S(1)} %copy-done.7, bf16[273,2,112]{2,1,0:T(2,128)(2,1)S(1)} %bitcast.38, bf16[2,273]{1,0:T(2,128)(2,1)S(1)} %bitcast.41, bf16[2,224]{1,0:T(2,128)(2,1)S(1)} %bitcast.42), custom_call_target="tpu_custom_call" | custom-call | tf_op jit(solution)/shard_map/fold/pallas_call | solution.py:25
  4.3 4.7 %collective-permute-start.6 = (bf16[2,160,128]{2,1,0:T(8,128)(2,1)S(1)}, bf16[2,160,128]{2,1,0:T(8,128)(2,1)S(1)}, u32[]{:S(2)}, u32[]{:S(2)}) collective-permute-start(bf16[2,160,128]{2,1,0:T(8,128)(2,1)S(1)} %fold.1), channel_id=1, source_target_pairs={{0,48},{8,56},{16,0},{24,8},{32,16},{40,24},{48,32},{56,40},{64,11... | collective-permute-start | bytes 245768 | tf_op jit(solution)/shard_map/ppermute | solution.py:301
  9.7 2.2 %collective-permute-done.6 = bf16[2,160,128]{2,1,0:T(8,128)(2,1)S(1)} collective-permute-done((bf16[2,160,128]{2,1,0:T(8,128)(2,1)S(1)}, bf16[2,160,128]{2,1,0:T(8,128)(2,1)S(1)}, u32[]{:S(2)}, u32[]{:S(2)}) %collective-permute-start.6) | collective-permute-done | bytes 81952 | tf_op jit(solution)/shard_map/ppermute | solution.py:301
  11.9 4.7 %collective-permute-done.5 = bf16[2,160,128]{2,1,0:T(8,128)(2,1)S(1)} collective-permute-done((bf16[2,160,128]{2,1,0:T(8,128)(2,1)S(1)}, bf16[2,160,128]{2,1,0:T(8,128)(2,1)S(1)}, u32[]{:S(2)}, u32[]{:S(2)}) %collective-permute-start.5) | collective-permute-done | bytes 81952 | tf_op jit(solution)/shard_map/ppermute | solution.py:301
  16.7 5.3 %collective-permute-start = (bf16[224,128]{1,0:T(8,128)(2,1)}, bf16[224,128]{1,0:T(8,128)(2,1)S(1)}, u32[]{:S(2)}, u32[]{:S(2)}) collective-permute-start(bf16[224,128]{1,0:T(8,128)(2,1)} %bitcast.44), channel_id=1, source_target_pairs={{0,1},{1,0},{2,3},{3,2},{4,5},{5,4},{6,7},{7,6},{8,9},{9,8},{10,11... | collective-permute-start | bytes 172040 | tf_op jit(solution)/shard_map/ppermute | solution.py:297
  22.0 3.3 %collective-permute-done = bf16[224,128]{1,0:T(8,128)(2,1)S(1)} collective-permute-done((bf16[224,128]{1,0:T(8,128)(2,1)}, bf16[224,128]{1,0:T(8,128)(2,1)S(1)}, u32[]{:S(2)}, u32[]{:S(2)}) %collective-permute-start) | collective-permute-done | bytes 57376 | tf_op jit(solution)/shard_map/ppermute | solution.py:297
  26.1 2.8 %collective-permute-start.3 = (bf16[2,224,128]{2,1,0:T(8,128)(2,1)S(1)}, bf16[2,224,128]{2,1,0:T(8,128)(2,1)S(1)}, u32[]{:S(2)}, u32[]{:S(2)}) collective-permute-start(bf16[2,224,128]{2,1,0:T(8,128)(2,1)S(1)} %pad_maximum_fusion.1.own_ref), channel_id=1, source_target_pairs={{0,6},{1,7},{2,0},{3,1},{4,2},{5,3},{6,4},{7,5},{8,14},{9,15},{10,... | collective-permute-start | bytes 344072 | tf_op jit(solution)/shard_map/ppermute | solution.py:294
  30.9 1.1 %select_sent.1 = (bf16[2,2,160,128]{3,2,1,0:T(8,128)(2,1)S(1)}, bf16[2,2,160,128]{3,2,1,0:T(8,128)(2,1)S(1)}, bf16[2,2,160,128]{3,2,1,0:T(8,128)(2,1)S(1)}) custom-call(s32[64]{0:T(128)S(1)} %copy-done.11, s32[32]{0:T(128)S(1)} %copy-done.13, s32[32]{0:T(128)S(1)} %copy-done.15, bf16[4,2,160,128]{3,2,1,0:T(8,128)(2,1)S(1)} %pad_maximum_fusion.mine_ref, ...), custom_call_target="tpu_custom_call" | custom-call | tf_op jit(solution)/shard_map/select_sent/pallas_call | solution.py:25
  32.0 1.7 %collective-permute-start.8 = (bf16[2,2,160,128]{3,2,1,0:T(8,128)(2,1)S(1)}, bf16[2,2,160,128]{3,2,1,0:T(8,128)(2,1)S(1)}, u32[]{:S(2)}, u32[]{:S(2)}) collective-permute-start(bf16[2,2,160,128]{3,2,1,0:T(8,128)(2,1)S(1)} %get-tuple-element.46), channel_id=1, source_target_pairs={{0,64},{8,72},{16,80},{24,88},{32,96},{40,104},{48,112},{56,120},{... | collective-permute-start | bytes 491528 | tf_op jit(solution)/shard_map/ppermute | solution.py:309
  33.7 0.9 collective-permute-start.9
  34.6 2.4 %collective-permute-start.10 = (bf16[2,2,160,128]{3,2,1,0:T(8,128)(2,1)S(1)}, bf16[2,2,160,128]{3,2,1,0:T(8,128)(2,1)S(1)}, u32[]{:S(2)}, u32[]{:S(2)}) collective-permute-start(bf16[2,2,160,128]{3,2,1,0:T(8,128)(2,1)S(1)} %get-tuple-element.48), channel_id=1, source_target_pairs={{0,192},{8,200},{16,208},{24,216},{32,224},{40,232},{48,240},{56,2... | collective-permute-start | bytes 491528 | tf_op jit(solution)/shard_map/ppermute | solution.py:309
  39.0 4.4 %collective-permute-done.2.r2_ref = bf16[2,224,128]{2,1,0:T(8,128)(2,1)S(1)} collective-permute-done((bf16[2,224,128]{2,1,0:T(8,128)(2,1)S(1)}, bf16[2,224,128]{2,1,0:T(8,128)(2,1)S(1)}, u32[]{:S(2)}, u32[]{:S(2)}) %collective-permute-start.2) | collective-permute-done | bytes 114720 | tf_op jit(solution)/shard_map/ppermute | solution.py:294
  43.4 1.2 %collective-permute-done.1.r1_ref = bf16[2,224,128]{2,1,0:T(8,128)(2,1)S(1)} collective-permute-done((bf16[2,224,128]{2,1,0:T(8,128)(2,1)S(1)}, bf16[2,224,128]{2,1,0:T(8,128)(2,1)S(1)}, u32[]{:S(2)}, u32[]{:S(2)}) %collective-permute-start.1) | collective-permute-done | bytes 114720 | tf_op jit(solution)/shard_map/ppermute | solution.py:294
  44.6 1.5 %local.1 = (f32[224,128]{1,0:T(8,128)S(1)}, f32[224,128]{1,0:T(8,128)S(1)}, bf16[2,128,128]{2,1,0:T(8,128)(2,1)S(1)}, f32[2,1,128]{2,1,0:T(1,128)S(1)}, bf16[2,3...) custom-call(bf16[2,224,128]{2,1,0:T(8,128)(2,1)S(1)} %pad_maximum_fusion.1.own_ref, ...), custom_call_target="tpu_custom_call" | custom-call | tf_op jit(solution)/shard_map/local/pallas_call | solution.py:25
  47.0 1.1 %mix.1 = (f32[2,224,128]{2,1,0:T(8,128)S(1)}, bf16[2,224,128]{2,1,0:T(8,128)(2,1)S(1)}, bf16[2,224,128]{2,1,0:T(8,128)(2,1)S(1)}, bf16[2,224,128]{2,1,0:T(8,128)(2,1)S(1)}) custom-call(f32[224,128]{1,0:T(8,128)S(1)} %get-tuple-element.34.conv_ref, f32[224,128]{1,0:T(8,128)S(1)} %get-tuple-element.35.silu_ref, ...), custom_call_target="tpu_custom_call" | custom-call | tf_op jit(solution)/shard_map/mix/pallas_call | solution.py:25
  48.2 2.0 %collective-permute-start.12 = (bf16[2,224,128]{2,1,0:T(8,128)(2,1)S(1)}, bf16[2,224,128]{2,1,0:T(8,128)(2,1)S(1)}, u32[]{:S(2)}, u32[]{:S(2)}) collective-permute-start(bf16[2,224,128]{2,1,0:T(8,128)(2,1)S(1)} %get-tuple-element.51), channel_id=1, source_target_pairs={{0,4},{1,5},{2,6},{3,7},{4,0},{5,1},{6,2},{7,3},{8,12},{9,13},{10,... | collective-permute-start | bytes 344072 | tf_op jit(solution)/shard_map/ppermute | solution.py:294
  50.2 1.4 %collective-permute-start.13 = (bf16[2,224,128]{2,1,0:T(8,128)(2,1)S(1)}, bf16[2,224,128]{2,1,0:T(8,128)(2,1)S(1)}, u32[]{:S(2)}, u32[]{:S(2)}) collective-permute-start(bf16[2,224,128]{2,1,0:T(8,128)(2,1)S(1)} %get-tuple-element.52), channel_id=1, source_target_pairs={{0,6},{1,7},{2,0},{3,1},{4,2},{5,3},{6,4},{7,5},{8,14},{9,15},{10,... | collective-permute-start | bytes 344072 | tf_op jit(solution)/shard_map/ppermute | solution.py:294
  51.6 3.8 %collective-permute-done.11 = bf16[2,224,128]{2,1,0:T(8,128)(2,1)S(1)} collective-permute-done((bf16[2,224,128]{2,1,0:T(8,128)(2,1)S(1)}, bf16[2,224,128]{2,1,0:T(8,128)(2,1)S(1)}, u32[]{:S(2)}, u32[]{:S(2)}) %collective-permute-start.11) | collective-permute-done | bytes 114720 | tf_op jit(solution)/shard_map/ppermute | solution.py:294
  55.4 0.9 collective-permute-done.13
  56.4 5.7 %collective-permute-start.14 = (bf16[2,224,128]{2,1,0:T(8,128)(2,1)S(1)}, bf16[2,224,128]{2,1,0:T(8,128)(2,1)S(1)}, u32[]{:S(2)}, u32[]{:S(2)}) collective-permute-start(bf16[2,224,128]{2,1,0:T(8,128)(2,1)S(1)} %pad_maximum_fusion.2), channel_id=1, source_target_pairs={{0,1},{1,0},{2,3},{3,2},{4,5},{5,4},{6,7},{7,6},{8,9},{9,8},{10,11... | collective-permute-start | bytes 344072 | tf_op jit(solution)/shard_map/ppermute | solution.py:297
  62.8 3.0 %collective-permute-done.14 = bf16[2,224,128]{2,1,0:T(8,128)(2,1)S(1)} collective-permute-done((bf16[2,224,128]{2,1,0:T(8,128)(2,1)S(1)}, bf16[2,224,128]{2,1,0:T(8,128)(2,1)S(1)}, u32[]{:S(2)}, u32[]{:S(2)}) %collective-permute-start.14) | collective-permute-done | bytes 114720 | tf_op jit(solution)/shard_map/ppermute | solution.py:297
  65.8 2.5 %collective-permute-start.17 = (bf16[2,224,128]{2,1,0:T(8,128)(2,1)S(1)}, bf16[2,224,128]{2,1,0:T(8,128)(2,1)S(1)}, u32[]{:S(2)}, u32[]{:S(2)}) collective-permute-start(bf16[2,224,128]{2,1,0:T(8,128)(2,1)S(1)} %add_convert_fusion.own_ref), channel_id=1, source_target_pairs={{0,6},{1,7},{2,0},{3,1},{4,2},{5,3},{6,4},{7,5},{8,14},{9,15},{10,... | collective-permute-start | bytes 344072 | tf_op jit(solution)/shard_map/ppermute | solution.py:294
  69.3 2.6 %collective-permute-done.17.r3_ref = bf16[2,224,128]{2,1,0:T(8,128)(2,1)S(1)} collective-permute-done((bf16[2,224,128]{2,1,0:T(8,128)(2,1)S(1)}, bf16[2,224,128]{2,1,0:T(8,128)(2,1)S(1)}, u32[]{:S(2)}, u32[]{:S(2)}) %collective-permute-start.17) | collective-permute-done | bytes 114720 | tf_op jit(solution)/shard_map/ppermute | solution.py:294
  71.9 3.5 %collective-permute-done.16.r2_ref = bf16[2,224,128]{2,1,0:T(8,128)(2,1)S(1)} collective-permute-done((bf16[2,224,128]{2,1,0:T(8,128)(2,1)S(1)}, bf16[2,224,128]{2,1,0:T(8,128)(2,1)S(1)}, u32[]{:S(2)}, u32[]{:S(2)}) %collective-permute-start.16) | collective-permute-done | bytes 114720 | tf_op jit(solution)/shard_map/ppermute | solution.py:294
  75.3 1.4 %collective-permute-done.15.r1_ref = bf16[2,224,128]{2,1,0:T(8,128)(2,1)S(1)} collective-permute-done((bf16[2,224,128]{2,1,0:T(8,128)(2,1)S(1)}, bf16[2,224,128]{2,1,0:T(8,128)(2,1)S(1)}, u32[]{:S(2)}, u32[]{:S(2)}) %collective-permute-start.15) | collective-permute-done | bytes 114720 | tf_op jit(solution)/shard_map/ppermute | solution.py:294
  76.8 2.2 %ffn.1 = (f32[2,224,128]{2,1,0:T(8,128)S(1)}, bf16[2,224,128]{2,1,0:T(8,128)(2,1)S(1)}, bf16[2,224,128]{2,1,0:T(8,128)(2,1)S(1)}, bf16[2,224,128]{2,1,0:T(8,128)(2,1)S(1)}) custom-call(bf16[2,224,128]{2,1,0:T(8,128)(2,1)S(1)} %add_convert_fusion.own_ref, bf16[2,224,128]{2,1,0:T(8,128)(2,1)S(1)} %collective-permute-done.15.r1_ref, ...), custom_call_target="tpu_custom_call" | custom-call | tf_op jit(solution)/shard_map/ffn/pallas_call | solution.py:25
  79.1 3.0 %collective-permute-start.19 = (bf16[2,224,128]{2,1,0:T(8,128)(2,1)S(1)}, bf16[2,224,128]{2,1,0:T(8,128)(2,1)S(1)}, u32[]{:S(2)}, u32[]{:S(2)}) collective-permute-start(bf16[2,224,128]{2,1,0:T(8,128)(2,1)S(1)} %get-tuple-element.59), channel_id=1, source_target_pairs={{0,4},{1,5},{2,6},{3,7},{4,0},{5,1},{6,2},{7,3},{8,12},{9,13},{10,... | collective-permute-start | bytes 344072 | tf_op jit(solution)/shard_map/ppermute | solution.py:294
  82.4 3.9 %collective-permute-done.18 = bf16[2,224,128]{2,1,0:T(8,128)(2,1)S(1)} collective-permute-done((bf16[2,224,128]{2,1,0:T(8,128)(2,1)S(1)}, bf16[2,224,128]{2,1,0:T(8,128)(2,1)S(1)}, u32[]{:S(2)}, u32[]{:S(2)}) %collective-permute-start.18) | collective-permute-done | bytes 114720 | tf_op jit(solution)/shard_map/ppermute | solution.py:294
  86.3 0.9 collective-permute-done.20
  87.3 4.4 %collective-permute-start.21 = (bf16[224,128]{1,0:T(8,128)(2,1)S(1)}, bf16[224,128]{1,0:T(8,128)(2,1)S(1)}, u32[]{:S(2)}, u32[]{:S(2)}) collective-permute-start(bf16[224,128]{1,0:T(8,128)(2,1)S(1)} %fusion.4), channel_id=1, source_target_pairs={{0,1},{1,0},{2,3},{3,2},{4,5},{5,4},{6,7},{7,6},{8,9},{9,8},{10,11... | collective-permute-start | bytes 172040 | tf_op jit(solution)/shard_map/ppermute | solution.py:297
  91.7 3.8 %collective-permute-done.21 = bf16[224,128]{1,0:T(8,128)(2,1)S(1)} collective-permute-done((bf16[224,128]{1,0:T(8,128)(2,1)S(1)}, bf16[224,128]{1,0:T(8,128)(2,1)S(1)}, u32[]{:S(2)}, u32[]{:S(2)}) %collective-permute-start.21) | collective-permute-done | bytes 57376 | tf_op jit(solution)/shard_map/ppermute | solution.py:297
  (77 shorter events, 11.7 us)
Async XLA Ops:
  0.0 38.7 %copy-start.5 = (bf16[224,1792]{1,0:T(8,128)(2,1)S(1)}, bf16[224,1792]{1,0:T(8,128)(2,1)}, u32[]{:S(2)}) copy-start(bf16[224,1792]{1,0:T(8,128)(2,1)} %in_ref.1) | copy-start | bytes 2408452
  0.0 44.5 %copy-start.4 = (bf16[1792,224]{0,1:T(8,128)(2,1)S(1)}, bf16[1792,224]{0,1:T(8,128)(2,1)}, u32[]{:S(2)}) copy-start(bf16[1792,224]{0,1:T(8,128)(2,1)} %param.33) | copy-start | bytes 2408452
  0.0 44.5 %copy-start.3 = (bf16[1792,224]{0,1:T(8,128)(2,1)S(1)}, bf16[1792,224]{0,1:T(8,128)(2,1)}, u32[]{:S(2)}) copy-start(bf16[1792,224]{0,1:T(8,128)(2,1)} %param.32) | copy-start | bytes 2408452
  3.3 41.2 %copy-start.8 = (bf16[1792,32]{0,1:T(8,128)(2,1)S(1)}, bf16[1792,32]{0,1:T(8,128)(2,1)}, u32[]{:S(2)}) copy-start(bf16[1792,32]{0,1:T(8,128)(2,1)} %param.30) | copy-start | bytes 344068
  3.3 41.2 %copy-start.9 = (bf16[1792,32]{0,1:T(8,128)(2,1)S(1)}, bf16[1792,32]{0,1:T(8,128)(2,1)}, u32[]{:S(2)}) copy-start(bf16[1792,32]{0,1:T(8,128)(2,1)} %param.31) | copy-start | bytes 344068
  3.3 41.2 %copy-start.10 = (f32[3,224]{1,0:T(4,128)S(1)}, f32[3,224]{1,0:T(4,128)}, u32[]{:S(2)}) copy-start(f32[3,224]{1,0:T(4,128)} %taps_ref.1) | copy-start | bytes 8068
  4.3 7.6 %collective-permute-start.6 = (bf16[2,160,128]{2,1,0:T(8,128)(2,1)S(1)}, bf16[2,160,128]{2,1,0:T(8,128)(2,1)S(1)}, u32[]{:S(2)}, u32[]{:S(2)}) collective-permute-start(bf16[2,160,128]{2,1,0:T(8,128)(2,1)S(1)} %fold.1), channel_id=1, source_target_pairs={{0,48},{8,56},{16,0},{24,8},{32,16},{40,24},{48,32},{56,40},{64,11... | collective-permute-start | bytes 245768 | tf_op jit(solution)/shard_map/ppermute | solution.py:301
  9.0 7.5 %collective-permute-start.5 = (bf16[2,160,128]{2,1,0:T(8,128)(2,1)S(1)}, bf16[2,160,128]{2,1,0:T(8,128)(2,1)S(1)}, u32[]{:S(2)}, u32[]{:S(2)}) collective-permute-start(bf16[2,160,128]{2,1,0:T(8,128)(2,1)S(1)} %fold.1), channel_id=1, source_target_pairs={{0,32},{8,40},{16,48},{24,56},{32,0},{40,8},{48,16},{56,24},{64,96... | collective-permute-start | bytes 245768 | tf_op jit(solution)/shard_map/ppermute | solution.py:301
  9.0 7.5 %collective-permute-start.4 = (bf16[2,160,128]{2,1,0:T(8,128)(2,1)S(1)}, bf16[2,160,128]{2,1,0:T(8,128)(2,1)S(1)}, u32[]{:S(2)}, u32[]{:S(2)}) collective-permute-start(bf16[2,160,128]{2,1,0:T(8,128)(2,1)S(1)} %fold.1), channel_id=1, source_target_pairs={{0,16},{8,24},{16,32},{24,40},{32,48},{40,56},{48,0},{56,8},{64,80... | collective-permute-start | bytes 245768 | tf_op jit(solution)/shard_map/ppermute | solution.py:301
  16.6 12.3 %collective-permute-start.7 = (bf16[4,2,160,128]{3,2,1,0:T(8,128)(2,1)S(1)}, bf16[4,2,160,128]{3,2,1,0:T(8,128)(2,1)S(1)}, u32[]{:S(2)}, u32[]{:S(2)}) collective-permute-start(bf16[4,2,160,128]{3,2,1,0:T(8,128)(2,1)S(1)} %pad_maximum_fusion.mine_ref), channel_id=1, source_target_pairs={{0,8},{8,0},{16,24},{24,16},{32,40},{40,32},{48,56},{56,48},{64,72... | collective-permute-start | bytes 983048 | tf_op jit(solution)/shard_map/ppermute | solution.py:306
  16.7 8.6 %collective-permute-start = (bf16[224,128]{1,0:T(8,128)(2,1)}, bf16[224,128]{1,0:T(8,128)(2,1)S(1)}, u32[]{:S(2)}, u32[]{:S(2)}) collective-permute-start(bf16[224,128]{1,0:T(8,128)(2,1)} %bitcast.44), channel_id=1, source_target_pairs={{0,1},{1,0},{2,3},{3,2},{4,5},{5,4},{6,7},{7,6},{8,9},{9,8},{10,11... | collective-permute-start | bytes 172040 | tf_op jit(solution)/shard_map/ppermute | solution.py:297
  26.1 11.7 %collective-permute-start.3 = (bf16[2,224,128]{2,1,0:T(8,128)(2,1)S(1)}, bf16[2,224,128]{2,1,0:T(8,128)(2,1)S(1)}, u32[]{:S(2)}, u32[]{:S(2)}) collective-permute-start(bf16[2,224,128]{2,1,0:T(8,128)(2,1)S(1)} %pad_maximum_fusion.1.own_ref), channel_id=1, source_target_pairs={{0,6},{1,7},{2,0},{3,1},{4,2},{5,3},{6,4},{7,5},{8,14},{9,15},{10,... | collective-permute-start | bytes 344072 | tf_op jit(solution)/shard_map/ppermute | solution.py:294
  32.0 14.2 %copy-start.12 = (s32[64]{0:T(128)S(1)}, s32[64]{0:T(128)}, u32[]{:S(2)}) copy-start(s32[64]{0:T(128)} %leaf_ref.3) | copy-start | bytes 772
  32.0 15.0 %collective-permute-start.8 = (bf16[2,2,160,128]{3,2,1,0:T(8,128)(2,1)S(1)}, bf16[2,2,160,128]{3,2,1,0:T(8,128)(2,1)S(1)}, u32[]{:S(2)}, u32[]{:S(2)}) collective-permute-start(bf16[2,2,160,128]{3,2,1,0:T(8,128)(2,1)S(1)} %get-tuple-element.46), channel_id=1, source_target_pairs={{0,64},{8,72},{16,80},{24,88},{32,96},{40,104},{48,112},{56,120},{... | collective-permute-start | bytes 491528 | tf_op jit(solution)/shard_map/ppermute | solution.py:309
  33.7 13.3 %collective-permute-start.9 = (bf16[2,2,160,128]{3,2,1,0:T(8,128)(2,1)S(1)}, bf16[2,2,160,128]{3,2,1,0:T(8,128)(2,1)S(1)}, u32[]{:S(2)}, u32[]{:S(2)}) collective-permute-start(bf16[2,2,160,128]{3,2,1,0:T(8,128)(2,1)S(1)} %get-tuple-element.47), channel_id=1, source_target_pairs={{0,128},{8,136},{16,144},{24,152},{32,160},{40,168},{48,176},{56,1... | collective-permute-start | bytes 491528 | tf_op jit(solution)/shard_map/ppermute | solution.py:309
  34.6 12.4 %collective-permute-start.10 = (bf16[2,2,160,128]{3,2,1,0:T(8,128)(2,1)S(1)}, bf16[2,2,160,128]{3,2,1,0:T(8,128)(2,1)S(1)}, u32[]{:S(2)}, u32[]{:S(2)}) collective-permute-start(bf16[2,2,160,128]{3,2,1,0:T(8,128)(2,1)S(1)} %get-tuple-element.48), channel_id=1, source_target_pairs={{0,192},{8,200},{16,208},{24,216},{32,224},{40,232},{48,240},{56,2... | collective-permute-start | bytes 491528 | tf_op jit(solution)/shard_map/ppermute | solution.py:309
  37.0 6.4 %collective-permute-start.2 = (bf16[2,224,128]{2,1,0:T(8,128)(2,1)S(1)}, bf16[2,224,128]{2,1,0:T(8,128)(2,1)S(1)}, u32[]{:S(2)}, u32[]{:S(2)}) collective-permute-start(bf16[2,224,128]{2,1,0:T(8,128)(2,1)S(1)} %pad_maximum_fusion.1.own_ref), channel_id=1, source_target_pairs={{0,4},{1,5},{2,6},{3,7},{4,0},{5,1},{6,2},{7,3},{8,12},{9,13},{10,... | collective-permute-start | bytes 344072 | tf_op jit(solution)/shard_map/ppermute | solution.py:294
  37.8 6.7 %collective-permute-start.1 = (bf16[2,224,128]{2,1,0:T(8,128)(2,1)S(1)}, bf16[2,224,128]{2,1,0:T(8,128)(2,1)S(1)}, u32[]{:S(2)}, u32[]{:S(2)}) collective-permute-start(bf16[2,224,128]{2,1,0:T(8,128)(2,1)S(1)} %pad_maximum_fusion.1.own_ref), channel_id=1, source_target_pairs={{0,2},{1,3},{2,4},{3,5},{4,6},{5,7},{6,0},{7,1},{8,10},{9,11},{10,... | collective-permute-start | bytes 344072 | tf_op jit(solution)/shard_map/ppermute | solution.py:294
  46.2 16.0 %copy-start = (bf16[608,1792]{1,0:T(8,128)(2,1)S(1)}, bf16[608,1792]{1,0:T(8,128)(2,1)}, u32[]{:S(2)}) copy-start(bf16[608,1792]{1,0:T(8,128)(2,1)} %in_ref.2) | copy-start | bytes 6537220
  48.1 7.3 %collective-permute-start.11 = (bf16[2,224,128]{2,1,0:T(8,128)(2,1)S(1)}, bf16[2,224,128]{2,1,0:T(8,128)(2,1)S(1)}, u32[]{:S(2)}, u32[]{:S(2)}) collective-permute-start(bf16[2,224,128]{2,1,0:T(8,128)(2,1)S(1)} %get-tuple-element.50), channel_id=1, source_target_pairs={{0,2},{1,3},{2,4},{3,5},{4,6},{5,7},{6,0},{7,1},{8,10},{9,11},{10,... | collective-permute-start | bytes 344072 | tf_op jit(solution)/shard_map/ppermute | solution.py:294
  48.2 7.2 %collective-permute-start.12 = (bf16[2,224,128]{2,1,0:T(8,128)(2,1)S(1)}, bf16[2,224,128]{2,1,0:T(8,128)(2,1)S(1)}, u32[]{:S(2)}, u32[]{:S(2)}) collective-permute-start(bf16[2,224,128]{2,1,0:T(8,128)(2,1)S(1)} %get-tuple-element.51), channel_id=1, source_target_pairs={{0,4},{1,5},{2,6},{3,7},{4,0},{5,1},{6,2},{7,3},{8,12},{9,13},{10,... | collective-permute-start | bytes 344072 | tf_op jit(solution)/shard_map/ppermute | solution.py:294
  50.2 6.1 %collective-permute-start.13 = (bf16[2,224,128]{2,1,0:T(8,128)(2,1)S(1)}, bf16[2,224,128]{2,1,0:T(8,128)(2,1)S(1)}, u32[]{:S(2)}, u32[]{:S(2)}) collective-permute-start(bf16[2,224,128]{2,1,0:T(8,128)(2,1)S(1)} %get-tuple-element.52), channel_id=1, source_target_pairs={{0,6},{1,7},{2,0},{3,1},{4,2},{5,3},{6,4},{7,5},{8,14},{9,15},{10,... | collective-permute-start | bytes 344072 | tf_op jit(solution)/shard_map/ppermute | solution.py:294
  56.4 20.4 %copy-start.1 = (bf16[1792,608]{0,1:T(8,128)(2,1)S(1)}, bf16[1792,608]{0,1:T(8,128)(2,1)}, u32[]{:S(2)}) copy-start(bf16[1792,608]{0,1:T(8,128)(2,1)} %param.36) | copy-start | bytes 6537220
  56.4 20.4 %copy-start.2 = (bf16[1792,608]{0,1:T(8,128)(2,1)S(1)}, bf16[1792,608]{0,1:T(8,128)(2,1)}, u32[]{:S(2)}) copy-start(bf16[1792,608]{0,1:T(8,128)(2,1)} %param.37) | copy-start | bytes 6537220
  56.4 9.3 %collective-permute-start.14 = (bf16[2,224,128]{2,1,0:T(8,128)(2,1)S(1)}, bf16[2,224,128]{2,1,0:T(8,128)(2,1)S(1)}, u32[]{:S(2)}, u32[]{:S(2)}) collective-permute-start(bf16[2,224,128]{2,1,0:T(8,128)(2,1)S(1)} %pad_maximum_fusion.2), channel_id=1, source_target_pairs={{0,1},{1,0},{2,3},{3,2},{4,5},{5,4},{6,7},{7,6},{8,9},{9,8},{10,11... | collective-permute-start | bytes 344072 | tf_op jit(solution)/shard_map/ppermute | solution.py:297
  65.8 6.0 %collective-permute-start.17 = (bf16[2,224,128]{2,1,0:T(8,128)(2,1)S(1)}, bf16[2,224,128]{2,1,0:T(8,128)(2,1)S(1)}, u32[]{:S(2)}, u32[]{:S(2)}) collective-permute-start(bf16[2,224,128]{2,1,0:T(8,128)(2,1)S(1)} %add_convert_fusion.own_ref), channel_id=1, source_target_pairs={{0,6},{1,7},{2,0},{3,1},{4,2},{5,3},{6,4},{7,5},{8,14},{9,15},{10,... | collective-permute-start | bytes 344072 | tf_op jit(solution)/shard_map/ppermute | solution.py:294
  68.3 7.0 %collective-permute-start.16 = (bf16[2,224,128]{2,1,0:T(8,128)(2,1)S(1)}, bf16[2,224,128]{2,1,0:T(8,128)(2,1)S(1)}, u32[]{:S(2)}, u32[]{:S(2)}) collective-permute-start(bf16[2,224,128]{2,1,0:T(8,128)(2,1)S(1)} %add_convert_fusion.own_ref), channel_id=1, source_target_pairs={{0,4},{1,5},{2,6},{3,7},{4,0},{5,1},{6,2},{7,3},{8,12},{9,13},{10,... | collective-permute-start | bytes 344072 | tf_op jit(solution)/shard_map/ppermute | solution.py:294
  68.7 8.1 %collective-permute-start.15 = (bf16[2,224,128]{2,1,0:T(8,128)(2,1)S(1)}, bf16[2,224,128]{2,1,0:T(8,128)(2,1)S(1)}, u32[]{:S(2)}, u32[]{:S(2)}) collective-permute-start(bf16[2,224,128]{2,1,0:T(8,128)(2,1)S(1)} %add_convert_fusion.own_ref), channel_id=1, source_target_pairs={{0,2},{1,3},{2,4},{3,5},{4,6},{5,7},{6,0},{7,1},{8,10},{9,11},{10,... | collective-permute-start | bytes 344072 | tf_op jit(solution)/shard_map/ppermute | solution.py:294
  79.0 7.3 %collective-permute-start.18 = (bf16[2,224,128]{2,1,0:T(8,128)(2,1)S(1)}, bf16[2,224,128]{2,1,0:T(8,128)(2,1)S(1)}, u32[]{:S(2)}, u32[]{:S(2)}) collective-permute-start(bf16[2,224,128]{2,1,0:T(8,128)(2,1)S(1)} %get-tuple-element.58), channel_id=1, source_target_pairs={{0,2},{1,3},{2,4},{3,5},{4,6},{5,7},{6,0},{7,1},{8,10},{9,11},{10,... | collective-permute-start | bytes 344072 | tf_op jit(solution)/shard_map/ppermute | solution.py:294
  79.1 7.2 %collective-permute-start.19 = (bf16[2,224,128]{2,1,0:T(8,128)(2,1)S(1)}, bf16[2,224,128]{2,1,0:T(8,128)(2,1)S(1)}, u32[]{:S(2)}, u32[]{:S(2)}) collective-permute-start(bf16[2,224,128]{2,1,0:T(8,128)(2,1)S(1)} %get-tuple-element.59), channel_id=1, source_target_pairs={{0,4},{1,5},{2,6},{3,7},{4,0},{5,1},{6,2},{7,3},{8,12},{9,13},{10,... | collective-permute-start | bytes 344072 | tf_op jit(solution)/shard_map/ppermute | solution.py:294
  82.1 5.1 %collective-permute-start.20 = (bf16[2,224,128]{2,1,0:T(8,128)(2,1)S(1)}, bf16[2,224,128]{2,1,0:T(8,128)(2,1)S(1)}, u32[]{:S(2)}, u32[]{:S(2)}) collective-permute-start(bf16[2,224,128]{2,1,0:T(8,128)(2,1)S(1)} %get-tuple-element.60), channel_id=1, source_target_pairs={{0,6},{1,7},{2,0},{3,1},{4,2},{5,3},{6,4},{7,5},{8,14},{9,15},{10,... | collective-permute-start | bytes 344072 | tf_op jit(solution)/shard_map/ppermute | solution.py:294
  87.3 8.2 %collective-permute-start.21 = (bf16[224,128]{1,0:T(8,128)(2,1)S(1)}, bf16[224,128]{1,0:T(8,128)(2,1)S(1)}, u32[]{:S(2)}, u32[]{:S(2)}) collective-permute-start(bf16[224,128]{1,0:T(8,128)(2,1)S(1)} %fusion.4), channel_id=1, source_target_pairs={{0,1},{1,0},{2,3},{3,2},{4,5},{5,4},{6,7},{7,6},{8,9},{9,8},{10,11... | collective-permute-start | bytes 172040 | tf_op jit(solution)/shard_map/ppermute | solution.py:297
  (13 other events, 77.6 us)

commit v4 on v3

--- a/solution.py
+++ b/solution.py
@@ -60,8 +60,13 @@
     return jnp.where(lane == head_dim + 1, total + lost, total).astype(BF16)
 
 
-def fold_kernel(fold_hbm, state_hbm, norm_hbm, tail_hbm, out_ref, fold_ref, state_ref, norm_ref, tail_ref, sems):
-    pairs = ((state_hbm, state_ref), (fold_hbm, fold_ref), (norm_hbm, norm_ref), (tail_hbm, tail_ref))
+def fold_kernel(groups, held, *refs):
+    (fold_hbm, state_hbm, norm_hbm, tail_hbm, leaf_hbm, parent_hbm, owner_hbm, out_ref, slot_ref) = refs[:9]
+    fold_ref, state_ref, norm_ref, tail_ref, leaf_ref, parent_ref, owner_ref, sems = refs[9:]
+    pairs = (
+        (state_hbm, state_ref), (fold_hbm, fold_ref), (norm_hbm, norm_ref), (tail_hbm, tail_ref),
+        (leaf_hbm, leaf_ref), (parent_hbm, parent_ref), (owner_hbm, owner_ref),
+    )
     copies = [pltpu.make_async_copy(a, b, sems.at[i]) for i, (a, b) in enumerate(pairs)]
     for copy in copies:
         copy.start()
@@ -80,39 +85,42 @@
         out_ref[h, :, :head_dim] = state.astype(BF16)
         out_ref[h, TAIL_ROW : TAIL_ROW + 2, :head_dim] = tail_ref[:, h * head_dim : (h + 1) * head_dim]
 
-
-def select_kernel(groups, shifts, leaf_ref, parent_ref, owner_ref, mine_ref, other_ref, *rest):
-    outs, pool = rest[:-1], rest[-1]
-    held = mine_ref.shape[0]
-    heads = mine_ref.shape[1]
+    dev = lax.axis_index("req")
     count = 2 * held
-    for n in range(held):
-        pool[n] = mine_ref[n]
-        pool[held + n] = other_ref[n]
-    pool[count] = jnp.zeros(pool.shape[1:], BF16)
-    dev = lax.axis_index("req")
     total_dev = groups * count
     column = dev // count
     place = (dev % count) // 2
     core = dev % 2
+    per = leaf_ref.shape[0] // total_dev
 
     def slot(row):
-        here = (row // count) == column
-        at = (row % count) // 2
-        k = lax.rem(place - at + held, held)
+        k = lax.rem(place - (row % count) // 2 + held, held)
         k = k + jnp.where((row % 2) == core, 0, held)
-        return jnp.where(here, k, count)
-
-    per = leaf_ref.shape[0] // total_dev
-    rows = lax.broadcasted_iota(jnp.int32, (ROWS, LANES), 0)
-    is_tail = (rows >= TAIL_ROW) & (rows < TAIL_ROW + 2)
-    for out, k in zip(outs, shifts):
+        return jnp.where((row // count) == column, k, count)
+
+    for k in range(groups):
         target = lax.rem(dev + k * count, total_dev)
         for s in range(per):
             leaf = leaf_ref[target * per + s]
             middle = parent_ref[leaf]
             root = parent_ref[middle]
-            at = [slot(owner_ref[n]) for n in (leaf, middle, root)]
+            for i, node in enumerate((leaf, middle, root)):
+                slot_ref[(k * per + s) * 3 + i] = slot(owner_ref[node])
+
+
+def select_kernel(shifts, slot_ref, mine_ref, other_ref, *rest):
+    outs, pool = rest[:-1], rest[-1]
+    held, heads = mine_ref.shape[:2]
+    per = outs[0].shape[0]
+    for n in range(held):
+        pool[n] = mine_ref[n]
+        pool[held + n] = other_ref[n]
+    pool[2 * held] = jnp.zeros(pool.shape[1:], BF16)
+    rows = lax.broadcasted_iota(jnp.int32, (ROWS, LANES), 0)
+    is_tail = (rows >= TAIL_ROW) & (rows < TAIL_ROW + 2)
+    for out, k in zip(outs, shifts):
+        for s in range(per):
+            at = [slot_ref[(k * per + s) * 3 + i] for i in range(3)]
             for h in range(heads):
                 first, second, third = [pool[a, h].astype(F32) for a in at]
                 total = first + jnp.where(is_tail, 0.0, second + third)
@@ -311,35 +319,36 @@
     order = (1, 3, 2)
 
     fold = jnp.asarray(fold_matrix(feat_dim, feats), BF16)
-    hbm = pl.BlockSpec(memory_space=pltpu.MemorySpace.HBM)
+    def in_hbm(array):
+        return pltpu.with_memory_space_constraint(array, pltpu.HBM)
+
     state_in = jnp.transpose(node_state[0], (1, 0, 2))
-    payload = call(
-        fold_kernel,
-        sds((heads, ROWS, LANES), BF16),
-        [hbm] * 4,
-        (fold, state_in, node_norm[0], node_tail[0]),
-        scratch=[
-            pltpu.VMEM(fold.shape, BF16),
-            pltpu.VMEM(state_in.shape, BF16),
-            pltpu.VMEM(node_norm[0].shape, BF16),
-            pltpu.VMEM(node_tail[0].shape, BF16),
-            pltpu.SemaphoreType.DMA((4,)),
-        ],
+    fold_in = (fold, state_in, node_norm[0], node_tail[0], request_leaf, parent, owner_map)
+    payload, slots = pl.pallas_call(
+        functools.partial(fold_kernel, y_size, z_size),
+        out_shape=[sds((heads, ROWS, LANES), BF16), sds((y_size * per * 3,), jnp.int32)],
+        in_specs=[pl.BlockSpec(memory_space=pltpu.HBM)] * len(fold_in),
+        out_specs=[VMEM, SMEM],
+        scratch_shapes=[pltpu.VMEM(a.shape, BF16) for a in fold_in[:4]]
+        + [pltpu.SMEM(a.shape, jnp.int32) for a in fold_in[4:]]
+        + [pltpu.SemaphoreType.DMA((len(fold_in),))],
+        compiler_params=PARAMS,
         name="fold",
-    )
-    payload, own = lax.optimization_barrier((payload, stream.T))
+    )(*[in_hbm(a) for a in fold_in])
     from_z = {k: along_z(payload, k) for k in order}
 
+    own = stream.T
     pair = jnp.stack([own, across_z(own)])
 
-    mine = jnp.stack([payload, from_z[1], from_z[2], from_z[3]])
+    held_pair, *arrived = lax.optimization_barrier((pair, from_z[1], from_z[2], from_z[3]))
+    mine = jnp.stack([payload, *arrived])
     other = across_core(mine)
     def select(shifts, held, name):
         return call(
-            functools.partial(select_kernel, y_size, shifts),
+            functools.partial(select_kernel, shifts),
             [sds((per, heads, ROWS, LANES), BF16)] * len(shifts),
-            [SMEM] * 3 + [VMEM] * 2,
-            (request_leaf, parent, owner_map, *held),
+            [SMEM] + [VMEM] * 2,
+            (slots, *held),
             scratch=[pltpu.VMEM((2 * z_size + 1, heads, ROWS, LANES), BF16)],
             name=name,
         )
@@ -385,7 +394,7 @@
     share = parts[0] + got[1].astype(F32) + got[2].astype(F32) + got[3].astype(F32)
     crossing, down_in = lax.optimization_barrier((jnp.stack([share[1], share[0]]).astype(BF16), ffn_down))
     share_peer = across_z(crossing)
-    updated = (pair.astype(F32) + share + share_peer.astype(F32)).astype(BF16)
+    updated = (held_pair.astype(F32) + share + share_peer.astype(F32)).astype(BF16)
     updated, down_turned = lax.optimization_barrier((updated, turn(down_in, "turn_down")))
 
     wide = {k: along_x(updated, k) for k in order}

time: 97.9 us -> 90 us (0.919)
  local copies, waits for them, and re-layouts: 5.39 us -> 0.09 us
  starting transfers between devices: 40.7 us -> 37.8 us
  Pallas kernels: 8.63 us -> 10.1 us
    unnamed x46 -> x24, local copies, waits for them, and re-layouts: 5.36 us -> 0.06 us
    ppermute x3, starting transfers between devices: 15.4 us -> 10.2 us  [across_z(): return lax.ppermute(array, 'tp', [(i, i ^ 1) for i in range(tp_size)])]
    ppermute x12, starting transfers between devices: 14.8 us -> 19 us  [along_x(): lax.ppermute(array, 'tp', [(i, (i // 2 + k) % x_size * 2 + i % 2) for i i...]
    ppermute x3, waiting for transfers between devices: 10 us -> 14.1 us  [across_z(): return lax.ppermute(array, 'tp', [(i, i ^ 1) for i in range(tp_size)])]
    ppermute x12, waiting for transfers between devices: 22.5 us -> 18.5 us  [along_x(): lax.ppermute(array, 'tp', [(i, (i // 2 + k) % x_size * 2 + i % 2) for i i...]
    pallas_call x0 -> x1, Pallas kernels: none -> 2.55 us  [shards(): pl.pallas_call(functools.partial(fold_kernel, y_size, z_size), out_shape=...]
    ppermute x3, starting transfers between devices: 5.37 us -> 3.58 us  [along_z(): lax.ppermute(array, 'req', [(i, i // count * count + (i % count // 2 + k)...]
    pallas_call x8 -> x7, Pallas kernels: 8.63 us -> 7.51 us  [call(): pl.pallas_call(kernel, out_shape=out_shape, in_specs=specs, out_specs=VME...]
  transfers between devices with their start and end apart: 22 -> 22, of which waited for: 14 -> 13; matrix products, arithmetic and copies ran while one was open for 1% -> 1% of each run, Pallas kernels for 5% -> 8%
where the time goes in v4:
time: 90 us; the launch traced here: 88.5 us
  waiting for transfers between devices  38.5 us (43%)
  starting transfers between devices  37.8 us (42%)
  Pallas kernels  10.1 us (11%)
  other arithmetic  1.73 us (2%)
    ppermute x12, starting transfers between devices, along_x(): lax.ppermute(array, 'tp', [(i, (i // 2 + k) % x_size * 2 + i % 2) for i i...  19 us
    ppermute x12, waiting for transfers between devices, along_x(): lax.ppermute(array, 'tp', [(i, (i // 2 + k) % x_size * 2 + i % 2) for i i...  18.5 us
    ppermute x3, waiting for transfers between devices, across_z(): return lax.ppermute(array, 'tp', [(i, i ^ 1) for i in range(tp_size)])  14.1 us
    ppermute x3, starting transfers between devices, across_z(): return lax.ppermute(array, 'tp', [(i, i ^ 1) for i in range(tp_size)])  10.2 us
    pallas_call x7, Pallas kernels, call(): pl.pallas_call(kernel, out_shape=out_shape, in_specs=specs, out_specs=VME...  7.51 us
    ppermute x3, waiting for transfers between devices, along_z(): lax.ppermute(array, 'req', [(i, i // count * count + (i % count // 2 + k)...  5.83 us
    ppermute x3, starting transfers between devices, along_y(): lax.ppermute(array, 'req', [(i, (i + 2 * z_size * k) % req_size) for i in...  5 us
    ppermute x3, starting transfers between devices, along_z(): lax.ppermute(array, 'req', [(i, i // count * count + (i % count // 2 + k)...  3.58 us
  transfers between devices with their start and end apart: 22, of which 13 were waited for; matrix products, arithmetic and copies ran while one was open for 1% of the time, Pallas kernels for 8%

profile of v4, /device:TPU:8, one launch (start us, length us, event | category | flops | bytes accessed | tf_op | source)
XLA Modules:
  0.0 88.5 jit_solution(1393309368216503184)
XLA Ops:
  0.1 7.3 %collective-permute-start = (bf16[224,128]{1,0:T(8,128)(2,1)}, bf16[224,128]{1,0:T(8,128)(2,1)S(1)}, u32[]{:S(2)}, u32[]{:S(2)}) collective-permute-start(bf16[224,128]{1,0:T(8,128)(2,1)} %bitcast.46), channel_id=1, source_target_pairs={{0,1},{1,0},{2,3},{3,2},{4,5},{5,4},{6,7},{7,6},{8,9},{9,8},{10,11... | collective-permute-start | bytes 172040 | tf_op jit(solution)/shard_map/ppermute | solution.py:305
  7.3 2.5 %fold.1 = (bf16[2,160,128]{2,1,0:T(8,128)(2,1)S(1)}, s32[24]{0:T(128)S(1)}) custom-call(bf16[160,273]{1,0:T(8,128)(2,1)} %constant.5.clone.refs_0_, bf16[273,2,112]{2,1,0:T(2,128)(2,1)} %bitcast.42, bf16[2,273]{1,0:T(2,128)(2,1)} %bitcast.51, bf16[2,224]{1,0:T(2,128)(2,1)} %bitcast.52, s32[64]{0:T(128)} %refs_4_.1, s32[32]{0:T(128)} %refs_5_.1, s32[32]{0:T(128)} %refs_6_.1), custom_call_target="tpu_custom_call" | custom-call | tf_op jit(solution)/shard_map/fold/pallas_call | solution.py:327
  9.9 2.0 %collective-permute-start.3 = (bf16[2,160,128]{2,1,0:T(8,128)(2,1)S(1)}, bf16[2,160,128]{2,1,0:T(8,128)(2,1)S(1)}, u32[]{:S(2)}, u32[]{:S(2)}) collective-permute-start(bf16[2,160,128]{2,1,0:T(8,128)(2,1)S(1)} %get-tuple-element.37), channel_id=1, source_target_pairs={{0,48},{8,56},{16,0},{24,8},{32,16},{40,24},{48,32},{56,40},{64,11... | collective-permute-start | bytes 245768 | tf_op jit(solution)/shard_map/ppermute | solution.py:309
  12.5 1.0 %collective-permute-start.1 = (bf16[2,160,128]{2,1,0:T(8,128)(2,1)S(1)}, bf16[2,160,128]{2,1,0:T(8,128)(2,1)S(1)}, u32[]{:S(2)}, u32[]{:S(2)}) collective-permute-start(bf16[2,160,128]{2,1,0:T(8,128)(2,1)S(1)} %get-tuple-element.37), channel_id=1, source_target_pairs={{0,16},{8,24},{16,32},{24,40},{32,48},{40,56},{48,0},{56,8},{64,80... | collective-permute-start | bytes 245768 | tf_op jit(solution)/shard_map/ppermute | solution.py:309
  13.5 0.8 pad_maximum_fusion.1.own_ref
  14.8 5.3 %collective-permute-done.2 = bf16[2,160,128]{2,1,0:T(8,128)(2,1)S(1)} collective-permute-done((bf16[2,160,128]{2,1,0:T(8,128)(2,1)S(1)}, bf16[2,160,128]{2,1,0:T(8,128)(2,1)S(1)}, u32[]{:S(2)}, u32[]{:S(2)}) %collective-permute-start.2) | collective-permute-done | bytes 81952 | tf_op jit(solution)/shard_map/ppermute | solution.py:309
  20.3 2.8 %collective-permute-start.6 = (bf16[2,224,128]{2,1,0:T(8,128)(2,1)S(1)}, bf16[2,224,128]{2,1,0:T(8,128)(2,1)S(1)}, u32[]{:S(2)}, u32[]{:S(2)}) collective-permute-start(bf16[2,224,128]{2,1,0:T(8,128)(2,1)S(1)} %pad_maximum_fusion.1.own_ref), channel_id=1, source_target_pairs={{0,6},{1,7},{2,0},{3,1},{4,2},{5,3},{6,4},{7,5},{8,14},{9,15},{10,... | collective-permute-start | bytes 344072 | tf_op jit(solution)/shard_map/ppermute | solution.py:302
  23.1 1.0 %select_sent.1 = (bf16[2,2,160,128]{3,2,1,0:T(8,128)(2,1)S(1)}, bf16[2,2,160,128]{3,2,1,0:T(8,128)(2,1)S(1)}, bf16[2,2,160,128]{3,2,1,0:T(8,128)(2,1)S(1)}) custom-call(s32[24]{0:T(128)S(1)} %get-tuple-element.45.slot_ref, bf16[4,2,160,128]{3,2,1,0:T(8,128)(2,1)S(1)} %pad_maximum_fusion.mine_ref, bf16[4,2,160,128]{3,2,1,0:T(8,128)(2,1)S(1)} %collective-permute-done.7.other_ref), custom_call_target="tpu_custom_call" | custom-call | tf_op jit(solution)/shard_map/select_sent/pallas_call | solution.py:25
  24.1 1.7 %collective-permute-start.8 = (bf16[2,2,160,128]{3,2,1,0:T(8,128)(2,1)S(1)}, bf16[2,2,160,128]{3,2,1,0:T(8,128)(2,1)S(1)}, u32[]{:S(2)}, u32[]{:S(2)}) collective-permute-start(bf16[2,2,160,128]{3,2,1,0:T(8,128)(2,1)S(1)} %get-tuple-element.54), channel_id=1, source_target_pairs={{0,64},{8,72},{16,80},{24,88},{32,96},{40,104},{48,112},{56,120},{... | collective-permute-start | bytes 491528 | tf_op jit(solution)/shard_map/ppermute | solution.py:317
  25.7 0.9 %collective-permute-start.9 = (bf16[2,2,160,128]{3,2,1,0:T(8,128)(2,1)S(1)}, bf16[2,2,160,128]{3,2,1,0:T(8,128)(2,1)S(1)}, u32[]{:S(2)}, u32[]{:S(2)}) collective-permute-start(bf16[2,2,160,128]{3,2,1,0:T(8,128)(2,1)S(1)} %get-tuple-element.55), channel_id=1, source_target_pairs={{0,128},{8,136},{16,144},{24,152},{32,160},{40,168},{48,176},{56,1... | collective-permute-start | bytes 491528 | tf_op jit(solution)/shard_map/ppermute | solution.py:317
  26.7 2.4 %collective-permute-start.10 = (bf16[2,2,160,128]{3,2,1,0:T(8,128)(2,1)S(1)}, bf16[2,2,160,128]{3,2,1,0:T(8,128)(2,1)S(1)}, u32[]{:S(2)}, u32[]{:S(2)}) collective-permute-start(bf16[2,2,160,128]{3,2,1,0:T(8,128)(2,1)S(1)} %get-tuple-element.56), channel_id=1, source_target_pairs={{0,192},{8,200},{16,208},{24,216},{32,224},{40,232},{48,240},{56,2... | collective-permute-start | bytes 491528 | tf_op jit(solution)/shard_map/ppermute | solution.py:317
  29.1 1.8 %collective-permute-start.5 = (bf16[2,224,128]{2,1,0:T(8,128)(2,1)S(1)}, bf16[2,224,128]{2,1,0:T(8,128)(2,1)S(1)}, u32[]{:S(2)}, u32[]{:S(2)}) collective-permute-start(bf16[2,224,128]{2,1,0:T(8,128)(2,1)S(1)} %pad_maximum_fusion.1.own_ref), channel_id=1, source_target_pairs={{0,4},{1,5},{2,6},{3,7},{4,0},{5,1},{6,2},{7,3},{8,12},{9,13},{10,... | collective-permute-start | bytes 344072 | tf_op jit(solution)/shard_map/ppermute | solution.py:302
  31.8 4.4 %collective-permute-done.5.r2_ref = bf16[2,224,128]{2,1,0:T(8,128)(2,1)S(1)} collective-permute-done((bf16[2,224,128]{2,1,0:T(8,128)(2,1)S(1)}, bf16[2,224,128]{2,1,0:T(8,128)(2,1)S(1)}, u32[]{:S(2)}, u32[]{:S(2)}) %collective-permute-start.5) | collective-permute-done | bytes 114720 | tf_op jit(solution)/shard_map/ppermute | solution.py:302
  36.2 1.2 %collective-permute-done.4.r1_ref = bf16[2,224,128]{2,1,0:T(8,128)(2,1)S(1)} collective-permute-done((bf16[2,224,128]{2,1,0:T(8,128)(2,1)S(1)}, bf16[2,224,128]{2,1,0:T(8,128)(2,1)S(1)}, u32[]{:S(2)}, u32[]{:S(2)}) %collective-permute-start.4) | collective-permute-done | bytes 114720 | tf_op jit(solution)/shard_map/ppermute | solution.py:302
  37.5 1.5 %local.1 = (f32[224,128]{1,0:T(8,128)S(1)}, f32[224,128]{1,0:T(8,128)S(1)}, bf16[2,128,128]{2,1,0:T(8,128)(2,1)S(1)}, f32[2,1,128]{2,1,0:T(1,128)S(1)}, bf16[2,3...) custom-call(bf16[2,224,128]{2,1,0:T(8,128)(2,1)S(1)} %pad_maximum_fusion.1.own_ref, ...), custom_call_target="tpu_custom_call" | custom-call | tf_op jit(solution)/shard_map/local/pallas_call | solution.py:25
  39.8 1.1 %mix.1 = (f32[2,224,128]{2,1,0:T(8,128)S(1)}, bf16[2,224,128]{2,1,0:T(8,128)(2,1)S(1)}, bf16[2,224,128]{2,1,0:T(8,128)(2,1)S(1)}, bf16[2,224,128]{2,1,0:T(8,128)(2,1)S(1)}) custom-call(f32[224,128]{1,0:T(8,128)S(1)} %get-tuple-element.39.conv_ref, f32[224,128]{1,0:T(8,128)S(1)} %get-tuple-element.40.silu_ref, ...), custom_call_target="tpu_custom_call" | custom-call | tf_op jit(solution)/shard_map/mix/pallas_call | solution.py:25
  41.3 1.7 %collective-permute-start.12 = (bf16[2,224,128]{2,1,0:T(8,128)(2,1)S(1)}, bf16[2,224,128]{2,1,0:T(8,128)(2,1)S(1)}, u32[]{:S(2)}, u32[]{:S(2)}) collective-permute-start(bf16[2,224,128]{2,1,0:T(8,128)(2,1)S(1)} %get-tuple-element.59), channel_id=1, source_target_pairs={{0,4},{1,5},{2,6},{3,7},{4,0},{5,1},{6,2},{7,3},{8,12},{9,13},{10,... | collective-permute-start | bytes 344072 | tf_op jit(solution)/shard_map/ppermute | solution.py:302
  43.0 2.4 %collective-permute-start.13 = (bf16[2,224,128]{2,1,0:T(8,128)(2,1)S(1)}, bf16[2,224,128]{2,1,0:T(8,128)(2,1)S(1)}, u32[]{:S(2)}, u32[]{:S(2)}) collective-permute-start(bf16[2,224,128]{2,1,0:T(8,128)(2,1)S(1)} %get-tuple-element.60), channel_id=1, source_target_pairs={{0,6},{1,7},{2,0},{3,1},{4,2},{5,3},{6,4},{7,5},{8,14},{9,15},{10,... | collective-permute-start | bytes 344072 | tf_op jit(solution)/shard_map/ppermute | solution.py:302
  45.3 3.1 %collective-permute-done.11 = bf16[2,224,128]{2,1,0:T(8,128)(2,1)S(1)} collective-permute-done((bf16[2,224,128]{2,1,0:T(8,128)(2,1)S(1)}, bf16[2,224,128]{2,1,0:T(8,128)(2,1)S(1)}, u32[]{:S(2)}, u32[]{:S(2)}) %collective-permute-start.11) | collective-permute-done | bytes 114720 | tf_op jit(solution)/shard_map/ppermute | solution.py:302
  49.2 1.5 %collective-permute-start.14 = (bf16[2,224,128]{2,1,0:T(8,128)(2,1)S(1)}, bf16[2,224,128]{2,1,0:T(8,128)(2,1)S(1)}, u32[]{:S(2)}, u32[]{:S(2)}) collective-permute-start(bf16[2,224,128]{2,1,0:T(8,128)(2,1)S(1)} %pad_maximum_fusion.2), channel_id=1, source_target_pairs={{0,1},{1,0},{2,3},{3,2},{4,5},{5,4},{6,7},{7,6},{8,9},{9,8},{10,11... | collective-permute-start | bytes 344072 | tf_op jit(solution)/shard_map/ppermute | solution.py:305
  51.3 7.4 %collective-permute-done.14 = bf16[2,224,128]{2,1,0:T(8,128)(2,1)S(1)} collective-permute-done((bf16[2,224,128]{2,1,0:T(8,128)(2,1)S(1)}, bf16[2,224,128]{2,1,0:T(8,128)(2,1)S(1)}, u32[]{:S(2)}, u32[]{:S(2)}) %collective-permute-start.14) | collective-permute-done | bytes 114720 | tf_op jit(solution)/shard_map/ppermute | solution.py:305
  58.8 2.8 %collective-permute-start.17 = (bf16[2,224,128]{2,1,0:T(8,128)(2,1)S(1)}, bf16[2,224,128]{2,1,0:T(8,128)(2,1)S(1)}, u32[]{:S(2)}, u32[]{:S(2)}) collective-permute-start(bf16[2,224,128]{2,1,0:T(8,128)(2,1)S(1)} %add_convert_fusion.own_ref), channel_id=1, source_target_pairs={{0,6},{1,7},{2,0},{3,1},{4,2},{5,3},{6,4},{7,5},{8,14},{9,15},{10,... | collective-permute-start | bytes 344072 | tf_op jit(solution)/shard_map/ppermute | solution.py:302
  61.6 1.2 %collective-permute-start.16 = (bf16[2,224,128]{2,1,0:T(8,128)(2,1)S(1)}, bf16[2,224,128]{2,1,0:T(8,128)(2,1)S(1)}, u32[]{:S(2)}, u32[]{:S(2)}) collective-permute-start(bf16[2,224,128]{2,1,0:T(8,128)(2,1)S(1)} %add_convert_fusion.own_ref), channel_id=1, source_target_pairs={{0,4},{1,5},{2,6},{3,7},{4,0},{5,1},{6,2},{7,3},{8,12},{9,13},{10,... | collective-permute-start | bytes 344072 | tf_op jit(solution)/shard_map/ppermute | solution.py:302
  64.0 4.0 %collective-permute-done.16.r2_ref = bf16[2,224,128]{2,1,0:T(8,128)(2,1)S(1)} collective-permute-done((bf16[2,224,128]{2,1,0:T(8,128)(2,1)S(1)}, bf16[2,224,128]{2,1,0:T(8,128)(2,1)S(1)}, u32[]{:S(2)}, u32[]{:S(2)}) %collective-permute-start.16) | collective-permute-done | bytes 114720 | tf_op jit(solution)/shard_map/ppermute | solution.py:302
  68.0 1.2 %collective-permute-done.15.r1_ref = bf16[2,224,128]{2,1,0:T(8,128)(2,1)S(1)} collective-permute-done((bf16[2,224,128]{2,1,0:T(8,128)(2,1)S(1)}, bf16[2,224,128]{2,1,0:T(8,128)(2,1)S(1)}, u32[]{:S(2)}, u32[]{:S(2)}) %collective-permute-start.15) | collective-permute-done | bytes 114720 | tf_op jit(solution)/shard_map/ppermute | solution.py:302
  69.2 2.2 %ffn.1 = (f32[2,224,128]{2,1,0:T(8,128)S(1)}, bf16[2,224,128]{2,1,0:T(8,128)(2,1)S(1)}, bf16[2,224,128]{2,1,0:T(8,128)(2,1)S(1)}, bf16[2,224,128]{2,1,0:T(8,128)(2,1)S(1)}) custom-call(bf16[2,224,128]{2,1,0:T(8,128)(2,1)S(1)} %add_convert_fusion.own_ref, bf16[2,224,128]{2,1,0:T(8,128)(2,1)S(1)} %collective-permute-done.15.r1_ref, ...), custom_call_target="tpu_custom_call" | custom-call | tf_op jit(solution)/shard_map/ffn/pallas_call | solution.py:25
  71.5 2.7 %collective-permute-start.19 = (bf16[2,224,128]{2,1,0:T(8,128)(2,1)S(1)}, bf16[2,224,128]{2,1,0:T(8,128)(2,1)S(1)}, u32[]{:S(2)}, u32[]{:S(2)}) collective-permute-start(bf16[2,224,128]{2,1,0:T(8,128)(2,1)S(1)} %get-tuple-element.67), channel_id=1, source_target_pairs={{0,4},{1,5},{2,6},{3,7},{4,0},{5,1},{6,2},{7,3},{8,12},{9,13},{10,... | collective-permute-start | bytes 344072 | tf_op jit(solution)/shard_map/ppermute | solution.py:302
  74.2 1.9 %collective-permute-start.20 = (bf16[2,224,128]{2,1,0:T(8,128)(2,1)S(1)}, bf16[2,224,128]{2,1,0:T(8,128)(2,1)S(1)}, u32[]{:S(2)}, u32[]{:S(2)}) collective-permute-start(bf16[2,224,128]{2,1,0:T(8,128)(2,1)S(1)} %get-tuple-element.68), channel_id=1, source_target_pairs={{0,6},{1,7},{2,0},{3,1},{4,2},{5,3},{6,4},{7,5},{8,14},{9,15},{10,... | collective-permute-start | bytes 344072 | tf_op jit(solution)/shard_map/ppermute | solution.py:302
  76.1 2.7 %collective-permute-done.18 = bf16[2,224,128]{2,1,0:T(8,128)(2,1)S(1)} collective-permute-done((bf16[2,224,128]{2,1,0:T(8,128)(2,1)S(1)}, bf16[2,224,128]{2,1,0:T(8,128)(2,1)S(1)}, u32[]{:S(2)}, u32[]{:S(2)}) %collective-permute-start.18) | collective-permute-done | bytes 114720 | tf_op jit(solution)/shard_map/ppermute | solution.py:302
  78.7 0.9 collective-permute-done.20
  79.6 1.4 %collective-permute-start.21 = (bf16[224,128]{1,0:T(8,128)(2,1)S(1)}, bf16[224,128]{1,0:T(8,128)(2,1)S(1)}, u32[]{:S(2)}, u32[]{:S(2)}) collective-permute-start(bf16[224,128]{1,0:T(8,128)(2,1)S(1)} %fusion.4), channel_id=1, source_target_pairs={{0,1},{1,0},{2,3},{3,2},{4,5},{5,4},{6,7},{7,6},{8,9},{9,8},{10,11... | collective-permute-start | bytes 172040 | tf_op jit(solution)/shard_map/ppermute | solution.py:305
  81.0 6.8 %collective-permute-done.21 = bf16[224,128]{1,0:T(8,128)(2,1)S(1)} collective-permute-done((bf16[224,128]{1,0:T(8,128)(2,1)S(1)}, bf16[224,128]{1,0:T(8,128)(2,1)S(1)}, u32[]{:S(2)}, u32[]{:S(2)}) %collective-permute-start.21) | collective-permute-done | bytes 57376 | tf_op jit(solution)/shard_map/ppermute | solution.py:305
  (55 shorter events, 6.7 us)
Async XLA Ops:
  0.0 31.5 %copy-start.5 = (bf16[224,1792]{1,0:T(8,128)(2,1)S(1)}, bf16[224,1792]{1,0:T(8,128)(2,1)}, u32[]{:S(2)}) copy-start(bf16[224,1792]{1,0:T(8,128)(2,1)} %in_ref.1) | copy-start | bytes 2408452
  0.0 31.8 %copy-start.10 = (f32[1792]{0:T(1024)S(1)}, f32[1792]{0:T(1024)}, u32[]{:S(2)}) copy-start(f32[1792]{0:T(1024)} %param.28) | copy-start | bytes 21508
  0.0 37.4 %copy-start.8 = (f32[3,224]{1,0:T(4,128)S(1)}, f32[3,224]{1,0:T(4,128)}, u32[]{:S(2)}) copy-start(f32[3,224]{1,0:T(4,128)} %taps_ref.1) | copy-start | bytes 8068
  0.0 37.4 %copy-start.4 = (bf16[1792,224]{0,1:T(8,128)(2,1)S(1)}, bf16[1792,224]{0,1:T(8,128)(2,1)}, u32[]{:S(2)}) copy-start(bf16[1792,224]{0,1:T(8,128)(2,1)} %param.33) | copy-start | bytes 2408452
  0.0 37.4 %copy-start.3 = (bf16[1792,224]{0,1:T(8,128)(2,1)S(1)}, bf16[1792,224]{0,1:T(8,128)(2,1)}, u32[]{:S(2)}) copy-start(bf16[1792,224]{0,1:T(8,128)(2,1)} %param.32) | copy-start | bytes 2408452
  0.0 37.4 %copy-start.7 = (bf16[1792,32]{0,1:T(8,128)(2,1)S(1)}, bf16[1792,32]{0,1:T(8,128)(2,1)}, u32[]{:S(2)}) copy-start(bf16[1792,32]{0,1:T(8,128)(2,1)} %param.31) | copy-start | bytes 344068
  0.0 37.4 %copy-start.6 = (bf16[1792,32]{0,1:T(8,128)(2,1)S(1)}, bf16[1792,32]{0,1:T(8,128)(2,1)}, u32[]{:S(2)}) copy-start(bf16[1792,32]{0,1:T(8,128)(2,1)} %param.30) | copy-start | bytes 344068
  0.0 37.4 %copy-start.9 = (s32[128]{0:T(128)S(1)}, s32[128]{0:T(128)}, u32[]{:S(2)}) copy-start(s32[128]{0:T(128)} %param.21) | copy-start | bytes 1540
  0.1 13.4 %collective-permute-start = (bf16[224,128]{1,0:T(8,128)(2,1)}, bf16[224,128]{1,0:T(8,128)(2,1)S(1)}, u32[]{:S(2)}, u32[]{:S(2)}) collective-permute-start(bf16[224,128]{1,0:T(8,128)(2,1)} %bitcast.46), channel_id=1, source_target_pairs={{0,1},{1,0},{2,3},{3,2},{4,5},{5,4},{6,7},{7,6},{8,9},{9,8},{10,11... | collective-permute-start | bytes 172040 | tf_op jit(solution)/shard_map/ppermute | solution.py:305
  9.9 4.9 %collective-permute-start.3 = (bf16[2,160,128]{2,1,0:T(8,128)(2,1)S(1)}, bf16[2,160,128]{2,1,0:T(8,128)(2,1)S(1)}, u32[]{:S(2)}, u32[]{:S(2)}) collective-permute-start(bf16[2,160,128]{2,1,0:T(8,128)(2,1)S(1)} %get-tuple-element.37), channel_id=1, source_target_pairs={{0,48},{8,56},{16,0},{24,8},{32,16},{40,24},{48,32},{56,40},{64,11... | collective-permute-start | bytes 245768 | tf_op jit(solution)/shard_map/ppermute | solution.py:309
  11.9 8.2 %collective-permute-start.2 = (bf16[2,160,128]{2,1,0:T(8,128)(2,1)S(1)}, bf16[2,160,128]{2,1,0:T(8,128)(2,1)S(1)}, u32[]{:S(2)}, u32[]{:S(2)}) collective-permute-start(bf16[2,160,128]{2,1,0:T(8,128)(2,1)S(1)} %get-tuple-element.37), channel_id=1, source_target_pairs={{0,32},{8,40},{16,48},{24,56},{32,0},{40,8},{48,16},{56,24},{64,96... | collective-permute-start | bytes 245768 | tf_op jit(solution)/shard_map/ppermute | solution.py:309
  12.5 7.7 %collective-permute-start.1 = (bf16[2,160,128]{2,1,0:T(8,128)(2,1)S(1)}, bf16[2,160,128]{2,1,0:T(8,128)(2,1)S(1)}, u32[]{:S(2)}, u32[]{:S(2)}) collective-permute-start(bf16[2,160,128]{2,1,0:T(8,128)(2,1)S(1)} %get-tuple-element.37), channel_id=1, source_target_pairs={{0,16},{8,24},{16,32},{24,40},{32,48},{40,56},{48,0},{56,8},{64,80... | collective-permute-start | bytes 245768 | tf_op jit(solution)/shard_map/ppermute | solution.py:309
  20.2 2.9 %collective-permute-start.7 = (bf16[4,2,160,128]{3,2,1,0:T(8,128)(2,1)S(1)}, bf16[4,2,160,128]{3,2,1,0:T(8,128)(2,1)S(1)}, u32[]{:S(2)}, u32[]{:S(2)}) collective-permute-start(bf16[4,2,160,128]{3,2,1,0:T(8,128)(2,1)S(1)} %pad_maximum_fusion.mine_ref), channel_id=1, source_target_pairs={{0,8},{8,0},{16,24},{24,16},{32,40},{40,32},{48,56},{56,48},{64,72... | collective-permute-start | bytes 983048 | tf_op jit(solution)/shard_map/ppermute | solution.py:314
  20.3 10.6 %collective-permute-start.6 = (bf16[2,224,128]{2,1,0:T(8,128)(2,1)S(1)}, bf16[2,224,128]{2,1,0:T(8,128)(2,1)S(1)}, u32[]{:S(2)}, u32[]{:S(2)}) collective-permute-start(bf16[2,224,128]{2,1,0:T(8,128)(2,1)S(1)} %pad_maximum_fusion.1.own_ref), channel_id=1, source_target_pairs={{0,6},{1,7},{2,0},{3,1},{4,2},{5,3},{6,4},{7,5},{8,14},{9,15},{10,... | collective-permute-start | bytes 344072 | tf_op jit(solution)/shard_map/ppermute | solution.py:302
  24.1 15.7 %collective-permute-start.8 = (bf16[2,2,160,128]{3,2,1,0:T(8,128)(2,1)S(1)}, bf16[2,2,160,128]{3,2,1,0:T(8,128)(2,1)S(1)}, u32[]{:S(2)}, u32[]{:S(2)}) collective-permute-start(bf16[2,2,160,128]{3,2,1,0:T(8,128)(2,1)S(1)} %get-tuple-element.54), channel_id=1, source_target_pairs={{0,64},{8,72},{16,80},{24,88},{32,96},{40,104},{48,112},{56,120},{... | collective-permute-start | bytes 491528 | tf_op jit(solution)/shard_map/ppermute | solution.py:317
  25.7 14.0 %collective-permute-start.9 = (bf16[2,2,160,128]{3,2,1,0:T(8,128)(2,1)S(1)}, bf16[2,2,160,128]{3,2,1,0:T(8,128)(2,1)S(1)}, u32[]{:S(2)}, u32[]{:S(2)}) collective-permute-start(bf16[2,2,160,128]{3,2,1,0:T(8,128)(2,1)S(1)} %get-tuple-element.55), channel_id=1, source_target_pairs={{0,128},{8,136},{16,144},{24,152},{32,160},{40,168},{48,176},{56,1... | collective-permute-start | bytes 491528 | tf_op jit(solution)/shard_map/ppermute | solution.py:317
  26.7 13.1 %collective-permute-start.10 = (bf16[2,2,160,128]{3,2,1,0:T(8,128)(2,1)S(1)}, bf16[2,2,160,128]{3,2,1,0:T(8,128)(2,1)S(1)}, u32[]{:S(2)}, u32[]{:S(2)}) collective-permute-start(bf16[2,2,160,128]{3,2,1,0:T(8,128)(2,1)S(1)} %get-tuple-element.56), channel_id=1, source_target_pairs={{0,192},{8,200},{16,208},{24,216},{32,224},{40,232},{48,240},{56,2... | collective-permute-start | bytes 491528 | tf_op jit(solution)/shard_map/ppermute | solution.py:317
  29.1 7.1 %collective-permute-start.5 = (bf16[2,224,128]{2,1,0:T(8,128)(2,1)S(1)}, bf16[2,224,128]{2,1,0:T(8,128)(2,1)S(1)}, u32[]{:S(2)}, u32[]{:S(2)}) collective-permute-start(bf16[2,224,128]{2,1,0:T(8,128)(2,1)S(1)} %pad_maximum_fusion.1.own_ref), channel_id=1, source_target_pairs={{0,4},{1,5},{2,6},{3,7},{4,0},{5,1},{6,2},{7,3},{8,12},{9,13},{10,... | collective-permute-start | bytes 344072 | tf_op jit(solution)/shard_map/ppermute | solution.py:302
  30.9 6.5 %collective-permute-start.4 = (bf16[2,224,128]{2,1,0:T(8,128)(2,1)S(1)}, bf16[2,224,128]{2,1,0:T(8,128)(2,1)S(1)}, u32[]{:S(2)}, u32[]{:S(2)}) collective-permute-start(bf16[2,224,128]{2,1,0:T(8,128)(2,1)S(1)} %pad_maximum_fusion.1.own_ref), channel_id=1, source_target_pairs={{0,2},{1,3},{2,4},{3,5},{4,6},{5,7},{6,0},{7,1},{8,10},{9,11},{10,... | collective-permute-start | bytes 344072 | tf_op jit(solution)/shard_map/ppermute | solution.py:302
  40.9 7.6 %collective-permute-start.11 = (bf16[2,224,128]{2,1,0:T(8,128)(2,1)S(1)}, bf16[2,224,128]{2,1,0:T(8,128)(2,1)S(1)}, u32[]{:S(2)}, u32[]{:S(2)}) collective-permute-start(bf16[2,224,128]{2,1,0:T(8,128)(2,1)S(1)} %get-tuple-element.58), channel_id=1, source_target_pairs={{0,2},{1,3},{2,4},{3,5},{4,6},{5,7},{6,0},{7,1},{8,10},{9,11},{10,... | collective-permute-start | bytes 344072 | tf_op jit(solution)/shard_map/ppermute | solution.py:302
  41.3 7.2 %collective-permute-start.12 = (bf16[2,224,128]{2,1,0:T(8,128)(2,1)S(1)}, bf16[2,224,128]{2,1,0:T(8,128)(2,1)S(1)}, u32[]{:S(2)}, u32[]{:S(2)}) collective-permute-start(bf16[2,224,128]{2,1,0:T(8,128)(2,1)S(1)} %get-tuple-element.59), channel_id=1, source_target_pairs={{0,4},{1,5},{2,6},{3,7},{4,0},{5,1},{6,2},{7,3},{8,12},{9,13},{10,... | collective-permute-start | bytes 344072 | tf_op jit(solution)/shard_map/ppermute | solution.py:302
  43.0 6.1 %collective-permute-start.13 = (bf16[2,224,128]{2,1,0:T(8,128)(2,1)S(1)}, bf16[2,224,128]{2,1,0:T(8,128)(2,1)S(1)}, u32[]{:S(2)}, u32[]{:S(2)}) collective-permute-start(bf16[2,224,128]{2,1,0:T(8,128)(2,1)S(1)} %get-tuple-element.60), channel_id=1, source_target_pairs={{0,6},{1,7},{2,0},{3,1},{4,2},{5,3},{6,4},{7,5},{8,14},{9,15},{10,... | collective-permute-start | bytes 344072 | tf_op jit(solution)/shard_map/ppermute | solution.py:302
  49.2 20.0 %copy-start.1 = (bf16[1792,608]{0,1:T(8,128)(2,1)S(1)}, bf16[1792,608]{0,1:T(8,128)(2,1)}, u32[]{:S(2)}) copy-start(bf16[1792,608]{0,1:T(8,128)(2,1)} %param.36) | copy-start | bytes 6537220
  49.2 20.0 %copy-start.2 = (bf16[1792,608]{0,1:T(8,128)(2,1)S(1)}, bf16[1792,608]{0,1:T(8,128)(2,1)}, u32[]{:S(2)}) copy-start(bf16[1792,608]{0,1:T(8,128)(2,1)} %param.37) | copy-start | bytes 6537220
  49.2 9.5 %collective-permute-start.14 = (bf16[2,224,128]{2,1,0:T(8,128)(2,1)S(1)}, bf16[2,224,128]{2,1,0:T(8,128)(2,1)S(1)}, u32[]{:S(2)}, u32[]{:S(2)}) collective-permute-start(bf16[2,224,128]{2,1,0:T(8,128)(2,1)S(1)} %pad_maximum_fusion.2), channel_id=1, source_target_pairs={{0,1},{1,0},{2,3},{3,2},{4,5},{5,4},{6,7},{7,6},{8,9},{9,8},{10,11... | collective-permute-start | bytes 344072 | tf_op jit(solution)/shard_map/ppermute | solution.py:305
  58.8 5.2 %collective-permute-start.17 = (bf16[2,224,128]{2,1,0:T(8,128)(2,1)S(1)}, bf16[2,224,128]{2,1,0:T(8,128)(2,1)S(1)}, u32[]{:S(2)}, u32[]{:S(2)}) collective-permute-start(bf16[2,224,128]{2,1,0:T(8,128)(2,1)S(1)} %add_convert_fusion.own_ref), channel_id=1, source_target_pairs={{0,6},{1,7},{2,0},{3,1},{4,2},{5,3},{6,4},{7,5},{8,14},{9,15},{10,... | collective-permute-start | bytes 344072 | tf_op jit(solution)/shard_map/ppermute | solution.py:302
  61.6 6.3 %collective-permute-start.16 = (bf16[2,224,128]{2,1,0:T(8,128)(2,1)S(1)}, bf16[2,224,128]{2,1,0:T(8,128)(2,1)S(1)}, u32[]{:S(2)}, u32[]{:S(2)}) collective-permute-start(bf16[2,224,128]{2,1,0:T(8,128)(2,1)S(1)} %add_convert_fusion.own_ref), channel_id=1, source_target_pairs={{0,4},{1,5},{2,6},{3,7},{4,0},{5,1},{6,2},{7,3},{8,12},{9,13},{10,... | collective-permute-start | bytes 344072 | tf_op jit(solution)/shard_map/ppermute | solution.py:302
  62.8 6.3 %collective-permute-start.15 = (bf16[2,224,128]{2,1,0:T(8,128)(2,1)S(1)}, bf16[2,224,128]{2,1,0:T(8,128)(2,1)S(1)}, u32[]{:S(2)}, u32[]{:S(2)}) collective-permute-start(bf16[2,224,128]{2,1,0:T(8,128)(2,1)S(1)} %add_convert_fusion.own_ref), channel_id=1, source_target_pairs={{0,2},{1,3},{2,4},{3,5},{4,6},{5,7},{6,0},{7,1},{8,10},{9,11},{10,... | collective-permute-start | bytes 344072 | tf_op jit(solution)/shard_map/ppermute | solution.py:302
  71.4 7.3 %collective-permute-start.18 = (bf16[2,224,128]{2,1,0:T(8,128)(2,1)S(1)}, bf16[2,224,128]{2,1,0:T(8,128)(2,1)S(1)}, u32[]{:S(2)}, u32[]{:S(2)}) collective-permute-start(bf16[2,224,128]{2,1,0:T(8,128)(2,1)S(1)} %get-tuple-element.66), channel_id=1, source_target_pairs={{0,2},{1,3},{2,4},{3,5},{4,6},{5,7},{6,0},{7,1},{8,10},{9,11},{10,... | collective-permute-start | bytes 344072 | tf_op jit(solution)/shard_map/ppermute | solution.py:302
  71.5 7.2 %collective-permute-start.19 = (bf16[2,224,128]{2,1,0:T(8,128)(2,1)S(1)}, bf16[2,224,128]{2,1,0:T(8,128)(2,1)S(1)}, u32[]{:S(2)}, u32[]{:S(2)}) collective-permute-start(bf16[2,224,128]{2,1,0:T(8,128)(2,1)S(1)} %get-tuple-element.67), channel_id=1, source_target_pairs={{0,4},{1,5},{2,6},{3,7},{4,0},{5,1},{6,2},{7,3},{8,12},{9,13},{10,... | collective-permute-start | bytes 344072 | tf_op jit(solution)/shard_map/ppermute | solution.py:302
  74.2 5.4 %collective-permute-start.20 = (bf16[2,224,128]{2,1,0:T(8,128)(2,1)S(1)}, bf16[2,224,128]{2,1,0:T(8,128)(2,1)S(1)}, u32[]{:S(2)}, u32[]{:S(2)}) collective-permute-start(bf16[2,224,128]{2,1,0:T(8,128)(2,1)S(1)} %get-tuple-element.68), channel_id=1, source_target_pairs={{0,6},{1,7},{2,0},{3,1},{4,2},{5,3},{6,4},{7,5},{8,14},{9,15},{10,... | collective-permute-start | bytes 344072 | tf_op jit(solution)/shard_map/ppermute | solution.py:302
  79.6 8.2 %collective-permute-start.21 = (bf16[224,128]{1,0:T(8,128)(2,1)S(1)}, bf16[224,128]{1,0:T(8,128)(2,1)S(1)}, u32[]{:S(2)}, u32[]{:S(2)}) collective-permute-start(bf16[224,128]{1,0:T(8,128)(2,1)S(1)} %fusion.4), channel_id=1, source_target_pairs={{0,1},{1,0},{2,3},{3,2},{4,5},{5,4},{6,7},{7,6},{8,9},{9,8},{10,11... | collective-permute-start | bytes 172040 | tf_op jit(solution)/shard_map/ppermute | solution.py:305
  (2 other events, 26.0 us)

commit v5 on v4

--- a/solution.py
+++ b/solution.py
@@ -61,11 +61,12 @@
 
 
 def fold_kernel(groups, held, *refs):
-    (fold_hbm, state_hbm, norm_hbm, tail_hbm, leaf_hbm, parent_hbm, owner_hbm, out_ref, slot_ref) = refs[:9]
-    fold_ref, state_ref, norm_ref, tail_ref, leaf_ref, parent_ref, owner_ref, sems = refs[9:]
+    (fold_hbm, state_hbm, norm_hbm, tail_hbm, leaf_hbm, parent_hbm, owner_hbm, own_hbm) = refs[:8]
+    out_ref, slot_ref, own_ref = refs[8:11]
+    fold_ref, state_ref, norm_ref, tail_ref, leaf_ref, parent_ref, owner_ref, sems = refs[11:]
     pairs = (
         (state_hbm, state_ref), (fold_hbm, fold_ref), (norm_hbm, norm_ref), (tail_hbm, tail_ref),
-        (leaf_hbm, leaf_ref), (parent_hbm, parent_ref), (owner_hbm, owner_ref),
+        (leaf_hbm, leaf_ref), (parent_hbm, parent_ref), (owner_hbm, owner_ref), (own_hbm, own_ref),
     )
     copies = [pltpu.make_async_copy(a, b, sems.at[i]) for i, (a, b) in enumerate(pairs)]
     for copy in copies:
@@ -94,12 +95,11 @@
     per = leaf_ref.shape[0] // total_dev
 
     def slot(row):
-        k = lax.rem(place - (row % count) // 2 + held, held)
-        k = k + jnp.where((row % 2) == core, 0, held)
+        k = (place ^ ((row % count) // 2)) + jnp.where((row % 2) == core, 0, held)
         return jnp.where((row // count) == column, k, count)
 
     for k in range(groups):
-        target = lax.rem(dev + k * count, total_dev)
+        target = dev ^ (k * count)
         for s in range(per):
             leaf = leaf_ref[target * per + s]
             middle = parent_ref[leaf]
@@ -134,10 +134,9 @@
 
 def place_blocks(scratch, blocks):
     x, z = tp_place()
-    n = len(blocks)
     rows = blocks[0].shape[1]
     for k, block in enumerate(blocks):
-        source = lax.rem(x - k + n, n)
+        source = x ^ k
         scratch[pl.ds(pl.multiple_of((2 * source + z) * rows, 32), rows), :] = block[0]
         scratch[pl.ds(pl.multiple_of((2 * source + 1 - z) * rows, 32), rows), :] = block[1]
 
@@ -221,6 +220,11 @@
         scores_ref[h] = scores.astype(BF16)
 
 
+def stack_kernel(first_ref, second_ref, out_ref):
+    out_ref[0] = first_ref[...]
+    out_ref[1] = second_ref[...]
+
+
 def turn_kernel(in_ref, out_ref):
     for j in range(out_ref.shape[0] // LANES):
         at = slice(j * LANES, (j + 1) * LANES)
@@ -266,10 +270,9 @@
 
 def spread_blocks(outs, weight_ref, right):
     x, z = tp_place()
-    n = len(outs)
     rows = outs[0].shape[1]
     for k, out in enumerate(outs):
-        to = lax.rem(x + k, n)
+        to = x ^ k
         for half, at in ((0, 2 * to + z), (1, 2 * to + 1 - z)):
             block = weight_ref[pl.ds(pl.multiple_of(at * rows, 32), rows), :]
             out[half] = jnp.dot(block, right, preferred_element_type=F32).astype(out.dtype)
@@ -294,27 +297,23 @@
     model = value_weight.shape[0]
     req_size = lax.axis_size("req")
     tp_size = lax.axis_size("tp")
-    x_size = tp_size // 2
     y_size, z_size = 4, req_size // 8
     per = request_leaf.shape[0] // req_size
 
     def along_x(array, k):
-        return lax.ppermute(array, "tp", [(i, ((i // 2 + k) % x_size) * 2 + i % 2) for i in range(tp_size)])
+        return lax.ppermute(array, "tp", [(i, i ^ (2 * k)) for i in range(tp_size)])
 
     def across_z(array):
         return lax.ppermute(array, "tp", [(i, i ^ 1) for i in range(tp_size)])
 
     def along_z(array, k):
-        count = 2 * z_size
-        return lax.ppermute(
-            array, "req", [(i, (i // count) * count + (((i % count) // 2 + k) % z_size) * 2 + i % 2) for i in range(req_size)]
-        )
+        return lax.ppermute(array, "req", [(i, i ^ (2 * k)) for i in range(req_size)])
 
     def across_core(array):
         return lax.ppermute(array, "req", [(i, i ^ 1) for i in range(req_size)])
 
     def along_y(array, k):
-        return lax.ppermute(array, "req", [(i, (i + 2 * z_size * k) % req_size) for i in range(req_size)])
+        return lax.ppermute(array, "req", [(i, i ^ (2 * z_size * k)) for i in range(req_size)])
 
     order = (1, 3, 2)
 
@@ -323,22 +322,23 @@
         return pltpu.with_memory_space_constraint(array, pltpu.HBM)
 
     state_in = jnp.transpose(node_state[0], (1, 0, 2))
-    fold_in = (fold, state_in, node_norm[0], node_tail[0], request_leaf, parent, owner_map)
-    payload, slots = pl.pallas_call(
+    own = stream.T
+    fold_in = (fold, state_in, node_norm[0], node_tail[0], request_leaf, parent, owner_map, own)
+    payload, slots, own_near = pl.pallas_call(
         functools.partial(fold_kernel, y_size, z_size),
-        out_shape=[sds((heads, ROWS, LANES), BF16), sds((y_size * per * 3,), jnp.int32)],
+        out_shape=[sds((heads, ROWS, LANES), BF16), sds((y_size * per * 3,), jnp.int32), sds(own.shape, BF16)],
         in_specs=[pl.BlockSpec(memory_space=pltpu.HBM)] * len(fold_in),
-        out_specs=[VMEM, SMEM],
+        out_specs=[VMEM, SMEM, VMEM],
         scratch_shapes=[pltpu.VMEM(a.shape, BF16) for a in fold_in[:4]]
-        + [pltpu.SMEM(a.shape, jnp.int32) for a in fold_in[4:]]
+        + [pltpu.SMEM(a.shape, jnp.int32) for a in fold_in[4:7]]
         + [pltpu.SemaphoreType.DMA((len(fold_in),))],
         compiler_params=PARAMS,
         name="fold",
     )(*[in_hbm(a) for a in fold_in])
     from_z = {k: along_z(payload, k) for k in order}
 
-    own = stream.T
-    pair = jnp.stack([own, across_z(own)])
+    pair = call(stack_kernel, sds((2, width, tokens), BF16), [VMEM] * 2, (own_near, across_z(own)), name="stack_pair")
+    rows = {k: along_x(pair, k) for k in order}
 
     held_pair, *arrived = lax.optimization_barrier((pair, from_z[1], from_z[2], from_z[3]))
     mine = jnp.stack([payload, *arrived])
@@ -358,7 +358,6 @@
     [kept] = select((0,), (mine, other), "select_kept")
     from_y = {k: along_y(sent[k], k) for k in order}
 
-    rows = {k: along_x(pair, k) for k in order}
     gain_rows = model // LANES
 
     def gain_block(gain):
@@ -384,7 +383,7 @@
     )
     parts = call(
         mix_kernel,
-        [sds((2, width, tokens), F32)] + [sds((2, width, tokens), BF16)] * (x_size - 1),
+        [sds((2, width, tokens), F32)] + [sds((2, width, tokens), BF16)] * 3,
         [VMEM] * 11,
         (*local, kept, from_y[1], from_y[2], from_y[3], turn(out_weight, "turn_out")),
         scratch=[pltpu.VMEM((width, tokens), BF16)],
@@ -400,7 +399,7 @@
     wide = {k: along_x(updated, k) for k in order}
     downs = call(
         ffn_kernel,
-        [sds((2, width, tokens), F32)] + [sds((2, width, tokens), BF16)] * (x_size - 1),
+        [sds((2, width, tokens), F32)] + [sds((2, width, tokens), BF16)] * 3,
         [VMEM] * 8,
         (updated, wide[1], wide[2], wide[3], gain_block(ffn_gain), ffn_gate.T, ffn_up.T, down_turned),
         scratch=[pltpu.VMEM((model, tokens), BF16)],

time: 90 us -> 88.5 us (0.983)
  the two profiles are of different devices: /device:TPU:8 before, /device:TPU:32 now
where the time goes in v5:
time: 88.5 us; the launch traced here: 88.4 us
  starting transfers between devices  40.1 us (45%)
  waiting for transfers between devices  36.9 us (42%)
  Pallas kernels  10.2 us (12%)
  other arithmetic  0.9 us (1%)
    ppermute x12, starting transfers between devices, along_x(): return lax.ppermute(array, 'tp', [(i, i ^ 2 * k) for i in range(tp_size)])  19 us
    ppermute x3, waiting for transfers between devices, across_z(): return lax.ppermute(array, 'tp', [(i, i ^ 1) for i in range(tp_size)])  18.5 us
    ppermute x12, waiting for transfers between devices, along_x(): return lax.ppermute(array, 'tp', [(i, i ^ 2 * k) for i in range(tp_size)])  17.8 us
    ppermute x3, starting transfers between devices, across_z(): return lax.ppermute(array, 'tp', [(i, i ^ 1) for i in range(tp_size)])  11.4 us
    pallas_call x8, Pallas kernels, call(): pl.pallas_call(kernel, out_shape=out_shape, in_specs=specs, out_specs=VME...  7.52 us
    ppermute x3, starting transfers between devices, along_z(): return lax.ppermute(array, 'req', [(i, i ^ 2 * k) for i in range(req_size)])  4.82 us
    ppermute x3, starting transfers between devices, along_y(): lax.ppermute(array, 'req', [(i, i ^ 2 * z_size * k) for i in range(req_si...  4.79 us
    pallas_call x1, Pallas kernels, shards(): pl.pallas_call(functools.partial(fold_kernel, y_size, z_size), out_shape=...  2.64 us
  transfers between devices with their start and end apart: 22, of which 14 were waited for; matrix products, arithmetic and copies ran while one was open for 0% of the time, Pallas kernels for 5%

profile of v5, /device:TPU:32, one launch (start us, length us, event | category | flops | bytes accessed | tf_op | source)
XLA Modules:
  0.0 88.4 jit_solution(2228285282255806498)
XLA Ops:
  0.1 2.6 %fold.1 = (bf16[2,160,128]{2,1,0:T(8,128)(2,1)S(1)}, s32[24]{0:T(128)S(1)}, bf16[224,128]{1,0:T(8,128)(2,1)S(1)}) custom-call(bf16[160,273]{1,0:T(8,128)(2,1)} %constant.5.clone.refs_0_, bf16[273,2,112]{2,1,0:T(2,128)(2,1)} %bitcast.39, bf16[2,273]{1,0:T(2,128)(2,1)} %bitcast.47, bf16[2,224]{1,0:T(2,128)(2,1)} %bitcast.48, s32[64]{0:T(128)} %refs_4_.1, ...), custom_call_target="tpu_custom_call" | custom-call | tf_op jit(solution)/shard_map/fold/pallas_call | solution.py:327
  2.7 2.0 %collective-permute-start.3 = (bf16[2,160,128]{2,1,0:T(8,128)(2,1)S(1)}, bf16[2,160,128]{2,1,0:T(8,128)(2,1)S(1)}, u32[]{:S(2)}, u32[]{:S(2)}) collective-permute-start(bf16[2,160,128]{2,1,0:T(8,128)(2,1)S(1)} %get-tuple-element.39), channel_id=1, source_target_pairs={{0,48},{8,56},{16,32},{24,40},{32,16},{40,24},{48,0},{56,8},{64,11... | collective-permute-start | bytes 245768 | tf_op jit(solution)/shard_map/ppermute | solution.py:310
  4.7 2.3 %collective-permute-start.2 = (bf16[2,160,128]{2,1,0:T(8,128)(2,1)S(1)}, bf16[2,160,128]{2,1,0:T(8,128)(2,1)S(1)}, u32[]{:S(2)}, u32[]{:S(2)}) collective-permute-start(bf16[2,160,128]{2,1,0:T(8,128)(2,1)S(1)} %get-tuple-element.39), channel_id=1, source_target_pairs={{0,32},{8,40},{16,48},{24,56},{32,0},{40,8},{48,16},{56,24},{64,96... | collective-permute-start | bytes 245768 | tf_op jit(solution)/shard_map/ppermute | solution.py:310
  7.5 5.0 %collective-permute-start = (bf16[224,128]{1,0:T(8,128)(2,1)}, bf16[224,128]{1,0:T(8,128)(2,1)S(1)}, u32[]{:S(2)}, u32[]{:S(2)}) collective-permute-start(bf16[224,128]{1,0:T(8,128)(2,1)} %bitcast.44), channel_id=1, source_target_pairs={{0,1},{1,0},{2,3},{3,2},{4,5},{5,4},{6,7},{7,6},{8,9},{9,8},{10,11... | collective-permute-start | bytes 172040 | tf_op jit(solution)/shard_map/ppermute | solution.py:307
  12.6 6.1 %collective-permute-done.second_ref = bf16[224,128]{1,0:T(8,128)(2,1)S(1)} collective-permute-done((bf16[224,128]{1,0:T(8,128)(2,1)}, bf16[224,128]{1,0:T(8,128)(2,1)S(1)}, u32[]{:S(2)}, u32[]{:S(2)}) %collective-permute-start) | collective-permute-done | bytes 57376 | tf_op jit(solution)/shard_map/ppermute | solution.py:307
  18.9 2.9 %collective-permute-start.6 = (bf16[2,224,128]{2,1,0:T(8,128)(2,1)S(1)}, bf16[2,224,128]{2,1,0:T(8,128)(2,1)S(1)}, u32[]{:S(2)}, u32[]{:S(2)}) collective-permute-start(bf16[2,224,128]{2,1,0:T(8,128)(2,1)S(1)} %stack_pair.1.own_ref), channel_id=1, source_target_pairs={{0,6},{1,7},{2,4},{3,5},{4,2},{5,3},{6,0},{7,1},{8,14},{9,15},{10,... | collective-permute-start | bytes 344072 | tf_op jit(solution)/shard_map/ppermute | solution.py:304
  21.7 1.0 %select_sent.1 = (bf16[2,2,160,128]{3,2,1,0:T(8,128)(2,1)S(1)}, bf16[2,2,160,128]{3,2,1,0:T(8,128)(2,1)S(1)}, bf16[2,2,160,128]{3,2,1,0:T(8,128)(2,1)S(1)}) custom-call(s32[24]{0:T(128)S(1)} %get-tuple-element.47.slot_ref, bf16[4,2,160,128]{3,2,1,0:T(8,128)(2,1)S(1)} %pad_maximum_fusion.mine_ref, bf16[4,2,160,128]{3,2,1,0:T(8,128)(2,1)S(1)} %collective-permute-done.7.other_ref), custom_call_target="tpu_custom_call" | custom-call | tf_op jit(solution)/shard_map/select_sent/pallas_call | solution.py:25
  22.7 1.7 %collective-permute-start.8 = (bf16[2,2,160,128]{3,2,1,0:T(8,128)(2,1)S(1)}, bf16[2,2,160,128]{3,2,1,0:T(8,128)(2,1)S(1)}, u32[]{:S(2)}, u32[]{:S(2)}) collective-permute-start(bf16[2,2,160,128]{3,2,1,0:T(8,128)(2,1)S(1)} %get-tuple-element.56), channel_id=1, source_target_pairs={{0,64},{8,72},{16,80},{24,88},{32,96},{40,104},{48,112},{56,120},{... | collective-permute-start | bytes 491528 | tf_op jit(solution)/shard_map/ppermute | solution.py:316
  24.3 2.9 %collective-permute-start.9 = (bf16[2,2,160,128]{3,2,1,0:T(8,128)(2,1)S(1)}, bf16[2,2,160,128]{3,2,1,0:T(8,128)(2,1)S(1)}, u32[]{:S(2)}, u32[]{:S(2)}) collective-permute-start(bf16[2,2,160,128]{3,2,1,0:T(8,128)(2,1)S(1)} %get-tuple-element.57), channel_id=1, source_target_pairs={{0,128},{8,136},{16,144},{24,152},{32,160},{40,168},{48,176},{56,1... | collective-permute-start | bytes 491528 | tf_op jit(solution)/shard_map/ppermute | solution.py:316
  27.5 1.8 %collective-permute-start.5 = (bf16[2,224,128]{2,1,0:T(8,128)(2,1)S(1)}, bf16[2,224,128]{2,1,0:T(8,128)(2,1)S(1)}, u32[]{:S(2)}, u32[]{:S(2)}) collective-permute-start(bf16[2,224,128]{2,1,0:T(8,128)(2,1)S(1)} %stack_pair.1.own_ref), channel_id=1, source_target_pairs={{0,4},{1,5},{2,6},{3,7},{4,0},{5,1},{6,2},{7,3},{8,12},{9,13},{10,... | collective-permute-start | bytes 344072 | tf_op jit(solution)/shard_map/ppermute | solution.py:304
  30.2 4.4 %collective-permute-done.5.r2_ref = bf16[2,224,128]{2,1,0:T(8,128)(2,1)S(1)} collective-permute-done((bf16[2,224,128]{2,1,0:T(8,128)(2,1)S(1)}, bf16[2,224,128]{2,1,0:T(8,128)(2,1)S(1)}, u32[]{:S(2)}, u32[]{:S(2)}) %collective-permute-start.5) | collective-permute-done | bytes 114720 | tf_op jit(solution)/shard_map/ppermute | solution.py:304
  34.7 1.5 %local.1 = (f32[224,128]{1,0:T(8,128)S(1)}, f32[224,128]{1,0:T(8,128)S(1)}, bf16[2,128,128]{2,1,0:T(8,128)(2,1)S(1)}, f32[2,1,128]{2,1,0:T(1,128)S(1)}, bf16[2,3...) custom-call(bf16[2,224,128]{2,1,0:T(8,128)(2,1)S(1)} %stack_pair.1.own_ref, ...), custom_call_target="tpu_custom_call" | custom-call | tf_op jit(solution)/shard_map/local/pallas_call | solution.py:25
  37.7 1.1 %mix.1 = (f32[2,224,128]{2,1,0:T(8,128)S(1)}, bf16[2,224,128]{2,1,0:T(8,128)(2,1)S(1)}, bf16[2,224,128]{2,1,0:T(8,128)(2,1)S(1)}, bf16[2,224,128]{2,1,0:T(8,128)(2,1)S(1)}) custom-call(f32[224,128]{1,0:T(8,128)S(1)} %get-tuple-element.41.conv_ref, f32[224,128]{1,0:T(8,128)S(1)} %get-tuple-element.42.silu_ref, ...), custom_call_target="tpu_custom_call" | custom-call | tf_op jit(solution)/shard_map/mix/pallas_call | solution.py:25
  38.7 0.9 %collective-permute-start.11 = (bf16[2,224,128]{2,1,0:T(8,128)(2,1)S(1)}, bf16[2,224,128]{2,1,0:T(8,128)(2,1)S(1)}, u32[]{:S(2)}, u32[]{:S(2)}) collective-permute-start(bf16[2,224,128]{2,1,0:T(8,128)(2,1)S(1)} %get-tuple-element.60), channel_id=1, source_target_pairs={{0,2},{1,3},{2,0},{3,1},{4,6},{5,7},{6,4},{7,5},{8,10},{9,11},{10,... | collective-permute-start | bytes 344072 | tf_op jit(solution)/shard_map/ppermute | solution.py:304
  39.6 2.1 %collective-permute-start.12 = (bf16[2,224,128]{2,1,0:T(8,128)(2,1)S(1)}, bf16[2,224,128]{2,1,0:T(8,128)(2,1)S(1)}, u32[]{:S(2)}, u32[]{:S(2)}) collective-permute-start(bf16[2,224,128]{2,1,0:T(8,128)(2,1)S(1)} %get-tuple-element.61), channel_id=1, source_target_pairs={{0,4},{1,5},{2,6},{3,7},{4,0},{5,1},{6,2},{7,3},{8,12},{9,13},{10,... | collective-permute-start | bytes 344072 | tf_op jit(solution)/shard_map/ppermute | solution.py:304
  41.8 1.7 %collective-permute-start.13 = (bf16[2,224,128]{2,1,0:T(8,128)(2,1)S(1)}, bf16[2,224,128]{2,1,0:T(8,128)(2,1)S(1)}, u32[]{:S(2)}, u32[]{:S(2)}) collective-permute-start(bf16[2,224,128]{2,1,0:T(8,128)(2,1)S(1)} %get-tuple-element.62), channel_id=1, source_target_pairs={{0,6},{1,7},{2,4},{3,5},{4,2},{5,3},{6,0},{7,1},{8,14},{9,15},{10,... | collective-permute-start | bytes 344072 | tf_op jit(solution)/shard_map/ppermute | solution.py:304
  43.5 0.9 %collective-permute-done.11 = bf16[2,224,128]{2,1,0:T(8,128)(2,1)S(1)} collective-permute-done((bf16[2,224,128]{2,1,0:T(8,128)(2,1)S(1)}, bf16[2,224,128]{2,1,0:T(8,128)(2,1)S(1)}, u32[]{:S(2)}, u32[]{:S(2)}) %collective-permute-start.11) | collective-permute-done | bytes 114720 | tf_op jit(solution)/shard_map/ppermute | solution.py:304
  44.5 2.3 %collective-permute-done.12 = bf16[2,224,128]{2,1,0:T(8,128)(2,1)S(1)} collective-permute-done((bf16[2,224,128]{2,1,0:T(8,128)(2,1)S(1)}, bf16[2,224,128]{2,1,0:T(8,128)(2,1)S(1)}, u32[]{:S(2)}, u32[]{:S(2)}) %collective-permute-start.12) | collective-permute-done | bytes 114720 | tf_op jit(solution)/shard_map/ppermute | solution.py:304
  46.7 1.6 %collective-permute-done.13 = bf16[2,224,128]{2,1,0:T(8,128)(2,1)S(1)} collective-permute-done((bf16[2,224,128]{2,1,0:T(8,128)(2,1)S(1)}, bf16[2,224,128]{2,1,0:T(8,128)(2,1)S(1)}, u32[]{:S(2)}, u32[]{:S(2)}) %collective-permute-start.13) | collective-permute-done | bytes 114720 | tf_op jit(solution)/shard_map/ppermute | solution.py:304
  48.5 2.9 %collective-permute-start.14 = (bf16[2,224,128]{2,1,0:T(8,128)(2,1)S(1)}, bf16[2,224,128]{2,1,0:T(8,128)(2,1)S(1)}, u32[]{:S(2)}, u32[]{:S(2)}) collective-permute-start(bf16[2,224,128]{2,1,0:T(8,128)(2,1)S(1)} %pad_maximum_fusion.1), channel_id=1, source_target_pairs={{0,1},{1,0},{2,3},{3,2},{4,5},{5,4},{6,7},{7,6},{8,9},{9,8},{10,11... | collective-permute-start | bytes 344072 | tf_op jit(solution)/shard_map/ppermute | solution.py:307
  52.1 7.3 %collective-permute-done.14 = bf16[2,224,128]{2,1,0:T(8,128)(2,1)S(1)} collective-permute-done((bf16[2,224,128]{2,1,0:T(8,128)(2,1)S(1)}, bf16[2,224,128]{2,1,0:T(8,128)(2,1)S(1)}, u32[]{:S(2)}, u32[]{:S(2)}) %collective-permute-start.14) | collective-permute-done | bytes 114720 | tf_op jit(solution)/shard_map/ppermute | solution.py:307
  59.5 1.8 %collective-permute-start.17 = (bf16[2,224,128]{2,1,0:T(8,128)(2,1)S(1)}, bf16[2,224,128]{2,1,0:T(8,128)(2,1)S(1)}, u32[]{:S(2)}, u32[]{:S(2)}) collective-permute-start(bf16[2,224,128]{2,1,0:T(8,128)(2,1)S(1)} %add_convert_fusion.own_ref), channel_id=1, source_target_pairs={{0,6},{1,7},{2,4},{3,5},{4,2},{5,3},{6,0},{7,1},{8,14},{9,15},{10,... | collective-permute-start | bytes 344072 | tf_op jit(solution)/shard_map/ppermute | solution.py:304
  61.3 2.3 %collective-permute-start.15 = (bf16[2,224,128]{2,1,0:T(8,128)(2,1)S(1)}, bf16[2,224,128]{2,1,0:T(8,128)(2,1)S(1)}, u32[]{:S(2)}, u32[]{:S(2)}) collective-permute-start(bf16[2,224,128]{2,1,0:T(8,128)(2,1)S(1)} %add_convert_fusion.own_ref), channel_id=1, source_target_pairs={{0,2},{1,3},{2,0},{3,1},{4,6},{5,7},{6,4},{7,5},{8,10},{9,11},{10,... | collective-permute-start | bytes 344072 | tf_op jit(solution)/shard_map/ppermute | solution.py:304
  63.7 1.9 %collective-permute-done.17.r3_ref = bf16[2,224,128]{2,1,0:T(8,128)(2,1)S(1)} collective-permute-done((bf16[2,224,128]{2,1,0:T(8,128)(2,1)S(1)}, bf16[2,224,128]{2,1,0:T(8,128)(2,1)S(1)}, u32[]{:S(2)}, u32[]{:S(2)}) %collective-permute-start.17) | collective-permute-done | bytes 114720 | tf_op jit(solution)/shard_map/ppermute | solution.py:304
  65.6 2.1 %collective-permute-done.16.r2_ref = bf16[2,224,128]{2,1,0:T(8,128)(2,1)S(1)} collective-permute-done((bf16[2,224,128]{2,1,0:T(8,128)(2,1)S(1)}, bf16[2,224,128]{2,1,0:T(8,128)(2,1)S(1)}, u32[]{:S(2)}, u32[]{:S(2)}) %collective-permute-start.16) | collective-permute-done | bytes 114720 | tf_op jit(solution)/shard_map/ppermute | solution.py:304
  67.6 2.2 %ffn.1 = (f32[2,224,128]{2,1,0:T(8,128)S(1)}, bf16[2,224,128]{2,1,0:T(8,128)(2,1)S(1)}, bf16[2,224,128]{2,1,0:T(8,128)(2,1)S(1)}, bf16[2,224,128]{2,1,0:T(8,128)(2,1)S(1)}) custom-call(bf16[2,224,128]{2,1,0:T(8,128)(2,1)S(1)} %add_convert_fusion.own_ref, bf16[2,224,128]{2,1,0:T(8,128)(2,1)S(1)} %collective-permute-done.15.r1_ref, ...), custom_call_target="tpu_custom_call" | custom-call | tf_op jit(solution)/shard_map/ffn/pallas_call | solution.py:25
  70.8 2.4 %collective-permute-start.19 = (bf16[2,224,128]{2,1,0:T(8,128)(2,1)S(1)}, bf16[2,224,128]{2,1,0:T(8,128)(2,1)S(1)}, u32[]{:S(2)}, u32[]{:S(2)}) collective-permute-start(bf16[2,224,128]{2,1,0:T(8,128)(2,1)S(1)} %get-tuple-element.69), channel_id=1, source_target_pairs={{0,4},{1,5},{2,6},{3,7},{4,0},{5,1},{6,2},{7,3},{8,12},{9,13},{10,... | collective-permute-start | bytes 344072 | tf_op jit(solution)/shard_map/ppermute | solution.py:304
  73.2 1.5 %collective-permute-start.20 = (bf16[2,224,128]{2,1,0:T(8,128)(2,1)S(1)}, bf16[2,224,128]{2,1,0:T(8,128)(2,1)S(1)}, u32[]{:S(2)}, u32[]{:S(2)}) collective-permute-start(bf16[2,224,128]{2,1,0:T(8,128)(2,1)S(1)} %get-tuple-element.70), channel_id=1, source_target_pairs={{0,6},{1,7},{2,4},{3,5},{4,2},{5,3},{6,0},{7,1},{8,14},{9,15},{10,... | collective-permute-start | bytes 344072 | tf_op jit(solution)/shard_map/ppermute | solution.py:304
  74.8 2.4 %collective-permute-done.19 = bf16[2,224,128]{2,1,0:T(8,128)(2,1)S(1)} collective-permute-done((bf16[2,224,128]{2,1,0:T(8,128)(2,1)S(1)}, bf16[2,224,128]{2,1,0:T(8,128)(2,1)S(1)}, u32[]{:S(2)}, u32[]{:S(2)}) %collective-permute-start.19) | collective-permute-done | bytes 114720 | tf_op jit(solution)/shard_map/ppermute | solution.py:304
  77.2 2.0 %collective-permute-done.20 = bf16[2,224,128]{2,1,0:T(8,128)(2,1)S(1)} collective-permute-done((bf16[2,224,128]{2,1,0:T(8,128)(2,1)S(1)}, bf16[2,224,128]{2,1,0:T(8,128)(2,1)S(1)}, u32[]{:S(2)}, u32[]{:S(2)}) %collective-permute-start.20) | collective-permute-done | bytes 114720 | tf_op jit(solution)/shard_map/ppermute | solution.py:304
  79.3 3.4 %collective-permute-start.21 = (bf16[224,128]{1,0:T(8,128)(2,1)S(1)}, bf16[224,128]{1,0:T(8,128)(2,1)S(1)}, u32[]{:S(2)}, u32[]{:S(2)}) collective-permute-start(bf16[224,128]{1,0:T(8,128)(2,1)S(1)} %fusion.4), channel_id=1, source_target_pairs={{0,1},{1,0},{2,3},{3,2},{4,5},{5,4},{6,7},{7,6},{8,9},{9,8},{10,11... | collective-permute-start | bytes 172040 | tf_op jit(solution)/shard_map/ppermute | solution.py:307
  82.7 5.1 %collective-permute-done.21 = bf16[224,128]{1,0:T(8,128)(2,1)S(1)} collective-permute-done((bf16[224,128]{1,0:T(8,128)(2,1)S(1)}, bf16[224,128]{1,0:T(8,128)(2,1)S(1)}, u32[]{:S(2)}, u32[]{:S(2)}) %collective-permute-start.21) | collective-permute-done | bytes 57376 | tf_op jit(solution)/shard_map/ppermute | solution.py:307
  (55 shorter events, 5.9 us)
Async XLA Ops:
  0.0 29.9 %copy-start.5 = (bf16[224,1792]{1,0:T(8,128)(2,1)S(1)}, bf16[224,1792]{1,0:T(8,128)(2,1)}, u32[]{:S(2)}) copy-start(bf16[224,1792]{1,0:T(8,128)(2,1)} %in_ref.1) | copy-start | bytes 2408452
  0.0 30.2 %copy-start.10 = (f32[1792]{0:T(1024)S(1)}, f32[1792]{0:T(1024)}, u32[]{:S(2)}) copy-start(f32[1792]{0:T(1024)} %param.28) | copy-start | bytes 21508
  0.0 34.7 %copy-start.8 = (f32[3,224]{1,0:T(4,128)S(1)}, f32[3,224]{1,0:T(4,128)}, u32[]{:S(2)}) copy-start(f32[3,224]{1,0:T(4,128)} %taps_ref.1) | copy-start | bytes 8068
  0.0 34.7 %copy-start.4 = (bf16[1792,224]{0,1:T(8,128)(2,1)S(1)}, bf16[1792,224]{0,1:T(8,128)(2,1)}, u32[]{:S(2)}) copy-start(bf16[1792,224]{0,1:T(8,128)(2,1)} %param.33) | copy-start | bytes 2408452
  0.0 34.7 %copy-start.3 = (bf16[1792,224]{0,1:T(8,128)(2,1)S(1)}, bf16[1792,224]{0,1:T(8,128)(2,1)}, u32[]{:S(2)}) copy-start(bf16[1792,224]{0,1:T(8,128)(2,1)} %param.32) | copy-start | bytes 2408452
  0.0 34.7 %copy-start.7 = (bf16[1792,32]{0,1:T(8,128)(2,1)S(1)}, bf16[1792,32]{0,1:T(8,128)(2,1)}, u32[]{:S(2)}) copy-start(bf16[1792,32]{0,1:T(8,128)(2,1)} %param.31) | copy-start | bytes 344068
  0.0 34.7 %copy-start.6 = (bf16[1792,32]{0,1:T(8,128)(2,1)S(1)}, bf16[1792,32]{0,1:T(8,128)(2,1)}, u32[]{:S(2)}) copy-start(bf16[1792,32]{0,1:T(8,128)(2,1)} %param.30) | copy-start | bytes 344068
  0.0 34.7 %copy-start.9 = (s32[128]{0:T(128)S(1)}, s32[128]{0:T(128)}, u32[]{:S(2)}) copy-start(s32[128]{0:T(128)} %param.21) | copy-start | bytes 1540
  2.7 16.0 %collective-permute-start.3 = (bf16[2,160,128]{2,1,0:T(8,128)(2,1)S(1)}, bf16[2,160,128]{2,1,0:T(8,128)(2,1)S(1)}, u32[]{:S(2)}, u32[]{:S(2)}) collective-permute-start(bf16[2,160,128]{2,1,0:T(8,128)(2,1)S(1)} %get-tuple-element.39), channel_id=1, source_target_pairs={{0,48},{8,56},{16,32},{24,40},{32,16},{40,24},{48,0},{56,8},{64,11... | collective-permute-start | bytes 245768 | tf_op jit(solution)/shard_map/ppermute | solution.py:310
  4.7 14.0 %collective-permute-start.2 = (bf16[2,160,128]{2,1,0:T(8,128)(2,1)S(1)}, bf16[2,160,128]{2,1,0:T(8,128)(2,1)S(1)}, u32[]{:S(2)}, u32[]{:S(2)}) collective-permute-start(bf16[2,160,128]{2,1,0:T(8,128)(2,1)S(1)} %get-tuple-element.39), channel_id=1, source_target_pairs={{0,32},{8,40},{16,48},{24,56},{32,0},{40,8},{48,16},{56,24},{64,96... | collective-permute-start | bytes 245768 | tf_op jit(solution)/shard_map/ppermute | solution.py:310
  7.0 11.7 %collective-permute-start.1 = (bf16[2,160,128]{2,1,0:T(8,128)(2,1)S(1)}, bf16[2,160,128]{2,1,0:T(8,128)(2,1)S(1)}, u32[]{:S(2)}, u32[]{:S(2)}) collective-permute-start(bf16[2,160,128]{2,1,0:T(8,128)(2,1)S(1)} %get-tuple-element.39), channel_id=1, source_target_pairs={{0,16},{8,24},{16,0},{24,8},{32,48},{40,56},{48,32},{56,40},{64,80... | collective-permute-start | bytes 245768 | tf_op jit(solution)/shard_map/ppermute | solution.py:310
  7.5 11.1 %collective-permute-start = (bf16[224,128]{1,0:T(8,128)(2,1)}, bf16[224,128]{1,0:T(8,128)(2,1)S(1)}, u32[]{:S(2)}, u32[]{:S(2)}) collective-permute-start(bf16[224,128]{1,0:T(8,128)(2,1)} %bitcast.44), channel_id=1, source_target_pairs={{0,1},{1,0},{2,3},{3,2},{4,5},{5,4},{6,7},{7,6},{8,9},{9,8},{10,11... | collective-permute-start | bytes 172040 | tf_op jit(solution)/shard_map/ppermute | solution.py:307
  18.8 3.0 %collective-permute-start.7 = (bf16[4,2,160,128]{3,2,1,0:T(8,128)(2,1)S(1)}, bf16[4,2,160,128]{3,2,1,0:T(8,128)(2,1)S(1)}, u32[]{:S(2)}, u32[]{:S(2)}) collective-permute-start(bf16[4,2,160,128]{3,2,1,0:T(8,128)(2,1)S(1)} %pad_maximum_fusion.mine_ref), channel_id=1, source_target_pairs={{0,8},{8,0},{16,24},{24,16},{32,40},{40,32},{48,56},{56,48},{64,72... | collective-permute-start | bytes 983048 | tf_op jit(solution)/shard_map/ppermute | solution.py:313
  18.9 10.4 %collective-permute-start.6 = (bf16[2,224,128]{2,1,0:T(8,128)(2,1)S(1)}, bf16[2,224,128]{2,1,0:T(8,128)(2,1)S(1)}, u32[]{:S(2)}, u32[]{:S(2)}) collective-permute-start(bf16[2,224,128]{2,1,0:T(8,128)(2,1)S(1)} %stack_pair.1.own_ref), channel_id=1, source_target_pairs={{0,6},{1,7},{2,4},{3,5},{4,2},{5,3},{6,0},{7,1},{8,14},{9,15},{10,... | collective-permute-start | bytes 344072 | tf_op jit(solution)/shard_map/ppermute | solution.py:304
  22.7 14.4 %collective-permute-start.8 = (bf16[2,2,160,128]{3,2,1,0:T(8,128)(2,1)S(1)}, bf16[2,2,160,128]{3,2,1,0:T(8,128)(2,1)S(1)}, u32[]{:S(2)}, u32[]{:S(2)}) collective-permute-start(bf16[2,2,160,128]{3,2,1,0:T(8,128)(2,1)S(1)} %get-tuple-element.56), channel_id=1, source_target_pairs={{0,64},{8,72},{16,80},{24,88},{32,96},{40,104},{48,112},{56,120},{... | collective-permute-start | bytes 491528 | tf_op jit(solution)/shard_map/ppermute | solution.py:316
  24.3 12.7 %collective-permute-start.9 = (bf16[2,2,160,128]{3,2,1,0:T(8,128)(2,1)S(1)}, bf16[2,2,160,128]{3,2,1,0:T(8,128)(2,1)S(1)}, u32[]{:S(2)}, u32[]{:S(2)}) collective-permute-start(bf16[2,2,160,128]{3,2,1,0:T(8,128)(2,1)S(1)} %get-tuple-element.57), channel_id=1, source_target_pairs={{0,128},{8,136},{16,144},{24,152},{32,160},{40,168},{48,176},{56,1... | collective-permute-start | bytes 491528 | tf_op jit(solution)/shard_map/ppermute | solution.py:316
  27.2 10.4 %collective-permute-start.10 = (bf16[2,2,160,128]{3,2,1,0:T(8,128)(2,1)S(1)}, bf16[2,2,160,128]{3,2,1,0:T(8,128)(2,1)S(1)}, u32[]{:S(2)}, u32[]{:S(2)}) collective-permute-start(bf16[2,2,160,128]{3,2,1,0:T(8,128)(2,1)S(1)} %get-tuple-element.58), channel_id=1, source_target_pairs={{0,192},{8,200},{16,208},{24,216},{32,224},{40,232},{48,240},{56,2... | collective-permute-start | bytes 491528 | tf_op jit(solution)/shard_map/ppermute | solution.py:316
  27.5 7.2 %collective-permute-start.5 = (bf16[2,224,128]{2,1,0:T(8,128)(2,1)S(1)}, bf16[2,224,128]{2,1,0:T(8,128)(2,1)S(1)}, u32[]{:S(2)}, u32[]{:S(2)}) collective-permute-start(bf16[2,224,128]{2,1,0:T(8,128)(2,1)S(1)} %stack_pair.1.own_ref), channel_id=1, source_target_pairs={{0,4},{1,5},{2,6},{3,7},{4,0},{5,1},{6,2},{7,3},{8,12},{9,13},{10,... | collective-permute-start | bytes 344072 | tf_op jit(solution)/shard_map/ppermute | solution.py:304
  29.3 5.4 %collective-permute-start.4 = (bf16[2,224,128]{2,1,0:T(8,128)(2,1)S(1)}, bf16[2,224,128]{2,1,0:T(8,128)(2,1)S(1)}, u32[]{:S(2)}, u32[]{:S(2)}) collective-permute-start(bf16[2,224,128]{2,1,0:T(8,128)(2,1)S(1)} %stack_pair.1.own_ref), channel_id=1, source_target_pairs={{0,2},{1,3},{2,0},{3,1},{4,6},{5,7},{6,4},{7,5},{8,10},{9,11},{10,... | collective-permute-start | bytes 344072 | tf_op jit(solution)/shard_map/ppermute | solution.py:304
  38.7 5.7 %collective-permute-start.11 = (bf16[2,224,128]{2,1,0:T(8,128)(2,1)S(1)}, bf16[2,224,128]{2,1,0:T(8,128)(2,1)S(1)}, u32[]{:S(2)}, u32[]{:S(2)}) collective-permute-start(bf16[2,224,128]{2,1,0:T(8,128)(2,1)S(1)} %get-tuple-element.60), channel_id=1, source_target_pairs={{0,2},{1,3},{2,0},{3,1},{4,6},{5,7},{6,4},{7,5},{8,10},{9,11},{10,... | collective-permute-start | bytes 344072 | tf_op jit(solution)/shard_map/ppermute | solution.py:304
  39.6 7.1 %collective-permute-start.12 = (bf16[2,224,128]{2,1,0:T(8,128)(2,1)S(1)}, bf16[2,224,128]{2,1,0:T(8,128)(2,1)S(1)}, u32[]{:S(2)}, u32[]{:S(2)}) collective-permute-start(bf16[2,224,128]{2,1,0:T(8,128)(2,1)S(1)} %get-tuple-element.61), channel_id=1, source_target_pairs={{0,4},{1,5},{2,6},{3,7},{4,0},{5,1},{6,2},{7,3},{8,12},{9,13},{10,... | collective-permute-start | bytes 344072 | tf_op jit(solution)/shard_map/ppermute | solution.py:304
  41.8 6.6 %collective-permute-start.13 = (bf16[2,224,128]{2,1,0:T(8,128)(2,1)S(1)}, bf16[2,224,128]{2,1,0:T(8,128)(2,1)S(1)}, u32[]{:S(2)}, u32[]{:S(2)}) collective-permute-start(bf16[2,224,128]{2,1,0:T(8,128)(2,1)S(1)} %get-tuple-element.62), channel_id=1, source_target_pairs={{0,6},{1,7},{2,4},{3,5},{4,2},{5,3},{6,0},{7,1},{8,14},{9,15},{10,... | collective-permute-start | bytes 344072 | tf_op jit(solution)/shard_map/ppermute | solution.py:304
  48.5 19.2 %copy-start.1 = (bf16[1792,608]{0,1:T(8,128)(2,1)S(1)}, bf16[1792,608]{0,1:T(8,128)(2,1)}, u32[]{:S(2)}) copy-start(bf16[1792,608]{0,1:T(8,128)(2,1)} %param.36) | copy-start | bytes 6537220
  48.5 19.2 %copy-start.2 = (bf16[1792,608]{0,1:T(8,128)(2,1)S(1)}, bf16[1792,608]{0,1:T(8,128)(2,1)}, u32[]{:S(2)}) copy-start(bf16[1792,608]{0,1:T(8,128)(2,1)} %param.37) | copy-start | bytes 6537220
  48.5 10.9 %collective-permute-start.14 = (bf16[2,224,128]{2,1,0:T(8,128)(2,1)S(1)}, bf16[2,224,128]{2,1,0:T(8,128)(2,1)S(1)}, u32[]{:S(2)}, u32[]{:S(2)}) collective-permute-start(bf16[2,224,128]{2,1,0:T(8,128)(2,1)S(1)} %pad_maximum_fusion.1), channel_id=1, source_target_pairs={{0,1},{1,0},{2,3},{3,2},{4,5},{5,4},{6,7},{7,6},{8,9},{9,8},{10,11... | collective-permute-start | bytes 344072 | tf_op jit(solution)/shard_map/ppermute | solution.py:307
  59.5 6.1 %collective-permute-start.17 = (bf16[2,224,128]{2,1,0:T(8,128)(2,1)S(1)}, bf16[2,224,128]{2,1,0:T(8,128)(2,1)S(1)}, u32[]{:S(2)}, u32[]{:S(2)}) collective-permute-start(bf16[2,224,128]{2,1,0:T(8,128)(2,1)S(1)} %add_convert_fusion.own_ref), channel_id=1, source_target_pairs={{0,6},{1,7},{2,4},{3,5},{4,2},{5,3},{6,0},{7,1},{8,14},{9,15},{10,... | collective-permute-start | bytes 344072 | tf_op jit(solution)/shard_map/ppermute | solution.py:304
  61.3 6.3 %collective-permute-start.16 = (bf16[2,224,128]{2,1,0:T(8,128)(2,1)S(1)}, bf16[2,224,128]{2,1,0:T(8,128)(2,1)S(1)}, u32[]{:S(2)}, u32[]{:S(2)}) collective-permute-start(bf16[2,224,128]{2,1,0:T(8,128)(2,1)S(1)} %add_convert_fusion.own_ref), channel_id=1, source_target_pairs={{0,4},{1,5},{2,6},{3,7},{4,0},{5,1},{6,2},{7,3},{8,12},{9,13},{10,... | collective-permute-start | bytes 344072 | tf_op jit(solution)/shard_map/ppermute | solution.py:304
  61.3 6.3 %collective-permute-start.15 = (bf16[2,224,128]{2,1,0:T(8,128)(2,1)S(1)}, bf16[2,224,128]{2,1,0:T(8,128)(2,1)S(1)}, u32[]{:S(2)}, u32[]{:S(2)}) collective-permute-start(bf16[2,224,128]{2,1,0:T(8,128)(2,1)S(1)} %add_convert_fusion.own_ref), channel_id=1, source_target_pairs={{0,2},{1,3},{2,0},{3,1},{4,6},{5,7},{6,4},{7,5},{8,10},{9,11},{10,... | collective-permute-start | bytes 344072 | tf_op jit(solution)/shard_map/ppermute | solution.py:304
  69.9 4.9 %collective-permute-start.18 = (bf16[2,224,128]{2,1,0:T(8,128)(2,1)S(1)}, bf16[2,224,128]{2,1,0:T(8,128)(2,1)S(1)}, u32[]{:S(2)}, u32[]{:S(2)}) collective-permute-start(bf16[2,224,128]{2,1,0:T(8,128)(2,1)S(1)} %get-tuple-element.68), channel_id=1, source_target_pairs={{0,2},{1,3},{2,0},{3,1},{4,6},{5,7},{6,4},{7,5},{8,10},{9,11},{10,... | collective-permute-start | bytes 344072 | tf_op jit(solution)/shard_map/ppermute | solution.py:304
  70.8 6.4 %collective-permute-start.19 = (bf16[2,224,128]{2,1,0:T(8,128)(2,1)S(1)}, bf16[2,224,128]{2,1,0:T(8,128)(2,1)S(1)}, u32[]{:S(2)}, u32[]{:S(2)}) collective-permute-start(bf16[2,224,128]{2,1,0:T(8,128)(2,1)S(1)} %get-tuple-element.69), channel_id=1, source_target_pairs={{0,4},{1,5},{2,6},{3,7},{4,0},{5,1},{6,2},{7,3},{8,12},{9,13},{10,... | collective-permute-start | bytes 344072 | tf_op jit(solution)/shard_map/ppermute | solution.py:304
  73.2 6.0 %collective-permute-start.20 = (bf16[2,224,128]{2,1,0:T(8,128)(2,1)S(1)}, bf16[2,224,128]{2,1,0:T(8,128)(2,1)S(1)}, u32[]{:S(2)}, u32[]{:S(2)}) collective-permute-start(bf16[2,224,128]{2,1,0:T(8,128)(2,1)S(1)} %get-tuple-element.70), channel_id=1, source_target_pairs={{0,6},{1,7},{2,4},{3,5},{4,2},{5,3},{6,0},{7,1},{8,14},{9,15},{10,... | collective-permute-start | bytes 344072 | tf_op jit(solution)/shard_map/ppermute | solution.py:304
  79.3 8.5 %collective-permute-start.21 = (bf16[224,128]{1,0:T(8,128)(2,1)S(1)}, bf16[224,128]{1,0:T(8,128)(2,1)S(1)}, u32[]{:S(2)}, u32[]{:S(2)}) collective-permute-start(bf16[224,128]{1,0:T(8,128)(2,1)S(1)} %fusion.4), channel_id=1, source_target_pairs={{0,1},{1,0},{2,3},{3,2},{4,5},{5,4},{6,7},{7,6},{8,9},{9,8},{10,11... | collective-permute-start | bytes 172040 | tf_op jit(solution)/shard_map/ppermute | solution.py:307
  (2 other events, 30.4 us)

commit v6 on v5

--- a/solution.py
+++ b/solution.py
@@ -60,18 +60,24 @@
     return jnp.where(lane == head_dim + 1, total + lost, total).astype(BF16)
 
 
-def fold_kernel(groups, held, *refs):
-    (fold_hbm, state_hbm, norm_hbm, tail_hbm, leaf_hbm, parent_hbm, owner_hbm, own_hbm) = refs[:8]
-    out_ref, slot_ref, own_ref = refs[8:11]
-    fold_ref, state_ref, norm_ref, tail_ref, leaf_ref, parent_ref, owner_ref, sems = refs[11:]
-    pairs = (
-        (state_hbm, state_ref), (fold_hbm, fold_ref), (norm_hbm, norm_ref), (tail_hbm, tail_ref),
-        (leaf_hbm, leaf_ref), (parent_hbm, parent_ref), (owner_hbm, owner_ref), (own_hbm, own_ref),
-    )
+def fetch(pairs, sems):
     copies = [pltpu.make_async_copy(a, b, sems.at[i]) for i, (a, b) in enumerate(pairs)]
     for copy in copies:
         copy.start()
-    for copy in copies:
+    return copies
+
+
+def fold_kernel(
+    fold_hbm, state_hbm, norm_hbm, tail_hbm, own_hbm, out_ref, own_ref, fold_ref, state_ref, norm_ref, tail_ref, sems
+):
+    copies = fetch(
+        (
+            (state_hbm, state_ref), (fold_hbm, fold_ref), (norm_hbm, norm_ref), (tail_hbm, tail_ref),
+            (own_hbm, own_ref),
+        ),
+        sems,
+    )
+    for copy in copies[:4]:
         copy.wait()
     feats, heads, head_dim = state_ref.shape
     fold = fold_ref[...]
@@ -85,7 +91,27 @@
         out_ref[h] = cols.astype(BF16)
         out_ref[h, :, :head_dim] = state.astype(BF16)
         out_ref[h, TAIL_ROW : TAIL_ROW + 2, :head_dim] = tail_ref[:, h * head_dim : (h + 1) * head_dim]
-
+    copies[4].wait()
+
+
+def turn_block(in_ref, out_ref):
+    for j in range(out_ref.shape[0] // LANES):
+        at = slice(j * LANES, (j + 1) * LANES)
+        out_ref[at, :] = in_ref[:, at].T
+
+
+def turn_kernel(in_ref, out_ref):
+    turn_block(in_ref, out_ref)
+
+
+def turn_and_slots_kernel(
+    groups, held, in_hbm, leaf_hbm, parent_hbm, owner_hbm, out_ref, slot_ref, in_ref, leaf_ref, parent_ref, owner_ref, sems
+):
+    copies = fetch(
+        ((in_hbm, in_ref), (leaf_hbm, leaf_ref), (parent_hbm, parent_ref), (owner_hbm, owner_ref)), sems
+    )
+    for copy in copies:
+        copy.wait()
     dev = lax.axis_index("req")
     count = 2 * held
     total_dev = groups * count
@@ -106,6 +132,7 @@
             root = parent_ref[middle]
             for i, node in enumerate((leaf, middle, root)):
                 slot_ref[(k * per + s) * 3 + i] = slot(owner_ref[node])
+    turn_block(in_ref, out_ref)
 
 
 def select_kernel(shifts, slot_ref, mine_ref, other_ref, *rest):
@@ -225,16 +252,6 @@
     out_ref[1] = second_ref[...]
 
 
-def turn_kernel(in_ref, out_ref):
-    for j in range(out_ref.shape[0] // LANES):
-        at = slice(j * LANES, (j + 1) * LANES)
-        out_ref[at, :] = in_ref[:, at].T
-
-
-def turn(weight, name):
-    return call(turn_kernel, sds(weight.shape[::-1], weight.dtype), [VMEM], (weight,), name=name)
-
-
 def mix_kernel(
     conv_ref, silu_ref, scores_ref, den_ref, right_ref, taps_ref, p0_ref, p1_ref, p2_ref, p3_ref,
     out_weight_ref, *rest,
@@ -323,24 +340,37 @@
 
     state_in = jnp.transpose(node_state[0], (1, 0, 2))
     own = stream.T
-    fold_in = (fold, state_in, node_norm[0], node_tail[0], request_leaf, parent, owner_map, own)
-    payload, slots, own_near = pl.pallas_call(
-        functools.partial(fold_kernel, y_size, z_size),
-        out_shape=[sds((heads, ROWS, LANES), BF16), sds((y_size * per * 3,), jnp.int32), sds(own.shape, BF16)],
-        in_specs=[pl.BlockSpec(memory_space=pltpu.HBM)] * len(fold_in),
-        out_specs=[VMEM, SMEM, VMEM],
-        scratch_shapes=[pltpu.VMEM(a.shape, BF16) for a in fold_in[:4]]
-        + [pltpu.SMEM(a.shape, jnp.int32) for a in fold_in[4:7]]
-        + [pltpu.SemaphoreType.DMA((len(fold_in),))],
+    hbm = pl.BlockSpec(memory_space=pltpu.HBM)
+    fold_in = (fold, state_in, node_norm[0], node_tail[0], own)
+    payload, own_near = pl.pallas_call(
+        fold_kernel,
+        out_shape=[sds((heads, ROWS, LANES), BF16), sds(own.shape, BF16)],
+        in_specs=[hbm] * len(fold_in),
+        out_specs=[VMEM] * 2,
+        scratch_shapes=[pltpu.VMEM(a.shape, BF16) for a in fold_in[:4]] + [pltpu.SemaphoreType.DMA((len(fold_in),))],
         compiler_params=PARAMS,
         name="fold",
     )(*[in_hbm(a) for a in fold_in])
+    path_in = (out_weight, request_leaf, parent, owner_map)
+    out_turned, slots = pl.pallas_call(
+        functools.partial(turn_and_slots_kernel, y_size, z_size),
+        out_shape=[sds(out_weight.shape[::-1], BF16), sds((y_size * per * 3,), jnp.int32)],
+        in_specs=[hbm] * len(path_in),
+        out_specs=[VMEM, SMEM],
+        scratch_shapes=[pltpu.VMEM(out_weight.shape, BF16)]
+        + [pltpu.SMEM(a.shape, jnp.int32) for a in path_in[1:]]
+        + [pltpu.SemaphoreType.DMA((len(path_in),))],
+        compiler_params=PARAMS,
+        name="turn_out",
+    )(*[in_hbm(a) for a in path_in])
     from_z = {k: along_z(payload, k) for k in order}
 
     pair = call(stack_kernel, sds((2, width, tokens), BF16), [VMEM] * 2, (own_near, across_z(own)), name="stack_pair")
     rows = {k: along_x(pair, k) for k in order}
 
-    held_pair, *arrived = lax.optimization_barrier((pair, from_z[1], from_z[2], from_z[3]))
+    held_pair, out_turned, *arrived = lax.optimization_barrier(
+        (pair, out_turned, from_z[1], from_z[2], from_z[3])
+    )
     mine = jnp.stack([payload, *arrived])
     other = across_core(mine)
     def select(shifts, held, name):
@@ -363,6 +393,7 @@
     def gain_block(gain):
         return jnp.pad(gain.reshape(gain_rows, LANES), ((0, -gain_rows % 8), (0, 0)))
 
+    kept, mixer_rows = lax.optimization_barrier((kept, gain_block(mixer_gain)))
     local = call(
         functools.partial(local_kernel, request_leaf.shape[0]),
         [
@@ -375,7 +406,7 @@
         ],
         [VMEM] * 11,
         (
-            pair, rows[1], rows[2], rows[3], gain_block(mixer_gain), token_req.reshape(1, tokens),
+            pair, rows[1], rows[2], rows[3], mixer_rows, token_req.reshape(1, tokens),
             query_weight.T, key_weight.T, value_weight.T, conv_gate_weight.T, conv_kernel,
         ),
         scratch=[pltpu.VMEM((model, tokens), BF16)],
@@ -385,7 +416,7 @@
         mix_kernel,
         [sds((2, width, tokens), F32)] + [sds((2, width, tokens), BF16)] * 3,
         [VMEM] * 11,
-        (*local, kept, from_y[1], from_y[2], from_y[3], turn(out_weight, "turn_out")),
+        (*local, kept, from_y[1], from_y[2], from_y[3], out_turned),
         scratch=[pltpu.VMEM((width, tokens), BF16)],
         name="mix",
     )
@@ -394,7 +425,8 @@
     crossing, down_in = lax.optimization_barrier((jnp.stack([share[1], share[0]]).astype(BF16), ffn_down))
     share_peer = across_z(crossing)
     updated = (held_pair.astype(F32) + share + share_peer.astype(F32)).astype(BF16)
-    updated, down_turned = lax.optimization_barrier((updated, turn(down_in, "turn_down")))
+    turned_down = call(turn_kernel, sds(down_in.shape[::-1], BF16), [VMEM], (down_in,), name="turn_down")
+    updated, down_turned = lax.optimization_barrier((updated, turned_down))
 
     wide = {k: along_x(updated, k) for k in order}
     downs = call(

time: 88.5 us -> 87.6 us (0.990)
  waiting for transfers between devices: 36.9 us -> 34.9 us
  Pallas kernels: 10.2 us -> 11.3 us
    ppermute x3, waiting for transfers between devices: 18.5 us -> 16.1 us  [across_z(): return lax.ppermute(array, 'tp', [(i, i ^ 1) for i in range(tp_size)])]
    pallas_call x1 -> x2, Pallas kernels: 2.64 us -> 4.09 us  [the longest x1 2.35 us: shards(): pl.pallas_call(functools.partial(turn_and_slots_kernel, y_size, z_size),...]
    pallas_call x8 -> x7, Pallas kernels: 7.52 us -> 7.21 us  [call(): pl.pallas_call(kernel, out_shape=out_shape, in_specs=specs, out_specs=VME...]
  transfers between devices with their start and end apart: 22 -> 22, of which waited for: 14 -> 15; matrix products, arithmetic and copies ran while one was open for 0% -> 0% of each run, Pallas kernels for 5% -> 7%
where the time goes in v6:
time: 87.6 us; the launch traced here: 87.5 us
  starting transfers between devices  40.1 us (46%)
  waiting for transfers between devices  34.9 us (40%)
  Pallas kernels  11.3 us (13%)
  other arithmetic  0.91 us (1%)
    ppermute x12, starting transfers between devices, along_x(): return lax.ppermute(array, 'tp', [(i, i ^ 2 * k) for i in range(tp_size)])  19 us
    ppermute x12, waiting for transfers between devices, along_x(): return lax.ppermute(array, 'tp', [(i, i ^ 2 * k) for i in range(tp_size)])  17.4 us
    ppermute x3, waiting for transfers between devices, across_z(): return lax.ppermute(array, 'tp', [(i, i ^ 1) for i in range(tp_size)])  16.1 us
    ppermute x3, starting transfers between devices, across_z(): return lax.ppermute(array, 'tp', [(i, i ^ 1) for i in range(tp_size)])  11.4 us
    pallas_call x7, Pallas kernels, call(): pl.pallas_call(kernel, out_shape=out_shape, in_specs=specs, out_specs=VME...  7.21 us
    ppermute x3, starting transfers between devices, along_z(): return lax.ppermute(array, 'req', [(i, i ^ 2 * k) for i in range(req_size)])  4.82 us
    ppermute x3, starting transfers between devices, along_y(): lax.ppermute(array, 'req', [(i, i ^ 2 * z_size * k) for i in range(req_si...  4.79 us
    pallas_call x1, Pallas kernels, shards(): pl.pallas_call(functools.partial(turn_and_slots_kernel, y_size, z_size),...  2.35 us
  transfers between devices with their start and end apart: 22, of which 15 were waited for; matrix products, arithmetic and copies ran while one was open for 0% of the time, Pallas kernels for 7%

profile of v6, /device:TPU:32, one launch (start us, length us, event | category | flops | bytes accessed | tf_op | source)
XLA Modules:
  0.0 87.5 jit_solution(13126292865796419708)
XLA Ops:
  0.0 1.7 %fold.1 = (bf16[2,160,128]{2,1,0:T(8,128)(2,1)S(1)}, bf16[224,128]{1,0:T(8,128)(2,1)S(1)}) custom-call(bf16[160,273]{1,0:T(8,128)(2,1)} %constant.5.clone.fold_hbm, bf16[273,2,112]{2,1,0:T(2,128)(2,1)} %bitcast.39, bf16[2,273]{1,0:T(2,128)(2,1)} %bitcast.47, bf16[2,224]{1,0:T(2,128)(2,1)} %bitcast.48, bf16[224,128]{1,0:T(8,128)(2,1)} %bitcast.43), custom_call_target="tpu_custom_call" | custom-call | tf_op jit(solution)/shard_map/fold/pallas_call | solution.py:345
  1.8 2.0 %collective-permute-start.3 = (bf16[2,160,128]{2,1,0:T(8,128)(2,1)S(1)}, bf16[2,160,128]{2,1,0:T(8,128)(2,1)S(1)}, u32[]{:S(2)}, u32[]{:S(2)}) collective-permute-start(bf16[2,160,128]{2,1,0:T(8,128)(2,1)S(1)} %get-tuple-element.44), channel_id=1, source_target_pairs={{0,48},{8,56},{16,32},{24,40},{32,16},{40,24},{48,0},{56,8},{64,11... | collective-permute-start | bytes 245768 | tf_op jit(solution)/shard_map/ppermute | solution.py:327
  3.8 2.3 %collective-permute-start.2 = (bf16[2,160,128]{2,1,0:T(8,128)(2,1)S(1)}, bf16[2,160,128]{2,1,0:T(8,128)(2,1)S(1)}, u32[]{:S(2)}, u32[]{:S(2)}) collective-permute-start(bf16[2,160,128]{2,1,0:T(8,128)(2,1)S(1)} %get-tuple-element.44), channel_id=1, source_target_pairs={{0,32},{8,40},{16,48},{24,56},{32,0},{40,8},{48,16},{56,24},{64,96... | collective-permute-start | bytes 245768 | tf_op jit(solution)/shard_map/ppermute | solution.py:327
  6.6 5.0 %collective-permute-start = (bf16[224,128]{1,0:T(8,128)(2,1)}, bf16[224,128]{1,0:T(8,128)(2,1)S(1)}, u32[]{:S(2)}, u32[]{:S(2)}) collective-permute-start(bf16[224,128]{1,0:T(8,128)(2,1)} %bitcast.44), channel_id=1, source_target_pairs={{0,1},{1,0},{2,3},{3,2},{4,5},{5,4},{6,7},{7,6},{8,9},{9,8},{10,11... | collective-permute-start | bytes 172040 | tf_op jit(solution)/shard_map/ppermute | solution.py:324
  11.7 2.4 %turn_out.1 = (bf16[1792,224]{1,0:T(8,128)(2,1)S(1)}, s32[24]{0:T(128)S(1)}) custom-call(bf16[224,1792]{1,0:T(8,128)(2,1)} %in_hbm.1, s32[64]{0:T(128)} %leaf_hbm.1, s32[32]{0:T(128)} %parent_hbm.1, s32[32]{0:T(128)} %owner_hbm.1), custom_call_target="tpu_custom_call" | custom-call | tf_op jit(solution)/shard_map/turn_out/pallas_call | solution.py:355
  14.0 3.7 %collective-permute-done.second_ref = bf16[224,128]{1,0:T(8,128)(2,1)S(1)} collective-permute-done((bf16[224,128]{1,0:T(8,128)(2,1)}, bf16[224,128]{1,0:T(8,128)(2,1)S(1)}, u32[]{:S(2)}, u32[]{:S(2)}) %collective-permute-start) | collective-permute-done | bytes 57376 | tf_op jit(solution)/shard_map/ppermute | solution.py:324
  17.9 2.8 %collective-permute-start.6 = (bf16[2,224,128]{2,1,0:T(8,128)(2,1)S(1)}, bf16[2,224,128]{2,1,0:T(8,128)(2,1)S(1)}, u32[]{:S(2)}, u32[]{:S(2)}) collective-permute-start(bf16[2,224,128]{2,1,0:T(8,128)(2,1)S(1)} %stack_pair.1.own_ref), channel_id=1, source_target_pairs={{0,6},{1,7},{2,4},{3,5},{4,2},{5,3},{6,0},{7,1},{8,14},{9,15},{10,... | collective-permute-start | bytes 344072 | tf_op jit(solution)/shard_map/ppermute | solution.py:321
  20.8 1.0 %select_sent.1 = (bf16[2,2,160,128]{3,2,1,0:T(8,128)(2,1)S(1)}, bf16[2,2,160,128]{3,2,1,0:T(8,128)(2,1)S(1)}, bf16[2,2,160,128]{3,2,1,0:T(8,128)(2,1)S(1)}) custom-call(s32[24]{0:T(128)S(1)} %get-tuple-element.46.slot_ref, bf16[4,2,160,128]{3,2,1,0:T(8,128)(2,1)S(1)} %pad_maximum_fusion.mine_ref, bf16[4,2,160,128]{3,2,1,0:T(8,128)(2,1)S(1)} %collective-permute-done.7.other_ref), custom_call_target="tpu_custom_call" | custom-call | tf_op jit(solution)/shard_map/select_sent/pallas_call | solution.py:25
  21.8 1.7 %collective-permute-start.8 = (bf16[2,2,160,128]{3,2,1,0:T(8,128)(2,1)S(1)}, bf16[2,2,160,128]{3,2,1,0:T(8,128)(2,1)S(1)}, u32[]{:S(2)}, u32[]{:S(2)}) collective-permute-start(bf16[2,2,160,128]{3,2,1,0:T(8,128)(2,1)S(1)} %get-tuple-element.63), channel_id=1, source_target_pairs={{0,64},{8,72},{16,80},{24,88},{32,96},{40,104},{48,112},{56,120},{... | collective-permute-start | bytes 491528 | tf_op jit(solution)/shard_map/ppermute | solution.py:333
  23.4 2.9 %collective-permute-start.9 = (bf16[2,2,160,128]{3,2,1,0:T(8,128)(2,1)S(1)}, bf16[2,2,160,128]{3,2,1,0:T(8,128)(2,1)S(1)}, u32[]{:S(2)}, u32[]{:S(2)}) collective-permute-start(bf16[2,2,160,128]{3,2,1,0:T(8,128)(2,1)S(1)} %get-tuple-element.64), channel_id=1, source_target_pairs={{0,128},{8,136},{16,144},{24,152},{32,160},{40,168},{48,176},{56,1... | collective-permute-start | bytes 491528 | tf_op jit(solution)/shard_map/ppermute | solution.py:333
  26.6 1.8 %collective-permute-start.5 = (bf16[2,224,128]{2,1,0:T(8,128)(2,1)S(1)}, bf16[2,224,128]{2,1,0:T(8,128)(2,1)S(1)}, u32[]{:S(2)}, u32[]{:S(2)}) collective-permute-start(bf16[2,224,128]{2,1,0:T(8,128)(2,1)S(1)} %stack_pair.1.own_ref), channel_id=1, source_target_pairs={{0,4},{1,5},{2,6},{3,7},{4,0},{5,1},{6,2},{7,3},{8,12},{9,13},{10,... | collective-permute-start | bytes 344072 | tf_op jit(solution)/shard_map/ppermute | solution.py:321
  29.7 4.0 %collective-permute-done.5.r2_ref = bf16[2,224,128]{2,1,0:T(8,128)(2,1)S(1)} collective-permute-done((bf16[2,224,128]{2,1,0:T(8,128)(2,1)S(1)}, bf16[2,224,128]{2,1,0:T(8,128)(2,1)S(1)}, u32[]{:S(2)}, u32[]{:S(2)}) %collective-permute-start.5) | collective-permute-done | bytes 114720 | tf_op jit(solution)/shard_map/ppermute | solution.py:321
  33.8 1.5 %local.1 = (f32[224,128]{1,0:T(8,128)S(1)}, f32[224,128]{1,0:T(8,128)S(1)}, bf16[2,128,128]{2,1,0:T(8,128)(2,1)S(1)}, f32[2,1,128]{2,1,0:T(1,128)S(1)}, bf16[2,3...) custom-call(bf16[2,224,128]{2,1,0:T(8,128)(2,1)S(1)} %stack_pair.1.own_ref, ...), custom_call_target="tpu_custom_call" | custom-call | tf_op jit(solution)/shard_map/local/pallas_call | solution.py:25
  35.4 1.4 %collective-permute-done.10.p3_ref = bf16[2,2,160,128]{3,2,1,0:T(8,128)(2,1)S(1)} collective-permute-done((bf16[2,2,160,128]{3,2,1,0:T(8,128)(2,1)S(1)}, bf16[2,2,160,128]{3,2,1,0:T(8,128)(2,1)S(1)}, u32[]{:S(2)}, u32[]{:S(2)}) %collective-permute-start.10) | collective-permute-done | bytes 163872 | tf_op jit(solution)/shard_map/ppermute | solution.py:333
  36.8 1.1 %mix.1 = (f32[2,224,128]{2,1,0:T(8,128)S(1)}, bf16[2,224,128]{2,1,0:T(8,128)(2,1)S(1)}, bf16[2,224,128]{2,1,0:T(8,128)(2,1)S(1)}, bf16[2,224,128]{2,1,0:T(8,128)(2,1)S(1)}) custom-call(f32[224,128]{1,0:T(8,128)S(1)} %get-tuple-element.56.conv_ref, f32[224,128]{1,0:T(8,128)S(1)} %get-tuple-element.57.silu_ref, ...), custom_call_target="tpu_custom_call" | custom-call | tf_op jit(solution)/shard_map/mix/pallas_call | solution.py:25
  38.1 2.7 %collective-permute-start.12 = (bf16[2,224,128]{2,1,0:T(8,128)(2,1)S(1)}, bf16[2,224,128]{2,1,0:T(8,128)(2,1)S(1)}, u32[]{:S(2)}, u32[]{:S(2)}) collective-permute-start(bf16[2,224,128]{2,1,0:T(8,128)(2,1)S(1)} %get-tuple-element.69), channel_id=1, source_target_pairs={{0,4},{1,5},{2,6},{3,7},{4,0},{5,1},{6,2},{7,3},{8,12},{9,13},{10,... | collective-permute-start | bytes 344072 | tf_op jit(solution)/shard_map/ppermute | solution.py:321
  40.9 1.7 %collective-permute-start.13 = (bf16[2,224,128]{2,1,0:T(8,128)(2,1)S(1)}, bf16[2,224,128]{2,1,0:T(8,128)(2,1)S(1)}, u32[]{:S(2)}, u32[]{:S(2)}) collective-permute-start(bf16[2,224,128]{2,1,0:T(8,128)(2,1)S(1)} %get-tuple-element.70), channel_id=1, source_target_pairs={{0,6},{1,7},{2,4},{3,5},{4,2},{5,3},{6,0},{7,1},{8,14},{9,15},{10,... | collective-permute-start | bytes 344072 | tf_op jit(solution)/shard_map/ppermute | solution.py:321
  43.5 2.3 %collective-permute-done.12 = bf16[2,224,128]{2,1,0:T(8,128)(2,1)S(1)} collective-permute-done((bf16[2,224,128]{2,1,0:T(8,128)(2,1)S(1)}, bf16[2,224,128]{2,1,0:T(8,128)(2,1)S(1)}, u32[]{:S(2)}, u32[]{:S(2)}) %collective-permute-start.12) | collective-permute-done | bytes 114720 | tf_op jit(solution)/shard_map/ppermute | solution.py:321
  45.8 1.6 %collective-permute-done.13 = bf16[2,224,128]{2,1,0:T(8,128)(2,1)S(1)} collective-permute-done((bf16[2,224,128]{2,1,0:T(8,128)(2,1)S(1)}, bf16[2,224,128]{2,1,0:T(8,128)(2,1)S(1)}, u32[]{:S(2)}, u32[]{:S(2)}) %collective-permute-start.13) | collective-permute-done | bytes 114720 | tf_op jit(solution)/shard_map/ppermute | solution.py:321
  47.6 2.9 %collective-permute-start.14 = (bf16[2,224,128]{2,1,0:T(8,128)(2,1)S(1)}, bf16[2,224,128]{2,1,0:T(8,128)(2,1)S(1)}, u32[]{:S(2)}, u32[]{:S(2)}) collective-permute-start(bf16[2,224,128]{2,1,0:T(8,128)(2,1)S(1)} %pad_maximum_fusion.1), channel_id=1, source_target_pairs={{0,1},{1,0},{2,3},{3,2},{4,5},{5,4},{6,7},{7,6},{8,9},{9,8},{10,11... | collective-permute-start | bytes 344072 | tf_op jit(solution)/shard_map/ppermute | solution.py:324
  51.2 7.3 %collective-permute-done.14 = bf16[2,224,128]{2,1,0:T(8,128)(2,1)S(1)} collective-permute-done((bf16[2,224,128]{2,1,0:T(8,128)(2,1)S(1)}, bf16[2,224,128]{2,1,0:T(8,128)(2,1)S(1)}, u32[]{:S(2)}, u32[]{:S(2)}) %collective-permute-start.14) | collective-permute-done | bytes 114720 | tf_op jit(solution)/shard_map/ppermute | solution.py:324
  58.6 1.8 %collective-permute-start.17 = (bf16[2,224,128]{2,1,0:T(8,128)(2,1)S(1)}, bf16[2,224,128]{2,1,0:T(8,128)(2,1)S(1)}, u32[]{:S(2)}, u32[]{:S(2)}) collective-permute-start(bf16[2,224,128]{2,1,0:T(8,128)(2,1)S(1)} %add_convert_fusion.own_ref), channel_id=1, source_target_pairs={{0,6},{1,7},{2,4},{3,5},{4,2},{5,3},{6,0},{7,1},{8,14},{9,15},{10,... | collective-permute-start | bytes 344072 | tf_op jit(solution)/shard_map/ppermute | solution.py:321
  60.4 2.4 %collective-permute-start.15 = (bf16[2,224,128]{2,1,0:T(8,128)(2,1)S(1)}, bf16[2,224,128]{2,1,0:T(8,128)(2,1)S(1)}, u32[]{:S(2)}, u32[]{:S(2)}) collective-permute-start(bf16[2,224,128]{2,1,0:T(8,128)(2,1)S(1)} %add_convert_fusion.own_ref), channel_id=1, source_target_pairs={{0,2},{1,3},{2,0},{3,1},{4,6},{5,7},{6,4},{7,5},{8,10},{9,11},{10,... | collective-permute-start | bytes 344072 | tf_op jit(solution)/shard_map/ppermute | solution.py:321
  62.7 1.9 %collective-permute-done.17.r3_ref = bf16[2,224,128]{2,1,0:T(8,128)(2,1)S(1)} collective-permute-done((bf16[2,224,128]{2,1,0:T(8,128)(2,1)S(1)}, bf16[2,224,128]{2,1,0:T(8,128)(2,1)S(1)}, u32[]{:S(2)}, u32[]{:S(2)}) %collective-permute-start.17) | collective-permute-done | bytes 114720 | tf_op jit(solution)/shard_map/ppermute | solution.py:321
  64.6 2.0 %collective-permute-done.16.r2_ref = bf16[2,224,128]{2,1,0:T(8,128)(2,1)S(1)} collective-permute-done((bf16[2,224,128]{2,1,0:T(8,128)(2,1)S(1)}, bf16[2,224,128]{2,1,0:T(8,128)(2,1)S(1)}, u32[]{:S(2)}, u32[]{:S(2)}) %collective-permute-start.16) | collective-permute-done | bytes 114720 | tf_op jit(solution)/shard_map/ppermute | solution.py:321
  66.7 2.2 %ffn.1 = (f32[2,224,128]{2,1,0:T(8,128)S(1)}, bf16[2,224,128]{2,1,0:T(8,128)(2,1)S(1)}, bf16[2,224,128]{2,1,0:T(8,128)(2,1)S(1)}, bf16[2,224,128]{2,1,0:T(8,128)(2,1)S(1)}) custom-call(bf16[2,224,128]{2,1,0:T(8,128)(2,1)S(1)} %add_convert_fusion.own_ref, bf16[2,224,128]{2,1,0:T(8,128)(2,1)S(1)} %collective-permute-done.15.r1_ref, ...), custom_call_target="tpu_custom_call" | custom-call | tf_op jit(solution)/shard_map/ffn/pallas_call | solution.py:25
  69.9 2.4 %collective-permute-start.19 = (bf16[2,224,128]{2,1,0:T(8,128)(2,1)S(1)}, bf16[2,224,128]{2,1,0:T(8,128)(2,1)S(1)}, u32[]{:S(2)}, u32[]{:S(2)}) collective-permute-start(bf16[2,224,128]{2,1,0:T(8,128)(2,1)S(1)} %get-tuple-element.77), channel_id=1, source_target_pairs={{0,4},{1,5},{2,6},{3,7},{4,0},{5,1},{6,2},{7,3},{8,12},{9,13},{10,... | collective-permute-start | bytes 344072 | tf_op jit(solution)/shard_map/ppermute | solution.py:321
  72.3 1.5 %collective-permute-start.20 = (bf16[2,224,128]{2,1,0:T(8,128)(2,1)S(1)}, bf16[2,224,128]{2,1,0:T(8,128)(2,1)S(1)}, u32[]{:S(2)}, u32[]{:S(2)}) collective-permute-start(bf16[2,224,128]{2,1,0:T(8,128)(2,1)S(1)} %get-tuple-element.78), channel_id=1, source_target_pairs={{0,6},{1,7},{2,4},{3,5},{4,2},{5,3},{6,0},{7,1},{8,14},{9,15},{10,... | collective-permute-start | bytes 344072 | tf_op jit(solution)/shard_map/ppermute | solution.py:321
  73.9 2.4 %collective-permute-done.19 = bf16[2,224,128]{2,1,0:T(8,128)(2,1)S(1)} collective-permute-done((bf16[2,224,128]{2,1,0:T(8,128)(2,1)S(1)}, bf16[2,224,128]{2,1,0:T(8,128)(2,1)S(1)}, u32[]{:S(2)}, u32[]{:S(2)}) %collective-permute-start.19) | collective-permute-done | bytes 114720 | tf_op jit(solution)/shard_map/ppermute | solution.py:321
  76.3 2.0 %collective-permute-done.20 = bf16[2,224,128]{2,1,0:T(8,128)(2,1)S(1)} collective-permute-done((bf16[2,224,128]{2,1,0:T(8,128)(2,1)S(1)}, bf16[2,224,128]{2,1,0:T(8,128)(2,1)S(1)}, u32[]{:S(2)}, u32[]{:S(2)}) %collective-permute-start.20) | collective-permute-done | bytes 114720 | tf_op jit(solution)/shard_map/ppermute | solution.py:321
  78.3 3.5 %collective-permute-start.21 = (bf16[224,128]{1,0:T(8,128)(2,1)S(1)}, bf16[224,128]{1,0:T(8,128)(2,1)S(1)}, u32[]{:S(2)}, u32[]{:S(2)}) collective-permute-start(bf16[224,128]{1,0:T(8,128)(2,1)S(1)} %fusion.4), channel_id=1, source_target_pairs={{0,1},{1,0},{2,3},{3,2},{4,5},{5,4},{6,7},{7,6},{8,9},{9,8},{10,11... | collective-permute-start | bytes 172040 | tf_op jit(solution)/shard_map/ppermute | solution.py:324
  81.8 5.1 %collective-permute-done.21 = bf16[224,128]{1,0:T(8,128)(2,1)S(1)} collective-permute-done((bf16[224,128]{1,0:T(8,128)(2,1)S(1)}, bf16[224,128]{1,0:T(8,128)(2,1)S(1)}, u32[]{:S(2)}, u32[]{:S(2)}) %collective-permute-start.21) | collective-permute-done | bytes 57376 | tf_op jit(solution)/shard_map/ppermute | solution.py:324
  (53 shorter events, 6.2 us)
Async XLA Ops:
  0.0 28.9 %copy-start.9 = (f32[1792]{0:T(1024)S(1)}, f32[1792]{0:T(1024)}, u32[]{:S(2)}) copy-start(f32[1792]{0:T(1024)} %param.28) | copy-start | bytes 21508
  0.0 33.8 %copy-start.7 = (f32[3,224]{1,0:T(4,128)S(1)}, f32[3,224]{1,0:T(4,128)}, u32[]{:S(2)}) copy-start(f32[3,224]{1,0:T(4,128)} %taps_ref.1) | copy-start | bytes 8068
  0.0 33.8 %copy-start.4 = (bf16[1792,224]{0,1:T(8,128)(2,1)S(1)}, bf16[1792,224]{0,1:T(8,128)(2,1)}, u32[]{:S(2)}) copy-start(bf16[1792,224]{0,1:T(8,128)(2,1)} %param.33) | copy-start | bytes 2408452
  0.0 33.8 %copy-start.3 = (bf16[1792,224]{0,1:T(8,128)(2,1)S(1)}, bf16[1792,224]{0,1:T(8,128)(2,1)}, u32[]{:S(2)}) copy-start(bf16[1792,224]{0,1:T(8,128)(2,1)} %param.32) | copy-start | bytes 2408452
  0.0 33.8 %copy-start.6 = (bf16[1792,32]{0,1:T(8,128)(2,1)S(1)}, bf16[1792,32]{0,1:T(8,128)(2,1)}, u32[]{:S(2)}) copy-start(bf16[1792,32]{0,1:T(8,128)(2,1)} %param.31) | copy-start | bytes 344068
  0.0 33.8 %copy-start.5 = (bf16[1792,32]{0,1:T(8,128)(2,1)S(1)}, bf16[1792,32]{0,1:T(8,128)(2,1)}, u32[]{:S(2)}) copy-start(bf16[1792,32]{0,1:T(8,128)(2,1)} %param.30) | copy-start | bytes 344068
  0.0 33.8 %copy-start.8 = (s32[128]{0:T(128)S(1)}, s32[128]{0:T(128)}, u32[]{:S(2)}) copy-start(s32[128]{0:T(128)} %param.21) | copy-start | bytes 1540
  1.8 16.0 %collective-permute-start.3 = (bf16[2,160,128]{2,1,0:T(8,128)(2,1)S(1)}, bf16[2,160,128]{2,1,0:T(8,128)(2,1)S(1)}, u32[]{:S(2)}, u32[]{:S(2)}) collective-permute-start(bf16[2,160,128]{2,1,0:T(8,128)(2,1)S(1)} %get-tuple-element.44), channel_id=1, source_target_pairs={{0,48},{8,56},{16,32},{24,40},{32,16},{40,24},{48,0},{56,8},{64,11... | collective-permute-start | bytes 245768 | tf_op jit(solution)/shard_map/ppermute | solution.py:327
  3.8 14.0 %collective-permute-start.2 = (bf16[2,160,128]{2,1,0:T(8,128)(2,1)S(1)}, bf16[2,160,128]{2,1,0:T(8,128)(2,1)S(1)}, u32[]{:S(2)}, u32[]{:S(2)}) collective-permute-start(bf16[2,160,128]{2,1,0:T(8,128)(2,1)S(1)} %get-tuple-element.44), channel_id=1, source_target_pairs={{0,32},{8,40},{16,48},{24,56},{32,0},{40,8},{48,16},{56,24},{64,96... | collective-permute-start | bytes 245768 | tf_op jit(solution)/shard_map/ppermute | solution.py:327
  6.1 11.7 %collective-permute-start.1 = (bf16[2,160,128]{2,1,0:T(8,128)(2,1)S(1)}, bf16[2,160,128]{2,1,0:T(8,128)(2,1)S(1)}, u32[]{:S(2)}, u32[]{:S(2)}) collective-permute-start(bf16[2,160,128]{2,1,0:T(8,128)(2,1)S(1)} %get-tuple-element.44), channel_id=1, source_target_pairs={{0,16},{8,24},{16,0},{24,8},{32,48},{40,56},{48,32},{56,40},{64,80... | collective-permute-start | bytes 245768 | tf_op jit(solution)/shard_map/ppermute | solution.py:327
  6.6 11.1 %collective-permute-start = (bf16[224,128]{1,0:T(8,128)(2,1)}, bf16[224,128]{1,0:T(8,128)(2,1)S(1)}, u32[]{:S(2)}, u32[]{:S(2)}) collective-permute-start(bf16[224,128]{1,0:T(8,128)(2,1)} %bitcast.44), channel_id=1, source_target_pairs={{0,1},{1,0},{2,3},{3,2},{4,5},{5,4},{6,7},{7,6},{8,9},{9,8},{10,11... | collective-permute-start | bytes 172040 | tf_op jit(solution)/shard_map/ppermute | solution.py:324
  17.8 3.0 %collective-permute-start.7 = (bf16[4,2,160,128]{3,2,1,0:T(8,128)(2,1)S(1)}, bf16[4,2,160,128]{3,2,1,0:T(8,128)(2,1)S(1)}, u32[]{:S(2)}, u32[]{:S(2)}) collective-permute-start(bf16[4,2,160,128]{3,2,1,0:T(8,128)(2,1)S(1)} %pad_maximum_fusion.mine_ref), channel_id=1, source_target_pairs={{0,8},{8,0},{16,24},{24,16},{32,40},{40,32},{48,56},{56,48},{64,72... | collective-permute-start | bytes 983048 | tf_op jit(solution)/shard_map/ppermute | solution.py:330
  17.9 10.4 %collective-permute-start.6 = (bf16[2,224,128]{2,1,0:T(8,128)(2,1)S(1)}, bf16[2,224,128]{2,1,0:T(8,128)(2,1)S(1)}, u32[]{:S(2)}, u32[]{:S(2)}) collective-permute-start(bf16[2,224,128]{2,1,0:T(8,128)(2,1)S(1)} %stack_pair.1.own_ref), channel_id=1, source_target_pairs={{0,6},{1,7},{2,4},{3,5},{4,2},{5,3},{6,0},{7,1},{8,14},{9,15},{10,... | collective-permute-start | bytes 344072 | tf_op jit(solution)/shard_map/ppermute | solution.py:321
  21.8 13.6 %collective-permute-start.8 = (bf16[2,2,160,128]{3,2,1,0:T(8,128)(2,1)S(1)}, bf16[2,2,160,128]{3,2,1,0:T(8,128)(2,1)S(1)}, u32[]{:S(2)}, u32[]{:S(2)}) collective-permute-start(bf16[2,2,160,128]{3,2,1,0:T(8,128)(2,1)S(1)} %get-tuple-element.63), channel_id=1, source_target_pairs={{0,64},{8,72},{16,80},{24,88},{32,96},{40,104},{48,112},{56,120},{... | collective-permute-start | bytes 491528 | tf_op jit(solution)/shard_map/ppermute | solution.py:333
  23.4 12.0 %collective-permute-start.9 = (bf16[2,2,160,128]{3,2,1,0:T(8,128)(2,1)S(1)}, bf16[2,2,160,128]{3,2,1,0:T(8,128)(2,1)S(1)}, u32[]{:S(2)}, u32[]{:S(2)}) collective-permute-start(bf16[2,2,160,128]{3,2,1,0:T(8,128)(2,1)S(1)} %get-tuple-element.64), channel_id=1, source_target_pairs={{0,128},{8,136},{16,144},{24,152},{32,160},{40,168},{48,176},{56,1... | collective-permute-start | bytes 491528 | tf_op jit(solution)/shard_map/ppermute | solution.py:333
  26.3 10.4 %collective-permute-start.10 = (bf16[2,2,160,128]{3,2,1,0:T(8,128)(2,1)S(1)}, bf16[2,2,160,128]{3,2,1,0:T(8,128)(2,1)S(1)}, u32[]{:S(2)}, u32[]{:S(2)}) collective-permute-start(bf16[2,2,160,128]{3,2,1,0:T(8,128)(2,1)S(1)} %get-tuple-element.65), channel_id=1, source_target_pairs={{0,192},{8,200},{16,208},{24,216},{32,224},{40,232},{48,240},{56,2... | collective-permute-start | bytes 491528 | tf_op jit(solution)/shard_map/ppermute | solution.py:333
  26.6 7.2 %collective-permute-start.5 = (bf16[2,224,128]{2,1,0:T(8,128)(2,1)S(1)}, bf16[2,224,128]{2,1,0:T(8,128)(2,1)S(1)}, u32[]{:S(2)}, u32[]{:S(2)}) collective-permute-start(bf16[2,224,128]{2,1,0:T(8,128)(2,1)S(1)} %stack_pair.1.own_ref), channel_id=1, source_target_pairs={{0,4},{1,5},{2,6},{3,7},{4,0},{5,1},{6,2},{7,3},{8,12},{9,13},{10,... | collective-permute-start | bytes 344072 | tf_op jit(solution)/shard_map/ppermute | solution.py:321
  28.4 5.4 %collective-permute-start.4 = (bf16[2,224,128]{2,1,0:T(8,128)(2,1)S(1)}, bf16[2,224,128]{2,1,0:T(8,128)(2,1)S(1)}, u32[]{:S(2)}, u32[]{:S(2)}) collective-permute-start(bf16[2,224,128]{2,1,0:T(8,128)(2,1)S(1)} %stack_pair.1.own_ref), channel_id=1, source_target_pairs={{0,2},{1,3},{2,0},{3,1},{4,6},{5,7},{6,4},{7,5},{8,10},{9,11},{10,... | collective-permute-start | bytes 344072 | tf_op jit(solution)/shard_map/ppermute | solution.py:321
  37.8 5.7 %collective-permute-start.11 = (bf16[2,224,128]{2,1,0:T(8,128)(2,1)S(1)}, bf16[2,224,128]{2,1,0:T(8,128)(2,1)S(1)}, u32[]{:S(2)}, u32[]{:S(2)}) collective-permute-start(bf16[2,224,128]{2,1,0:T(8,128)(2,1)S(1)} %get-tuple-element.68), channel_id=1, source_target_pairs={{0,2},{1,3},{2,0},{3,1},{4,6},{5,7},{6,4},{7,5},{8,10},{9,11},{10,... | collective-permute-start | bytes 344072 | tf_op jit(solution)/shard_map/ppermute | solution.py:321
  38.1 7.7 %collective-permute-start.12 = (bf16[2,224,128]{2,1,0:T(8,128)(2,1)S(1)}, bf16[2,224,128]{2,1,0:T(8,128)(2,1)S(1)}, u32[]{:S(2)}, u32[]{:S(2)}) collective-permute-start(bf16[2,224,128]{2,1,0:T(8,128)(2,1)S(1)} %get-tuple-element.69), channel_id=1, source_target_pairs={{0,4},{1,5},{2,6},{3,7},{4,0},{5,1},{6,2},{7,3},{8,12},{9,13},{10,... | collective-permute-start | bytes 344072 | tf_op jit(solution)/shard_map/ppermute | solution.py:321
  40.9 6.6 %collective-permute-start.13 = (bf16[2,224,128]{2,1,0:T(8,128)(2,1)S(1)}, bf16[2,224,128]{2,1,0:T(8,128)(2,1)S(1)}, u32[]{:S(2)}, u32[]{:S(2)}) collective-permute-start(bf16[2,224,128]{2,1,0:T(8,128)(2,1)S(1)} %get-tuple-element.70), channel_id=1, source_target_pairs={{0,6},{1,7},{2,4},{3,5},{4,2},{5,3},{6,0},{7,1},{8,14},{9,15},{10,... | collective-permute-start | bytes 344072 | tf_op jit(solution)/shard_map/ppermute | solution.py:321
  47.5 15.2 %copy-start.10 = (f32[1792]{0:T(1024)S(1)}, f32[1792]{0:T(1024)}, u32[]{:S(2)}) copy-start(f32[1792]{0:T(1024)} %param.29) | copy-start | bytes 21508
  47.5 19.2 %copy-start.1 = (bf16[1792,608]{0,1:T(8,128)(2,1)S(1)}, bf16[1792,608]{0,1:T(8,128)(2,1)}, u32[]{:S(2)}) copy-start(bf16[1792,608]{0,1:T(8,128)(2,1)} %param.36) | copy-start | bytes 6537220
  47.6 19.2 %copy-start.2 = (bf16[1792,608]{0,1:T(8,128)(2,1)S(1)}, bf16[1792,608]{0,1:T(8,128)(2,1)}, u32[]{:S(2)}) copy-start(bf16[1792,608]{0,1:T(8,128)(2,1)} %param.37) | copy-start | bytes 6537220
  47.6 10.9 %collective-permute-start.14 = (bf16[2,224,128]{2,1,0:T(8,128)(2,1)S(1)}, bf16[2,224,128]{2,1,0:T(8,128)(2,1)S(1)}, u32[]{:S(2)}, u32[]{:S(2)}) collective-permute-start(bf16[2,224,128]{2,1,0:T(8,128)(2,1)S(1)} %pad_maximum_fusion.1), channel_id=1, source_target_pairs={{0,1},{1,0},{2,3},{3,2},{4,5},{5,4},{6,7},{7,6},{8,9},{9,8},{10,11... | collective-permute-start | bytes 344072 | tf_op jit(solution)/shard_map/ppermute | solution.py:324
  58.6 6.1 %collective-permute-start.17 = (bf16[2,224,128]{2,1,0:T(8,128)(2,1)S(1)}, bf16[2,224,128]{2,1,0:T(8,128)(2,1)S(1)}, u32[]{:S(2)}, u32[]{:S(2)}) collective-permute-start(bf16[2,224,128]{2,1,0:T(8,128)(2,1)S(1)} %add_convert_fusion.own_ref), channel_id=1, source_target_pairs={{0,6},{1,7},{2,4},{3,5},{4,2},{5,3},{6,0},{7,1},{8,14},{9,15},{10,... | collective-permute-start | bytes 344072 | tf_op jit(solution)/shard_map/ppermute | solution.py:321
  60.4 6.3 %collective-permute-start.16 = (bf16[2,224,128]{2,1,0:T(8,128)(2,1)S(1)}, bf16[2,224,128]{2,1,0:T(8,128)(2,1)S(1)}, u32[]{:S(2)}, u32[]{:S(2)}) collective-permute-start(bf16[2,224,128]{2,1,0:T(8,128)(2,1)S(1)} %add_convert_fusion.own_ref), channel_id=1, source_target_pairs={{0,4},{1,5},{2,6},{3,7},{4,0},{5,1},{6,2},{7,3},{8,12},{9,13},{10,... | collective-permute-start | bytes 344072 | tf_op jit(solution)/shard_map/ppermute | solution.py:321
  60.4 6.3 %collective-permute-start.15 = (bf16[2,224,128]{2,1,0:T(8,128)(2,1)S(1)}, bf16[2,224,128]{2,1,0:T(8,128)(2,1)S(1)}, u32[]{:S(2)}, u32[]{:S(2)}) collective-permute-start(bf16[2,224,128]{2,1,0:T(8,128)(2,1)S(1)} %add_convert_fusion.own_ref), channel_id=1, source_target_pairs={{0,2},{1,3},{2,0},{3,1},{4,6},{5,7},{6,4},{7,5},{8,10},{9,11},{10,... | collective-permute-start | bytes 344072 | tf_op jit(solution)/shard_map/ppermute | solution.py:321
  69.0 4.9 %collective-permute-start.18 = (bf16[2,224,128]{2,1,0:T(8,128)(2,1)S(1)}, bf16[2,224,128]{2,1,0:T(8,128)(2,1)S(1)}, u32[]{:S(2)}, u32[]{:S(2)}) collective-permute-start(bf16[2,224,128]{2,1,0:T(8,128)(2,1)S(1)} %get-tuple-element.76), channel_id=1, source_target_pairs={{0,2},{1,3},{2,0},{3,1},{4,6},{5,7},{6,4},{7,5},{8,10},{9,11},{10,... | collective-permute-start | bytes 344072 | tf_op jit(solution)/shard_map/ppermute | solution.py:321
  69.9 6.4 %collective-permute-start.19 = (bf16[2,224,128]{2,1,0:T(8,128)(2,1)S(1)}, bf16[2,224,128]{2,1,0:T(8,128)(2,1)S(1)}, u32[]{:S(2)}, u32[]{:S(2)}) collective-permute-start(bf16[2,224,128]{2,1,0:T(8,128)(2,1)S(1)} %get-tuple-element.77), channel_id=1, source_target_pairs={{0,4},{1,5},{2,6},{3,7},{4,0},{5,1},{6,2},{7,3},{8,12},{9,13},{10,... | collective-permute-start | bytes 344072 | tf_op jit(solution)/shard_map/ppermute | solution.py:321
  72.3 6.0 %collective-permute-start.20 = (bf16[2,224,128]{2,1,0:T(8,128)(2,1)S(1)}, bf16[2,224,128]{2,1,0:T(8,128)(2,1)S(1)}, u32[]{:S(2)}, u32[]{:S(2)}) collective-permute-start(bf16[2,224,128]{2,1,0:T(8,128)(2,1)S(1)} %get-tuple-element.78), channel_id=1, source_target_pairs={{0,6},{1,7},{2,4},{3,5},{4,2},{5,3},{6,0},{7,1},{8,14},{9,15},{10,... | collective-permute-start | bytes 344072 | tf_op jit(solution)/shard_map/ppermute | solution.py:321
  78.3 8.5 %collective-permute-start.21 = (bf16[224,128]{1,0:T(8,128)(2,1)S(1)}, bf16[224,128]{1,0:T(8,128)(2,1)S(1)}, u32[]{:S(2)}, u32[]{:S(2)}) collective-permute-start(bf16[224,128]{1,0:T(8,128)(2,1)S(1)} %fusion.4), channel_id=1, source_target_pairs={{0,1},{1,0},{2,3},{3,2},{4,5},{5,4},{6,7},{7,6},{8,9},{9,8},{10,11... | collective-permute-start | bytes 172040 | tf_op jit(solution)/shard_map/ppermute | solution.py:324
  (1 other events, 15.1 us)

commit v7 on v6

--- a/solution.py
+++ b/solution.py
@@ -184,7 +184,7 @@
 
 
 def local_kernel(
-    total_req, own_ref, r1_ref, r2_ref, r3_ref, gain_ref, token_ref, query_ref, key_ref, value_ref, gate_ref,
+    total_req, own_ref, r1_ref, r3_ref, r2_ref, gain_ref, token_ref, query_ref, key_ref, value_ref, gate_ref,
     taps_ref, conv_ref, silu_ref, scores_ref, den_ref, right_ref, turned_ref, scratch,
 ):
     place_blocks(scratch, [own_ref, r1_ref, r2_ref, r3_ref])
@@ -332,7 +332,7 @@
     def along_y(array, k):
         return lax.ppermute(array, "req", [(i, i ^ (2 * z_size * k)) for i in range(req_size)])
 
-    order = (1, 3, 2)
+    order = (2, 1, 3)
 
     fold = jnp.asarray(fold_matrix(feat_dim, feats), BF16)
     def in_hbm(array):
@@ -406,7 +406,7 @@
         ],
         [VMEM] * 11,
         (
-            pair, rows[1], rows[2], rows[3], mixer_rows, token_req.reshape(1, tokens),
+            pair, rows[1], rows[3], rows[2], mixer_rows, token_req.reshape(1, tokens),
             query_weight.T, key_weight.T, value_weight.T, conv_gate_weight.T, conv_kernel,
         ),
         scratch=[pltpu.VMEM((model, tokens), BF16)],
@@ -416,12 +416,12 @@
         mix_kernel,
         [sds((2, width, tokens), F32)] + [sds((2, width, tokens), BF16)] * 3,
         [VMEM] * 11,
-        (*local, kept, from_y[1], from_y[2], from_y[3], out_turned),
+        (*local, kept, from_y[2], from_y[1], from_y[3], out_turned),
         scratch=[pltpu.VMEM((width, tokens), BF16)],
         name="mix",
     )
     got = {k: along_x(parts[k], k) for k in order}
-    share = parts[0] + got[1].astype(F32) + got[2].astype(F32) + got[3].astype(F32)
+    share = parts[0] + got[2].astype(F32) + got[1].astype(F32) + got[3].astype(F32)
     crossing, down_in = lax.optimization_barrier((jnp.stack([share[1], share[0]]).astype(BF16), ffn_down))
     share_peer = across_z(crossing)
     updated = (held_pair.astype(F32) + share + share_peer.astype(F32)).astype(BF16)
@@ -438,7 +438,7 @@
         name="ffn",
     )
     back = {k: along_x(downs[k], k) for k in order}
-    down_share = downs[0] + back[1].astype(F32) + back[2].astype(F32) + back[3].astype(F32)
+    down_share = downs[0] + back[2].astype(F32) + back[1].astype(F32) + back[3].astype(F32)
     down_peer = across_z(down_share[1].astype(BF16))
     result = updated[0].astype(F32) + down_share[0] + down_peer.astype(F32)
     return result.astype(BF16).T

time: 87.6 us -> 83.5 us (0.953)
  the two profiles are of different devices: /device:TPU:32 before, /device:TPU:8 now
where the time goes in v7:
time: 83.5 us; the launch traced here: 82.8 us
  starting transfers between devices  39.9 us (48%)
  waiting for transfers between devices  30.3 us (36%)
  Pallas kernels  11.3 us (14%)
  other arithmetic  0.91 us (1%)
    ppermute x12, waiting for transfers between devices, along_x(): return lax.ppermute(array, 'tp', [(i, i ^ 2 * k) for i in range(tp_size)])  17.7 us
    ppermute x12, starting transfers between devices, along_x(): return lax.ppermute(array, 'tp', [(i, i ^ 2 * k) for i in range(tp_size)])  17.1 us
    ppermute x3, starting transfers between devices, across_z(): return lax.ppermute(array, 'tp', [(i, i ^ 1) for i in range(tp_size)])  13.2 us
    ppermute x3, waiting for transfers between devices, across_z(): return lax.ppermute(array, 'tp', [(i, i ^ 1) for i in range(tp_size)])  12.6 us
    pallas_call x7, Pallas kernels, call(): pl.pallas_call(kernel, out_shape=out_shape, in_specs=specs, out_specs=VME...  7.21 us
    ppermute x3, starting transfers between devices, along_z(): return lax.ppermute(array, 'req', [(i, i ^ 2 * k) for i in range(req_size)])  5.37 us
    ppermute x3, starting transfers between devices, along_y(): lax.ppermute(array, 'req', [(i, i ^ 2 * z_size * k) for i in range(req_si...  4.18 us
    pallas_call x1, Pallas kernels, shards(): pl.pallas_call(functools.partial(turn_and_slots_kernel, y_size, z_size),...  2.35 us
  transfers between devices with their start and end apart: 22, of which 12 were waited for; matrix products, arithmetic and copies ran while one was open for 0% of the time, Pallas kernels for 8%

profile of v7, /device:TPU:8, one launch (start us, length us, event | category | flops | bytes accessed | tf_op | source)
XLA Modules:
  0.0 82.8 jit_solution(7100565130345199165)
XLA Ops:
  0.0 1.7 %fold.1 = (bf16[2,160,128]{2,1,0:T(8,128)(2,1)S(1)}, bf16[224,128]{1,0:T(8,128)(2,1)S(1)}) custom-call(bf16[160,273]{1,0:T(8,128)(2,1)} %constant.5.clone.fold_hbm, bf16[273,2,112]{2,1,0:T(2,128)(2,1)} %bitcast.39, bf16[2,273]{1,0:T(2,128)(2,1)} %bitcast.47, bf16[2,224]{1,0:T(2,128)(2,1)} %bitcast.48, bf16[224,128]{1,0:T(8,128)(2,1)} %bitcast.43), custom_call_target="tpu_custom_call" | custom-call | tf_op jit(solution)/shard_map/fold/pallas_call | solution.py:345
  1.8 4.7 %collective-permute-start.3 = (bf16[2,160,128]{2,1,0:T(8,128)(2,1)S(1)}, bf16[2,160,128]{2,1,0:T(8,128)(2,1)S(1)}, u32[]{:S(2)}, u32[]{:S(2)}) collective-permute-start(bf16[2,160,128]{2,1,0:T(8,128)(2,1)S(1)} %get-tuple-element.44), channel_id=1, source_target_pairs={{0,48},{8,56},{16,32},{24,40},{32,16},{40,24},{48,0},{56,8},{64,11... | collective-permute-start | bytes 245768 | tf_op jit(solution)/shard_map/ppermute | solution.py:327
  7.2 6.3 %collective-permute-start = (bf16[224,128]{1,0:T(8,128)(2,1)}, bf16[224,128]{1,0:T(8,128)(2,1)S(1)}, u32[]{:S(2)}, u32[]{:S(2)}) collective-permute-start(bf16[224,128]{1,0:T(8,128)(2,1)} %bitcast.44), channel_id=1, source_target_pairs={{0,1},{1,0},{2,3},{3,2},{4,5},{5,4},{6,7},{7,6},{8,9},{9,8},{10,11... | collective-permute-start | bytes 172040 | tf_op jit(solution)/shard_map/ppermute | solution.py:324
  13.5 2.4 %turn_out.1 = (bf16[1792,224]{1,0:T(8,128)(2,1)S(1)}, s32[24]{0:T(128)S(1)}) custom-call(bf16[224,1792]{1,0:T(8,128)(2,1)} %in_hbm.1, s32[64]{0:T(128)} %leaf_hbm.1, s32[32]{0:T(128)} %parent_hbm.1, s32[32]{0:T(128)} %owner_hbm.1), custom_call_target="tpu_custom_call" | custom-call | tf_op jit(solution)/shard_map/turn_out/pallas_call | solution.py:355
  15.8 2.9 %collective-permute-done.second_ref = bf16[224,128]{1,0:T(8,128)(2,1)S(1)} collective-permute-done((bf16[224,128]{1,0:T(8,128)(2,1)}, bf16[224,128]{1,0:T(8,128)(2,1)S(1)}, u32[]{:S(2)}, u32[]{:S(2)}) %collective-permute-start) | collective-permute-done | bytes 57376 | tf_op jit(solution)/shard_map/ppermute | solution.py:324
  18.9 3.1 %collective-permute-start.6 = (bf16[2,224,128]{2,1,0:T(8,128)(2,1)S(1)}, bf16[2,224,128]{2,1,0:T(8,128)(2,1)S(1)}, u32[]{:S(2)}, u32[]{:S(2)}) collective-permute-start(bf16[2,224,128]{2,1,0:T(8,128)(2,1)S(1)} %stack_pair.1.own_ref), channel_id=1, source_target_pairs={{0,4},{1,5},{2,6},{3,7},{4,0},{5,1},{6,2},{7,3},{8,12},{9,13},{10,... | collective-permute-start | bytes 344072 | tf_op jit(solution)/shard_map/ppermute | solution.py:321
  22.0 1.0 %select_sent.1 = (bf16[2,2,160,128]{3,2,1,0:T(8,128)(2,1)S(1)}, bf16[2,2,160,128]{3,2,1,0:T(8,128)(2,1)S(1)}, bf16[2,2,160,128]{3,2,1,0:T(8,128)(2,1)S(1)}) custom-call(s32[24]{0:T(128)S(1)} %get-tuple-element.46.slot_ref, bf16[4,2,160,128]{3,2,1,0:T(8,128)(2,1)S(1)} %pad_maximum_fusion.mine_ref, bf16[4,2,160,128]{3,2,1,0:T(8,128)(2,1)S(1)} %collective-permute-done.7.other_ref), custom_call_target="tpu_custom_call" | custom-call | tf_op jit(solution)/shard_map/select_sent/pallas_call | solution.py:25
  23.0 2.4 %collective-permute-start.8 = (bf16[2,2,160,128]{3,2,1,0:T(8,128)(2,1)S(1)}, bf16[2,2,160,128]{3,2,1,0:T(8,128)(2,1)S(1)}, u32[]{:S(2)}, u32[]{:S(2)}) collective-permute-start(bf16[2,2,160,128]{3,2,1,0:T(8,128)(2,1)S(1)} %get-tuple-element.63), channel_id=1, source_target_pairs={{0,128},{8,136},{16,144},{24,152},{32,160},{40,168},{48,176},{56,1... | collective-permute-start | bytes 491528 | tf_op jit(solution)/shard_map/ppermute | solution.py:333
  25.4 1.3 %collective-permute-start.9 = (bf16[2,2,160,128]{3,2,1,0:T(8,128)(2,1)S(1)}, bf16[2,2,160,128]{3,2,1,0:T(8,128)(2,1)S(1)}, u32[]{:S(2)}, u32[]{:S(2)}) collective-permute-start(bf16[2,2,160,128]{3,2,1,0:T(8,128)(2,1)S(1)} %get-tuple-element.64), channel_id=1, source_target_pairs={{0,64},{8,72},{16,80},{24,88},{32,96},{40,104},{48,112},{56,120},{... | collective-permute-start | bytes 491528 | tf_op jit(solution)/shard_map/ppermute | solution.py:333
  27.2 1.3 %collective-permute-start.5 = (bf16[2,224,128]{2,1,0:T(8,128)(2,1)S(1)}, bf16[2,224,128]{2,1,0:T(8,128)(2,1)S(1)}, u32[]{:S(2)}, u32[]{:S(2)}) collective-permute-start(bf16[2,224,128]{2,1,0:T(8,128)(2,1)S(1)} %stack_pair.1.own_ref), channel_id=1, source_target_pairs={{0,6},{1,7},{2,4},{3,5},{4,2},{5,3},{6,0},{7,1},{8,14},{9,15},{10,... | collective-permute-start | bytes 344072 | tf_op jit(solution)/shard_map/ppermute | solution.py:321
  28.7 0.8 select_kept.1.p0_ref
  29.4 3.7 %collective-permute-done.5.r3_ref = bf16[2,224,128]{2,1,0:T(8,128)(2,1)S(1)} collective-permute-done((bf16[2,224,128]{2,1,0:T(8,128)(2,1)S(1)}, bf16[2,224,128]{2,1,0:T(8,128)(2,1)S(1)}, u32[]{:S(2)}, u32[]{:S(2)}) %collective-permute-start.5) | collective-permute-done | bytes 114720 | tf_op jit(solution)/shard_map/ppermute | solution.py:321
  33.3 1.5 %local.1 = (f32[224,128]{1,0:T(8,128)S(1)}, f32[224,128]{1,0:T(8,128)S(1)}, bf16[2,128,128]{2,1,0:T(8,128)(2,1)S(1)}, f32[2,1,128]{2,1,0:T(1,128)S(1)}, bf16[2,3...) custom-call(bf16[2,224,128]{2,1,0:T(8,128)(2,1)S(1)} %stack_pair.1.own_ref, ...), custom_call_target="tpu_custom_call" | custom-call | tf_op jit(solution)/shard_map/local/pallas_call | solution.py:25
  34.8 1.1 %mix.1 = (f32[2,224,128]{2,1,0:T(8,128)S(1)}, bf16[2,224,128]{2,1,0:T(8,128)(2,1)S(1)}, bf16[2,224,128]{2,1,0:T(8,128)(2,1)S(1)}, bf16[2,224,128]{2,1,0:T(8,128)(2,1)S(1)}) custom-call(f32[224,128]{1,0:T(8,128)S(1)} %get-tuple-element.56.conv_ref, f32[224,128]{1,0:T(8,128)S(1)} %get-tuple-element.57.silu_ref, ...), custom_call_target="tpu_custom_call" | custom-call | tf_op jit(solution)/shard_map/mix/pallas_call | solution.py:25
  35.9 1.5 %collective-permute-start.11 = (bf16[2,224,128]{2,1,0:T(8,128)(2,1)S(1)}, bf16[2,224,128]{2,1,0:T(8,128)(2,1)S(1)}, u32[]{:S(2)}, u32[]{:S(2)}) collective-permute-start(bf16[2,224,128]{2,1,0:T(8,128)(2,1)S(1)} %get-tuple-element.68), channel_id=1, source_target_pairs={{0,4},{1,5},{2,6},{3,7},{4,0},{5,1},{6,2},{7,3},{8,12},{9,13},{10,... | collective-permute-start | bytes 344072 | tf_op jit(solution)/shard_map/ppermute | solution.py:321
  37.4 1.4 %collective-permute-start.12 = (bf16[2,224,128]{2,1,0:T(8,128)(2,1)S(1)}, bf16[2,224,128]{2,1,0:T(8,128)(2,1)S(1)}, u32[]{:S(2)}, u32[]{:S(2)}) collective-permute-start(bf16[2,224,128]{2,1,0:T(8,128)(2,1)S(1)} %get-tuple-element.69), channel_id=1, source_target_pairs={{0,2},{1,3},{2,0},{3,1},{4,6},{5,7},{6,4},{7,5},{8,10},{9,11},{10,... | collective-permute-start | bytes 344072 | tf_op jit(solution)/shard_map/ppermute | solution.py:321
  38.8 1.3 %collective-permute-start.13 = (bf16[2,224,128]{2,1,0:T(8,128)(2,1)S(1)}, bf16[2,224,128]{2,1,0:T(8,128)(2,1)S(1)}, u32[]{:S(2)}, u32[]{:S(2)}) collective-permute-start(bf16[2,224,128]{2,1,0:T(8,128)(2,1)S(1)} %get-tuple-element.70), channel_id=1, source_target_pairs={{0,6},{1,7},{2,4},{3,5},{4,2},{5,3},{6,0},{7,1},{8,14},{9,15},{10,... | collective-permute-start | bytes 344072 | tf_op jit(solution)/shard_map/ppermute | solution.py:321
  40.1 3.2 %collective-permute-done.11 = bf16[2,224,128]{2,1,0:T(8,128)(2,1)S(1)} collective-permute-done((bf16[2,224,128]{2,1,0:T(8,128)(2,1)S(1)}, bf16[2,224,128]{2,1,0:T(8,128)(2,1)S(1)}, u32[]{:S(2)}, u32[]{:S(2)}) %collective-permute-start.11) | collective-permute-done | bytes 114720 | tf_op jit(solution)/shard_map/ppermute | solution.py:321
  43.3 1.5 %collective-permute-done.13 = bf16[2,224,128]{2,1,0:T(8,128)(2,1)S(1)} collective-permute-done((bf16[2,224,128]{2,1,0:T(8,128)(2,1)S(1)}, bf16[2,224,128]{2,1,0:T(8,128)(2,1)S(1)}, u32[]{:S(2)}, u32[]{:S(2)}) %collective-permute-start.13) | collective-permute-done | bytes 114720 | tf_op jit(solution)/shard_map/ppermute | solution.py:321
  45.0 3.5 %collective-permute-start.14 = (bf16[2,224,128]{2,1,0:T(8,128)(2,1)S(1)}, bf16[2,224,128]{2,1,0:T(8,128)(2,1)S(1)}, u32[]{:S(2)}, u32[]{:S(2)}) collective-permute-start(bf16[2,224,128]{2,1,0:T(8,128)(2,1)S(1)} %pad_maximum_fusion.1), channel_id=1, source_target_pairs={{0,1},{1,0},{2,3},{3,2},{4,5},{5,4},{6,7},{7,6},{8,9},{9,8},{10,11... | collective-permute-start | bytes 344072 | tf_op jit(solution)/shard_map/ppermute | solution.py:324
  49.1 4.9 %collective-permute-done.14 = bf16[2,224,128]{2,1,0:T(8,128)(2,1)S(1)} collective-permute-done((bf16[2,224,128]{2,1,0:T(8,128)(2,1)S(1)}, bf16[2,224,128]{2,1,0:T(8,128)(2,1)S(1)}, u32[]{:S(2)}, u32[]{:S(2)}) %collective-permute-start.14) | collective-permute-done | bytes 114720 | tf_op jit(solution)/shard_map/ppermute | solution.py:324
  54.1 2.5 %collective-permute-start.17 = (bf16[2,224,128]{2,1,0:T(8,128)(2,1)S(1)}, bf16[2,224,128]{2,1,0:T(8,128)(2,1)S(1)}, u32[]{:S(2)}, u32[]{:S(2)}) collective-permute-start(bf16[2,224,128]{2,1,0:T(8,128)(2,1)S(1)} %add_convert_fusion.own_ref), channel_id=1, source_target_pairs={{0,6},{1,7},{2,4},{3,5},{4,2},{5,3},{6,0},{7,1},{8,14},{9,15},{10,... | collective-permute-start | bytes 344072 | tf_op jit(solution)/shard_map/ppermute | solution.py:321
  57.4 0.9 %collective-permute-start.15 = (bf16[2,224,128]{2,1,0:T(8,128)(2,1)S(1)}, bf16[2,224,128]{2,1,0:T(8,128)(2,1)S(1)}, u32[]{:S(2)}, u32[]{:S(2)}) collective-permute-start(bf16[2,224,128]{2,1,0:T(8,128)(2,1)S(1)} %add_convert_fusion.own_ref), channel_id=1, source_target_pairs={{0,2},{1,3},{2,0},{3,1},{4,6},{5,7},{6,4},{7,5},{8,10},{9,11},{10,... | collective-permute-start | bytes 344072 | tf_op jit(solution)/shard_map/ppermute | solution.py:321
  58.3 1.9 %collective-permute-done.17.r3_ref = bf16[2,224,128]{2,1,0:T(8,128)(2,1)S(1)} collective-permute-done((bf16[2,224,128]{2,1,0:T(8,128)(2,1)S(1)}, bf16[2,224,128]{2,1,0:T(8,128)(2,1)S(1)}, u32[]{:S(2)}, u32[]{:S(2)}) %collective-permute-start.17) | collective-permute-done | bytes 114720 | tf_op jit(solution)/shard_map/ppermute | solution.py:321
  60.2 2.7 %collective-permute-done.16.r2_ref = bf16[2,224,128]{2,1,0:T(8,128)(2,1)S(1)} collective-permute-done((bf16[2,224,128]{2,1,0:T(8,128)(2,1)S(1)}, bf16[2,224,128]{2,1,0:T(8,128)(2,1)S(1)}, u32[]{:S(2)}, u32[]{:S(2)}) %collective-permute-start.16) | collective-permute-done | bytes 114720 | tf_op jit(solution)/shard_map/ppermute | solution.py:321
  63.0 2.2 %ffn.1 = (f32[2,224,128]{2,1,0:T(8,128)S(1)}, bf16[2,224,128]{2,1,0:T(8,128)(2,1)S(1)}, bf16[2,224,128]{2,1,0:T(8,128)(2,1)S(1)}, bf16[2,224,128]{2,1,0:T(8,128)(2,1)S(1)}) custom-call(bf16[2,224,128]{2,1,0:T(8,128)(2,1)S(1)} %add_convert_fusion.own_ref, bf16[2,224,128]{2,1,0:T(8,128)(2,1)S(1)} %collective-permute-done.15.r1_ref, ...), custom_call_target="tpu_custom_call" | custom-call | tf_op jit(solution)/shard_map/ffn/pallas_call | solution.py:25
  65.2 2.1 %collective-permute-start.18 = (bf16[2,224,128]{2,1,0:T(8,128)(2,1)S(1)}, bf16[2,224,128]{2,1,0:T(8,128)(2,1)S(1)}, u32[]{:S(2)}, u32[]{:S(2)}) collective-permute-start(bf16[2,224,128]{2,1,0:T(8,128)(2,1)S(1)} %get-tuple-element.76), channel_id=1, source_target_pairs={{0,4},{1,5},{2,6},{3,7},{4,0},{5,1},{6,2},{7,3},{8,12},{9,13},{10,... | collective-permute-start | bytes 344072 | tf_op jit(solution)/shard_map/ppermute | solution.py:321
  67.9 1.4 %collective-permute-start.20 = (bf16[2,224,128]{2,1,0:T(8,128)(2,1)S(1)}, bf16[2,224,128]{2,1,0:T(8,128)(2,1)S(1)}, u32[]{:S(2)}, u32[]{:S(2)}) collective-permute-start(bf16[2,224,128]{2,1,0:T(8,128)(2,1)S(1)} %get-tuple-element.78), channel_id=1, source_target_pairs={{0,6},{1,7},{2,4},{3,5},{4,2},{5,3},{6,0},{7,1},{8,14},{9,15},{10,... | collective-permute-start | bytes 344072 | tf_op jit(solution)/shard_map/ppermute | solution.py:321
  69.4 2.2 %collective-permute-done.18 = bf16[2,224,128]{2,1,0:T(8,128)(2,1)S(1)} collective-permute-done((bf16[2,224,128]{2,1,0:T(8,128)(2,1)S(1)}, bf16[2,224,128]{2,1,0:T(8,128)(2,1)S(1)}, u32[]{:S(2)}, u32[]{:S(2)}) %collective-permute-start.18) | collective-permute-done | bytes 114720 | tf_op jit(solution)/shard_map/ppermute | solution.py:321
  72.1 1.8 %collective-permute-done.20 = bf16[2,224,128]{2,1,0:T(8,128)(2,1)S(1)} collective-permute-done((bf16[2,224,128]{2,1,0:T(8,128)(2,1)S(1)}, bf16[2,224,128]{2,1,0:T(8,128)(2,1)S(1)}, u32[]{:S(2)}, u32[]{:S(2)}) %collective-permute-start.20) | collective-permute-done | bytes 114720 | tf_op jit(solution)/shard_map/ppermute | solution.py:321
  74.0 3.4 %collective-permute-start.21 = (bf16[224,128]{1,0:T(8,128)(2,1)S(1)}, bf16[224,128]{1,0:T(8,128)(2,1)S(1)}, u32[]{:S(2)}, u32[]{:S(2)}) collective-permute-start(bf16[224,128]{1,0:T(8,128)(2,1)S(1)} %fusion.4), channel_id=1, source_target_pairs={{0,1},{1,0},{2,3},{3,2},{4,5},{5,4},{6,7},{7,6},{8,9},{9,8},{10,11... | collective-permute-start | bytes 172040 | tf_op jit(solution)/shard_map/ppermute | solution.py:324
  77.4 4.8 %collective-permute-done.21 = bf16[224,128]{1,0:T(8,128)(2,1)S(1)} collective-permute-done((bf16[224,128]{1,0:T(8,128)(2,1)S(1)}, bf16[224,128]{1,0:T(8,128)(2,1)S(1)}, u32[]{:S(2)}, u32[]{:S(2)}) %collective-permute-start.21) | collective-permute-done | bytes 57376 | tf_op jit(solution)/shard_map/ppermute | solution.py:324
  (53 shorter events, 5.0 us)
Async XLA Ops:
  0.0 28.7 %copy-start.9 = (f32[1792]{0:T(1024)S(1)}, f32[1792]{0:T(1024)}, u32[]{:S(2)}) copy-start(f32[1792]{0:T(1024)} %param.28) | copy-start | bytes 21508
  0.0 33.2 %copy-start.7 = (f32[3,224]{1,0:T(4,128)S(1)}, f32[3,224]{1,0:T(4,128)}, u32[]{:S(2)}) copy-start(f32[3,224]{1,0:T(4,128)} %taps_ref.1) | copy-start | bytes 8068
  0.0 33.2 %copy-start.4 = (bf16[1792,224]{0,1:T(8,128)(2,1)S(1)}, bf16[1792,224]{0,1:T(8,128)(2,1)}, u32[]{:S(2)}) copy-start(bf16[1792,224]{0,1:T(8,128)(2,1)} %param.33) | copy-start | bytes 2408452
  0.0 33.2 %copy-start.3 = (bf16[1792,224]{0,1:T(8,128)(2,1)S(1)}, bf16[1792,224]{0,1:T(8,128)(2,1)}, u32[]{:S(2)}) copy-start(bf16[1792,224]{0,1:T(8,128)(2,1)} %param.32) | copy-start | bytes 2408452
  0.0 33.2 %copy-start.6 = (bf16[1792,32]{0,1:T(8,128)(2,1)S(1)}, bf16[1792,32]{0,1:T(8,128)(2,1)}, u32[]{:S(2)}) copy-start(bf16[1792,32]{0,1:T(8,128)(2,1)} %param.31) | copy-start | bytes 344068
  0.0 33.2 %copy-start.5 = (bf16[1792,32]{0,1:T(8,128)(2,1)S(1)}, bf16[1792,32]{0,1:T(8,128)(2,1)}, u32[]{:S(2)}) copy-start(bf16[1792,32]{0,1:T(8,128)(2,1)} %param.30) | copy-start | bytes 344068
  0.0 33.2 %copy-start.8 = (s32[128]{0:T(128)S(1)}, s32[128]{0:T(128)}, u32[]{:S(2)}) copy-start(s32[128]{0:T(128)} %param.21) | copy-start | bytes 1540
  1.8 16.9 %collective-permute-start.3 = (bf16[2,160,128]{2,1,0:T(8,128)(2,1)S(1)}, bf16[2,160,128]{2,1,0:T(8,128)(2,1)S(1)}, u32[]{:S(2)}, u32[]{:S(2)}) collective-permute-start(bf16[2,160,128]{2,1,0:T(8,128)(2,1)S(1)} %get-tuple-element.44), channel_id=1, source_target_pairs={{0,48},{8,56},{16,32},{24,40},{32,16},{40,24},{48,0},{56,8},{64,11... | collective-permute-start | bytes 245768 | tf_op jit(solution)/shard_map/ppermute | solution.py:327
  6.5 12.2 %collective-permute-start.2 = (bf16[2,160,128]{2,1,0:T(8,128)(2,1)S(1)}, bf16[2,160,128]{2,1,0:T(8,128)(2,1)S(1)}, u32[]{:S(2)}, u32[]{:S(2)}) collective-permute-start(bf16[2,160,128]{2,1,0:T(8,128)(2,1)S(1)} %get-tuple-element.44), channel_id=1, source_target_pairs={{0,32},{8,40},{16,48},{24,56},{32,0},{40,8},{48,16},{56,24},{64,96... | collective-permute-start | bytes 245768 | tf_op jit(solution)/shard_map/ppermute | solution.py:327
  6.5 12.2 %collective-permute-start.1 = (bf16[2,160,128]{2,1,0:T(8,128)(2,1)S(1)}, bf16[2,160,128]{2,1,0:T(8,128)(2,1)S(1)}, u32[]{:S(2)}, u32[]{:S(2)}) collective-permute-start(bf16[2,160,128]{2,1,0:T(8,128)(2,1)S(1)} %get-tuple-element.44), channel_id=1, source_target_pairs={{0,16},{8,24},{16,0},{24,8},{32,48},{40,56},{48,32},{56,40},{64,80... | collective-permute-start | bytes 245768 | tf_op jit(solution)/shard_map/ppermute | solution.py:327
  7.2 11.5 %collective-permute-start = (bf16[224,128]{1,0:T(8,128)(2,1)}, bf16[224,128]{1,0:T(8,128)(2,1)S(1)}, u32[]{:S(2)}, u32[]{:S(2)}) collective-permute-start(bf16[224,128]{1,0:T(8,128)(2,1)} %bitcast.44), channel_id=1, source_target_pairs={{0,1},{1,0},{2,3},{3,2},{4,5},{5,4},{6,7},{7,6},{8,9},{9,8},{10,11... | collective-permute-start | bytes 172040 | tf_op jit(solution)/shard_map/ppermute | solution.py:324
  18.8 3.2 %collective-permute-start.7 = (bf16[4,2,160,128]{3,2,1,0:T(8,128)(2,1)S(1)}, bf16[4,2,160,128]{3,2,1,0:T(8,128)(2,1)S(1)}, u32[]{:S(2)}, u32[]{:S(2)}) collective-permute-start(bf16[4,2,160,128]{3,2,1,0:T(8,128)(2,1)S(1)} %pad_maximum_fusion.mine_ref), channel_id=1, source_target_pairs={{0,8},{8,0},{16,24},{24,16},{32,40},{40,32},{48,56},{56,48},{64,72... | collective-permute-start | bytes 983048 | tf_op jit(solution)/shard_map/ppermute | solution.py:330
  18.9 9.5 %collective-permute-start.6 = (bf16[2,224,128]{2,1,0:T(8,128)(2,1)S(1)}, bf16[2,224,128]{2,1,0:T(8,128)(2,1)S(1)}, u32[]{:S(2)}, u32[]{:S(2)}) collective-permute-start(bf16[2,224,128]{2,1,0:T(8,128)(2,1)S(1)} %stack_pair.1.own_ref), channel_id=1, source_target_pairs={{0,4},{1,5},{2,6},{3,7},{4,0},{5,1},{6,2},{7,3},{8,12},{9,13},{10,... | collective-permute-start | bytes 344072 | tf_op jit(solution)/shard_map/ppermute | solution.py:321
  23.0 11.8 %collective-permute-start.8 = (bf16[2,2,160,128]{3,2,1,0:T(8,128)(2,1)S(1)}, bf16[2,2,160,128]{3,2,1,0:T(8,128)(2,1)S(1)}, u32[]{:S(2)}, u32[]{:S(2)}) collective-permute-start(bf16[2,2,160,128]{3,2,1,0:T(8,128)(2,1)S(1)} %get-tuple-element.63), channel_id=1, source_target_pairs={{0,128},{8,136},{16,144},{24,152},{32,160},{40,168},{48,176},{56,1... | collective-permute-start | bytes 491528 | tf_op jit(solution)/shard_map/ppermute | solution.py:333
  25.4 9.5 %collective-permute-start.9 = (bf16[2,2,160,128]{3,2,1,0:T(8,128)(2,1)S(1)}, bf16[2,2,160,128]{3,2,1,0:T(8,128)(2,1)S(1)}, u32[]{:S(2)}, u32[]{:S(2)}) collective-permute-start(bf16[2,2,160,128]{3,2,1,0:T(8,128)(2,1)S(1)} %get-tuple-element.64), channel_id=1, source_target_pairs={{0,64},{8,72},{16,80},{24,88},{32,96},{40,104},{48,112},{56,120},{... | collective-permute-start | bytes 491528 | tf_op jit(solution)/shard_map/ppermute | solution.py:333
  26.7 8.1 %collective-permute-start.10 = (bf16[2,2,160,128]{3,2,1,0:T(8,128)(2,1)S(1)}, bf16[2,2,160,128]{3,2,1,0:T(8,128)(2,1)S(1)}, u32[]{:S(2)}, u32[]{:S(2)}) collective-permute-start(bf16[2,2,160,128]{3,2,1,0:T(8,128)(2,1)S(1)} %get-tuple-element.65), channel_id=1, source_target_pairs={{0,192},{8,200},{16,208},{24,216},{32,224},{40,232},{48,240},{56,2... | collective-permute-start | bytes 491528 | tf_op jit(solution)/shard_map/ppermute | solution.py:333
  27.2 6.0 %collective-permute-start.5 = (bf16[2,224,128]{2,1,0:T(8,128)(2,1)S(1)}, bf16[2,224,128]{2,1,0:T(8,128)(2,1)S(1)}, u32[]{:S(2)}, u32[]{:S(2)}) collective-permute-start(bf16[2,224,128]{2,1,0:T(8,128)(2,1)S(1)} %stack_pair.1.own_ref), channel_id=1, source_target_pairs={{0,6},{1,7},{2,4},{3,5},{4,2},{5,3},{6,0},{7,1},{8,14},{9,15},{10,... | collective-permute-start | bytes 344072 | tf_op jit(solution)/shard_map/ppermute | solution.py:321
  28.4 4.8 %collective-permute-start.4 = (bf16[2,224,128]{2,1,0:T(8,128)(2,1)S(1)}, bf16[2,224,128]{2,1,0:T(8,128)(2,1)S(1)}, u32[]{:S(2)}, u32[]{:S(2)}) collective-permute-start(bf16[2,224,128]{2,1,0:T(8,128)(2,1)S(1)} %stack_pair.1.own_ref), channel_id=1, source_target_pairs={{0,2},{1,3},{2,0},{3,1},{4,6},{5,7},{6,4},{7,5},{8,10},{9,11},{10,... | collective-permute-start | bytes 344072 | tf_op jit(solution)/shard_map/ppermute | solution.py:321
  34.8 13.6 %copy-start = (bf16[608,1792]{1,0:T(8,128)(2,1)S(1)}, bf16[608,1792]{1,0:T(8,128)(2,1)}, u32[]{:S(2)}) copy-start(bf16[608,1792]{1,0:T(8,128)(2,1)} %in_ref) | copy-start | bytes 6537220
  35.9 7.4 %collective-permute-start.11 = (bf16[2,224,128]{2,1,0:T(8,128)(2,1)S(1)}, bf16[2,224,128]{2,1,0:T(8,128)(2,1)S(1)}, u32[]{:S(2)}, u32[]{:S(2)}) collective-permute-start(bf16[2,224,128]{2,1,0:T(8,128)(2,1)S(1)} %get-tuple-element.68), channel_id=1, source_target_pairs={{0,4},{1,5},{2,6},{3,7},{4,0},{5,1},{6,2},{7,3},{8,12},{9,13},{10,... | collective-permute-start | bytes 344072 | tf_op jit(solution)/shard_map/ppermute | solution.py:321
  37.4 5.9 %collective-permute-start.12 = (bf16[2,224,128]{2,1,0:T(8,128)(2,1)S(1)}, bf16[2,224,128]{2,1,0:T(8,128)(2,1)S(1)}, u32[]{:S(2)}, u32[]{:S(2)}) collective-permute-start(bf16[2,224,128]{2,1,0:T(8,128)(2,1)S(1)} %get-tuple-element.69), channel_id=1, source_target_pairs={{0,2},{1,3},{2,0},{3,1},{4,6},{5,7},{6,4},{7,5},{8,10},{9,11},{10,... | collective-permute-start | bytes 344072 | tf_op jit(solution)/shard_map/ppermute | solution.py:321
  38.8 6.0 %collective-permute-start.13 = (bf16[2,224,128]{2,1,0:T(8,128)(2,1)S(1)}, bf16[2,224,128]{2,1,0:T(8,128)(2,1)S(1)}, u32[]{:S(2)}, u32[]{:S(2)}) collective-permute-start(bf16[2,224,128]{2,1,0:T(8,128)(2,1)S(1)} %get-tuple-element.70), channel_id=1, source_target_pairs={{0,6},{1,7},{2,4},{3,5},{4,2},{5,3},{6,0},{7,1},{8,14},{9,15},{10,... | collective-permute-start | bytes 344072 | tf_op jit(solution)/shard_map/ppermute | solution.py:321
  44.9 18.0 %copy-start.1 = (bf16[1792,608]{0,1:T(8,128)(2,1)S(1)}, bf16[1792,608]{0,1:T(8,128)(2,1)}, u32[]{:S(2)}) copy-start(bf16[1792,608]{0,1:T(8,128)(2,1)} %param.36) | copy-start | bytes 6537220
  45.0 18.0 %copy-start.2 = (bf16[1792,608]{0,1:T(8,128)(2,1)S(1)}, bf16[1792,608]{0,1:T(8,128)(2,1)}, u32[]{:S(2)}) copy-start(bf16[1792,608]{0,1:T(8,128)(2,1)} %param.37) | copy-start | bytes 6537220
  45.0 9.1 %collective-permute-start.14 = (bf16[2,224,128]{2,1,0:T(8,128)(2,1)S(1)}, bf16[2,224,128]{2,1,0:T(8,128)(2,1)S(1)}, u32[]{:S(2)}, u32[]{:S(2)}) collective-permute-start(bf16[2,224,128]{2,1,0:T(8,128)(2,1)S(1)} %pad_maximum_fusion.1), channel_id=1, source_target_pairs={{0,1},{1,0},{2,3},{3,2},{4,5},{5,4},{6,7},{7,6},{8,9},{9,8},{10,11... | collective-permute-start | bytes 344072 | tf_op jit(solution)/shard_map/ppermute | solution.py:324
  54.1 6.1 %collective-permute-start.17 = (bf16[2,224,128]{2,1,0:T(8,128)(2,1)S(1)}, bf16[2,224,128]{2,1,0:T(8,128)(2,1)S(1)}, u32[]{:S(2)}, u32[]{:S(2)}) collective-permute-start(bf16[2,224,128]{2,1,0:T(8,128)(2,1)S(1)} %add_convert_fusion.own_ref), channel_id=1, source_target_pairs={{0,6},{1,7},{2,4},{3,5},{4,2},{5,3},{6,0},{7,1},{8,14},{9,15},{10,... | collective-permute-start | bytes 344072 | tf_op jit(solution)/shard_map/ppermute | solution.py:321
  56.7 6.3 %collective-permute-start.16 = (bf16[2,224,128]{2,1,0:T(8,128)(2,1)S(1)}, bf16[2,224,128]{2,1,0:T(8,128)(2,1)S(1)}, u32[]{:S(2)}, u32[]{:S(2)}) collective-permute-start(bf16[2,224,128]{2,1,0:T(8,128)(2,1)S(1)} %add_convert_fusion.own_ref), channel_id=1, source_target_pairs={{0,4},{1,5},{2,6},{3,7},{4,0},{5,1},{6,2},{7,3},{8,12},{9,13},{10,... | collective-permute-start | bytes 344072 | tf_op jit(solution)/shard_map/ppermute | solution.py:321
  57.4 5.6 %collective-permute-start.15 = (bf16[2,224,128]{2,1,0:T(8,128)(2,1)S(1)}, bf16[2,224,128]{2,1,0:T(8,128)(2,1)S(1)}, u32[]{:S(2)}, u32[]{:S(2)}) collective-permute-start(bf16[2,224,128]{2,1,0:T(8,128)(2,1)S(1)} %add_convert_fusion.own_ref), channel_id=1, source_target_pairs={{0,2},{1,3},{2,0},{3,1},{4,6},{5,7},{6,4},{7,5},{8,10},{9,11},{10,... | collective-permute-start | bytes 344072 | tf_op jit(solution)/shard_map/ppermute | solution.py:321
  65.2 6.4 %collective-permute-start.18 = (bf16[2,224,128]{2,1,0:T(8,128)(2,1)S(1)}, bf16[2,224,128]{2,1,0:T(8,128)(2,1)S(1)}, u32[]{:S(2)}, u32[]{:S(2)}) collective-permute-start(bf16[2,224,128]{2,1,0:T(8,128)(2,1)S(1)} %get-tuple-element.76), channel_id=1, source_target_pairs={{0,4},{1,5},{2,6},{3,7},{4,0},{5,1},{6,2},{7,3},{8,12},{9,13},{10,... | collective-permute-start | bytes 344072 | tf_op jit(solution)/shard_map/ppermute | solution.py:321
  67.3 4.8 %collective-permute-start.19 = (bf16[2,224,128]{2,1,0:T(8,128)(2,1)S(1)}, bf16[2,224,128]{2,1,0:T(8,128)(2,1)S(1)}, u32[]{:S(2)}, u32[]{:S(2)}) collective-permute-start(bf16[2,224,128]{2,1,0:T(8,128)(2,1)S(1)} %get-tuple-element.77), channel_id=1, source_target_pairs={{0,2},{1,3},{2,0},{3,1},{4,6},{5,7},{6,4},{7,5},{8,10},{9,11},{10,... | collective-permute-start | bytes 344072 | tf_op jit(solution)/shard_map/ppermute | solution.py:321
  67.9 6.0 %collective-permute-start.20 = (bf16[2,224,128]{2,1,0:T(8,128)(2,1)S(1)}, bf16[2,224,128]{2,1,0:T(8,128)(2,1)S(1)}, u32[]{:S(2)}, u32[]{:S(2)}) collective-permute-start(bf16[2,224,128]{2,1,0:T(8,128)(2,1)S(1)} %get-tuple-element.78), channel_id=1, source_target_pairs={{0,6},{1,7},{2,4},{3,5},{4,2},{5,3},{6,0},{7,1},{8,14},{9,15},{10,... | collective-permute-start | bytes 344072 | tf_op jit(solution)/shard_map/ppermute | solution.py:321
  74.0 8.2 %collective-permute-start.21 = (bf16[224,128]{1,0:T(8,128)(2,1)S(1)}, bf16[224,128]{1,0:T(8,128)(2,1)S(1)}, u32[]{:S(2)}, u32[]{:S(2)}) collective-permute-start(bf16[224,128]{1,0:T(8,128)(2,1)S(1)} %fusion.4), channel_id=1, source_target_pairs={{0,1},{1,0},{2,3},{3,2},{4,5},{5,4},{6,7},{7,6},{8,9},{9,8},{10,11... | collective-permute-start | bytes 172040 | tf_op jit(solution)/shard_map/ppermute | solution.py:324
  (1 other events, 13.4 us)

commit v8 on v7

--- a/solution.py
+++ b/solution.py
@@ -100,18 +100,28 @@
         out_ref[at, :] = in_ref[:, at].T
 
 
-def turn_kernel(in_ref, out_ref):
-    turn_block(in_ref, out_ref)
-
-
-def turn_and_slots_kernel(
-    groups, held, in_hbm, leaf_hbm, parent_hbm, owner_hbm, out_ref, slot_ref, in_ref, leaf_ref, parent_ref, owner_ref, sems
-):
-    copies = fetch(
-        ((in_hbm, in_ref), (leaf_hbm, leaf_ref), (parent_hbm, parent_ref), (owner_hbm, owner_ref)), sems
-    )
+def scale_block(in_ref, gain_ref, out_ref):
+    for j in range(in_ref.shape[1] // LANES):
+        at = slice(j * LANES, (j + 1) * LANES)
+        out_ref[:, at] = (in_ref[:, at].astype(F32) * gain_ref[j : j + 1, :]).astype(BF16)
+
+
+def ffn_weights_kernel(down_ref, gate_ref, up_ref, gain_ref, turned_ref, gate_out_ref, up_out_ref):
+    turn_block(down_ref, turned_ref)
+    scale_block(gate_ref, gain_ref, gate_out_ref)
+    scale_block(up_ref, gain_ref, up_out_ref)
+
+
+def mixer_weights_kernel(groups, held, *refs):
+    out_ref, slot_ref, wide_ref = refs[9:12]
+    copies = fetch(tuple(zip(refs[:9], refs[12:21])), refs[21])
+    in_ref, leaf_ref, parent_ref, owner_ref, query_ref, key_ref, value_ref, gate_ref, gain_ref = refs[12:21]
     for copy in copies:
         copy.wait()
+    row = 0
+    for part in (query_ref, key_ref, value_ref, gate_ref):
+        scale_block(part, gain_ref, wide_ref.at[row : row + part.shape[0]])
+        row += part.shape[0]
     dev = lax.axis_index("req")
     count = 2 * held
     total_dev = groups * count
@@ -168,13 +178,11 @@
         scratch[pl.ds(pl.multiple_of((2 * source + 1 - z) * rows, 32), rows), :] = block[1]
 
 
-def scaled_rows(scratch, gain_ref):
-    gain = gain_ref[...].T
+def row_scale(scratch):
     squares = jnp.zeros((LANES, scratch.shape[1]), F32)
     for j in range(scratch.shape[0] // LANES):
         rows = scratch[j * LANES : (j + 1) * LANES, :].astype(F32)
         squares = squares + rows * rows
-        scratch[j * LANES : (j + 1) * LANES, :] = (rows * gain[:, j : j + 1]).astype(BF16)
     mean = jnp.sum(squares, axis=0, keepdims=True) / scratch.shape[0]
     return lax.rsqrt(mean + EPSILON)
 
@@ -184,17 +192,20 @@
 
 
 def local_kernel(
-    total_req, own_ref, r1_ref, r3_ref, r2_ref, gain_ref, token_ref, query_ref, key_ref, value_ref, gate_ref,
+    total_req, own_ref, r1_ref, r3_ref, r2_ref, token_ref, weight_ref, kept_ref,
     taps_ref, conv_ref, silu_ref, scores_ref, den_ref, right_ref, turned_ref, scratch,
 ):
     place_blocks(scratch, [own_ref, r1_ref, r2_ref, r3_ref])
-    scale = scaled_rows(scratch, gain_ref)
-    rows = scratch[...]
-    queries = jnp.dot(query_ref[...], rows, preferred_element_type=F32) * scale
-    keys = jnp.dot(key_ref[...], rows, preferred_element_type=F32) * scale
-    values = (jnp.dot(value_ref[...], rows, preferred_element_type=F32) * scale).astype(BF16).astype(F32)
-    gates = jnp.dot(gate_ref[...], rows, preferred_element_type=F32) * scale
+    del kept_ref
+    scale = row_scale(scratch)
     heads = scores_ref.shape[0]
+    proj = jnp.dot(weight_ref[...], scratch[...], preferred_element_type=F32) * scale
+    value_dim = conv_ref.shape[0]
+    narrow = (proj.shape[0] - 2 * value_dim) // 2
+    queries = proj[:narrow]
+    keys = proj[narrow : 2 * narrow]
+    values = proj[2 * narrow : 2 * narrow + value_dim].astype(BF16).astype(F32)
+    gates = proj[2 * narrow + value_dim :]
     per = right_ref.shape[1] // ROWS
     feat_dim = queries.shape[0] // heads
     tokens = token_ref.shape[1]
@@ -295,10 +306,10 @@
             out[half] = jnp.dot(block, right, preferred_element_type=F32).astype(out.dtype)
 
 
-def ffn_kernel(own_ref, r1_ref, r2_ref, r3_ref, gain_ref, gate_ref, up_ref, down_ref, *rest):
+def ffn_kernel(own_ref, r1_ref, r3_ref, r2_ref, gate_ref, up_ref, down_ref, *rest):
     outs, scratch = rest[:4], rest[4]
     place_blocks(scratch, [own_ref, r1_ref, r2_ref, r3_ref])
-    scale = scaled_rows(scratch, gain_ref)
+    scale = row_scale(scratch)
     gate = jnp.dot(gate_ref[...], scratch[...], preferred_element_type=F32) * scale
     up = jnp.dot(up_ref[...], scratch[...], preferred_element_type=F32) * scale
     spread_blocks(outs, down_ref, (silu(gate) * up).astype(BF16))
@@ -351,18 +362,29 @@
         compiler_params=PARAMS,
         name="fold",
     )(*[in_hbm(a) for a in fold_in])
-    path_in = (out_weight, request_leaf, parent, owner_map)
-    out_turned, slots = pl.pallas_call(
-        functools.partial(turn_and_slots_kernel, y_size, z_size),
-        out_shape=[sds(out_weight.shape[::-1], BF16), sds((y_size * per * 3,), jnp.int32)],
-        in_specs=[hbm] * len(path_in),
-        out_specs=[VMEM, SMEM],
-        scratch_shapes=[pltpu.VMEM(out_weight.shape, BF16)]
-        + [pltpu.SMEM(a.shape, jnp.int32) for a in path_in[1:]]
-        + [pltpu.SemaphoreType.DMA((len(path_in),))],
+    gain_rows = model // LANES
+
+    def gain_block(gain):
+        return jnp.pad(gain.reshape(gain_rows, LANES), ((0, -gain_rows % 8), (0, 0)))
+
+    narrow = (query_weight.T, key_weight.T, value_weight.T, conv_gate_weight.T)
+    ready_in = (out_weight, request_leaf, parent, owner_map, *narrow, gain_block(mixer_gain))
+    out_turned, slots, wide_weight = pl.pallas_call(
+        functools.partial(mixer_weights_kernel, y_size, z_size),
+        out_shape=[
+            sds(out_weight.shape[::-1], BF16),
+            sds((y_size * per * 3,), jnp.int32),
+            sds((sum(a.shape[0] for a in narrow), model), BF16),
+        ],
+        in_specs=[hbm] * len(ready_in),
+        out_specs=[VMEM, SMEM, VMEM],
+        scratch_shapes=[
+            pltpu.SMEM(a.shape, a.dtype) if a.dtype == jnp.int32 else pltpu.VMEM(a.shape, a.dtype) for a in ready_in
+        ]
+        + [pltpu.SemaphoreType.DMA((len(ready_in),))],
         compiler_params=PARAMS,
-        name="turn_out",
-    )(*[in_hbm(a) for a in path_in])
+        name="mixer_weights",
+    )(*[in_hbm(a) for a in ready_in])
     from_z = {k: along_z(payload, k) for k in order}
 
     pair = call(stack_kernel, sds((2, width, tokens), BF16), [VMEM] * 2, (own_near, across_z(own)), name="stack_pair")
@@ -388,12 +410,6 @@
     [kept] = select((0,), (mine, other), "select_kept")
     from_y = {k: along_y(sent[k], k) for k in order}
 
-    gain_rows = model // LANES
-
-    def gain_block(gain):
-        return jnp.pad(gain.reshape(gain_rows, LANES), ((0, -gain_rows % 8), (0, 0)))
-
-    kept, mixer_rows = lax.optimization_barrier((kept, gain_block(mixer_gain)))
     local = call(
         functools.partial(local_kernel, request_leaf.shape[0]),
         [
@@ -404,10 +420,9 @@
             sds((heads, per * ROWS, 3 * tokens), BF16),
             sds((width, 8), F32),
         ],
-        [VMEM] * 11,
+        [VMEM] * 6 + [pl.BlockSpec(memory_space=pl.ANY), VMEM],
         (
-            pair, rows[1], rows[3], rows[2], mixer_rows, token_req.reshape(1, tokens),
-            query_weight.T, key_weight.T, value_weight.T, conv_gate_weight.T, conv_kernel,
+            pair, rows[1], rows[3], rows[2], token_req.reshape(1, tokens), wide_weight, kept, conv_kernel,
         ),
         scratch=[pltpu.VMEM((model, tokens), BF16)],
         name="local",
@@ -424,16 +439,23 @@
     share = parts[0] + got[2].astype(F32) + got[1].astype(F32) + got[3].astype(F32)
     crossing, down_in = lax.optimization_barrier((jnp.stack([share[1], share[0]]).astype(BF16), ffn_down))
     share_peer = across_z(crossing)
+    ffn_shape = ffn_gate.shape[::-1]
+    ready = call(
+        ffn_weights_kernel,
+        [sds(down_in.shape[::-1], BF16), sds(ffn_shape, BF16), sds(ffn_shape, BF16)],
+        [VMEM] * 4,
+        (down_in, ffn_gate.T, ffn_up.T, gain_block(ffn_gain)),
+        name="ffn_weights",
+    )
     updated = (held_pair.astype(F32) + share + share_peer.astype(F32)).astype(BF16)
-    turned_down = call(turn_kernel, sds(down_in.shape[::-1], BF16), [VMEM], (down_in,), name="turn_down")
-    updated, down_turned = lax.optimization_barrier((updated, turned_down))
+    updated, down_turned, gate_scaled, up_scaled = lax.optimization_barrier((updated, *ready))
 
     wide = {k: along_x(updated, k) for k in order}
     downs = call(
         ffn_kernel,
         [sds((2, width, tokens), F32)] + [sds((2, width, tokens), BF16)] * 3,
-        [VMEM] * 8,
-        (updated, wide[1], wide[2], wide[3], gain_block(ffn_gain), ffn_gate.T, ffn_up.T, down_turned),
+        [VMEM] * 7,
+        (updated, wide[1], wide[3], wide[2], gate_scaled, up_scaled, down_turned),
         scratch=[pltpu.VMEM((model, tokens), BF16)],
         name="ffn",
     )

time: 83.5 us -> 82.9 us (level)
  waiting for transfers between devices: 30.3 us -> 27.8 us
  Pallas kernels: 11.3 us -> 12.6 us
  local copies, waits for them, and re-layouts: 0.08 us -> 1.35 us
    ppermute x3, waiting for transfers between devices: 12.6 us -> 10.1 us  [across_z(): return lax.ppermute(array, 'tp', [(i, i ^ 1) for i in range(tp_size)])]
    pad x2, local copies, waits for them, and re-layouts: 0.01 us -> 1.3 us  [gain_block(): jnp.pad(gain.reshape(gain_rows, LANES), ((0, -gain_rows % 8), (0, 0)))]
    pallas_call x1, Pallas kernels: 2.35 us -> 3.24 us  [shards(): pl.pallas_call(functools.partial(mixer_weights_kernel, y_size, z_size), o...]
  transfers between devices with their start and end apart: 22 -> 22, of which waited for: 12 -> 14; matrix products, arithmetic and copies ran while one was open for 0% -> 2% of each run, Pallas kernels for 8% -> 10%
where the time goes in v8:
time: 82.9 us; the launch traced here: 82 us
  starting transfers between devices  39.2 us (47%)
  waiting for transfers between devices  27.8 us (34%)
  Pallas kernels  12.6 us (15%)
  local copies, waits for them, and re-layouts  1.35 us (2%)
  other arithmetic  0.92 us (1%)
    ppermute x12, waiting for transfers between devices, along_x(): return lax.ppermute(array, 'tp', [(i, i ^ 2 * k) for i in range(tp_size)])  17.6 us
    ppermute x12, starting transfers between devices, along_x(): return lax.ppermute(array, 'tp', [(i, i ^ 2 * k) for i in range(tp_size)])  16.8 us
    ppermute x3, starting transfers between devices, across_z(): return lax.ppermute(array, 'tp', [(i, i ^ 1) for i in range(tp_size)])  12.7 us
    ppermute x3, waiting for transfers between devices, across_z(): return lax.ppermute(array, 'tp', [(i, i ^ 1) for i in range(tp_size)])  10.1 us
    pallas_call x7, Pallas kernels, call(): pl.pallas_call(kernel, out_shape=out_shape, in_specs=specs, out_specs=VME...  7.76 us
    ppermute x3, starting transfers between devices, along_z(): return lax.ppermute(array, 'req', [(i, i ^ 2 * k) for i in range(req_size)])  5.37 us
    ppermute x3, starting transfers between devices, along_y(): lax.ppermute(array, 'req', [(i, i ^ 2 * z_size * k) for i in range(req_si...  4.18 us
    pallas_call x1, Pallas kernels, shards(): pl.pallas_call(functools.partial(mixer_weights_kernel, y_size, z_size), o...  3.24 us
  transfers between devices with their start and end apart: 22, of which 14 were waited for; matrix products, arithmetic and copies ran while one was open for 2% of the time, Pallas kernels for 10%

profile of v8, /device:TPU:8, one launch (start us, length us, event | category | flops | bytes accessed | tf_op | source)
XLA Modules:
  0.0 82.0 jit_solution(15016244751141585770)
XLA Ops:
  0.0 1.6 %fold.1 = (bf16[2,160,128]{2,1,0:T(8,128)(2,1)S(1)}, bf16[224,128]{1,0:T(8,128)(2,1)S(1)}) custom-call(bf16[160,273]{1,0:T(8,128)(2,1)} %constant.5.clone.fold_hbm, bf16[273,2,112]{2,1,0:T(2,128)(2,1)} %bitcast.37, bf16[2,273]{1,0:T(2,128)(2,1)} %bitcast.47, bf16[2,224]{1,0:T(2,128)(2,1)} %bitcast.48, bf16[224,128]{1,0:T(8,128)(2,1)} %bitcast.43), custom_call_target="tpu_custom_call" | custom-call | tf_op jit(solution)/shard_map/fold/pallas_call | solution.py:356
  1.6 4.7 %collective-permute-start.3 = (bf16[2,160,128]{2,1,0:T(8,128)(2,1)S(1)}, bf16[2,160,128]{2,1,0:T(8,128)(2,1)S(1)}, u32[]{:S(2)}, u32[]{:S(2)}) collective-permute-start(bf16[2,160,128]{2,1,0:T(8,128)(2,1)S(1)} %get-tuple-element.48), channel_id=1, source_target_pairs={{0,48},{8,56},{16,32},{24,40},{32,16},{40,24},{48,0},{56,8},{64,11... | collective-permute-start | bytes 245768 | tf_op jit(solution)/shard_map/ppermute | solution.py:338
  7.0 6.3 %collective-permute-start = (bf16[224,128]{1,0:T(8,128)(2,1)}, bf16[224,128]{1,0:T(8,128)(2,1)S(1)}, u32[]{:S(2)}, u32[]{:S(2)}) collective-permute-start(bf16[224,128]{1,0:T(8,128)(2,1)} %bitcast.44), channel_id=1, source_target_pairs={{0,1},{1,0},{2,3},{3,2},{4,5},{5,4},{6,7},{7,6},{8,9},{9,8},{10,11... | collective-permute-start | bytes 172040 | tf_op jit(solution)/shard_map/ppermute | solution.py:335
  13.3 1.3 %pad.7.refs_8_ = f32[16,128]{1,0:T(8,128)} pad(f32[14,128]{1,0:T(8,128)} %bitcast.45, f32[]{:T(128)} %constant.4.clone.1), padding=0_2x0_0 | pad | bytes 15364 | tf_op jit(solution)/shard_map/jit(_pad)/pad | solution.py:368
  14.6 3.2 %mixer_weights.1 = (bf16[1792,224]{1,0:T(8,128)(2,1)S(1)}, s32[24]{0:T(128)S(1)}, bf16[512,1792]{1,0:T(8,128)(2,1)S(1)}) custom-call(bf16[224,1792]{1,0:T(8,128)(2,1)} %refs_0_.1, s32[64]{0:T(128)} %refs_1_.1, s32[32]{0:T(128)} %refs_2_.1, s32[32]{0:T(128)} %refs_3_.1, bf16[32,1792]{1,0:T(8,128)(2,1)} %bitcast.38, bf16[32,1792]{1,0:T(8,128)(2,1)} %bitcast.39, ...), custom_call_target="tpu_custom_call" | custom-call | tf_op jit(solution)/shard_map/mixer_weights/pallas_call | solution.py:372
  18.7 3.1 %collective-permute-start.6 = (bf16[2,224,128]{2,1,0:T(8,128)(2,1)S(1)}, bf16[2,224,128]{2,1,0:T(8,128)(2,1)S(1)}, u32[]{:S(2)}, u32[]{:S(2)}) collective-permute-start(bf16[2,224,128]{2,1,0:T(8,128)(2,1)S(1)} %stack_pair.1.own_ref), channel_id=1, source_target_pairs={{0,4},{1,5},{2,6},{3,7},{4,0},{5,1},{6,2},{7,3},{8,12},{9,13},{10,... | collective-permute-start | bytes 344072 | tf_op jit(solution)/shard_map/ppermute | solution.py:332
  21.8 1.0 %select_sent.1 = (bf16[2,2,160,128]{3,2,1,0:T(8,128)(2,1)S(1)}, bf16[2,2,160,128]{3,2,1,0:T(8,128)(2,1)S(1)}, bf16[2,2,160,128]{3,2,1,0:T(8,128)(2,1)S(1)}) custom-call(s32[24]{0:T(128)S(1)} %get-tuple-element.51.slot_ref, bf16[4,2,160,128]{3,2,1,0:T(8,128)(2,1)S(1)} %pad_maximum_fusion.mine_ref, bf16[4,2,160,128]{3,2,1,0:T(8,128)(2,1)S(1)} %collective-permute-done.7.other_ref), custom_call_target="tpu_custom_call" | custom-call | tf_op jit(solution)/shard_map/select_sent/pallas_call | solution.py:25
  22.8 2.4 %collective-permute-start.8 = (bf16[2,2,160,128]{3,2,1,0:T(8,128)(2,1)S(1)}, bf16[2,2,160,128]{3,2,1,0:T(8,128)(2,1)S(1)}, u32[]{:S(2)}, u32[]{:S(2)}) collective-permute-start(bf16[2,2,160,128]{3,2,1,0:T(8,128)(2,1)S(1)} %get-tuple-element.66), channel_id=1, source_target_pairs={{0,128},{8,136},{16,144},{24,152},{32,160},{40,168},{48,176},{56,1... | collective-permute-start | bytes 491528 | tf_op jit(solution)/shard_map/ppermute | solution.py:344
  25.2 1.3 %collective-permute-start.9 = (bf16[2,2,160,128]{3,2,1,0:T(8,128)(2,1)S(1)}, bf16[2,2,160,128]{3,2,1,0:T(8,128)(2,1)S(1)}, u32[]{:S(2)}, u32[]{:S(2)}) collective-permute-start(bf16[2,2,160,128]{3,2,1,0:T(8,128)(2,1)S(1)} %get-tuple-element.67), channel_id=1, source_target_pairs={{0,64},{8,72},{16,80},{24,88},{32,96},{40,104},{48,112},{56,120},{... | collective-permute-start | bytes 491528 | tf_op jit(solution)/shard_map/ppermute | solution.py:344
  27.0 1.3 %collective-permute-start.5 = (bf16[2,224,128]{2,1,0:T(8,128)(2,1)S(1)}, bf16[2,224,128]{2,1,0:T(8,128)(2,1)S(1)}, u32[]{:S(2)}, u32[]{:S(2)}) collective-permute-start(bf16[2,224,128]{2,1,0:T(8,128)(2,1)S(1)} %stack_pair.1.own_ref), channel_id=1, source_target_pairs={{0,6},{1,7},{2,4},{3,5},{4,2},{5,3},{6,0},{7,1},{8,14},{9,15},{10,... | collective-permute-start | bytes 344072 | tf_op jit(solution)/shard_map/ppermute | solution.py:332
  29.2 3.8 %collective-permute-done.5.r3_ref = bf16[2,224,128]{2,1,0:T(8,128)(2,1)S(1)} collective-permute-done((bf16[2,224,128]{2,1,0:T(8,128)(2,1)S(1)}, bf16[2,224,128]{2,1,0:T(8,128)(2,1)S(1)}, u32[]{:S(2)}, u32[]{:S(2)}) %collective-permute-start.5) | collective-permute-done | bytes 114720 | tf_op jit(solution)/shard_map/ppermute | solution.py:332
  33.0 1.1 %local.1 = (f32[224,128]{1,0:T(8,128)S(1)}, f32[224,128]{1,0:T(8,128)S(1)}, bf16[2,128,128]{2,1,0:T(8,128)(2,1)S(1)}, f32[2,1,128]{2,1,0:T(1,128)S(1)}, bf16[2,3...) custom-call(bf16[2,224,128]{2,1,0:T(8,128)(2,1)S(1)} %stack_pair.1.own_ref, ...), custom_call_target="tpu_custom_call" | custom-call | tf_op jit(solution)/shard_map/local/pallas_call | solution.py:25
  34.3 1.1 %mix.1 = (f32[2,224,128]{2,1,0:T(8,128)S(1)}, bf16[2,224,128]{2,1,0:T(8,128)(2,1)S(1)}, bf16[2,224,128]{2,1,0:T(8,128)(2,1)S(1)}, bf16[2,224,128]{2,1,0:T(8,128)(2,1)S(1)}) custom-call(f32[224,128]{1,0:T(8,128)S(1)} %get-tuple-element.60.conv_ref, f32[224,128]{1,0:T(8,128)S(1)} %get-tuple-element.61.silu_ref, ...), custom_call_target="tpu_custom_call" | custom-call | tf_op jit(solution)/shard_map/mix/pallas_call | solution.py:25
  35.4 1.6 %collective-permute-start.11 = (bf16[2,224,128]{2,1,0:T(8,128)(2,1)S(1)}, bf16[2,224,128]{2,1,0:T(8,128)(2,1)S(1)}, u32[]{:S(2)}, u32[]{:S(2)}) collective-permute-start(bf16[2,224,128]{2,1,0:T(8,128)(2,1)S(1)} %get-tuple-element.71), channel_id=1, source_target_pairs={{0,4},{1,5},{2,6},{3,7},{4,0},{5,1},{6,2},{7,3},{8,12},{9,13},{10,... | collective-permute-start | bytes 344072 | tf_op jit(solution)/shard_map/ppermute | solution.py:332
  37.0 1.3 %collective-permute-start.12 = (bf16[2,224,128]{2,1,0:T(8,128)(2,1)S(1)}, bf16[2,224,128]{2,1,0:T(8,128)(2,1)S(1)}, u32[]{:S(2)}, u32[]{:S(2)}) collective-permute-start(bf16[2,224,128]{2,1,0:T(8,128)(2,1)S(1)} %get-tuple-element.72), channel_id=1, source_target_pairs={{0,2},{1,3},{2,0},{3,1},{4,6},{5,7},{6,4},{7,5},{8,10},{9,11},{10,... | collective-permute-start | bytes 344072 | tf_op jit(solution)/shard_map/ppermute | solution.py:332
  38.2 1.3 %collective-permute-start.13 = (bf16[2,224,128]{2,1,0:T(8,128)(2,1)S(1)}, bf16[2,224,128]{2,1,0:T(8,128)(2,1)S(1)}, u32[]{:S(2)}, u32[]{:S(2)}) collective-permute-start(bf16[2,224,128]{2,1,0:T(8,128)(2,1)S(1)} %get-tuple-element.73), channel_id=1, source_target_pairs={{0,6},{1,7},{2,4},{3,5},{4,2},{5,3},{6,0},{7,1},{8,14},{9,15},{10,... | collective-permute-start | bytes 344072 | tf_op jit(solution)/shard_map/ppermute | solution.py:332
  39.6 3.4 %collective-permute-done.11 = bf16[2,224,128]{2,1,0:T(8,128)(2,1)S(1)} collective-permute-done((bf16[2,224,128]{2,1,0:T(8,128)(2,1)S(1)}, bf16[2,224,128]{2,1,0:T(8,128)(2,1)S(1)}, u32[]{:S(2)}, u32[]{:S(2)}) %collective-permute-start.11) | collective-permute-done | bytes 114720 | tf_op jit(solution)/shard_map/ppermute | solution.py:332
  43.0 1.3 %collective-permute-done.13 = bf16[2,224,128]{2,1,0:T(8,128)(2,1)S(1)} collective-permute-done((bf16[2,224,128]{2,1,0:T(8,128)(2,1)S(1)}, bf16[2,224,128]{2,1,0:T(8,128)(2,1)S(1)}, u32[]{:S(2)}, u32[]{:S(2)}) %collective-permute-start.13) | collective-permute-done | bytes 114720 | tf_op jit(solution)/shard_map/ppermute | solution.py:332
  44.4 3.5 %collective-permute-start.14 = (bf16[2,224,128]{2,1,0:T(8,128)(2,1)S(1)}, bf16[2,224,128]{2,1,0:T(8,128)(2,1)S(1)}, u32[]{:S(2)}, u32[]{:S(2)}) collective-permute-start(bf16[2,224,128]{2,1,0:T(8,128)(2,1)S(1)} %pad_maximum_fusion.1), channel_id=1, source_target_pairs={{0,1},{1,0},{2,3},{3,2},{4,5},{5,4},{6,7},{7,6},{8,9},{9,8},{10,11... | collective-permute-start | bytes 344072 | tf_op jit(solution)/shard_map/ppermute | solution.py:335
  47.9 1.8 %ffn_weights.1 = (bf16[1792,608]{1,0:T(8,128)(2,1)S(1)}, bf16[608,1792]{1,0:T(8,128)(2,1)S(1)}, bf16[608,1792]{1,0:T(8,128)(2,1)S(1)}) custom-call(bf16[608,1792]{1,0:T(8,128)(2,1)S(1)} %copy-done, bf16[608,1792]{1,0:T(8,128)(2,1)S(1)} %bitcast.31, bf16[608,1792]{1,0:T(8,128)(2,1)S(1)} %bitcast.32, f32[16,128]{1,0:T(8,128)S(1)} %pad.8.gain_ref), custom_call_target="tpu_custom_call" | custom-call | tf_op jit(solution)/shard_map/ffn_weights/pallas_call | solution.py:25
  49.7 4.2 %collective-permute-done.14 = bf16[2,224,128]{2,1,0:T(8,128)(2,1)S(1)} collective-permute-done((bf16[2,224,128]{2,1,0:T(8,128)(2,1)S(1)}, bf16[2,224,128]{2,1,0:T(8,128)(2,1)S(1)}, u32[]{:S(2)}, u32[]{:S(2)}) %collective-permute-start.14) | collective-permute-done | bytes 114720 | tf_op jit(solution)/shard_map/ppermute | solution.py:335
  54.0 1.9 %collective-permute-start.17 = (bf16[2,224,128]{2,1,0:T(8,128)(2,1)S(1)}, bf16[2,224,128]{2,1,0:T(8,128)(2,1)S(1)}, u32[]{:S(2)}, u32[]{:S(2)}) collective-permute-start(bf16[2,224,128]{2,1,0:T(8,128)(2,1)S(1)} %add_convert_fusion.own_ref), channel_id=1, source_target_pairs={{0,4},{1,5},{2,6},{3,7},{4,0},{5,1},{6,2},{7,3},{8,12},{9,13},{10,... | collective-permute-start | bytes 344072 | tf_op jit(solution)/shard_map/ppermute | solution.py:332
  55.9 1.9 %collective-permute-start.16 = (bf16[2,224,128]{2,1,0:T(8,128)(2,1)S(1)}, bf16[2,224,128]{2,1,0:T(8,128)(2,1)S(1)}, u32[]{:S(2)}, u32[]{:S(2)}) collective-permute-start(bf16[2,224,128]{2,1,0:T(8,128)(2,1)S(1)} %add_convert_fusion.own_ref), channel_id=1, source_target_pairs={{0,6},{1,7},{2,4},{3,5},{4,2},{5,3},{6,0},{7,1},{8,14},{9,15},{10,... | collective-permute-start | bytes 344072 | tf_op jit(solution)/shard_map/ppermute | solution.py:332
  57.9 2.6 %collective-permute-done.17.r2_ref = bf16[2,224,128]{2,1,0:T(8,128)(2,1)S(1)} collective-permute-done((bf16[2,224,128]{2,1,0:T(8,128)(2,1)S(1)}, bf16[2,224,128]{2,1,0:T(8,128)(2,1)S(1)}, u32[]{:S(2)}, u32[]{:S(2)}) %collective-permute-start.17) | collective-permute-done | bytes 114720 | tf_op jit(solution)/shard_map/ppermute | solution.py:332
  60.4 1.5 %collective-permute-done.16.r3_ref = bf16[2,224,128]{2,1,0:T(8,128)(2,1)S(1)} collective-permute-done((bf16[2,224,128]{2,1,0:T(8,128)(2,1)S(1)}, bf16[2,224,128]{2,1,0:T(8,128)(2,1)S(1)}, u32[]{:S(2)}, u32[]{:S(2)}) %collective-permute-start.16) | collective-permute-done | bytes 114720 | tf_op jit(solution)/shard_map/ppermute | solution.py:332
  62.7 2.1 %ffn.1 = (f32[2,224,128]{2,1,0:T(8,128)S(1)}, bf16[2,224,128]{2,1,0:T(8,128)(2,1)S(1)}, bf16[2,224,128]{2,1,0:T(8,128)(2,1)S(1)}, bf16[2,224,128]{2,1,0:T(8,128)(2,1)S(1)}) custom-call(bf16[2,224,128]{2,1,0:T(8,128)(2,1)S(1)} %add_convert_fusion.own_ref, bf16[2,224,128]{2,1,0:T(8,128)(2,1)S(1)} %collective-permute-done.15.r1_ref, ...), custom_call_target="tpu_custom_call" | custom-call | tf_op jit(solution)/shard_map/ffn/pallas_call | solution.py:25
  64.7 1.7 %collective-permute-start.18 = (bf16[2,224,128]{2,1,0:T(8,128)(2,1)S(1)}, bf16[2,224,128]{2,1,0:T(8,128)(2,1)S(1)}, u32[]{:S(2)}, u32[]{:S(2)}) collective-permute-start(bf16[2,224,128]{2,1,0:T(8,128)(2,1)S(1)} %get-tuple-element.84), channel_id=1, source_target_pairs={{0,4},{1,5},{2,6},{3,7},{4,0},{5,1},{6,2},{7,3},{8,12},{9,13},{10,... | collective-permute-start | bytes 344072 | tf_op jit(solution)/shard_map/ppermute | solution.py:332
  67.1 1.8 %collective-permute-start.20 = (bf16[2,224,128]{2,1,0:T(8,128)(2,1)S(1)}, bf16[2,224,128]{2,1,0:T(8,128)(2,1)S(1)}, u32[]{:S(2)}, u32[]{:S(2)}) collective-permute-start(bf16[2,224,128]{2,1,0:T(8,128)(2,1)S(1)} %get-tuple-element.86), channel_id=1, source_target_pairs={{0,6},{1,7},{2,4},{3,5},{4,2},{5,3},{6,0},{7,1},{8,14},{9,15},{10,... | collective-permute-start | bytes 344072 | tf_op jit(solution)/shard_map/ppermute | solution.py:332
  68.9 2.2 %collective-permute-done.18 = bf16[2,224,128]{2,1,0:T(8,128)(2,1)S(1)} collective-permute-done((bf16[2,224,128]{2,1,0:T(8,128)(2,1)S(1)}, bf16[2,224,128]{2,1,0:T(8,128)(2,1)S(1)}, u32[]{:S(2)}, u32[]{:S(2)}) %collective-permute-start.18) | collective-permute-done | bytes 114720 | tf_op jit(solution)/shard_map/ppermute | solution.py:332
  71.2 1.9 %collective-permute-done.20 = bf16[2,224,128]{2,1,0:T(8,128)(2,1)S(1)} collective-permute-done((bf16[2,224,128]{2,1,0:T(8,128)(2,1)S(1)}, bf16[2,224,128]{2,1,0:T(8,128)(2,1)S(1)}, u32[]{:S(2)}, u32[]{:S(2)}) %collective-permute-start.20) | collective-permute-done | bytes 114720 | tf_op jit(solution)/shard_map/ppermute | solution.py:332
  73.2 2.9 %collective-permute-start.21 = (bf16[224,128]{1,0:T(8,128)(2,1)S(1)}, bf16[224,128]{1,0:T(8,128)(2,1)S(1)}, u32[]{:S(2)}, u32[]{:S(2)}) collective-permute-start(bf16[224,128]{1,0:T(8,128)(2,1)S(1)} %fusion.4), channel_id=1, source_target_pairs={{0,1},{1,0},{2,3},{3,2},{4,5},{5,4},{6,7},{7,6},{8,9},{9,8},{10,11... | collective-permute-start | bytes 172040 | tf_op jit(solution)/shard_map/ppermute | solution.py:335
  76.1 5.2 %collective-permute-done.21 = bf16[224,128]{1,0:T(8,128)(2,1)S(1)} collective-permute-done((bf16[224,128]{1,0:T(8,128)(2,1)S(1)}, bf16[224,128]{1,0:T(8,128)(2,1)S(1)}, u32[]{:S(2)}, u32[]{:S(2)}) %collective-permute-start.21) | collective-permute-done | bytes 57376 | tf_op jit(solution)/shard_map/ppermute | solution.py:335
  (43 shorter events, 5.5 us)
Async XLA Ops:
  1.6 16.9 %collective-permute-start.3 = (bf16[2,160,128]{2,1,0:T(8,128)(2,1)S(1)}, bf16[2,160,128]{2,1,0:T(8,128)(2,1)S(1)}, u32[]{:S(2)}, u32[]{:S(2)}) collective-permute-start(bf16[2,160,128]{2,1,0:T(8,128)(2,1)S(1)} %get-tuple-element.48), channel_id=1, source_target_pairs={{0,48},{8,56},{16,32},{24,40},{32,16},{40,24},{48,0},{56,8},{64,11... | collective-permute-start | bytes 245768 | tf_op jit(solution)/shard_map/ppermute | solution.py:338
  6.3 12.2 %collective-permute-start.2 = (bf16[2,160,128]{2,1,0:T(8,128)(2,1)S(1)}, bf16[2,160,128]{2,1,0:T(8,128)(2,1)S(1)}, u32[]{:S(2)}, u32[]{:S(2)}) collective-permute-start(bf16[2,160,128]{2,1,0:T(8,128)(2,1)S(1)} %get-tuple-element.48), channel_id=1, source_target_pairs={{0,32},{8,40},{16,48},{24,56},{32,0},{40,8},{48,16},{56,24},{64,96... | collective-permute-start | bytes 245768 | tf_op jit(solution)/shard_map/ppermute | solution.py:338
  6.3 12.2 %collective-permute-start.1 = (bf16[2,160,128]{2,1,0:T(8,128)(2,1)S(1)}, bf16[2,160,128]{2,1,0:T(8,128)(2,1)S(1)}, u32[]{:S(2)}, u32[]{:S(2)}) collective-permute-start(bf16[2,160,128]{2,1,0:T(8,128)(2,1)S(1)} %get-tuple-element.48), channel_id=1, source_target_pairs={{0,16},{8,24},{16,0},{24,8},{32,48},{40,56},{48,32},{56,40},{64,80... | collective-permute-start | bytes 245768 | tf_op jit(solution)/shard_map/ppermute | solution.py:338
  7.0 11.5 %collective-permute-start = (bf16[224,128]{1,0:T(8,128)(2,1)}, bf16[224,128]{1,0:T(8,128)(2,1)S(1)}, u32[]{:S(2)}, u32[]{:S(2)}) collective-permute-start(bf16[224,128]{1,0:T(8,128)(2,1)} %bitcast.44), channel_id=1, source_target_pairs={{0,1},{1,0},{2,3},{3,2},{4,5},{5,4},{6,7},{7,6},{8,9},{9,8},{10,11... | collective-permute-start | bytes 172040 | tf_op jit(solution)/shard_map/ppermute | solution.py:335
  14.6 18.5 %copy-start.3 = (f32[3,224]{1,0:T(4,128)S(1)}, f32[3,224]{1,0:T(4,128)}, u32[]{:S(2)}) copy-start(f32[3,224]{1,0:T(4,128)} %taps_ref.1) | copy-start | bytes 8068
  14.6 18.5 %copy-start.4 = (s32[128]{0:T(128)S(1)}, s32[128]{0:T(128)}, u32[]{:S(2)}) copy-start(s32[128]{0:T(128)} %param.21) | copy-start | bytes 1540
  18.6 3.2 %collective-permute-start.7 = (bf16[4,2,160,128]{3,2,1,0:T(8,128)(2,1)S(1)}, bf16[4,2,160,128]{3,2,1,0:T(8,128)(2,1)S(1)}, u32[]{:S(2)}, u32[]{:S(2)}) collective-permute-start(bf16[4,2,160,128]{3,2,1,0:T(8,128)(2,1)S(1)} %pad_maximum_fusion.mine_ref), channel_id=1, source_target_pairs={{0,8},{8,0},{16,24},{24,16},{32,40},{40,32},{48,56},{56,48},{64,72... | collective-permute-start | bytes 983048 | tf_op jit(solution)/shard_map/ppermute | solution.py:341
  18.7 9.5 %collective-permute-start.6 = (bf16[2,224,128]{2,1,0:T(8,128)(2,1)S(1)}, bf16[2,224,128]{2,1,0:T(8,128)(2,1)S(1)}, u32[]{:S(2)}, u32[]{:S(2)}) collective-permute-start(bf16[2,224,128]{2,1,0:T(8,128)(2,1)S(1)} %stack_pair.1.own_ref), channel_id=1, source_target_pairs={{0,4},{1,5},{2,6},{3,7},{4,0},{5,1},{6,2},{7,3},{8,12},{9,13},{10,... | collective-permute-start | bytes 344072 | tf_op jit(solution)/shard_map/ppermute | solution.py:332
  22.8 11.4 %collective-permute-start.8 = (bf16[2,2,160,128]{3,2,1,0:T(8,128)(2,1)S(1)}, bf16[2,2,160,128]{3,2,1,0:T(8,128)(2,1)S(1)}, u32[]{:S(2)}, u32[]{:S(2)}) collective-permute-start(bf16[2,2,160,128]{3,2,1,0:T(8,128)(2,1)S(1)} %get-tuple-element.66), channel_id=1, source_target_pairs={{0,128},{8,136},{16,144},{24,152},{32,160},{40,168},{48,176},{56,1... | collective-permute-start | bytes 491528 | tf_op jit(solution)/shard_map/ppermute | solution.py:344
  25.2 9.1 %collective-permute-start.9 = (bf16[2,2,160,128]{3,2,1,0:T(8,128)(2,1)S(1)}, bf16[2,2,160,128]{3,2,1,0:T(8,128)(2,1)S(1)}, u32[]{:S(2)}, u32[]{:S(2)}) collective-permute-start(bf16[2,2,160,128]{3,2,1,0:T(8,128)(2,1)S(1)} %get-tuple-element.67), channel_id=1, source_target_pairs={{0,64},{8,72},{16,80},{24,88},{32,96},{40,104},{48,112},{56,120},{... | collective-permute-start | bytes 491528 | tf_op jit(solution)/shard_map/ppermute | solution.py:344
  26.5 7.8 %collective-permute-start.10 = (bf16[2,2,160,128]{3,2,1,0:T(8,128)(2,1)S(1)}, bf16[2,2,160,128]{3,2,1,0:T(8,128)(2,1)S(1)}, u32[]{:S(2)}, u32[]{:S(2)}) collective-permute-start(bf16[2,2,160,128]{3,2,1,0:T(8,128)(2,1)S(1)} %get-tuple-element.68), channel_id=1, source_target_pairs={{0,192},{8,200},{16,208},{24,216},{32,224},{40,232},{48,240},{56,2... | collective-permute-start | bytes 491528 | tf_op jit(solution)/shard_map/ppermute | solution.py:344
  27.0 6.0 %collective-permute-start.5 = (bf16[2,224,128]{2,1,0:T(8,128)(2,1)S(1)}, bf16[2,224,128]{2,1,0:T(8,128)(2,1)S(1)}, u32[]{:S(2)}, u32[]{:S(2)}) collective-permute-start(bf16[2,224,128]{2,1,0:T(8,128)(2,1)S(1)} %stack_pair.1.own_ref), channel_id=1, source_target_pairs={{0,6},{1,7},{2,4},{3,5},{4,2},{5,3},{6,0},{7,1},{8,14},{9,15},{10,... | collective-permute-start | bytes 344072 | tf_op jit(solution)/shard_map/ppermute | solution.py:332
  28.2 4.8 %collective-permute-start.4 = (bf16[2,224,128]{2,1,0:T(8,128)(2,1)S(1)}, bf16[2,224,128]{2,1,0:T(8,128)(2,1)S(1)}, u32[]{:S(2)}, u32[]{:S(2)}) collective-permute-start(bf16[2,224,128]{2,1,0:T(8,128)(2,1)S(1)} %stack_pair.1.own_ref), channel_id=1, source_target_pairs={{0,2},{1,3},{2,0},{3,1},{4,6},{5,7},{6,4},{7,5},{8,10},{9,11},{10,... | collective-permute-start | bytes 344072 | tf_op jit(solution)/shard_map/ppermute | solution.py:332
  28.5 19.4 %copy-start.2 = (bf16[1792,608]{0,1:T(8,128)(2,1)S(1)}, bf16[1792,608]{0,1:T(8,128)(2,1)}, u32[]{:S(2)}) copy-start(bf16[1792,608]{0,1:T(8,128)(2,1)} %param.37) | copy-start | bytes 6537220
  33.0 14.9 %copy-start.1 = (bf16[1792,608]{0,1:T(8,128)(2,1)S(1)}, bf16[1792,608]{0,1:T(8,128)(2,1)}, u32[]{:S(2)}) copy-start(bf16[1792,608]{0,1:T(8,128)(2,1)} %param.36) | copy-start | bytes 6537220
  34.2 13.7 %copy-start.5 = (f32[1792]{0:T(1024)S(1)}, f32[1792]{0:T(1024)}, u32[]{:S(2)}) copy-start(f32[1792]{0:T(1024)} %param.29) | copy-start | bytes 21508
  34.2 13.7 %copy-start = (bf16[608,1792]{1,0:T(8,128)(2,1)S(1)}, bf16[608,1792]{1,0:T(8,128)(2,1)}, u32[]{:S(2)}) copy-start(bf16[608,1792]{1,0:T(8,128)(2,1)} %down_ref) | copy-start | bytes 6537220
  35.4 7.6 %collective-permute-start.11 = (bf16[2,224,128]{2,1,0:T(8,128)(2,1)S(1)}, bf16[2,224,128]{2,1,0:T(8,128)(2,1)S(1)}, u32[]{:S(2)}, u32[]{:S(2)}) collective-permute-start(bf16[2,224,128]{2,1,0:T(8,128)(2,1)S(1)} %get-tuple-element.71), channel_id=1, source_target_pairs={{0,4},{1,5},{2,6},{3,7},{4,0},{5,1},{6,2},{7,3},{8,12},{9,13},{10,... | collective-permute-start | bytes 344072 | tf_op jit(solution)/shard_map/ppermute | solution.py:332
  37.0 6.0 %collective-permute-start.12 = (bf16[2,224,128]{2,1,0:T(8,128)(2,1)S(1)}, bf16[2,224,128]{2,1,0:T(8,128)(2,1)S(1)}, u32[]{:S(2)}, u32[]{:S(2)}) collective-permute-start(bf16[2,224,128]{2,1,0:T(8,128)(2,1)S(1)} %get-tuple-element.72), channel_id=1, source_target_pairs={{0,2},{1,3},{2,0},{3,1},{4,6},{5,7},{6,4},{7,5},{8,10},{9,11},{10,... | collective-permute-start | bytes 344072 | tf_op jit(solution)/shard_map/ppermute | solution.py:332
  38.2 6.1 %collective-permute-start.13 = (bf16[2,224,128]{2,1,0:T(8,128)(2,1)S(1)}, bf16[2,224,128]{2,1,0:T(8,128)(2,1)S(1)}, u32[]{:S(2)}, u32[]{:S(2)}) collective-permute-start(bf16[2,224,128]{2,1,0:T(8,128)(2,1)S(1)} %get-tuple-element.73), channel_id=1, source_target_pairs={{0,6},{1,7},{2,4},{3,5},{4,2},{5,3},{6,0},{7,1},{8,14},{9,15},{10,... | collective-permute-start | bytes 344072 | tf_op jit(solution)/shard_map/ppermute | solution.py:332
  44.4 9.5 %collective-permute-start.14 = (bf16[2,224,128]{2,1,0:T(8,128)(2,1)S(1)}, bf16[2,224,128]{2,1,0:T(8,128)(2,1)S(1)}, u32[]{:S(2)}, u32[]{:S(2)}) collective-permute-start(bf16[2,224,128]{2,1,0:T(8,128)(2,1)S(1)} %pad_maximum_fusion.1), channel_id=1, source_target_pairs={{0,1},{1,0},{2,3},{3,2},{4,5},{5,4},{6,7},{7,6},{8,9},{9,8},{10,11... | collective-permute-start | bytes 344072 | tf_op jit(solution)/shard_map/ppermute | solution.py:335
  54.0 6.4 %collective-permute-start.17 = (bf16[2,224,128]{2,1,0:T(8,128)(2,1)S(1)}, bf16[2,224,128]{2,1,0:T(8,128)(2,1)S(1)}, u32[]{:S(2)}, u32[]{:S(2)}) collective-permute-start(bf16[2,224,128]{2,1,0:T(8,128)(2,1)S(1)} %add_convert_fusion.own_ref), channel_id=1, source_target_pairs={{0,4},{1,5},{2,6},{3,7},{4,0},{5,1},{6,2},{7,3},{8,12},{9,13},{10,... | collective-permute-start | bytes 344072 | tf_op jit(solution)/shard_map/ppermute | solution.py:332
  55.9 6.0 %collective-permute-start.16 = (bf16[2,224,128]{2,1,0:T(8,128)(2,1)S(1)}, bf16[2,224,128]{2,1,0:T(8,128)(2,1)S(1)}, u32[]{:S(2)}, u32[]{:S(2)}) collective-permute-start(bf16[2,224,128]{2,1,0:T(8,128)(2,1)S(1)} %add_convert_fusion.own_ref), channel_id=1, source_target_pairs={{0,6},{1,7},{2,4},{3,5},{4,2},{5,3},{6,0},{7,1},{8,14},{9,15},{10,... | collective-permute-start | bytes 344072 | tf_op jit(solution)/shard_map/ppermute | solution.py:332
  57.9 4.8 %collective-permute-start.15 = (bf16[2,224,128]{2,1,0:T(8,128)(2,1)S(1)}, bf16[2,224,128]{2,1,0:T(8,128)(2,1)S(1)}, u32[]{:S(2)}, u32[]{:S(2)}) collective-permute-start(bf16[2,224,128]{2,1,0:T(8,128)(2,1)S(1)} %add_convert_fusion.own_ref), channel_id=1, source_target_pairs={{0,2},{1,3},{2,0},{3,1},{4,6},{5,7},{6,4},{7,5},{8,10},{9,11},{10,... | collective-permute-start | bytes 344072 | tf_op jit(solution)/shard_map/ppermute | solution.py:332
  64.7 6.4 %collective-permute-start.18 = (bf16[2,224,128]{2,1,0:T(8,128)(2,1)S(1)}, bf16[2,224,128]{2,1,0:T(8,128)(2,1)S(1)}, u32[]{:S(2)}, u32[]{:S(2)}) collective-permute-start(bf16[2,224,128]{2,1,0:T(8,128)(2,1)S(1)} %get-tuple-element.84), channel_id=1, source_target_pairs={{0,4},{1,5},{2,6},{3,7},{4,0},{5,1},{6,2},{7,3},{8,12},{9,13},{10,... | collective-permute-start | bytes 344072 | tf_op jit(solution)/shard_map/ppermute | solution.py:332
  66.5 4.8 %collective-permute-start.19 = (bf16[2,224,128]{2,1,0:T(8,128)(2,1)S(1)}, bf16[2,224,128]{2,1,0:T(8,128)(2,1)S(1)}, u32[]{:S(2)}, u32[]{:S(2)}) collective-permute-start(bf16[2,224,128]{2,1,0:T(8,128)(2,1)S(1)} %get-tuple-element.85), channel_id=1, source_target_pairs={{0,2},{1,3},{2,0},{3,1},{4,6},{5,7},{6,4},{7,5},{8,10},{9,11},{10,... | collective-permute-start | bytes 344072 | tf_op jit(solution)/shard_map/ppermute | solution.py:332
  67.1 6.0 %collective-permute-start.20 = (bf16[2,224,128]{2,1,0:T(8,128)(2,1)S(1)}, bf16[2,224,128]{2,1,0:T(8,128)(2,1)S(1)}, u32[]{:S(2)}, u32[]{:S(2)}) collective-permute-start(bf16[2,224,128]{2,1,0:T(8,128)(2,1)S(1)} %get-tuple-element.86), channel_id=1, source_target_pairs={{0,6},{1,7},{2,4},{3,5},{4,2},{5,3},{6,0},{7,1},{8,14},{9,15},{10,... | collective-permute-start | bytes 344072 | tf_op jit(solution)/shard_map/ppermute | solution.py:332
  73.2 8.2 %collective-permute-start.21 = (bf16[224,128]{1,0:T(8,128)(2,1)S(1)}, bf16[224,128]{1,0:T(8,128)(2,1)S(1)}, u32[]{:S(2)}, u32[]{:S(2)}) collective-permute-start(bf16[224,128]{1,0:T(8,128)(2,1)S(1)} %fusion.4), channel_id=1, source_target_pairs={{0,1},{1,0},{2,3},{3,2},{4,5},{5,4},{6,7},{7,6},{8,9},{9,8},{10,11... | collective-permute-start | bytes 172040 | tf_op jit(solution)/shard_map/ppermute | solution.py:335

commit v9 on v8

--- a/solution.py
+++ b/solution.py
@@ -106,10 +106,11 @@
         out_ref[:, at] = (in_ref[:, at].astype(F32) * gain_ref[j : j + 1, :]).astype(BF16)
 
 
-def ffn_weights_kernel(down_ref, gate_ref, up_ref, gain_ref, turned_ref, gate_out_ref, up_out_ref):
+def ffn_weights_kernel(down_ref, gate_ref, up_ref, gain_ref, turned_ref, both_ref):
+    hidden = gate_ref.shape[0]
     turn_block(down_ref, turned_ref)
-    scale_block(gate_ref, gain_ref, gate_out_ref)
-    scale_block(up_ref, gain_ref, up_out_ref)
+    scale_block(gate_ref, gain_ref, both_ref.at[:hidden])
+    scale_block(up_ref, gain_ref, both_ref.at[hidden:])
 
 
 def mixer_weights_kernel(groups, held, *refs):
@@ -306,12 +307,13 @@
             out[half] = jnp.dot(block, right, preferred_element_type=F32).astype(out.dtype)
 
 
-def ffn_kernel(own_ref, r1_ref, r3_ref, r2_ref, gate_ref, up_ref, down_ref, *rest):
+def ffn_kernel(own_ref, r1_ref, r3_ref, r2_ref, both_ref, down_ref, *rest):
     outs, scratch = rest[:4], rest[4]
     place_blocks(scratch, [own_ref, r1_ref, r2_ref, r3_ref])
     scale = row_scale(scratch)
-    gate = jnp.dot(gate_ref[...], scratch[...], preferred_element_type=F32) * scale
-    up = jnp.dot(up_ref[...], scratch[...], preferred_element_type=F32) * scale
+    hidden = both_ref.shape[0] // 2
+    both = jnp.dot(both_ref[...], scratch[...], preferred_element_type=F32) * scale
+    gate, up = both[:hidden], both[hidden:]
     spread_blocks(outs, down_ref, (silu(gate) * up).astype(BF16))
 
 
@@ -442,20 +444,20 @@
     ffn_shape = ffn_gate.shape[::-1]
     ready = call(
         ffn_weights_kernel,
-        [sds(down_in.shape[::-1], BF16), sds(ffn_shape, BF16), sds(ffn_shape, BF16)],
+        [sds(down_in.shape[::-1], BF16), sds((2 * ffn_shape[0], ffn_shape[1]), BF16)],
         [VMEM] * 4,
         (down_in, ffn_gate.T, ffn_up.T, gain_block(ffn_gain)),
         name="ffn_weights",
     )
     updated = (held_pair.astype(F32) + share + share_peer.astype(F32)).astype(BF16)
-    updated, down_turned, gate_scaled, up_scaled = lax.optimization_barrier((updated, *ready))
+    updated, down_turned, gate_up = lax.optimization_barrier((updated, *ready))
 
     wide = {k: along_x(updated, k) for k in order}
     downs = call(
         ffn_kernel,
         [sds((2, width, tokens), F32)] + [sds((2, width, tokens), BF16)] * 3,
-        [VMEM] * 7,
-        (updated, wide[1], wide[3], wide[2], gate_scaled, up_scaled, down_turned),
+        [VMEM] * 6,
+        (updated, wide[1], wide[3], wide[2], gate_up, down_turned),
         scratch=[pltpu.VMEM((model, tokens), BF16)],
         name="ffn",
     )

time: 82.9 us -> 83.9 us (1.012)
  Pallas kernels: 12.6 us -> 13.7 us
    pallas_call x7, Pallas kernels: 7.76 us -> 8.87 us  [call(): pl.pallas_call(kernel, out_shape=out_shape, in_specs=specs, out_specs=VME...]
  transfers between devices with their start and end apart: 22 -> 22, of which waited for: 14 -> 14; matrix products, arithmetic and copies ran while one was open for 2% -> 2% of each run, Pallas kernels for 10% -> 9%
where the time goes in v9:
time: 83.9 us; the launch traced here: 83.1 us
  starting transfers between devices  39.2 us (47%)
  waiting for transfers between devices  27.8 us (33%)
  Pallas kernels  13.7 us (16%)
  local copies, waits for them, and re-layouts  1.35 us (2%)
  other arithmetic  0.91 us (1%)
    ppermute x12, waiting for transfers between devices, along_x(): return lax.ppermute(array, 'tp', [(i, i ^ 2 * k) for i in range(tp_size)])  17.6 us
    ppermute x12, starting transfers between devices, along_x(): return lax.ppermute(array, 'tp', [(i, i ^ 2 * k) for i in range(tp_size)])  16.8 us
    ppermute x3, starting transfers between devices, across_z(): return lax.ppermute(array, 'tp', [(i, i ^ 1) for i in range(tp_size)])  12.7 us
    ppermute x3, waiting for transfers between devices, across_z(): return lax.ppermute(array, 'tp', [(i, i ^ 1) for i in range(tp_size)])  10.1 us
    pallas_call x7, Pallas kernels, call(): pl.pallas_call(kernel, out_shape=out_shape, in_specs=specs, out_specs=VME...  8.87 us
    ppermute x3, starting transfers between devices, along_z(): return lax.ppermute(array, 'req', [(i, i ^ 2 * k) for i in range(req_size)])  5.37 us
    ppermute x3, starting transfers between devices, along_y(): lax.ppermute(array, 'req', [(i, i ^ 2 * z_size * k) for i in range(req_si...  4.18 us
    pallas_call x1, Pallas kernels, shards(): pl.pallas_call(functools.partial(mixer_weights_kernel, y_size, z_size), o...  3.24 us
  transfers between devices with their start and end apart: 22, of which 14 were waited for; matrix products, arithmetic and copies ran while one was open for 2% of the time, Pallas kernels for 9%

profile of v9, /device:TPU:8, one launch (start us, length us, event | category | flops | bytes accessed | tf_op | source)
XLA Modules:
  0.0 83.1 jit_solution(2126147413106479990)
XLA Ops:
  0.0 1.6 %fold.1 = (bf16[2,160,128]{2,1,0:T(8,128)(2,1)S(1)}, bf16[224,128]{1,0:T(8,128)(2,1)S(1)}) custom-call(bf16[160,273]{1,0:T(8,128)(2,1)} %constant.5.clone.fold_hbm, bf16[273,2,112]{2,1,0:T(2,128)(2,1)} %bitcast.37, bf16[2,273]{1,0:T(2,128)(2,1)} %bitcast.47, bf16[2,224]{1,0:T(2,128)(2,1)} %bitcast.48, bf16[224,128]{1,0:T(8,128)(2,1)} %bitcast.43), custom_call_target="tpu_custom_call" | custom-call | tf_op jit(solution)/shard_map/fold/pallas_call | solution.py:358
  1.6 4.7 %collective-permute-start.3 = (bf16[2,160,128]{2,1,0:T(8,128)(2,1)S(1)}, bf16[2,160,128]{2,1,0:T(8,128)(2,1)S(1)}, u32[]{:S(2)}, u32[]{:S(2)}) collective-permute-start(bf16[2,160,128]{2,1,0:T(8,128)(2,1)S(1)} %get-tuple-element.46), channel_id=1, source_target_pairs={{0,48},{8,56},{16,32},{24,40},{32,16},{40,24},{48,0},{56,8},{64,11... | collective-permute-start | bytes 245768 | tf_op jit(solution)/shard_map/ppermute | solution.py:340
  7.0 6.3 %collective-permute-start = (bf16[224,128]{1,0:T(8,128)(2,1)}, bf16[224,128]{1,0:T(8,128)(2,1)S(1)}, u32[]{:S(2)}, u32[]{:S(2)}) collective-permute-start(bf16[224,128]{1,0:T(8,128)(2,1)} %bitcast.44), channel_id=1, source_target_pairs={{0,1},{1,0},{2,3},{3,2},{4,5},{5,4},{6,7},{7,6},{8,9},{9,8},{10,11... | collective-permute-start | bytes 172040 | tf_op jit(solution)/shard_map/ppermute | solution.py:337
  13.3 1.3 %pad.7.refs_8_ = f32[16,128]{1,0:T(8,128)} pad(f32[14,128]{1,0:T(8,128)} %bitcast.45, f32[]{:T(128)} %constant.4.clone.1), padding=0_2x0_0 | pad | bytes 15364 | tf_op jit(solution)/shard_map/jit(_pad)/pad | solution.py:370
  14.6 3.2 %mixer_weights.1 = (bf16[1792,224]{1,0:T(8,128)(2,1)S(1)}, s32[24]{0:T(128)S(1)}, bf16[512,1792]{1,0:T(8,128)(2,1)S(1)}) custom-call(bf16[224,1792]{1,0:T(8,128)(2,1)} %refs_0_.1, s32[64]{0:T(128)} %refs_1_.1, s32[32]{0:T(128)} %refs_2_.1, s32[32]{0:T(128)} %refs_3_.1, bf16[32,1792]{1,0:T(8,128)(2,1)} %bitcast.38, bf16[32,1792]{1,0:T(8,128)(2,1)} %bitcast.39, ...), custom_call_target="tpu_custom_call" | custom-call | tf_op jit(solution)/shard_map/mixer_weights/pallas_call | solution.py:374
  18.7 3.1 %collective-permute-start.6 = (bf16[2,224,128]{2,1,0:T(8,128)(2,1)S(1)}, bf16[2,224,128]{2,1,0:T(8,128)(2,1)S(1)}, u32[]{:S(2)}, u32[]{:S(2)}) collective-permute-start(bf16[2,224,128]{2,1,0:T(8,128)(2,1)S(1)} %stack_pair.1.own_ref), channel_id=1, source_target_pairs={{0,4},{1,5},{2,6},{3,7},{4,0},{5,1},{6,2},{7,3},{8,12},{9,13},{10,... | collective-permute-start | bytes 344072 | tf_op jit(solution)/shard_map/ppermute | solution.py:334
  21.8 1.0 %select_sent.1 = (bf16[2,2,160,128]{3,2,1,0:T(8,128)(2,1)S(1)}, bf16[2,2,160,128]{3,2,1,0:T(8,128)(2,1)S(1)}, bf16[2,2,160,128]{3,2,1,0:T(8,128)(2,1)S(1)}) custom-call(s32[24]{0:T(128)S(1)} %get-tuple-element.49.slot_ref, bf16[4,2,160,128]{3,2,1,0:T(8,128)(2,1)S(1)} %pad_maximum_fusion.mine_ref, bf16[4,2,160,128]{3,2,1,0:T(8,128)(2,1)S(1)} %collective-permute-done.7.other_ref), custom_call_target="tpu_custom_call" | custom-call | tf_op jit(solution)/shard_map/select_sent/pallas_call | solution.py:25
  22.8 2.4 %collective-permute-start.8 = (bf16[2,2,160,128]{3,2,1,0:T(8,128)(2,1)S(1)}, bf16[2,2,160,128]{3,2,1,0:T(8,128)(2,1)S(1)}, u32[]{:S(2)}, u32[]{:S(2)}) collective-permute-start(bf16[2,2,160,128]{3,2,1,0:T(8,128)(2,1)S(1)} %get-tuple-element.64), channel_id=1, source_target_pairs={{0,128},{8,136},{16,144},{24,152},{32,160},{40,168},{48,176},{56,1... | collective-permute-start | bytes 491528 | tf_op jit(solution)/shard_map/ppermute | solution.py:346
  25.2 1.3 %collective-permute-start.9 = (bf16[2,2,160,128]{3,2,1,0:T(8,128)(2,1)S(1)}, bf16[2,2,160,128]{3,2,1,0:T(8,128)(2,1)S(1)}, u32[]{:S(2)}, u32[]{:S(2)}) collective-permute-start(bf16[2,2,160,128]{3,2,1,0:T(8,128)(2,1)S(1)} %get-tuple-element.65), channel_id=1, source_target_pairs={{0,64},{8,72},{16,80},{24,88},{32,96},{40,104},{48,112},{56,120},{... | collective-permute-start | bytes 491528 | tf_op jit(solution)/shard_map/ppermute | solution.py:346
  27.0 1.3 %collective-permute-start.5 = (bf16[2,224,128]{2,1,0:T(8,128)(2,1)S(1)}, bf16[2,224,128]{2,1,0:T(8,128)(2,1)S(1)}, u32[]{:S(2)}, u32[]{:S(2)}) collective-permute-start(bf16[2,224,128]{2,1,0:T(8,128)(2,1)S(1)} %stack_pair.1.own_ref), channel_id=1, source_target_pairs={{0,6},{1,7},{2,4},{3,5},{4,2},{5,3},{6,0},{7,1},{8,14},{9,15},{10,... | collective-permute-start | bytes 344072 | tf_op jit(solution)/shard_map/ppermute | solution.py:334
  29.2 3.8 %collective-permute-done.5.r3_ref = bf16[2,224,128]{2,1,0:T(8,128)(2,1)S(1)} collective-permute-done((bf16[2,224,128]{2,1,0:T(8,128)(2,1)S(1)}, bf16[2,224,128]{2,1,0:T(8,128)(2,1)S(1)}, u32[]{:S(2)}, u32[]{:S(2)}) %collective-permute-start.5) | collective-permute-done | bytes 114720 | tf_op jit(solution)/shard_map/ppermute | solution.py:334
  33.0 1.1 %local.1 = (f32[224,128]{1,0:T(8,128)S(1)}, f32[224,128]{1,0:T(8,128)S(1)}, bf16[2,128,128]{2,1,0:T(8,128)(2,1)S(1)}, f32[2,1,128]{2,1,0:T(1,128)S(1)}, bf16[2,3...) custom-call(bf16[2,224,128]{2,1,0:T(8,128)(2,1)S(1)} %stack_pair.1.own_ref, ...), custom_call_target="tpu_custom_call" | custom-call | tf_op jit(solution)/shard_map/local/pallas_call | solution.py:25
  34.3 1.1 %mix.1 = (f32[2,224,128]{2,1,0:T(8,128)S(1)}, bf16[2,224,128]{2,1,0:T(8,128)(2,1)S(1)}, bf16[2,224,128]{2,1,0:T(8,128)(2,1)S(1)}, bf16[2,224,128]{2,1,0:T(8,128)(2,1)S(1)}) custom-call(f32[224,128]{1,0:T(8,128)S(1)} %get-tuple-element.58.conv_ref, f32[224,128]{1,0:T(8,128)S(1)} %get-tuple-element.59.silu_ref, ...), custom_call_target="tpu_custom_call" | custom-call | tf_op jit(solution)/shard_map/mix/pallas_call | solution.py:25
  35.4 1.6 %collective-permute-start.11 = (bf16[2,224,128]{2,1,0:T(8,128)(2,1)S(1)}, bf16[2,224,128]{2,1,0:T(8,128)(2,1)S(1)}, u32[]{:S(2)}, u32[]{:S(2)}) collective-permute-start(bf16[2,224,128]{2,1,0:T(8,128)(2,1)S(1)} %get-tuple-element.69), channel_id=1, source_target_pairs={{0,4},{1,5},{2,6},{3,7},{4,0},{5,1},{6,2},{7,3},{8,12},{9,13},{10,... | collective-permute-start | bytes 344072 | tf_op jit(solution)/shard_map/ppermute | solution.py:334
  37.0 1.3 %collective-permute-start.12 = (bf16[2,224,128]{2,1,0:T(8,128)(2,1)S(1)}, bf16[2,224,128]{2,1,0:T(8,128)(2,1)S(1)}, u32[]{:S(2)}, u32[]{:S(2)}) collective-permute-start(bf16[2,224,128]{2,1,0:T(8,128)(2,1)S(1)} %get-tuple-element.70), channel_id=1, source_target_pairs={{0,2},{1,3},{2,0},{3,1},{4,6},{5,7},{6,4},{7,5},{8,10},{9,11},{10,... | collective-permute-start | bytes 344072 | tf_op jit(solution)/shard_map/ppermute | solution.py:334
  38.2 1.3 %collective-permute-start.13 = (bf16[2,224,128]{2,1,0:T(8,128)(2,1)S(1)}, bf16[2,224,128]{2,1,0:T(8,128)(2,1)S(1)}, u32[]{:S(2)}, u32[]{:S(2)}) collective-permute-start(bf16[2,224,128]{2,1,0:T(8,128)(2,1)S(1)} %get-tuple-element.71), channel_id=1, source_target_pairs={{0,6},{1,7},{2,4},{3,5},{4,2},{5,3},{6,0},{7,1},{8,14},{9,15},{10,... | collective-permute-start | bytes 344072 | tf_op jit(solution)/shard_map/ppermute | solution.py:334
  39.6 3.4 %collective-permute-done.11 = bf16[2,224,128]{2,1,0:T(8,128)(2,1)S(1)} collective-permute-done((bf16[2,224,128]{2,1,0:T(8,128)(2,1)S(1)}, bf16[2,224,128]{2,1,0:T(8,128)(2,1)S(1)}, u32[]{:S(2)}, u32[]{:S(2)}) %collective-permute-start.11) | collective-permute-done | bytes 114720 | tf_op jit(solution)/shard_map/ppermute | solution.py:334
  43.0 1.3 %collective-permute-done.13 = bf16[2,224,128]{2,1,0:T(8,128)(2,1)S(1)} collective-permute-done((bf16[2,224,128]{2,1,0:T(8,128)(2,1)S(1)}, bf16[2,224,128]{2,1,0:T(8,128)(2,1)S(1)}, u32[]{:S(2)}, u32[]{:S(2)}) %collective-permute-start.13) | collective-permute-done | bytes 114720 | tf_op jit(solution)/shard_map/ppermute | solution.py:334
  44.4 3.5 %collective-permute-start.14 = (bf16[2,224,128]{2,1,0:T(8,128)(2,1)S(1)}, bf16[2,224,128]{2,1,0:T(8,128)(2,1)S(1)}, u32[]{:S(2)}, u32[]{:S(2)}) collective-permute-start(bf16[2,224,128]{2,1,0:T(8,128)(2,1)S(1)} %pad_maximum_fusion.1), channel_id=1, source_target_pairs={{0,1},{1,0},{2,3},{3,2},{4,5},{5,4},{6,7},{7,6},{8,9},{9,8},{10,11... | collective-permute-start | bytes 344072 | tf_op jit(solution)/shard_map/ppermute | solution.py:337
  47.9 1.8 %ffn_weights.1 = (bf16[1792,608]{1,0:T(8,128)(2,1)S(1)}, bf16[1216,1792]{1,0:T(8,128)(2,1)S(1)}) custom-call(bf16[608,1792]{1,0:T(8,128)(2,1)S(1)} %copy-done, bf16[608,1792]{1,0:T(8,128)(2,1)S(1)} %bitcast.31, bf16[608,1792]{1,0:T(8,128)(2,1)S(1)} %bitcast.32, f32[16,128]{1,0:T(8,128)S(1)} %pad.8.gain_ref), custom_call_target="tpu_custom_call" | custom-call | tf_op jit(solution)/shard_map/ffn_weights/pallas_call | solution.py:25
  49.7 4.2 %collective-permute-done.14 = bf16[2,224,128]{2,1,0:T(8,128)(2,1)S(1)} collective-permute-done((bf16[2,224,128]{2,1,0:T(8,128)(2,1)S(1)}, bf16[2,224,128]{2,1,0:T(8,128)(2,1)S(1)}, u32[]{:S(2)}, u32[]{:S(2)}) %collective-permute-start.14) | collective-permute-done | bytes 114720 | tf_op jit(solution)/shard_map/ppermute | solution.py:337
  54.0 1.9 %collective-permute-start.17 = (bf16[2,224,128]{2,1,0:T(8,128)(2,1)S(1)}, bf16[2,224,128]{2,1,0:T(8,128)(2,1)S(1)}, u32[]{:S(2)}, u32[]{:S(2)}) collective-permute-start(bf16[2,224,128]{2,1,0:T(8,128)(2,1)S(1)} %add_convert_fusion.own_ref), channel_id=1, source_target_pairs={{0,4},{1,5},{2,6},{3,7},{4,0},{5,1},{6,2},{7,3},{8,12},{9,13},{10,... | collective-permute-start | bytes 344072 | tf_op jit(solution)/shard_map/ppermute | solution.py:334
  55.9 1.9 %collective-permute-start.16 = (bf16[2,224,128]{2,1,0:T(8,128)(2,1)S(1)}, bf16[2,224,128]{2,1,0:T(8,128)(2,1)S(1)}, u32[]{:S(2)}, u32[]{:S(2)}) collective-permute-start(bf16[2,224,128]{2,1,0:T(8,128)(2,1)S(1)} %add_convert_fusion.own_ref), channel_id=1, source_target_pairs={{0,6},{1,7},{2,4},{3,5},{4,2},{5,3},{6,0},{7,1},{8,14},{9,15},{10,... | collective-permute-start | bytes 344072 | tf_op jit(solution)/shard_map/ppermute | solution.py:334
  57.9 2.6 %collective-permute-done.17.r2_ref = bf16[2,224,128]{2,1,0:T(8,128)(2,1)S(1)} collective-permute-done((bf16[2,224,128]{2,1,0:T(8,128)(2,1)S(1)}, bf16[2,224,128]{2,1,0:T(8,128)(2,1)S(1)}, u32[]{:S(2)}, u32[]{:S(2)}) %collective-permute-start.17) | collective-permute-done | bytes 114720 | tf_op jit(solution)/shard_map/ppermute | solution.py:334
  60.4 1.5 %collective-permute-done.16.r3_ref = bf16[2,224,128]{2,1,0:T(8,128)(2,1)S(1)} collective-permute-done((bf16[2,224,128]{2,1,0:T(8,128)(2,1)S(1)}, bf16[2,224,128]{2,1,0:T(8,128)(2,1)S(1)}, u32[]{:S(2)}, u32[]{:S(2)}) %collective-permute-start.16) | collective-permute-done | bytes 114720 | tf_op jit(solution)/shard_map/ppermute | solution.py:334
  62.7 3.2 %ffn.1 = (f32[2,224,128]{2,1,0:T(8,128)S(1)}, bf16[2,224,128]{2,1,0:T(8,128)(2,1)S(1)}, bf16[2,224,128]{2,1,0:T(8,128)(2,1)S(1)}, bf16[2,224,128]{2,1,0:T(8,128)(2,1)S(1)}) custom-call(bf16[2,224,128]{2,1,0:T(8,128)(2,1)S(1)} %add_convert_fusion.own_ref, bf16[2,224,128]{2,1,0:T(8,128)(2,1)S(1)} %collective-permute-done.15.r1_ref, ...), custom_call_target="tpu_custom_call" | custom-call | tf_op jit(solution)/shard_map/ffn/pallas_call | solution.py:25
  65.8 1.7 %collective-permute-start.18 = (bf16[2,224,128]{2,1,0:T(8,128)(2,1)S(1)}, bf16[2,224,128]{2,1,0:T(8,128)(2,1)S(1)}, u32[]{:S(2)}, u32[]{:S(2)}) collective-permute-start(bf16[2,224,128]{2,1,0:T(8,128)(2,1)S(1)} %get-tuple-element.80), channel_id=1, source_target_pairs={{0,4},{1,5},{2,6},{3,7},{4,0},{5,1},{6,2},{7,3},{8,12},{9,13},{10,... | collective-permute-start | bytes 344072 | tf_op jit(solution)/shard_map/ppermute | solution.py:334
  68.2 1.8 %collective-permute-start.20 = (bf16[2,224,128]{2,1,0:T(8,128)(2,1)S(1)}, bf16[2,224,128]{2,1,0:T(8,128)(2,1)S(1)}, u32[]{:S(2)}, u32[]{:S(2)}) collective-permute-start(bf16[2,224,128]{2,1,0:T(8,128)(2,1)S(1)} %get-tuple-element.82), channel_id=1, source_target_pairs={{0,6},{1,7},{2,4},{3,5},{4,2},{5,3},{6,0},{7,1},{8,14},{9,15},{10,... | collective-permute-start | bytes 344072 | tf_op jit(solution)/shard_map/ppermute | solution.py:334
  70.0 2.2 %collective-permute-done.18 = bf16[2,224,128]{2,1,0:T(8,128)(2,1)S(1)} collective-permute-done((bf16[2,224,128]{2,1,0:T(8,128)(2,1)S(1)}, bf16[2,224,128]{2,1,0:T(8,128)(2,1)S(1)}, u32[]{:S(2)}, u32[]{:S(2)}) %collective-permute-start.18) | collective-permute-done | bytes 114720 | tf_op jit(solution)/shard_map/ppermute | solution.py:334
  72.4 1.9 %collective-permute-done.20 = bf16[2,224,128]{2,1,0:T(8,128)(2,1)S(1)} collective-permute-done((bf16[2,224,128]{2,1,0:T(8,128)(2,1)S(1)}, bf16[2,224,128]{2,1,0:T(8,128)(2,1)S(1)}, u32[]{:S(2)}, u32[]{:S(2)}) %collective-permute-start.20) | collective-permute-done | bytes 114720 | tf_op jit(solution)/shard_map/ppermute | solution.py:334
  74.3 2.9 %collective-permute-start.21 = (bf16[224,128]{1,0:T(8,128)(2,1)S(1)}, bf16[224,128]{1,0:T(8,128)(2,1)S(1)}, u32[]{:S(2)}, u32[]{:S(2)}) collective-permute-start(bf16[224,128]{1,0:T(8,128)(2,1)S(1)} %fusion.4), channel_id=1, source_target_pairs={{0,1},{1,0},{2,3},{3,2},{4,5},{5,4},{6,7},{7,6},{8,9},{9,8},{10,11... | collective-permute-start | bytes 172040 | tf_op jit(solution)/shard_map/ppermute | solution.py:337
  77.3 5.2 %collective-permute-done.21 = bf16[224,128]{1,0:T(8,128)(2,1)S(1)} collective-permute-done((bf16[224,128]{1,0:T(8,128)(2,1)S(1)}, bf16[224,128]{1,0:T(8,128)(2,1)S(1)}, u32[]{:S(2)}, u32[]{:S(2)}) %collective-permute-start.21) | collective-permute-done | bytes 57376 | tf_op jit(solution)/shard_map/ppermute | solution.py:337
  (43 shorter events, 5.5 us)
Async XLA Ops:
  1.6 16.9 %collective-permute-start.3 = (bf16[2,160,128]{2,1,0:T(8,128)(2,1)S(1)}, bf16[2,160,128]{2,1,0:T(8,128)(2,1)S(1)}, u32[]{:S(2)}, u32[]{:S(2)}) collective-permute-start(bf16[2,160,128]{2,1,0:T(8,128)(2,1)S(1)} %get-tuple-element.46), channel_id=1, source_target_pairs={{0,48},{8,56},{16,32},{24,40},{32,16},{40,24},{48,0},{56,8},{64,11... | collective-permute-start | bytes 245768 | tf_op jit(solution)/shard_map/ppermute | solution.py:340
  6.3 12.2 %collective-permute-start.2 = (bf16[2,160,128]{2,1,0:T(8,128)(2,1)S(1)}, bf16[2,160,128]{2,1,0:T(8,128)(2,1)S(1)}, u32[]{:S(2)}, u32[]{:S(2)}) collective-permute-start(bf16[2,160,128]{2,1,0:T(8,128)(2,1)S(1)} %get-tuple-element.46), channel_id=1, source_target_pairs={{0,32},{8,40},{16,48},{24,56},{32,0},{40,8},{48,16},{56,24},{64,96... | collective-permute-start | bytes 245768 | tf_op jit(solution)/shard_map/ppermute | solution.py:340
  6.3 12.2 %collective-permute-start.1 = (bf16[2,160,128]{2,1,0:T(8,128)(2,1)S(1)}, bf16[2,160,128]{2,1,0:T(8,128)(2,1)S(1)}, u32[]{:S(2)}, u32[]{:S(2)}) collective-permute-start(bf16[2,160,128]{2,1,0:T(8,128)(2,1)S(1)} %get-tuple-element.46), channel_id=1, source_target_pairs={{0,16},{8,24},{16,0},{24,8},{32,48},{40,56},{48,32},{56,40},{64,80... | collective-permute-start | bytes 245768 | tf_op jit(solution)/shard_map/ppermute | solution.py:340
  7.0 11.5 %collective-permute-start = (bf16[224,128]{1,0:T(8,128)(2,1)}, bf16[224,128]{1,0:T(8,128)(2,1)S(1)}, u32[]{:S(2)}, u32[]{:S(2)}) collective-permute-start(bf16[224,128]{1,0:T(8,128)(2,1)} %bitcast.44), channel_id=1, source_target_pairs={{0,1},{1,0},{2,3},{3,2},{4,5},{5,4},{6,7},{7,6},{8,9},{9,8},{10,11... | collective-permute-start | bytes 172040 | tf_op jit(solution)/shard_map/ppermute | solution.py:337
  14.6 18.5 %copy-start.3 = (f32[3,224]{1,0:T(4,128)S(1)}, f32[3,224]{1,0:T(4,128)}, u32[]{:S(2)}) copy-start(f32[3,224]{1,0:T(4,128)} %taps_ref.1) | copy-start | bytes 8068
  14.6 18.5 %copy-start.4 = (s32[128]{0:T(128)S(1)}, s32[128]{0:T(128)}, u32[]{:S(2)}) copy-start(s32[128]{0:T(128)} %param.21) | copy-start | bytes 1540
  18.6 3.2 %collective-permute-start.7 = (bf16[4,2,160,128]{3,2,1,0:T(8,128)(2,1)S(1)}, bf16[4,2,160,128]{3,2,1,0:T(8,128)(2,1)S(1)}, u32[]{:S(2)}, u32[]{:S(2)}) collective-permute-start(bf16[4,2,160,128]{3,2,1,0:T(8,128)(2,1)S(1)} %pad_maximum_fusion.mine_ref), channel_id=1, source_target_pairs={{0,8},{8,0},{16,24},{24,16},{32,40},{40,32},{48,56},{56,48},{64,72... | collective-permute-start | bytes 983048 | tf_op jit(solution)/shard_map/ppermute | solution.py:343
  18.7 9.5 %collective-permute-start.6 = (bf16[2,224,128]{2,1,0:T(8,128)(2,1)S(1)}, bf16[2,224,128]{2,1,0:T(8,128)(2,1)S(1)}, u32[]{:S(2)}, u32[]{:S(2)}) collective-permute-start(bf16[2,224,128]{2,1,0:T(8,128)(2,1)S(1)} %stack_pair.1.own_ref), channel_id=1, source_target_pairs={{0,4},{1,5},{2,6},{3,7},{4,0},{5,1},{6,2},{7,3},{8,12},{9,13},{10,... | collective-permute-start | bytes 344072 | tf_op jit(solution)/shard_map/ppermute | solution.py:334
  22.8 11.4 %collective-permute-start.8 = (bf16[2,2,160,128]{3,2,1,0:T(8,128)(2,1)S(1)}, bf16[2,2,160,128]{3,2,1,0:T(8,128)(2,1)S(1)}, u32[]{:S(2)}, u32[]{:S(2)}) collective-permute-start(bf16[2,2,160,128]{3,2,1,0:T(8,128)(2,1)S(1)} %get-tuple-element.64), channel_id=1, source_target_pairs={{0,128},{8,136},{16,144},{24,152},{32,160},{40,168},{48,176},{56,1... | collective-permute-start | bytes 491528 | tf_op jit(solution)/shard_map/ppermute | solution.py:346
  25.2 9.1 %collective-permute-start.9 = (bf16[2,2,160,128]{3,2,1,0:T(8,128)(2,1)S(1)}, bf16[2,2,160,128]{3,2,1,0:T(8,128)(2,1)S(1)}, u32[]{:S(2)}, u32[]{:S(2)}) collective-permute-start(bf16[2,2,160,128]{3,2,1,0:T(8,128)(2,1)S(1)} %get-tuple-element.65), channel_id=1, source_target_pairs={{0,64},{8,72},{16,80},{24,88},{32,96},{40,104},{48,112},{56,120},{... | collective-permute-start | bytes 491528 | tf_op jit(solution)/shard_map/ppermute | solution.py:346
  26.5 7.8 %collective-permute-start.10 = (bf16[2,2,160,128]{3,2,1,0:T(8,128)(2,1)S(1)}, bf16[2,2,160,128]{3,2,1,0:T(8,128)(2,1)S(1)}, u32[]{:S(2)}, u32[]{:S(2)}) collective-permute-start(bf16[2,2,160,128]{3,2,1,0:T(8,128)(2,1)S(1)} %get-tuple-element.66), channel_id=1, source_target_pairs={{0,192},{8,200},{16,208},{24,216},{32,224},{40,232},{48,240},{56,2... | collective-permute-start | bytes 491528 | tf_op jit(solution)/shard_map/ppermute | solution.py:346
  27.0 6.0 %collective-permute-start.5 = (bf16[2,224,128]{2,1,0:T(8,128)(2,1)S(1)}, bf16[2,224,128]{2,1,0:T(8,128)(2,1)S(1)}, u32[]{:S(2)}, u32[]{:S(2)}) collective-permute-start(bf16[2,224,128]{2,1,0:T(8,128)(2,1)S(1)} %stack_pair.1.own_ref), channel_id=1, source_target_pairs={{0,6},{1,7},{2,4},{3,5},{4,2},{5,3},{6,0},{7,1},{8,14},{9,15},{10,... | collective-permute-start | bytes 344072 | tf_op jit(solution)/shard_map/ppermute | solution.py:334
  28.2 4.8 %collective-permute-start.4 = (bf16[2,224,128]{2,1,0:T(8,128)(2,1)S(1)}, bf16[2,224,128]{2,1,0:T(8,128)(2,1)S(1)}, u32[]{:S(2)}, u32[]{:S(2)}) collective-permute-start(bf16[2,224,128]{2,1,0:T(8,128)(2,1)S(1)} %stack_pair.1.own_ref), channel_id=1, source_target_pairs={{0,2},{1,3},{2,0},{3,1},{4,6},{5,7},{6,4},{7,5},{8,10},{9,11},{10,... | collective-permute-start | bytes 344072 | tf_op jit(solution)/shard_map/ppermute | solution.py:334
  28.5 19.4 %copy-start.2 = (bf16[1792,608]{0,1:T(8,128)(2,1)S(1)}, bf16[1792,608]{0,1:T(8,128)(2,1)}, u32[]{:S(2)}) copy-start(bf16[1792,608]{0,1:T(8,128)(2,1)} %param.37) | copy-start | bytes 6537220
  33.0 14.9 %copy-start.1 = (bf16[1792,608]{0,1:T(8,128)(2,1)S(1)}, bf16[1792,608]{0,1:T(8,128)(2,1)}, u32[]{:S(2)}) copy-start(bf16[1792,608]{0,1:T(8,128)(2,1)} %param.36) | copy-start | bytes 6537220
  34.2 13.7 %copy-start.5 = (f32[1792]{0:T(1024)S(1)}, f32[1792]{0:T(1024)}, u32[]{:S(2)}) copy-start(f32[1792]{0:T(1024)} %param.29) | copy-start | bytes 21508
  34.2 13.7 %copy-start = (bf16[608,1792]{1,0:T(8,128)(2,1)S(1)}, bf16[608,1792]{1,0:T(8,128)(2,1)}, u32[]{:S(2)}) copy-start(bf16[608,1792]{1,0:T(8,128)(2,1)} %down_ref) | copy-start | bytes 6537220
  35.4 7.6 %collective-permute-start.11 = (bf16[2,224,128]{2,1,0:T(8,128)(2,1)S(1)}, bf16[2,224,128]{2,1,0:T(8,128)(2,1)S(1)}, u32[]{:S(2)}, u32[]{:S(2)}) collective-permute-start(bf16[2,224,128]{2,1,0:T(8,128)(2,1)S(1)} %get-tuple-element.69), channel_id=1, source_target_pairs={{0,4},{1,5},{2,6},{3,7},{4,0},{5,1},{6,2},{7,3},{8,12},{9,13},{10,... | collective-permute-start | bytes 344072 | tf_op jit(solution)/shard_map/ppermute | solution.py:334
  37.0 6.0 %collective-permute-start.12 = (bf16[2,224,128]{2,1,0:T(8,128)(2,1)S(1)}, bf16[2,224,128]{2,1,0:T(8,128)(2,1)S(1)}, u32[]{:S(2)}, u32[]{:S(2)}) collective-permute-start(bf16[2,224,128]{2,1,0:T(8,128)(2,1)S(1)} %get-tuple-element.70), channel_id=1, source_target_pairs={{0,2},{1,3},{2,0},{3,1},{4,6},{5,7},{6,4},{7,5},{8,10},{9,11},{10,... | collective-permute-start | bytes 344072 | tf_op jit(solution)/shard_map/ppermute | solution.py:334
  38.2 6.1 %collective-permute-start.13 = (bf16[2,224,128]{2,1,0:T(8,128)(2,1)S(1)}, bf16[2,224,128]{2,1,0:T(8,128)(2,1)S(1)}, u32[]{:S(2)}, u32[]{:S(2)}) collective-permute-start(bf16[2,224,128]{2,1,0:T(8,128)(2,1)S(1)} %get-tuple-element.71), channel_id=1, source_target_pairs={{0,6},{1,7},{2,4},{3,5},{4,2},{5,3},{6,0},{7,1},{8,14},{9,15},{10,... | collective-permute-start | bytes 344072 | tf_op jit(solution)/shard_map/ppermute | solution.py:334
  44.4 9.5 %collective-permute-start.14 = (bf16[2,224,128]{2,1,0:T(8,128)(2,1)S(1)}, bf16[2,224,128]{2,1,0:T(8,128)(2,1)S(1)}, u32[]{:S(2)}, u32[]{:S(2)}) collective-permute-start(bf16[2,224,128]{2,1,0:T(8,128)(2,1)S(1)} %pad_maximum_fusion.1), channel_id=1, source_target_pairs={{0,1},{1,0},{2,3},{3,2},{4,5},{5,4},{6,7},{7,6},{8,9},{9,8},{10,11... | collective-permute-start | bytes 344072 | tf_op jit(solution)/shard_map/ppermute | solution.py:337
  54.0 6.4 %collective-permute-start.17 = (bf16[2,224,128]{2,1,0:T(8,128)(2,1)S(1)}, bf16[2,224,128]{2,1,0:T(8,128)(2,1)S(1)}, u32[]{:S(2)}, u32[]{:S(2)}) collective-permute-start(bf16[2,224,128]{2,1,0:T(8,128)(2,1)S(1)} %add_convert_fusion.own_ref), channel_id=1, source_target_pairs={{0,4},{1,5},{2,6},{3,7},{4,0},{5,1},{6,2},{7,3},{8,12},{9,13},{10,... | collective-permute-start | bytes 344072 | tf_op jit(solution)/shard_map/ppermute | solution.py:334
  55.9 6.0 %collective-permute-start.16 = (bf16[2,224,128]{2,1,0:T(8,128)(2,1)S(1)}, bf16[2,224,128]{2,1,0:T(8,128)(2,1)S(1)}, u32[]{:S(2)}, u32[]{:S(2)}) collective-permute-start(bf16[2,224,128]{2,1,0:T(8,128)(2,1)S(1)} %add_convert_fusion.own_ref), channel_id=1, source_target_pairs={{0,6},{1,7},{2,4},{3,5},{4,2},{5,3},{6,0},{7,1},{8,14},{9,15},{10,... | collective-permute-start | bytes 344072 | tf_op jit(solution)/shard_map/ppermute | solution.py:334
  57.9 4.8 %collective-permute-start.15 = (bf16[2,224,128]{2,1,0:T(8,128)(2,1)S(1)}, bf16[2,224,128]{2,1,0:T(8,128)(2,1)S(1)}, u32[]{:S(2)}, u32[]{:S(2)}) collective-permute-start(bf16[2,224,128]{2,1,0:T(8,128)(2,1)S(1)} %add_convert_fusion.own_ref), channel_id=1, source_target_pairs={{0,2},{1,3},{2,0},{3,1},{4,6},{5,7},{6,4},{7,5},{8,10},{9,11},{10,... | collective-permute-start | bytes 344072 | tf_op jit(solution)/shard_map/ppermute | solution.py:334
  65.8 6.4 %collective-permute-start.18 = (bf16[2,224,128]{2,1,0:T(8,128)(2,1)S(1)}, bf16[2,224,128]{2,1,0:T(8,128)(2,1)S(1)}, u32[]{:S(2)}, u32[]{:S(2)}) collective-permute-start(bf16[2,224,128]{2,1,0:T(8,128)(2,1)S(1)} %get-tuple-element.80), channel_id=1, source_target_pairs={{0,4},{1,5},{2,6},{3,7},{4,0},{5,1},{6,2},{7,3},{8,12},{9,13},{10,... | collective-permute-start | bytes 344072 | tf_op jit(solution)/shard_map/ppermute | solution.py:334
  67.6 4.8 %collective-permute-start.19 = (bf16[2,224,128]{2,1,0:T(8,128)(2,1)S(1)}, bf16[2,224,128]{2,1,0:T(8,128)(2,1)S(1)}, u32[]{:S(2)}, u32[]{:S(2)}) collective-permute-start(bf16[2,224,128]{2,1,0:T(8,128)(2,1)S(1)} %get-tuple-element.81), channel_id=1, source_target_pairs={{0,2},{1,3},{2,0},{3,1},{4,6},{5,7},{6,4},{7,5},{8,10},{9,11},{10,... | collective-permute-start | bytes 344072 | tf_op jit(solution)/shard_map/ppermute | solution.py:334
  68.2 6.0 %collective-permute-start.20 = (bf16[2,224,128]{2,1,0:T(8,128)(2,1)S(1)}, bf16[2,224,128]{2,1,0:T(8,128)(2,1)S(1)}, u32[]{:S(2)}, u32[]{:S(2)}) collective-permute-start(bf16[2,224,128]{2,1,0:T(8,128)(2,1)S(1)} %get-tuple-element.82), channel_id=1, source_target_pairs={{0,6},{1,7},{2,4},{3,5},{4,2},{5,3},{6,0},{7,1},{8,14},{9,15},{10,... | collective-permute-start | bytes 344072 | tf_op jit(solution)/shard_map/ppermute | solution.py:334
  74.3 8.2 %collective-permute-start.21 = (bf16[224,128]{1,0:T(8,128)(2,1)S(1)}, bf16[224,128]{1,0:T(8,128)(2,1)S(1)}, u32[]{:S(2)}, u32[]{:S(2)}) collective-permute-start(bf16[224,128]{1,0:T(8,128)(2,1)S(1)} %fusion.4), channel_id=1, source_target_pairs={{0,1},{1,0},{2,3},{3,2},{4,5},{5,4},{6,7},{7,6},{8,9},{9,8},{10,11... | collective-permute-start | bytes 172040 | tf_op jit(solution)/shard_map/ppermute | solution.py:337

commit v10 on v8

--- a/solution.py
+++ b/solution.py
@@ -307,12 +307,16 @@
 
 
 def ffn_kernel(own_ref, r1_ref, r3_ref, r2_ref, gate_ref, up_ref, down_ref, *rest):
-    outs, scratch = rest[:4], rest[4]
+    outs, scratch, active = rest[:4], rest[4], rest[5]
     place_blocks(scratch, [own_ref, r1_ref, r2_ref, r3_ref])
     scale = row_scale(scratch)
-    gate = jnp.dot(gate_ref[...], scratch[...], preferred_element_type=F32) * scale
-    up = jnp.dot(up_ref[...], scratch[...], preferred_element_type=F32) * scale
-    spread_blocks(outs, down_ref, (silu(gate) * up).astype(BF16))
+    rows = gate_ref.shape[0] // 2
+    for half in range(2):
+        at = slice(half * rows, (half + 1) * rows)
+        gate = jnp.dot(gate_ref[at, :], scratch[...], preferred_element_type=F32) * scale
+        up = jnp.dot(up_ref[at, :], scratch[...], preferred_element_type=F32) * scale
+        active[at, :] = (silu(gate) * up).astype(BF16)
+    spread_blocks(outs, down_ref, active[...])
 
 
 def shards(
@@ -456,7 +460,7 @@
         [sds((2, width, tokens), F32)] + [sds((2, width, tokens), BF16)] * 3,
         [VMEM] * 7,
         (updated, wide[1], wide[3], wide[2], gate_scaled, up_scaled, down_turned),
-        scratch=[pltpu.VMEM((model, tokens), BF16)],
+        scratch=[pltpu.VMEM((model, tokens), BF16), pltpu.VMEM((ffn_shape[0], tokens), BF16)],
         name="ffn",
     )
     back = {k: along_x(downs[k], k) for k in order}

time: 82.9 us -> 82.9 us (level)
  no operation moved by 1% of the time
where the time goes in v10:
time: 82.9 us; the launch traced here: 82.1 us
  starting transfers between devices  39.2 us (47%)
  waiting for transfers between devices  27.8 us (34%)
  Pallas kernels  12.6 us (15%)
  local copies, waits for them, and re-layouts  1.35 us (2%)
  other arithmetic  0.92 us (1%)
    ppermute x12, waiting for transfers between devices, along_x(): return lax.ppermute(array, 'tp', [(i, i ^ 2 * k) for i in range(tp_size)])  17.6 us
    ppermute x12, starting transfers between devices, along_x(): return lax.ppermute(array, 'tp', [(i, i ^ 2 * k) for i in range(tp_size)])  16.8 us
    ppermute x3, starting transfers between devices, across_z(): return lax.ppermute(array, 'tp', [(i, i ^ 1) for i in range(tp_size)])  12.7 us
    ppermute x3, waiting for transfers between devices, across_z(): return lax.ppermute(array, 'tp', [(i, i ^ 1) for i in range(tp_size)])  10.1 us
    pallas_call x7, Pallas kernels, call(): pl.pallas_call(kernel, out_shape=out_shape, in_specs=specs, out_specs=VME...  7.8 us
    ppermute x3, starting transfers between devices, along_z(): return lax.ppermute(array, 'req', [(i, i ^ 2 * k) for i in range(req_size)])  5.37 us
    ppermute x3, starting transfers between devices, along_y(): lax.ppermute(array, 'req', [(i, i ^ 2 * z_size * k) for i in range(req_si...  4.18 us
    pallas_call x1, Pallas kernels, shards(): pl.pallas_call(functools.partial(mixer_weights_kernel, y_size, z_size), o...  3.24 us
  transfers between devices with their start and end apart: 22, of which 14 were waited for; matrix products, arithmetic and copies ran while one was open for 2% of the time, Pallas kernels for 10%

profile of v10, /device:TPU:8, one launch (start us, length us, event | category | flops | bytes accessed | tf_op | source)
XLA Modules:
  0.0 82.1 jit_solution(4588377148647225668)
XLA Ops:
  0.0 1.6 %fold.1 = (bf16[2,160,128]{2,1,0:T(8,128)(2,1)S(1)}, bf16[224,128]{1,0:T(8,128)(2,1)S(1)}) custom-call(bf16[160,273]{1,0:T(8,128)(2,1)} %constant.5.clone.fold_hbm, bf16[273,2,112]{2,1,0:T(2,128)(2,1)} %bitcast.37, bf16[2,273]{1,0:T(2,128)(2,1)} %bitcast.47, bf16[2,224]{1,0:T(2,128)(2,1)} %bitcast.48, bf16[224,128]{1,0:T(8,128)(2,1)} %bitcast.43), custom_call_target="tpu_custom_call" | custom-call | tf_op jit(solution)/shard_map/fold/pallas_call | solution.py:360
  1.6 4.7 %collective-permute-start.3 = (bf16[2,160,128]{2,1,0:T(8,128)(2,1)S(1)}, bf16[2,160,128]{2,1,0:T(8,128)(2,1)S(1)}, u32[]{:S(2)}, u32[]{:S(2)}) collective-permute-start(bf16[2,160,128]{2,1,0:T(8,128)(2,1)S(1)} %get-tuple-element.48), channel_id=1, source_target_pairs={{0,48},{8,56},{16,32},{24,40},{32,16},{40,24},{48,0},{56,8},{64,11... | collective-permute-start | bytes 245768 | tf_op jit(solution)/shard_map/ppermute | solution.py:342
  7.0 6.3 %collective-permute-start = (bf16[224,128]{1,0:T(8,128)(2,1)}, bf16[224,128]{1,0:T(8,128)(2,1)S(1)}, u32[]{:S(2)}, u32[]{:S(2)}) collective-permute-start(bf16[224,128]{1,0:T(8,128)(2,1)} %bitcast.44), channel_id=1, source_target_pairs={{0,1},{1,0},{2,3},{3,2},{4,5},{5,4},{6,7},{7,6},{8,9},{9,8},{10,11... | collective-permute-start | bytes 172040 | tf_op jit(solution)/shard_map/ppermute | solution.py:339
  13.3 1.3 %pad.7.refs_8_ = f32[16,128]{1,0:T(8,128)} pad(f32[14,128]{1,0:T(8,128)} %bitcast.45, f32[]{:T(128)} %constant.4.clone.1), padding=0_2x0_0 | pad | bytes 15364 | tf_op jit(solution)/shard_map/jit(_pad)/pad | solution.py:372
  14.6 3.2 %mixer_weights.1 = (bf16[1792,224]{1,0:T(8,128)(2,1)S(1)}, s32[24]{0:T(128)S(1)}, bf16[512,1792]{1,0:T(8,128)(2,1)S(1)}) custom-call(bf16[224,1792]{1,0:T(8,128)(2,1)} %refs_0_.1, s32[64]{0:T(128)} %refs_1_.1, s32[32]{0:T(128)} %refs_2_.1, s32[32]{0:T(128)} %refs_3_.1, bf16[32,1792]{1,0:T(8,128)(2,1)} %bitcast.38, bf16[32,1792]{1,0:T(8,128)(2,1)} %bitcast.39, ...), custom_call_target="tpu_custom_call" | custom-call | tf_op jit(solution)/shard_map/mixer_weights/pallas_call | solution.py:376
  18.7 3.1 %collective-permute-start.6 = (bf16[2,224,128]{2,1,0:T(8,128)(2,1)S(1)}, bf16[2,224,128]{2,1,0:T(8,128)(2,1)S(1)}, u32[]{:S(2)}, u32[]{:S(2)}) collective-permute-start(bf16[2,224,128]{2,1,0:T(8,128)(2,1)S(1)} %stack_pair.1.own_ref), channel_id=1, source_target_pairs={{0,4},{1,5},{2,6},{3,7},{4,0},{5,1},{6,2},{7,3},{8,12},{9,13},{10,... | collective-permute-start | bytes 344072 | tf_op jit(solution)/shard_map/ppermute | solution.py:336
  21.8 1.0 %select_sent.1 = (bf16[2,2,160,128]{3,2,1,0:T(8,128)(2,1)S(1)}, bf16[2,2,160,128]{3,2,1,0:T(8,128)(2,1)S(1)}, bf16[2,2,160,128]{3,2,1,0:T(8,128)(2,1)S(1)}) custom-call(s32[24]{0:T(128)S(1)} %get-tuple-element.51.slot_ref, bf16[4,2,160,128]{3,2,1,0:T(8,128)(2,1)S(1)} %pad_maximum_fusion.mine_ref, bf16[4,2,160,128]{3,2,1,0:T(8,128)(2,1)S(1)} %collective-permute-done.7.other_ref), custom_call_target="tpu_custom_call" | custom-call | tf_op jit(solution)/shard_map/select_sent/pallas_call | solution.py:25
  22.8 2.4 %collective-permute-start.8 = (bf16[2,2,160,128]{3,2,1,0:T(8,128)(2,1)S(1)}, bf16[2,2,160,128]{3,2,1,0:T(8,128)(2,1)S(1)}, u32[]{:S(2)}, u32[]{:S(2)}) collective-permute-start(bf16[2,2,160,128]{3,2,1,0:T(8,128)(2,1)S(1)} %get-tuple-element.66), channel_id=1, source_target_pairs={{0,128},{8,136},{16,144},{24,152},{32,160},{40,168},{48,176},{56,1... | collective-permute-start | bytes 491528 | tf_op jit(solution)/shard_map/ppermute | solution.py:348
  25.2 1.3 %collective-permute-start.9 = (bf16[2,2,160,128]{3,2,1,0:T(8,128)(2,1)S(1)}, bf16[2,2,160,128]{3,2,1,0:T(8,128)(2,1)S(1)}, u32[]{:S(2)}, u32[]{:S(2)}) collective-permute-start(bf16[2,2,160,128]{3,2,1,0:T(8,128)(2,1)S(1)} %get-tuple-element.67), channel_id=1, source_target_pairs={{0,64},{8,72},{16,80},{24,88},{32,96},{40,104},{48,112},{56,120},{... | collective-permute-start | bytes 491528 | tf_op jit(solution)/shard_map/ppermute | solution.py:348
  27.0 1.3 %collective-permute-start.5 = (bf16[2,224,128]{2,1,0:T(8,128)(2,1)S(1)}, bf16[2,224,128]{2,1,0:T(8,128)(2,1)S(1)}, u32[]{:S(2)}, u32[]{:S(2)}) collective-permute-start(bf16[2,224,128]{2,1,0:T(8,128)(2,1)S(1)} %stack_pair.1.own_ref), channel_id=1, source_target_pairs={{0,6},{1,7},{2,4},{3,5},{4,2},{5,3},{6,0},{7,1},{8,14},{9,15},{10,... | collective-permute-start | bytes 344072 | tf_op jit(solution)/shard_map/ppermute | solution.py:336
  29.2 3.8 %collective-permute-done.5.r3_ref = bf16[2,224,128]{2,1,0:T(8,128)(2,1)S(1)} collective-permute-done((bf16[2,224,128]{2,1,0:T(8,128)(2,1)S(1)}, bf16[2,224,128]{2,1,0:T(8,128)(2,1)S(1)}, u32[]{:S(2)}, u32[]{:S(2)}) %collective-permute-start.5) | collective-permute-done | bytes 114720 | tf_op jit(solution)/shard_map/ppermute | solution.py:336
  33.0 1.1 %local.1 = (f32[224,128]{1,0:T(8,128)S(1)}, f32[224,128]{1,0:T(8,128)S(1)}, bf16[2,128,128]{2,1,0:T(8,128)(2,1)S(1)}, f32[2,1,128]{2,1,0:T(1,128)S(1)}, bf16[2,3...) custom-call(bf16[2,224,128]{2,1,0:T(8,128)(2,1)S(1)} %stack_pair.1.own_ref, ...), custom_call_target="tpu_custom_call" | custom-call | tf_op jit(solution)/shard_map/local/pallas_call | solution.py:25
  34.3 1.1 %mix.1 = (f32[2,224,128]{2,1,0:T(8,128)S(1)}, bf16[2,224,128]{2,1,0:T(8,128)(2,1)S(1)}, bf16[2,224,128]{2,1,0:T(8,128)(2,1)S(1)}, bf16[2,224,128]{2,1,0:T(8,128)(2,1)S(1)}) custom-call(f32[224,128]{1,0:T(8,128)S(1)} %get-tuple-element.60.conv_ref, f32[224,128]{1,0:T(8,128)S(1)} %get-tuple-element.61.silu_ref, ...), custom_call_target="tpu_custom_call" | custom-call | tf_op jit(solution)/shard_map/mix/pallas_call | solution.py:25
  35.4 1.6 %collective-permute-start.11 = (bf16[2,224,128]{2,1,0:T(8,128)(2,1)S(1)}, bf16[2,224,128]{2,1,0:T(8,128)(2,1)S(1)}, u32[]{:S(2)}, u32[]{:S(2)}) collective-permute-start(bf16[2,224,128]{2,1,0:T(8,128)(2,1)S(1)} %get-tuple-element.71), channel_id=1, source_target_pairs={{0,4},{1,5},{2,6},{3,7},{4,0},{5,1},{6,2},{7,3},{8,12},{9,13},{10,... | collective-permute-start | bytes 344072 | tf_op jit(solution)/shard_map/ppermute | solution.py:336
  37.0 1.3 %collective-permute-start.12 = (bf16[2,224,128]{2,1,0:T(8,128)(2,1)S(1)}, bf16[2,224,128]{2,1,0:T(8,128)(2,1)S(1)}, u32[]{:S(2)}, u32[]{:S(2)}) collective-permute-start(bf16[2,224,128]{2,1,0:T(8,128)(2,1)S(1)} %get-tuple-element.72), channel_id=1, source_target_pairs={{0,2},{1,3},{2,0},{3,1},{4,6},{5,7},{6,4},{7,5},{8,10},{9,11},{10,... | collective-permute-start | bytes 344072 | tf_op jit(solution)/shard_map/ppermute | solution.py:336
  38.2 1.3 %collective-permute-start.13 = (bf16[2,224,128]{2,1,0:T(8,128)(2,1)S(1)}, bf16[2,224,128]{2,1,0:T(8,128)(2,1)S(1)}, u32[]{:S(2)}, u32[]{:S(2)}) collective-permute-start(bf16[2,224,128]{2,1,0:T(8,128)(2,1)S(1)} %get-tuple-element.73), channel_id=1, source_target_pairs={{0,6},{1,7},{2,4},{3,5},{4,2},{5,3},{6,0},{7,1},{8,14},{9,15},{10,... | collective-permute-start | bytes 344072 | tf_op jit(solution)/shard_map/ppermute | solution.py:336
  39.6 3.4 %collective-permute-done.11 = bf16[2,224,128]{2,1,0:T(8,128)(2,1)S(1)} collective-permute-done((bf16[2,224,128]{2,1,0:T(8,128)(2,1)S(1)}, bf16[2,224,128]{2,1,0:T(8,128)(2,1)S(1)}, u32[]{:S(2)}, u32[]{:S(2)}) %collective-permute-start.11) | collective-permute-done | bytes 114720 | tf_op jit(solution)/shard_map/ppermute | solution.py:336
  43.0 1.3 %collective-permute-done.13 = bf16[2,224,128]{2,1,0:T(8,128)(2,1)S(1)} collective-permute-done((bf16[2,224,128]{2,1,0:T(8,128)(2,1)S(1)}, bf16[2,224,128]{2,1,0:T(8,128)(2,1)S(1)}, u32[]{:S(2)}, u32[]{:S(2)}) %collective-permute-start.13) | collective-permute-done | bytes 114720 | tf_op jit(solution)/shard_map/ppermute | solution.py:336
  44.4 3.5 %collective-permute-start.14 = (bf16[2,224,128]{2,1,0:T(8,128)(2,1)S(1)}, bf16[2,224,128]{2,1,0:T(8,128)(2,1)S(1)}, u32[]{:S(2)}, u32[]{:S(2)}) collective-permute-start(bf16[2,224,128]{2,1,0:T(8,128)(2,1)S(1)} %pad_maximum_fusion.1), channel_id=1, source_target_pairs={{0,1},{1,0},{2,3},{3,2},{4,5},{5,4},{6,7},{7,6},{8,9},{9,8},{10,11... | collective-permute-start | bytes 344072 | tf_op jit(solution)/shard_map/ppermute | solution.py:339
  47.9 1.8 %ffn_weights.1 = (bf16[1792,608]{1,0:T(8,128)(2,1)S(1)}, bf16[608,1792]{1,0:T(8,128)(2,1)S(1)}, bf16[608,1792]{1,0:T(8,128)(2,1)S(1)}) custom-call(bf16[608,1792]{1,0:T(8,128)(2,1)S(1)} %copy-done, bf16[608,1792]{1,0:T(8,128)(2,1)S(1)} %bitcast.31, bf16[608,1792]{1,0:T(8,128)(2,1)S(1)} %bitcast.32, f32[16,128]{1,0:T(8,128)S(1)} %pad.8.gain_ref), custom_call_target="tpu_custom_call" | custom-call | tf_op jit(solution)/shard_map/ffn_weights/pallas_call | solution.py:25
  49.7 4.2 %collective-permute-done.14 = bf16[2,224,128]{2,1,0:T(8,128)(2,1)S(1)} collective-permute-done((bf16[2,224,128]{2,1,0:T(8,128)(2,1)S(1)}, bf16[2,224,128]{2,1,0:T(8,128)(2,1)S(1)}, u32[]{:S(2)}, u32[]{:S(2)}) %collective-permute-start.14) | collective-permute-done | bytes 114720 | tf_op jit(solution)/shard_map/ppermute | solution.py:339
  54.0 1.9 %collective-permute-start.17 = (bf16[2,224,128]{2,1,0:T(8,128)(2,1)S(1)}, bf16[2,224,128]{2,1,0:T(8,128)(2,1)S(1)}, u32[]{:S(2)}, u32[]{:S(2)}) collective-permute-start(bf16[2,224,128]{2,1,0:T(8,128)(2,1)S(1)} %add_convert_fusion.own_ref), channel_id=1, source_target_pairs={{0,4},{1,5},{2,6},{3,7},{4,0},{5,1},{6,2},{7,3},{8,12},{9,13},{10,... | collective-permute-start | bytes 344072 | tf_op jit(solution)/shard_map/ppermute | solution.py:336
  55.9 1.9 %collective-permute-start.16 = (bf16[2,224,128]{2,1,0:T(8,128)(2,1)S(1)}, bf16[2,224,128]{2,1,0:T(8,128)(2,1)S(1)}, u32[]{:S(2)}, u32[]{:S(2)}) collective-permute-start(bf16[2,224,128]{2,1,0:T(8,128)(2,1)S(1)} %add_convert_fusion.own_ref), channel_id=1, source_target_pairs={{0,6},{1,7},{2,4},{3,5},{4,2},{5,3},{6,0},{7,1},{8,14},{9,15},{10,... | collective-permute-start | bytes 344072 | tf_op jit(solution)/shard_map/ppermute | solution.py:336
  57.9 2.6 %collective-permute-done.17.r2_ref = bf16[2,224,128]{2,1,0:T(8,128)(2,1)S(1)} collective-permute-done((bf16[2,224,128]{2,1,0:T(8,128)(2,1)S(1)}, bf16[2,224,128]{2,1,0:T(8,128)(2,1)S(1)}, u32[]{:S(2)}, u32[]{:S(2)}) %collective-permute-start.17) | collective-permute-done | bytes 114720 | tf_op jit(solution)/shard_map/ppermute | solution.py:336
  60.4 1.5 %collective-permute-done.16.r3_ref = bf16[2,224,128]{2,1,0:T(8,128)(2,1)S(1)} collective-permute-done((bf16[2,224,128]{2,1,0:T(8,128)(2,1)S(1)}, bf16[2,224,128]{2,1,0:T(8,128)(2,1)S(1)}, u32[]{:S(2)}, u32[]{:S(2)}) %collective-permute-start.16) | collective-permute-done | bytes 114720 | tf_op jit(solution)/shard_map/ppermute | solution.py:336
  62.7 2.1 %ffn.1 = (f32[2,224,128]{2,1,0:T(8,128)S(1)}, bf16[2,224,128]{2,1,0:T(8,128)(2,1)S(1)}, bf16[2,224,128]{2,1,0:T(8,128)(2,1)S(1)}, bf16[2,224,128]{2,1,0:T(8,128)(2,1)S(1)}) custom-call(bf16[2,224,128]{2,1,0:T(8,128)(2,1)S(1)} %add_convert_fusion.own_ref, bf16[2,224,128]{2,1,0:T(8,128)(2,1)S(1)} %collective-permute-done.15.r1_ref, ...), custom_call_target="tpu_custom_call" | custom-call | tf_op jit(solution)/shard_map/ffn/pallas_call | solution.py:25
  64.8 1.7 %collective-permute-start.18 = (bf16[2,224,128]{2,1,0:T(8,128)(2,1)S(1)}, bf16[2,224,128]{2,1,0:T(8,128)(2,1)S(1)}, u32[]{:S(2)}, u32[]{:S(2)}) collective-permute-start(bf16[2,224,128]{2,1,0:T(8,128)(2,1)S(1)} %get-tuple-element.84), channel_id=1, source_target_pairs={{0,4},{1,5},{2,6},{3,7},{4,0},{5,1},{6,2},{7,3},{8,12},{9,13},{10,... | collective-permute-start | bytes 344072 | tf_op jit(solution)/shard_map/ppermute | solution.py:336
  67.2 1.8 %collective-permute-start.20 = (bf16[2,224,128]{2,1,0:T(8,128)(2,1)S(1)}, bf16[2,224,128]{2,1,0:T(8,128)(2,1)S(1)}, u32[]{:S(2)}, u32[]{:S(2)}) collective-permute-start(bf16[2,224,128]{2,1,0:T(8,128)(2,1)S(1)} %get-tuple-element.86), channel_id=1, source_target_pairs={{0,6},{1,7},{2,4},{3,5},{4,2},{5,3},{6,0},{7,1},{8,14},{9,15},{10,... | collective-permute-start | bytes 344072 | tf_op jit(solution)/shard_map/ppermute | solution.py:336
  68.9 2.2 %collective-permute-done.18 = bf16[2,224,128]{2,1,0:T(8,128)(2,1)S(1)} collective-permute-done((bf16[2,224,128]{2,1,0:T(8,128)(2,1)S(1)}, bf16[2,224,128]{2,1,0:T(8,128)(2,1)S(1)}, u32[]{:S(2)}, u32[]{:S(2)}) %collective-permute-start.18) | collective-permute-done | bytes 114720 | tf_op jit(solution)/shard_map/ppermute | solution.py:336
  71.3 1.9 %collective-permute-done.20 = bf16[2,224,128]{2,1,0:T(8,128)(2,1)S(1)} collective-permute-done((bf16[2,224,128]{2,1,0:T(8,128)(2,1)S(1)}, bf16[2,224,128]{2,1,0:T(8,128)(2,1)S(1)}, u32[]{:S(2)}, u32[]{:S(2)}) %collective-permute-start.20) | collective-permute-done | bytes 114720 | tf_op jit(solution)/shard_map/ppermute | solution.py:336
  73.2 2.9 %collective-permute-start.21 = (bf16[224,128]{1,0:T(8,128)(2,1)S(1)}, bf16[224,128]{1,0:T(8,128)(2,1)S(1)}, u32[]{:S(2)}, u32[]{:S(2)}) collective-permute-start(bf16[224,128]{1,0:T(8,128)(2,1)S(1)} %fusion.4), channel_id=1, source_target_pairs={{0,1},{1,0},{2,3},{3,2},{4,5},{5,4},{6,7},{7,6},{8,9},{9,8},{10,11... | collective-permute-start | bytes 172040 | tf_op jit(solution)/shard_map/ppermute | solution.py:339
  76.2 5.2 %collective-permute-done.21 = bf16[224,128]{1,0:T(8,128)(2,1)S(1)} collective-permute-done((bf16[224,128]{1,0:T(8,128)(2,1)S(1)}, bf16[224,128]{1,0:T(8,128)(2,1)S(1)}, u32[]{:S(2)}, u32[]{:S(2)}) %collective-permute-start.21) | collective-permute-done | bytes 57376 | tf_op jit(solution)/shard_map/ppermute | solution.py:339
  (43 shorter events, 5.5 us)
Async XLA Ops:
  1.6 16.9 %collective-permute-start.3 = (bf16[2,160,128]{2,1,0:T(8,128)(2,1)S(1)}, bf16[2,160,128]{2,1,0:T(8,128)(2,1)S(1)}, u32[]{:S(2)}, u32[]{:S(2)}) collective-permute-start(bf16[2,160,128]{2,1,0:T(8,128)(2,1)S(1)} %get-tuple-element.48), channel_id=1, source_target_pairs={{0,48},{8,56},{16,32},{24,40},{32,16},{40,24},{48,0},{56,8},{64,11... | collective-permute-start | bytes 245768 | tf_op jit(solution)/shard_map/ppermute | solution.py:342
  6.3 12.2 %collective-permute-start.2 = (bf16[2,160,128]{2,1,0:T(8,128)(2,1)S(1)}, bf16[2,160,128]{2,1,0:T(8,128)(2,1)S(1)}, u32[]{:S(2)}, u32[]{:S(2)}) collective-permute-start(bf16[2,160,128]{2,1,0:T(8,128)(2,1)S(1)} %get-tuple-element.48), channel_id=1, source_target_pairs={{0,32},{8,40},{16,48},{24,56},{32,0},{40,8},{48,16},{56,24},{64,96... | collective-permute-start | bytes 245768 | tf_op jit(solution)/shard_map/ppermute | solution.py:342
  6.3 12.2 %collective-permute-start.1 = (bf16[2,160,128]{2,1,0:T(8,128)(2,1)S(1)}, bf16[2,160,128]{2,1,0:T(8,128)(2,1)S(1)}, u32[]{:S(2)}, u32[]{:S(2)}) collective-permute-start(bf16[2,160,128]{2,1,0:T(8,128)(2,1)S(1)} %get-tuple-element.48), channel_id=1, source_target_pairs={{0,16},{8,24},{16,0},{24,8},{32,48},{40,56},{48,32},{56,40},{64,80... | collective-permute-start | bytes 245768 | tf_op jit(solution)/shard_map/ppermute | solution.py:342
  7.0 11.5 %collective-permute-start = (bf16[224,128]{1,0:T(8,128)(2,1)}, bf16[224,128]{1,0:T(8,128)(2,1)S(1)}, u32[]{:S(2)}, u32[]{:S(2)}) collective-permute-start(bf16[224,128]{1,0:T(8,128)(2,1)} %bitcast.44), channel_id=1, source_target_pairs={{0,1},{1,0},{2,3},{3,2},{4,5},{5,4},{6,7},{7,6},{8,9},{9,8},{10,11... | collective-permute-start | bytes 172040 | tf_op jit(solution)/shard_map/ppermute | solution.py:339
  14.6 18.5 %copy-start.3 = (f32[3,224]{1,0:T(4,128)S(1)}, f32[3,224]{1,0:T(4,128)}, u32[]{:S(2)}) copy-start(f32[3,224]{1,0:T(4,128)} %taps_ref.1) | copy-start | bytes 8068
  14.6 18.5 %copy-start.4 = (s32[128]{0:T(128)S(1)}, s32[128]{0:T(128)}, u32[]{:S(2)}) copy-start(s32[128]{0:T(128)} %param.21) | copy-start | bytes 1540
  18.6 3.2 %collective-permute-start.7 = (bf16[4,2,160,128]{3,2,1,0:T(8,128)(2,1)S(1)}, bf16[4,2,160,128]{3,2,1,0:T(8,128)(2,1)S(1)}, u32[]{:S(2)}, u32[]{:S(2)}) collective-permute-start(bf16[4,2,160,128]{3,2,1,0:T(8,128)(2,1)S(1)} %pad_maximum_fusion.mine_ref), channel_id=1, source_target_pairs={{0,8},{8,0},{16,24},{24,16},{32,40},{40,32},{48,56},{56,48},{64,72... | collective-permute-start | bytes 983048 | tf_op jit(solution)/shard_map/ppermute | solution.py:345
  18.7 9.5 %collective-permute-start.6 = (bf16[2,224,128]{2,1,0:T(8,128)(2,1)S(1)}, bf16[2,224,128]{2,1,0:T(8,128)(2,1)S(1)}, u32[]{:S(2)}, u32[]{:S(2)}) collective-permute-start(bf16[2,224,128]{2,1,0:T(8,128)(2,1)S(1)} %stack_pair.1.own_ref), channel_id=1, source_target_pairs={{0,4},{1,5},{2,6},{3,7},{4,0},{5,1},{6,2},{7,3},{8,12},{9,13},{10,... | collective-permute-start | bytes 344072 | tf_op jit(solution)/shard_map/ppermute | solution.py:336
  22.8 11.4 %collective-permute-start.8 = (bf16[2,2,160,128]{3,2,1,0:T(8,128)(2,1)S(1)}, bf16[2,2,160,128]{3,2,1,0:T(8,128)(2,1)S(1)}, u32[]{:S(2)}, u32[]{:S(2)}) collective-permute-start(bf16[2,2,160,128]{3,2,1,0:T(8,128)(2,1)S(1)} %get-tuple-element.66), channel_id=1, source_target_pairs={{0,128},{8,136},{16,144},{24,152},{32,160},{40,168},{48,176},{56,1... | collective-permute-start | bytes 491528 | tf_op jit(solution)/shard_map/ppermute | solution.py:348
  25.2 9.1 %collective-permute-start.9 = (bf16[2,2,160,128]{3,2,1,0:T(8,128)(2,1)S(1)}, bf16[2,2,160,128]{3,2,1,0:T(8,128)(2,1)S(1)}, u32[]{:S(2)}, u32[]{:S(2)}) collective-permute-start(bf16[2,2,160,128]{3,2,1,0:T(8,128)(2,1)S(1)} %get-tuple-element.67), channel_id=1, source_target_pairs={{0,64},{8,72},{16,80},{24,88},{32,96},{40,104},{48,112},{56,120},{... | collective-permute-start | bytes 491528 | tf_op jit(solution)/shard_map/ppermute | solution.py:348
  26.5 7.8 %collective-permute-start.10 = (bf16[2,2,160,128]{3,2,1,0:T(8,128)(2,1)S(1)}, bf16[2,2,160,128]{3,2,1,0:T(8,128)(2,1)S(1)}, u32[]{:S(2)}, u32[]{:S(2)}) collective-permute-start(bf16[2,2,160,128]{3,2,1,0:T(8,128)(2,1)S(1)} %get-tuple-element.68), channel_id=1, source_target_pairs={{0,192},{8,200},{16,208},{24,216},{32,224},{40,232},{48,240},{56,2... | collective-permute-start | bytes 491528 | tf_op jit(solution)/shard_map/ppermute | solution.py:348
  27.0 6.0 %collective-permute-start.5 = (bf16[2,224,128]{2,1,0:T(8,128)(2,1)S(1)}, bf16[2,224,128]{2,1,0:T(8,128)(2,1)S(1)}, u32[]{:S(2)}, u32[]{:S(2)}) collective-permute-start(bf16[2,224,128]{2,1,0:T(8,128)(2,1)S(1)} %stack_pair.1.own_ref), channel_id=1, source_target_pairs={{0,6},{1,7},{2,4},{3,5},{4,2},{5,3},{6,0},{7,1},{8,14},{9,15},{10,... | collective-permute-start | bytes 344072 | tf_op jit(solution)/shard_map/ppermute | solution.py:336
  28.2 4.8 %collective-permute-start.4 = (bf16[2,224,128]{2,1,0:T(8,128)(2,1)S(1)}, bf16[2,224,128]{2,1,0:T(8,128)(2,1)S(1)}, u32[]{:S(2)}, u32[]{:S(2)}) collective-permute-start(bf16[2,224,128]{2,1,0:T(8,128)(2,1)S(1)} %stack_pair.1.own_ref), channel_id=1, source_target_pairs={{0,2},{1,3},{2,0},{3,1},{4,6},{5,7},{6,4},{7,5},{8,10},{9,11},{10,... | collective-permute-start | bytes 344072 | tf_op jit(solution)/shard_map/ppermute | solution.py:336
  28.5 19.4 %copy-start.2 = (bf16[1792,608]{0,1:T(8,128)(2,1)S(1)}, bf16[1792,608]{0,1:T(8,128)(2,1)}, u32[]{:S(2)}) copy-start(bf16[1792,608]{0,1:T(8,128)(2,1)} %param.37) | copy-start | bytes 6537220
  33.0 14.9 %copy-start.1 = (bf16[1792,608]{0,1:T(8,128)(2,1)S(1)}, bf16[1792,608]{0,1:T(8,128)(2,1)}, u32[]{:S(2)}) copy-start(bf16[1792,608]{0,1:T(8,128)(2,1)} %param.36) | copy-start | bytes 6537220
  34.2 13.7 %copy-start.5 = (f32[1792]{0:T(1024)S(1)}, f32[1792]{0:T(1024)}, u32[]{:S(2)}) copy-start(f32[1792]{0:T(1024)} %param.29) | copy-start | bytes 21508
  34.2 13.7 %copy-start = (bf16[608,1792]{1,0:T(8,128)(2,1)S(1)}, bf16[608,1792]{1,0:T(8,128)(2,1)}, u32[]{:S(2)}) copy-start(bf16[608,1792]{1,0:T(8,128)(2,1)} %down_ref) | copy-start | bytes 6537220
  35.4 7.6 %collective-permute-start.11 = (bf16[2,224,128]{2,1,0:T(8,128)(2,1)S(1)}, bf16[2,224,128]{2,1,0:T(8,128)(2,1)S(1)}, u32[]{:S(2)}, u32[]{:S(2)}) collective-permute-start(bf16[2,224,128]{2,1,0:T(8,128)(2,1)S(1)} %get-tuple-element.71), channel_id=1, source_target_pairs={{0,4},{1,5},{2,6},{3,7},{4,0},{5,1},{6,2},{7,3},{8,12},{9,13},{10,... | collective-permute-start | bytes 344072 | tf_op jit(solution)/shard_map/ppermute | solution.py:336
  37.0 6.0 %collective-permute-start.12 = (bf16[2,224,128]{2,1,0:T(8,128)(2,1)S(1)}, bf16[2,224,128]{2,1,0:T(8,128)(2,1)S(1)}, u32[]{:S(2)}, u32[]{:S(2)}) collective-permute-start(bf16[2,224,128]{2,1,0:T(8,128)(2,1)S(1)} %get-tuple-element.72), channel_id=1, source_target_pairs={{0,2},{1,3},{2,0},{3,1},{4,6},{5,7},{6,4},{7,5},{8,10},{9,11},{10,... | collective-permute-start | bytes 344072 | tf_op jit(solution)/shard_map/ppermute | solution.py:336
  38.2 6.1 %collective-permute-start.13 = (bf16[2,224,128]{2,1,0:T(8,128)(2,1)S(1)}, bf16[2,224,128]{2,1,0:T(8,128)(2,1)S(1)}, u32[]{:S(2)}, u32[]{:S(2)}) collective-permute-start(bf16[2,224,128]{2,1,0:T(8,128)(2,1)S(1)} %get-tuple-element.73), channel_id=1, source_target_pairs={{0,6},{1,7},{2,4},{3,5},{4,2},{5,3},{6,0},{7,1},{8,14},{9,15},{10,... | collective-permute-start | bytes 344072 | tf_op jit(solution)/shard_map/ppermute | solution.py:336
  44.4 9.5 %collective-permute-start.14 = (bf16[2,224,128]{2,1,0:T(8,128)(2,1)S(1)}, bf16[2,224,128]{2,1,0:T(8,128)(2,1)S(1)}, u32[]{:S(2)}, u32[]{:S(2)}) collective-permute-start(bf16[2,224,128]{2,1,0:T(8,128)(2,1)S(1)} %pad_maximum_fusion.1), channel_id=1, source_target_pairs={{0,1},{1,0},{2,3},{3,2},{4,5},{5,4},{6,7},{7,6},{8,9},{9,8},{10,11... | collective-permute-start | bytes 344072 | tf_op jit(solution)/shard_map/ppermute | solution.py:339
  54.0 6.4 %collective-permute-start.17 = (bf16[2,224,128]{2,1,0:T(8,128)(2,1)S(1)}, bf16[2,224,128]{2,1,0:T(8,128)(2,1)S(1)}, u32[]{:S(2)}, u32[]{:S(2)}) collective-permute-start(bf16[2,224,128]{2,1,0:T(8,128)(2,1)S(1)} %add_convert_fusion.own_ref), channel_id=1, source_target_pairs={{0,4},{1,5},{2,6},{3,7},{4,0},{5,1},{6,2},{7,3},{8,12},{9,13},{10,... | collective-permute-start | bytes 344072 | tf_op jit(solution)/shard_map/ppermute | solution.py:336
  55.9 6.0 %collective-permute-start.16 = (bf16[2,224,128]{2,1,0:T(8,128)(2,1)S(1)}, bf16[2,224,128]{2,1,0:T(8,128)(2,1)S(1)}, u32[]{:S(2)}, u32[]{:S(2)}) collective-permute-start(bf16[2,224,128]{2,1,0:T(8,128)(2,1)S(1)} %add_convert_fusion.own_ref), channel_id=1, source_target_pairs={{0,6},{1,7},{2,4},{3,5},{4,2},{5,3},{6,0},{7,1},{8,14},{9,15},{10,... | collective-permute-start | bytes 344072 | tf_op jit(solution)/shard_map/ppermute | solution.py:336
  57.9 4.8 %collective-permute-start.15 = (bf16[2,224,128]{2,1,0:T(8,128)(2,1)S(1)}, bf16[2,224,128]{2,1,0:T(8,128)(2,1)S(1)}, u32[]{:S(2)}, u32[]{:S(2)}) collective-permute-start(bf16[2,224,128]{2,1,0:T(8,128)(2,1)S(1)} %add_convert_fusion.own_ref), channel_id=1, source_target_pairs={{0,2},{1,3},{2,0},{3,1},{4,6},{5,7},{6,4},{7,5},{8,10},{9,11},{10,... | collective-permute-start | bytes 344072 | tf_op jit(solution)/shard_map/ppermute | solution.py:336
  64.8 6.4 %collective-permute-start.18 = (bf16[2,224,128]{2,1,0:T(8,128)(2,1)S(1)}, bf16[2,224,128]{2,1,0:T(8,128)(2,1)S(1)}, u32[]{:S(2)}, u32[]{:S(2)}) collective-permute-start(bf16[2,224,128]{2,1,0:T(8,128)(2,1)S(1)} %get-tuple-element.84), channel_id=1, source_target_pairs={{0,4},{1,5},{2,6},{3,7},{4,0},{5,1},{6,2},{7,3},{8,12},{9,13},{10,... | collective-permute-start | bytes 344072 | tf_op jit(solution)/shard_map/ppermute | solution.py:336
  66.5 4.8 %collective-permute-start.19 = (bf16[2,224,128]{2,1,0:T(8,128)(2,1)S(1)}, bf16[2,224,128]{2,1,0:T(8,128)(2,1)S(1)}, u32[]{:S(2)}, u32[]{:S(2)}) collective-permute-start(bf16[2,224,128]{2,1,0:T(8,128)(2,1)S(1)} %get-tuple-element.85), channel_id=1, source_target_pairs={{0,2},{1,3},{2,0},{3,1},{4,6},{5,7},{6,4},{7,5},{8,10},{9,11},{10,... | collective-permute-start | bytes 344072 | tf_op jit(solution)/shard_map/ppermute | solution.py:336
  67.2 6.0 %collective-permute-start.20 = (bf16[2,224,128]{2,1,0:T(8,128)(2,1)S(1)}, bf16[2,224,128]{2,1,0:T(8,128)(2,1)S(1)}, u32[]{:S(2)}, u32[]{:S(2)}) collective-permute-start(bf16[2,224,128]{2,1,0:T(8,128)(2,1)S(1)} %get-tuple-element.86), channel_id=1, source_target_pairs={{0,6},{1,7},{2,4},{3,5},{4,2},{5,3},{6,0},{7,1},{8,14},{9,15},{10,... | collective-permute-start | bytes 344072 | tf_op jit(solution)/shard_map/ppermute | solution.py:336
  73.2 8.2 %collective-permute-start.21 = (bf16[224,128]{1,0:T(8,128)(2,1)S(1)}, bf16[224,128]{1,0:T(8,128)(2,1)S(1)}, u32[]{:S(2)}, u32[]{:S(2)}) collective-permute-start(bf16[224,128]{1,0:T(8,128)(2,1)S(1)} %fusion.4), channel_id=1, source_target_pairs={{0,1},{1,0},{2,3},{3,2},{4,5},{5,4},{6,7},{7,6},{8,9},{9,8},{10,11... | collective-permute-start | bytes 172040 | tf_op jit(solution)/shard_map/ppermute | solution.py:339

commit v11 on v8

--- a/solution.py
+++ b/solution.py
@@ -106,10 +106,29 @@
         out_ref[:, at] = (in_ref[:, at].astype(F32) * gain_ref[j : j + 1, :]).astype(BF16)
 
 
-def ffn_weights_kernel(down_ref, gate_ref, up_ref, gain_ref, turned_ref, gate_out_ref, up_out_ref):
+def ready_ffn_weights(down_ref, gate_ref, up_ref, gain_ref, turned_ref, gate_out_ref, up_out_ref):
     turn_block(down_ref, turned_ref)
     scale_block(gate_ref, gain_ref, gate_out_ref)
     scale_block(up_ref, gain_ref, up_out_ref)
+
+
+def early_weights_kernel(*refs):
+    @pl.when((lax.axis_index("req") & 1) == 1)
+    def _():
+        ready_ffn_weights(*refs)
+
+
+def late_weights_kernel(*refs):
+    core = lax.axis_index("req") & 1
+
+    @pl.when(core == 0)
+    def _():
+        ready_ffn_weights(*refs[:4], *refs[7:])
+
+    @pl.when(core == 1)
+    def _():
+        for have, out in zip(refs[4:7], refs[7:]):
+            out[...] = have[...]
 
 
 def mixer_weights_kernel(groups, held, *refs):
@@ -438,15 +457,13 @@
     got = {k: along_x(parts[k], k) for k in order}
     share = parts[0] + got[2].astype(F32) + got[1].astype(F32) + got[3].astype(F32)
     crossing, down_in = lax.optimization_barrier((jnp.stack([share[1], share[0]]).astype(BF16), ffn_down))
+    ffn_shape = ffn_gate.shape[::-1]
+    ready_shape = [sds(down_in.shape[::-1], BF16), sds(ffn_shape, BF16), sds(ffn_shape, BF16)]
+    raw = (down_in, ffn_gate.T, ffn_up.T, gain_block(ffn_gain))
+    early = call(early_weights_kernel, ready_shape, [VMEM] * 4, raw, name="early_weights")
+    crossing, *early = lax.optimization_barrier((crossing, *early))
     share_peer = across_z(crossing)
-    ffn_shape = ffn_gate.shape[::-1]
-    ready = call(
-        ffn_weights_kernel,
-        [sds(down_in.shape[::-1], BF16), sds(ffn_shape, BF16), sds(ffn_shape, BF16)],
-        [VMEM] * 4,
-        (down_in, ffn_gate.T, ffn_up.T, gain_block(ffn_gain)),
-        name="ffn_weights",
-    )
+    ready = call(late_weights_kernel, ready_shape, [VMEM] * 7, (*raw, *early), name="late_weights")
     updated = (held_pair.astype(F32) + share + share_peer.astype(F32)).astype(BF16)
     updated, down_turned, gate_scaled, up_scaled = lax.optimization_barrier((updated, *ready))
 

time: 82.9 us -> 86.4 us (1.042)
  waiting for transfers between devices: 27.8 us -> 32.7 us
  starting transfers between devices: 39.2 us -> 38.1 us
    ppermute x3, waiting for transfers between devices: 10.1 us -> 13.5 us  [across_z(): return lax.ppermute(array, 'tp', [(i, i ^ 1) for i in range(tp_size)])]
    ppermute x12, waiting for transfers between devices: 17.6 us -> 19.1 us  [along_x(): return lax.ppermute(array, 'tp', [(i, i ^ 2 * k) for i in range(tp_size)])]
    pallas_call x7 -> x8, Pallas kernels: 7.76 us -> 7.96 us  [call(): pl.pallas_call(kernel, out_shape=out_shape, in_specs=specs, out_specs=VME...]
  transfers between devices with their start and end apart: 22 -> 22, of which waited for: 14 -> 13; matrix products, arithmetic and copies ran while one was open for 2% -> 2% of each run, Pallas kernels for 10% -> 9%
where the time goes in v11:
time: 86.4 us; the launch traced here: 86.1 us
  starting transfers between devices  38.1 us (44%)
  waiting for transfers between devices  32.7 us (38%)
  Pallas kernels  12.8 us (15%)
  local copies, waits for them, and re-layouts  1.35 us (2%)
  other arithmetic  0.91 us (1%)
    ppermute x12, waiting for transfers between devices, along_x(): return lax.ppermute(array, 'tp', [(i, i ^ 2 * k) for i in range(tp_size)])  19.1 us
    ppermute x12, starting transfers between devices, along_x(): return lax.ppermute(array, 'tp', [(i, i ^ 2 * k) for i in range(tp_size)])  16.5 us
    ppermute x3, waiting for transfers between devices, across_z(): return lax.ppermute(array, 'tp', [(i, i ^ 1) for i in range(tp_size)])  13.5 us
    ppermute x3, starting transfers between devices, across_z(): return lax.ppermute(array, 'tp', [(i, i ^ 1) for i in range(tp_size)])  11.9 us
    pallas_call x8, Pallas kernels, call(): pl.pallas_call(kernel, out_shape=out_shape, in_specs=specs, out_specs=VME...  7.96 us
    ppermute x3, starting transfers between devices, along_z(): return lax.ppermute(array, 'req', [(i, i ^ 2 * k) for i in range(req_size)])  5.37 us
    ppermute x3, starting transfers between devices, along_y(): lax.ppermute(array, 'req', [(i, i ^ 2 * z_size * k) for i in range(req_si...  4.18 us
    pallas_call x1, Pallas kernels, shards(): pl.pallas_call(functools.partial(mixer_weights_kernel, y_size, z_size), o...  3.24 us
  transfers between devices with their start and end apart: 22, of which 13 were waited for; matrix products, arithmetic and copies ran while one was open for 2% of the time, Pallas kernels for 9%

profile of v11, /device:TPU:8, one launch (start us, length us, event | category | flops | bytes accessed | tf_op | source)
XLA Modules:
  0.0 86.1 jit_solution(14193111696907623653)
XLA Ops:
  0.0 1.6 %fold.1 = (bf16[2,160,128]{2,1,0:T(8,128)(2,1)S(1)}, bf16[224,128]{1,0:T(8,128)(2,1)S(1)}) custom-call(bf16[160,273]{1,0:T(8,128)(2,1)} %constant.5.clone.fold_hbm, bf16[273,2,112]{2,1,0:T(2,128)(2,1)} %bitcast.39, bf16[2,273]{1,0:T(2,128)(2,1)} %bitcast.49, bf16[2,224]{1,0:T(2,128)(2,1)} %bitcast.50, bf16[224,128]{1,0:T(8,128)(2,1)} %bitcast.45), custom_call_target="tpu_custom_call" | custom-call | tf_op jit(solution)/shard_map/fold/pallas_call | solution.py:375
  1.6 4.7 %collective-permute-start.3 = (bf16[2,160,128]{2,1,0:T(8,128)(2,1)S(1)}, bf16[2,160,128]{2,1,0:T(8,128)(2,1)S(1)}, u32[]{:S(2)}, u32[]{:S(2)}) collective-permute-start(bf16[2,160,128]{2,1,0:T(8,128)(2,1)S(1)} %get-tuple-element.55), channel_id=1, source_target_pairs={{0,48},{8,56},{16,32},{24,40},{32,16},{40,24},{48,0},{56,8},{64,11... | collective-permute-start | bytes 245768 | tf_op jit(solution)/shard_map/ppermute | solution.py:357
  7.0 6.3 %collective-permute-start = (bf16[224,128]{1,0:T(8,128)(2,1)}, bf16[224,128]{1,0:T(8,128)(2,1)S(1)}, u32[]{:S(2)}, u32[]{:S(2)}) collective-permute-start(bf16[224,128]{1,0:T(8,128)(2,1)} %bitcast.46), channel_id=1, source_target_pairs={{0,1},{1,0},{2,3},{3,2},{4,5},{5,4},{6,7},{7,6},{8,9},{9,8},{10,11... | collective-permute-start | bytes 172040 | tf_op jit(solution)/shard_map/ppermute | solution.py:354
  13.3 1.3 %pad.7.refs_8_ = f32[16,128]{1,0:T(8,128)} pad(f32[14,128]{1,0:T(8,128)} %bitcast.47, f32[]{:T(128)} %constant.4.clone.1), padding=0_2x0_0 | pad | bytes 15364 | tf_op jit(solution)/shard_map/jit(_pad)/pad | solution.py:387
  14.6 3.2 %mixer_weights.1 = (bf16[1792,224]{1,0:T(8,128)(2,1)S(1)}, s32[24]{0:T(128)S(1)}, bf16[512,1792]{1,0:T(8,128)(2,1)S(1)}) custom-call(bf16[224,1792]{1,0:T(8,128)(2,1)} %refs_0_.1, s32[64]{0:T(128)} %refs_1_.1, s32[32]{0:T(128)} %refs_2_.1, s32[32]{0:T(128)} %refs_3_.1, bf16[32,1792]{1,0:T(8,128)(2,1)} %bitcast.40, bf16[32,1792]{1,0:T(8,128)(2,1)} %bitcast.41, ...), custom_call_target="tpu_custom_call" | custom-call | tf_op jit(solution)/shard_map/mixer_weights/pallas_call | solution.py:391
  18.7 3.1 %collective-permute-start.6 = (bf16[2,224,128]{2,1,0:T(8,128)(2,1)S(1)}, bf16[2,224,128]{2,1,0:T(8,128)(2,1)S(1)}, u32[]{:S(2)}, u32[]{:S(2)}) collective-permute-start(bf16[2,224,128]{2,1,0:T(8,128)(2,1)S(1)} %stack_pair.1.own_ref), channel_id=1, source_target_pairs={{0,4},{1,5},{2,6},{3,7},{4,0},{5,1},{6,2},{7,3},{8,12},{9,13},{10,... | collective-permute-start | bytes 344072 | tf_op jit(solution)/shard_map/ppermute | solution.py:351
  21.8 1.0 %select_sent.1 = (bf16[2,2,160,128]{3,2,1,0:T(8,128)(2,1)S(1)}, bf16[2,2,160,128]{3,2,1,0:T(8,128)(2,1)S(1)}, bf16[2,2,160,128]{3,2,1,0:T(8,128)(2,1)S(1)}) custom-call(s32[24]{0:T(128)S(1)} %get-tuple-element.58.slot_ref, bf16[4,2,160,128]{3,2,1,0:T(8,128)(2,1)S(1)} %pad_maximum_fusion.mine_ref, bf16[4,2,160,128]{3,2,1,0:T(8,128)(2,1)S(1)} %collective-permute-done.7.other_ref), custom_call_target="tpu_custom_call" | custom-call | tf_op jit(solution)/shard_map/select_sent/pallas_call | solution.py:25
  22.8 2.4 %collective-permute-start.8 = (bf16[2,2,160,128]{3,2,1,0:T(8,128)(2,1)S(1)}, bf16[2,2,160,128]{3,2,1,0:T(8,128)(2,1)S(1)}, u32[]{:S(2)}, u32[]{:S(2)}) collective-permute-start(bf16[2,2,160,128]{3,2,1,0:T(8,128)(2,1)S(1)} %get-tuple-element.73), channel_id=1, source_target_pairs={{0,128},{8,136},{16,144},{24,152},{32,160},{40,168},{48,176},{56,1... | collective-permute-start | bytes 491528 | tf_op jit(solution)/shard_map/ppermute | solution.py:363
  25.2 1.3 %collective-permute-start.9 = (bf16[2,2,160,128]{3,2,1,0:T(8,128)(2,1)S(1)}, bf16[2,2,160,128]{3,2,1,0:T(8,128)(2,1)S(1)}, u32[]{:S(2)}, u32[]{:S(2)}) collective-permute-start(bf16[2,2,160,128]{3,2,1,0:T(8,128)(2,1)S(1)} %get-tuple-element.74), channel_id=1, source_target_pairs={{0,64},{8,72},{16,80},{24,88},{32,96},{40,104},{48,112},{56,120},{... | collective-permute-start | bytes 491528 | tf_op jit(solution)/shard_map/ppermute | solution.py:363
  27.0 1.3 %collective-permute-start.5 = (bf16[2,224,128]{2,1,0:T(8,128)(2,1)S(1)}, bf16[2,224,128]{2,1,0:T(8,128)(2,1)S(1)}, u32[]{:S(2)}, u32[]{:S(2)}) collective-permute-start(bf16[2,224,128]{2,1,0:T(8,128)(2,1)S(1)} %stack_pair.1.own_ref), channel_id=1, source_target_pairs={{0,6},{1,7},{2,4},{3,5},{4,2},{5,3},{6,0},{7,1},{8,14},{9,15},{10,... | collective-permute-start | bytes 344072 | tf_op jit(solution)/shard_map/ppermute | solution.py:351
  29.2 3.8 %collective-permute-done.5.r3_ref = bf16[2,224,128]{2,1,0:T(8,128)(2,1)S(1)} collective-permute-done((bf16[2,224,128]{2,1,0:T(8,128)(2,1)S(1)}, bf16[2,224,128]{2,1,0:T(8,128)(2,1)S(1)}, u32[]{:S(2)}, u32[]{:S(2)}) %collective-permute-start.5) | collective-permute-done | bytes 114720 | tf_op jit(solution)/shard_map/ppermute | solution.py:351
  33.0 1.1 %local.1 = (f32[224,128]{1,0:T(8,128)S(1)}, f32[224,128]{1,0:T(8,128)S(1)}, bf16[2,128,128]{2,1,0:T(8,128)(2,1)S(1)}, f32[2,1,128]{2,1,0:T(1,128)S(1)}, bf16[2,3...) custom-call(bf16[2,224,128]{2,1,0:T(8,128)(2,1)S(1)} %stack_pair.1.own_ref, ...), custom_call_target="tpu_custom_call" | custom-call | tf_op jit(solution)/shard_map/local/pallas_call | solution.py:25
  34.3 1.1 %mix.1 = (f32[2,224,128]{2,1,0:T(8,128)S(1)}, bf16[2,224,128]{2,1,0:T(8,128)(2,1)S(1)}, bf16[2,224,128]{2,1,0:T(8,128)(2,1)S(1)}, bf16[2,224,128]{2,1,0:T(8,128)(2,1)S(1)}) custom-call(f32[224,128]{1,0:T(8,128)S(1)} %get-tuple-element.67.conv_ref, f32[224,128]{1,0:T(8,128)S(1)} %get-tuple-element.68.silu_ref, ...), custom_call_target="tpu_custom_call" | custom-call | tf_op jit(solution)/shard_map/mix/pallas_call | solution.py:25
  35.4 1.6 %collective-permute-start.11 = (bf16[2,224,128]{2,1,0:T(8,128)(2,1)S(1)}, bf16[2,224,128]{2,1,0:T(8,128)(2,1)S(1)}, u32[]{:S(2)}, u32[]{:S(2)}) collective-permute-start(bf16[2,224,128]{2,1,0:T(8,128)(2,1)S(1)} %get-tuple-element.78), channel_id=1, source_target_pairs={{0,4},{1,5},{2,6},{3,7},{4,0},{5,1},{6,2},{7,3},{8,12},{9,13},{10,... | collective-permute-start | bytes 344072 | tf_op jit(solution)/shard_map/ppermute | solution.py:351
  37.0 1.2 %collective-permute-start.12 = (bf16[2,224,128]{2,1,0:T(8,128)(2,1)S(1)}, bf16[2,224,128]{2,1,0:T(8,128)(2,1)S(1)}, u32[]{:S(2)}, u32[]{:S(2)}) collective-permute-start(bf16[2,224,128]{2,1,0:T(8,128)(2,1)S(1)} %get-tuple-element.79), channel_id=1, source_target_pairs={{0,2},{1,3},{2,0},{3,1},{4,6},{5,7},{6,4},{7,5},{8,10},{9,11},{10,... | collective-permute-start | bytes 344072 | tf_op jit(solution)/shard_map/ppermute | solution.py:351
  38.2 1.3 %collective-permute-start.13 = (bf16[2,224,128]{2,1,0:T(8,128)(2,1)S(1)}, bf16[2,224,128]{2,1,0:T(8,128)(2,1)S(1)}, u32[]{:S(2)}, u32[]{:S(2)}) collective-permute-start(bf16[2,224,128]{2,1,0:T(8,128)(2,1)S(1)} %get-tuple-element.80), channel_id=1, source_target_pairs={{0,6},{1,7},{2,4},{3,5},{4,2},{5,3},{6,0},{7,1},{8,14},{9,15},{10,... | collective-permute-start | bytes 344072 | tf_op jit(solution)/shard_map/ppermute | solution.py:351
  39.6 3.4 %collective-permute-done.11 = bf16[2,224,128]{2,1,0:T(8,128)(2,1)S(1)} collective-permute-done((bf16[2,224,128]{2,1,0:T(8,128)(2,1)S(1)}, bf16[2,224,128]{2,1,0:T(8,128)(2,1)S(1)}, u32[]{:S(2)}, u32[]{:S(2)}) %collective-permute-start.11) | collective-permute-done | bytes 114720 | tf_op jit(solution)/shard_map/ppermute | solution.py:351
  43.0 1.3 %collective-permute-done.13 = bf16[2,224,128]{2,1,0:T(8,128)(2,1)S(1)} collective-permute-done((bf16[2,224,128]{2,1,0:T(8,128)(2,1)S(1)}, bf16[2,224,128]{2,1,0:T(8,128)(2,1)S(1)}, u32[]{:S(2)}, u32[]{:S(2)}) %collective-permute-start.13) | collective-permute-done | bytes 114720 | tf_op jit(solution)/shard_map/ppermute | solution.py:351
  44.7 3.3 %collective-permute-start.14 = (bf16[2,224,128]{2,1,0:T(8,128)(2,1)S(1)}, bf16[2,224,128]{2,1,0:T(8,128)(2,1)S(1)}, u32[]{:S(2)}, u32[]{:S(2)}) collective-permute-start(bf16[2,224,128]{2,1,0:T(8,128)(2,1)S(1)} %pad_maximum_fusion.1), channel_id=1, source_target_pairs={{0,1},{1,0},{2,3},{3,2},{4,5},{5,4},{6,7},{7,6},{8,9},{9,8},{10,11... | collective-permute-start | bytes 344072 | tf_op jit(solution)/shard_map/ppermute | solution.py:354
  47.9 1.8 %late_weights.1 = (bf16[1792,608]{1,0:T(8,128)(2,1)S(1)}, bf16[608,1792]{1,0:T(8,128)(2,1)S(1)}, bf16[608,1792]{1,0:T(8,128)(2,1)S(1)}) custom-call(bf16[608,1792]{1,0:T(8,128)(2,1)S(1)} %copy-done, bf16[608,1792]{1,0:T(8,128)(2,1)S(1)} %bitcast.32, bf16[608,1792]{1,0:T(8,128)(2,1)S(1)} %bitcast.34, f32[16,128]{1,0:T(8,128)S(1)} %pad.8.refs_3_, ...), custom_call_target="tpu_custom_call" | custom-call | tf_op jit(solution)/shard_map/late_weights/pallas_call | solution.py:25
  49.7 6.4 %collective-permute-done.14 = bf16[2,224,128]{2,1,0:T(8,128)(2,1)S(1)} collective-permute-done((bf16[2,224,128]{2,1,0:T(8,128)(2,1)S(1)}, bf16[2,224,128]{2,1,0:T(8,128)(2,1)S(1)}, u32[]{:S(2)}, u32[]{:S(2)}) %collective-permute-start.14) | collective-permute-done | bytes 114720 | tf_op jit(solution)/shard_map/ppermute | solution.py:354
  56.2 1.8 %collective-permute-start.17 = (bf16[2,224,128]{2,1,0:T(8,128)(2,1)S(1)}, bf16[2,224,128]{2,1,0:T(8,128)(2,1)S(1)}, u32[]{:S(2)}, u32[]{:S(2)}) collective-permute-start(bf16[2,224,128]{2,1,0:T(8,128)(2,1)S(1)} %add_convert_fusion.own_ref), channel_id=1, source_target_pairs={{0,4},{1,5},{2,6},{3,7},{4,0},{5,1},{6,2},{7,3},{8,12},{9,13},{10,... | collective-permute-start | bytes 344072 | tf_op jit(solution)/shard_map/ppermute | solution.py:351
  58.0 1.6 %collective-permute-start.16 = (bf16[2,224,128]{2,1,0:T(8,128)(2,1)S(1)}, bf16[2,224,128]{2,1,0:T(8,128)(2,1)S(1)}, u32[]{:S(2)}, u32[]{:S(2)}) collective-permute-start(bf16[2,224,128]{2,1,0:T(8,128)(2,1)S(1)} %add_convert_fusion.own_ref), channel_id=1, source_target_pairs={{0,6},{1,7},{2,4},{3,5},{4,2},{5,3},{6,0},{7,1},{8,14},{9,15},{10,... | collective-permute-start | bytes 344072 | tf_op jit(solution)/shard_map/ppermute | solution.py:351
  59.8 2.9 %collective-permute-done.17.r2_ref = bf16[2,224,128]{2,1,0:T(8,128)(2,1)S(1)} collective-permute-done((bf16[2,224,128]{2,1,0:T(8,128)(2,1)S(1)}, bf16[2,224,128]{2,1,0:T(8,128)(2,1)S(1)}, u32[]{:S(2)}, u32[]{:S(2)}) %collective-permute-start.17) | collective-permute-done | bytes 114720 | tf_op jit(solution)/shard_map/ppermute | solution.py:351
  62.7 2.4 %collective-permute-done.16.r3_ref = bf16[2,224,128]{2,1,0:T(8,128)(2,1)S(1)} collective-permute-done((bf16[2,224,128]{2,1,0:T(8,128)(2,1)S(1)}, bf16[2,224,128]{2,1,0:T(8,128)(2,1)S(1)}, u32[]{:S(2)}, u32[]{:S(2)}) %collective-permute-start.16) | collective-permute-done | bytes 114720 | tf_op jit(solution)/shard_map/ppermute | solution.py:351
  65.0 2.1 %ffn.1 = (f32[2,224,128]{2,1,0:T(8,128)S(1)}, bf16[2,224,128]{2,1,0:T(8,128)(2,1)S(1)}, bf16[2,224,128]{2,1,0:T(8,128)(2,1)S(1)}, bf16[2,224,128]{2,1,0:T(8,128)(2,1)S(1)}) custom-call(bf16[2,224,128]{2,1,0:T(8,128)(2,1)S(1)} %add_convert_fusion.own_ref, bf16[2,224,128]{2,1,0:T(8,128)(2,1)S(1)} %collective-permute-done.15.r1_ref, ...), custom_call_target="tpu_custom_call" | custom-call | tf_op jit(solution)/shard_map/ffn/pallas_call | solution.py:25
  67.1 1.8 %collective-permute-start.18 = (bf16[2,224,128]{2,1,0:T(8,128)(2,1)S(1)}, bf16[2,224,128]{2,1,0:T(8,128)(2,1)S(1)}, u32[]{:S(2)}, u32[]{:S(2)}) collective-permute-start(bf16[2,224,128]{2,1,0:T(8,128)(2,1)S(1)} %get-tuple-element.98), channel_id=1, source_target_pairs={{0,4},{1,5},{2,6},{3,7},{4,0},{5,1},{6,2},{7,3},{8,12},{9,13},{10,... | collective-permute-start | bytes 344072 | tf_op jit(solution)/shard_map/ppermute | solution.py:351
  68.9 1.5 %collective-permute-start.19 = (bf16[2,224,128]{2,1,0:T(8,128)(2,1)S(1)}, bf16[2,224,128]{2,1,0:T(8,128)(2,1)S(1)}, u32[]{:S(2)}, u32[]{:S(2)}) collective-permute-start(bf16[2,224,128]{2,1,0:T(8,128)(2,1)S(1)} %get-tuple-element.99), channel_id=1, source_target_pairs={{0,2},{1,3},{2,0},{3,1},{4,6},{5,7},{6,4},{7,5},{8,10},{9,11},{10,... | collective-permute-start | bytes 344072 | tf_op jit(solution)/shard_map/ppermute | solution.py:351
  71.3 3.4 %collective-permute-done.18 = bf16[2,224,128]{2,1,0:T(8,128)(2,1)S(1)} collective-permute-done((bf16[2,224,128]{2,1,0:T(8,128)(2,1)S(1)}, bf16[2,224,128]{2,1,0:T(8,128)(2,1)S(1)}, u32[]{:S(2)}, u32[]{:S(2)}) %collective-permute-start.18) | collective-permute-done | bytes 114720 | tf_op jit(solution)/shard_map/ppermute | solution.py:351
  74.6 1.2 %collective-permute-done.19 = bf16[2,224,128]{2,1,0:T(8,128)(2,1)S(1)} collective-permute-done((bf16[2,224,128]{2,1,0:T(8,128)(2,1)S(1)}, bf16[2,224,128]{2,1,0:T(8,128)(2,1)S(1)}, u32[]{:S(2)}, u32[]{:S(2)}) %collective-permute-start.19) | collective-permute-done | bytes 114720 | tf_op jit(solution)/shard_map/ppermute | solution.py:351
  76.7 2.4 %collective-permute-start.21 = (bf16[224,128]{1,0:T(8,128)(2,1)S(1)}, bf16[224,128]{1,0:T(8,128)(2,1)S(1)}, u32[]{:S(2)}, u32[]{:S(2)}) collective-permute-start(bf16[224,128]{1,0:T(8,128)(2,1)S(1)} %fusion.4), channel_id=1, source_target_pairs={{0,1},{1,0},{2,3},{3,2},{4,5},{5,4},{6,7},{7,6},{8,9},{9,8},{10,11... | collective-permute-start | bytes 172040 | tf_op jit(solution)/shard_map/ppermute | solution.py:354
  79.0 6.4 %collective-permute-done.21 = bf16[224,128]{1,0:T(8,128)(2,1)S(1)} collective-permute-done((bf16[224,128]{1,0:T(8,128)(2,1)S(1)}, bf16[224,128]{1,0:T(8,128)(2,1)S(1)}, u32[]{:S(2)}, u32[]{:S(2)}) %collective-permute-start.21) | collective-permute-done | bytes 57376 | tf_op jit(solution)/shard_map/ppermute | solution.py:354
  (44 shorter events, 5.9 us)
Async XLA Ops:
  1.6 16.9 %collective-permute-start.3 = (bf16[2,160,128]{2,1,0:T(8,128)(2,1)S(1)}, bf16[2,160,128]{2,1,0:T(8,128)(2,1)S(1)}, u32[]{:S(2)}, u32[]{:S(2)}) collective-permute-start(bf16[2,160,128]{2,1,0:T(8,128)(2,1)S(1)} %get-tuple-element.55), channel_id=1, source_target_pairs={{0,48},{8,56},{16,32},{24,40},{32,16},{40,24},{48,0},{56,8},{64,11... | collective-permute-start | bytes 245768 | tf_op jit(solution)/shard_map/ppermute | solution.py:357
  6.3 12.2 %collective-permute-start.2 = (bf16[2,160,128]{2,1,0:T(8,128)(2,1)S(1)}, bf16[2,160,128]{2,1,0:T(8,128)(2,1)S(1)}, u32[]{:S(2)}, u32[]{:S(2)}) collective-permute-start(bf16[2,160,128]{2,1,0:T(8,128)(2,1)S(1)} %get-tuple-element.55), channel_id=1, source_target_pairs={{0,32},{8,40},{16,48},{24,56},{32,0},{40,8},{48,16},{56,24},{64,96... | collective-permute-start | bytes 245768 | tf_op jit(solution)/shard_map/ppermute | solution.py:357
  6.3 12.2 %collective-permute-start.1 = (bf16[2,160,128]{2,1,0:T(8,128)(2,1)S(1)}, bf16[2,160,128]{2,1,0:T(8,128)(2,1)S(1)}, u32[]{:S(2)}, u32[]{:S(2)}) collective-permute-start(bf16[2,160,128]{2,1,0:T(8,128)(2,1)S(1)} %get-tuple-element.55), channel_id=1, source_target_pairs={{0,16},{8,24},{16,0},{24,8},{32,48},{40,56},{48,32},{56,40},{64,80... | collective-permute-start | bytes 245768 | tf_op jit(solution)/shard_map/ppermute | solution.py:357
  7.0 11.5 %collective-permute-start = (bf16[224,128]{1,0:T(8,128)(2,1)}, bf16[224,128]{1,0:T(8,128)(2,1)S(1)}, u32[]{:S(2)}, u32[]{:S(2)}) collective-permute-start(bf16[224,128]{1,0:T(8,128)(2,1)} %bitcast.46), channel_id=1, source_target_pairs={{0,1},{1,0},{2,3},{3,2},{4,5},{5,4},{6,7},{7,6},{8,9},{9,8},{10,11... | collective-permute-start | bytes 172040 | tf_op jit(solution)/shard_map/ppermute | solution.py:354
  14.6 18.5 %copy-start.3 = (f32[3,224]{1,0:T(4,128)S(1)}, f32[3,224]{1,0:T(4,128)}, u32[]{:S(2)}) copy-start(f32[3,224]{1,0:T(4,128)} %taps_ref.1) | copy-start | bytes 8068
  14.6 18.5 %copy-start.4 = (s32[128]{0:T(128)S(1)}, s32[128]{0:T(128)}, u32[]{:S(2)}) copy-start(s32[128]{0:T(128)} %param.21) | copy-start | bytes 1540
  18.6 3.2 %collective-permute-start.7 = (bf16[4,2,160,128]{3,2,1,0:T(8,128)(2,1)S(1)}, bf16[4,2,160,128]{3,2,1,0:T(8,128)(2,1)S(1)}, u32[]{:S(2)}, u32[]{:S(2)}) collective-permute-start(bf16[4,2,160,128]{3,2,1,0:T(8,128)(2,1)S(1)} %pad_maximum_fusion.mine_ref), channel_id=1, source_target_pairs={{0,8},{8,0},{16,24},{24,16},{32,40},{40,32},{48,56},{56,48},{64,72... | collective-permute-start | bytes 983048 | tf_op jit(solution)/shard_map/ppermute | solution.py:360
  18.7 9.5 %collective-permute-start.6 = (bf16[2,224,128]{2,1,0:T(8,128)(2,1)S(1)}, bf16[2,224,128]{2,1,0:T(8,128)(2,1)S(1)}, u32[]{:S(2)}, u32[]{:S(2)}) collective-permute-start(bf16[2,224,128]{2,1,0:T(8,128)(2,1)S(1)} %stack_pair.1.own_ref), channel_id=1, source_target_pairs={{0,4},{1,5},{2,6},{3,7},{4,0},{5,1},{6,2},{7,3},{8,12},{9,13},{10,... | collective-permute-start | bytes 344072 | tf_op jit(solution)/shard_map/ppermute | solution.py:351
  22.8 11.4 %collective-permute-start.8 = (bf16[2,2,160,128]{3,2,1,0:T(8,128)(2,1)S(1)}, bf16[2,2,160,128]{3,2,1,0:T(8,128)(2,1)S(1)}, u32[]{:S(2)}, u32[]{:S(2)}) collective-permute-start(bf16[2,2,160,128]{3,2,1,0:T(8,128)(2,1)S(1)} %get-tuple-element.73), channel_id=1, source_target_pairs={{0,128},{8,136},{16,144},{24,152},{32,160},{40,168},{48,176},{56,1... | collective-permute-start | bytes 491528 | tf_op jit(solution)/shard_map/ppermute | solution.py:363
  25.2 9.1 %collective-permute-start.9 = (bf16[2,2,160,128]{3,2,1,0:T(8,128)(2,1)S(1)}, bf16[2,2,160,128]{3,2,1,0:T(8,128)(2,1)S(1)}, u32[]{:S(2)}, u32[]{:S(2)}) collective-permute-start(bf16[2,2,160,128]{3,2,1,0:T(8,128)(2,1)S(1)} %get-tuple-element.74), channel_id=1, source_target_pairs={{0,64},{8,72},{16,80},{24,88},{32,96},{40,104},{48,112},{56,120},{... | collective-permute-start | bytes 491528 | tf_op jit(solution)/shard_map/ppermute | solution.py:363
  26.5 7.8 %collective-permute-start.10 = (bf16[2,2,160,128]{3,2,1,0:T(8,128)(2,1)S(1)}, bf16[2,2,160,128]{3,2,1,0:T(8,128)(2,1)S(1)}, u32[]{:S(2)}, u32[]{:S(2)}) collective-permute-start(bf16[2,2,160,128]{3,2,1,0:T(8,128)(2,1)S(1)} %get-tuple-element.75), channel_id=1, source_target_pairs={{0,192},{8,200},{16,208},{24,216},{32,224},{40,232},{48,240},{56,2... | collective-permute-start | bytes 491528 | tf_op jit(solution)/shard_map/ppermute | solution.py:363
  27.0 6.0 %collective-permute-start.5 = (bf16[2,224,128]{2,1,0:T(8,128)(2,1)S(1)}, bf16[2,224,128]{2,1,0:T(8,128)(2,1)S(1)}, u32[]{:S(2)}, u32[]{:S(2)}) collective-permute-start(bf16[2,224,128]{2,1,0:T(8,128)(2,1)S(1)} %stack_pair.1.own_ref), channel_id=1, source_target_pairs={{0,6},{1,7},{2,4},{3,5},{4,2},{5,3},{6,0},{7,1},{8,14},{9,15},{10,... | collective-permute-start | bytes 344072 | tf_op jit(solution)/shard_map/ppermute | solution.py:351
  28.2 4.8 %collective-permute-start.4 = (bf16[2,224,128]{2,1,0:T(8,128)(2,1)S(1)}, bf16[2,224,128]{2,1,0:T(8,128)(2,1)S(1)}, u32[]{:S(2)}, u32[]{:S(2)}) collective-permute-start(bf16[2,224,128]{2,1,0:T(8,128)(2,1)S(1)} %stack_pair.1.own_ref), channel_id=1, source_target_pairs={{0,2},{1,3},{2,0},{3,1},{4,6},{5,7},{6,4},{7,5},{8,10},{9,11},{10,... | collective-permute-start | bytes 344072 | tf_op jit(solution)/shard_map/ppermute | solution.py:351
  28.5 16.0 %copy-start.2 = (bf16[1792,608]{0,1:T(8,128)(2,1)S(1)}, bf16[1792,608]{0,1:T(8,128)(2,1)}, u32[]{:S(2)}) copy-start(bf16[1792,608]{0,1:T(8,128)(2,1)} %param.37) | copy-start | bytes 6537220
  33.0 6.5 %copy-start.5 = (f32[1792]{0:T(1024)S(1)}, f32[1792]{0:T(1024)}, u32[]{:S(2)}) copy-start(f32[1792]{0:T(1024)} %param.29) | copy-start | bytes 21508
  33.0 11.4 %copy-start.1 = (bf16[1792,608]{0,1:T(8,128)(2,1)S(1)}, bf16[1792,608]{0,1:T(8,128)(2,1)}, u32[]{:S(2)}) copy-start(bf16[1792,608]{0,1:T(8,128)(2,1)} %param.36) | copy-start | bytes 6537220
  34.2 10.2 %copy-start = (bf16[608,1792]{1,0:T(8,128)(2,1)S(1)}, bf16[608,1792]{1,0:T(8,128)(2,1)}, u32[]{:S(2)}) copy-start(bf16[608,1792]{1,0:T(8,128)(2,1)} %refs_0_.3) | copy-start | bytes 6537220
  35.4 7.6 %collective-permute-start.11 = (bf16[2,224,128]{2,1,0:T(8,128)(2,1)S(1)}, bf16[2,224,128]{2,1,0:T(8,128)(2,1)S(1)}, u32[]{:S(2)}, u32[]{:S(2)}) collective-permute-start(bf16[2,224,128]{2,1,0:T(8,128)(2,1)S(1)} %get-tuple-element.78), channel_id=1, source_target_pairs={{0,4},{1,5},{2,6},{3,7},{4,0},{5,1},{6,2},{7,3},{8,12},{9,13},{10,... | collective-permute-start | bytes 344072 | tf_op jit(solution)/shard_map/ppermute | solution.py:351
  37.0 6.0 %collective-permute-start.12 = (bf16[2,224,128]{2,1,0:T(8,128)(2,1)S(1)}, bf16[2,224,128]{2,1,0:T(8,128)(2,1)S(1)}, u32[]{:S(2)}, u32[]{:S(2)}) collective-permute-start(bf16[2,224,128]{2,1,0:T(8,128)(2,1)S(1)} %get-tuple-element.79), channel_id=1, source_target_pairs={{0,2},{1,3},{2,0},{3,1},{4,6},{5,7},{6,4},{7,5},{8,10},{9,11},{10,... | collective-permute-start | bytes 344072 | tf_op jit(solution)/shard_map/ppermute | solution.py:351
  38.2 6.1 %collective-permute-start.13 = (bf16[2,224,128]{2,1,0:T(8,128)(2,1)S(1)}, bf16[2,224,128]{2,1,0:T(8,128)(2,1)S(1)}, u32[]{:S(2)}, u32[]{:S(2)}) collective-permute-start(bf16[2,224,128]{2,1,0:T(8,128)(2,1)S(1)} %get-tuple-element.80), channel_id=1, source_target_pairs={{0,6},{1,7},{2,4},{3,5},{4,2},{5,3},{6,0},{7,1},{8,14},{9,15},{10,... | collective-permute-start | bytes 344072 | tf_op jit(solution)/shard_map/ppermute | solution.py:351
  44.7 11.4 %collective-permute-start.14 = (bf16[2,224,128]{2,1,0:T(8,128)(2,1)S(1)}, bf16[2,224,128]{2,1,0:T(8,128)(2,1)S(1)}, u32[]{:S(2)}, u32[]{:S(2)}) collective-permute-start(bf16[2,224,128]{2,1,0:T(8,128)(2,1)S(1)} %pad_maximum_fusion.1), channel_id=1, source_target_pairs={{0,1},{1,0},{2,3},{3,2},{4,5},{5,4},{6,7},{7,6},{8,9},{9,8},{10,11... | collective-permute-start | bytes 344072 | tf_op jit(solution)/shard_map/ppermute | solution.py:354
  56.2 6.5 %collective-permute-start.17 = (bf16[2,224,128]{2,1,0:T(8,128)(2,1)S(1)}, bf16[2,224,128]{2,1,0:T(8,128)(2,1)S(1)}, u32[]{:S(2)}, u32[]{:S(2)}) collective-permute-start(bf16[2,224,128]{2,1,0:T(8,128)(2,1)S(1)} %add_convert_fusion.own_ref), channel_id=1, source_target_pairs={{0,4},{1,5},{2,6},{3,7},{4,0},{5,1},{6,2},{7,3},{8,12},{9,13},{10,... | collective-permute-start | bytes 344072 | tf_op jit(solution)/shard_map/ppermute | solution.py:351
  58.0 7.0 %collective-permute-start.16 = (bf16[2,224,128]{2,1,0:T(8,128)(2,1)S(1)}, bf16[2,224,128]{2,1,0:T(8,128)(2,1)S(1)}, u32[]{:S(2)}, u32[]{:S(2)}) collective-permute-start(bf16[2,224,128]{2,1,0:T(8,128)(2,1)S(1)} %add_convert_fusion.own_ref), channel_id=1, source_target_pairs={{0,6},{1,7},{2,4},{3,5},{4,2},{5,3},{6,0},{7,1},{8,14},{9,15},{10,... | collective-permute-start | bytes 344072 | tf_op jit(solution)/shard_map/ppermute | solution.py:351
  59.6 5.4 %collective-permute-start.15 = (bf16[2,224,128]{2,1,0:T(8,128)(2,1)S(1)}, bf16[2,224,128]{2,1,0:T(8,128)(2,1)S(1)}, u32[]{:S(2)}, u32[]{:S(2)}) collective-permute-start(bf16[2,224,128]{2,1,0:T(8,128)(2,1)S(1)} %add_convert_fusion.own_ref), channel_id=1, source_target_pairs={{0,2},{1,3},{2,0},{3,1},{4,6},{5,7},{6,4},{7,5},{8,10},{9,11},{10,... | collective-permute-start | bytes 344072 | tf_op jit(solution)/shard_map/ppermute | solution.py:351
  67.1 7.5 %collective-permute-start.18 = (bf16[2,224,128]{2,1,0:T(8,128)(2,1)S(1)}, bf16[2,224,128]{2,1,0:T(8,128)(2,1)S(1)}, u32[]{:S(2)}, u32[]{:S(2)}) collective-permute-start(bf16[2,224,128]{2,1,0:T(8,128)(2,1)S(1)} %get-tuple-element.98), channel_id=1, source_target_pairs={{0,4},{1,5},{2,6},{3,7},{4,0},{5,1},{6,2},{7,3},{8,12},{9,13},{10,... | collective-permute-start | bytes 344072 | tf_op jit(solution)/shard_map/ppermute | solution.py:351
  68.9 7.0 %collective-permute-start.19 = (bf16[2,224,128]{2,1,0:T(8,128)(2,1)S(1)}, bf16[2,224,128]{2,1,0:T(8,128)(2,1)S(1)}, u32[]{:S(2)}, u32[]{:S(2)}) collective-permute-start(bf16[2,224,128]{2,1,0:T(8,128)(2,1)S(1)} %get-tuple-element.99), channel_id=1, source_target_pairs={{0,2},{1,3},{2,0},{3,1},{4,6},{5,7},{6,4},{7,5},{8,10},{9,11},{10,... | collective-permute-start | bytes 344072 | tf_op jit(solution)/shard_map/ppermute | solution.py:351
  70.4 6.2 %collective-permute-start.20 = (bf16[2,224,128]{2,1,0:T(8,128)(2,1)S(1)}, bf16[2,224,128]{2,1,0:T(8,128)(2,1)S(1)}, u32[]{:S(2)}, u32[]{:S(2)}) collective-permute-start(bf16[2,224,128]{2,1,0:T(8,128)(2,1)S(1)} %get-tuple-element.100), channel_id=1, source_target_pairs={{0,6},{1,7},{2,4},{3,5},{4,2},{5,3},{6,0},{7,1},{8,14},{9,15},{10,... | collective-permute-start | bytes 344072 | tf_op jit(solution)/shard_map/ppermute | solution.py:351
  76.7 8.8 %collective-permute-start.21 = (bf16[224,128]{1,0:T(8,128)(2,1)S(1)}, bf16[224,128]{1,0:T(8,128)(2,1)S(1)}, u32[]{:S(2)}, u32[]{:S(2)}) collective-permute-start(bf16[224,128]{1,0:T(8,128)(2,1)S(1)} %fusion.4), channel_id=1, source_target_pairs={{0,1},{1,0},{2,3},{3,2},{4,5},{5,4},{6,7},{7,6},{8,9},{9,8},{10,11... | collective-permute-start | bytes 172040 | tf_op jit(solution)/shard_map/ppermute | solution.py:354

commit v12 on v8

--- a/solution.py
+++ b/solution.py
@@ -169,11 +169,18 @@
     return index >> 1, index & 1
 
 
+OTHER_CORE = {0: 0, 1: 3, 2: 1, 3: 2}
+
+
+def partner(k):
+    return jnp.where((lax.axis_index("req") & 1) == 1, OTHER_CORE[k], k)
+
+
 def place_blocks(scratch, blocks):
     x, z = tp_place()
     rows = blocks[0].shape[1]
     for k, block in enumerate(blocks):
-        source = x ^ k
+        source = x ^ partner(k)
         scratch[pl.ds(pl.multiple_of((2 * source + z) * rows, 32), rows), :] = block[0]
         scratch[pl.ds(pl.multiple_of((2 * source + 1 - z) * rows, 32), rows), :] = block[1]
 
@@ -300,7 +307,7 @@
     x, z = tp_place()
     rows = outs[0].shape[1]
     for k, out in enumerate(outs):
-        to = x ^ k
+        to = x ^ partner(k)
         for half, at in ((0, 2 * to + z), (1, 2 * to + 1 - z)):
             block = weight_ref[pl.ds(pl.multiple_of(at * rows, 32), rows), :]
             out[half] = jnp.dot(block, right, preferred_element_type=F32).astype(out.dtype)
@@ -329,7 +336,12 @@
     per = request_leaf.shape[0] // req_size
 
     def along_x(array, k):
-        return lax.ppermute(array, "tp", [(i, i ^ (2 * k)) for i in range(tp_size)])
+        pairs = [
+            (r * tp_size + i, r * tp_size + (i ^ (2 * (OTHER_CORE[k] if r % 2 else k))))
+            for r in range(req_size)
+            for i in range(tp_size)
+        ]
+        return lax.ppermute(array, ("req", "tp"), pairs)
 
     def across_z(array):
         return lax.ppermute(array, "tp", [(i, i ^ 1) for i in range(tp_size)])

time: 82.9 us -> 83.9 us (1.012)
  transfers between devices with their start and end apart: 22 -> 22, of which waited for: 14 -> 12; matrix products, arithmetic and copies ran while one was open for 2% -> 2% of each run, Pallas kernels for 10% -> 10%
where the time goes in v12:
time: 83.9 us; the launch traced here: 82.7 us
  starting transfers between devices  39.4 us (47%)
  waiting for transfers between devices  28.2 us (34%)
  Pallas kernels  12.6 us (15%)
  local copies, waits for them, and re-layouts  1.35 us (2%)
  other arithmetic  0.92 us (1%)
    ppermute x12, waiting for transfers between devices, along_x(): return lax.ppermute(array, ('req', 'tp'), pairs)  18 us
    ppermute x12, starting transfers between devices, along_x(): return lax.ppermute(array, ('req', 'tp'), pairs)  17.1 us
    ppermute x3, starting transfers between devices, across_z(): return lax.ppermute(array, 'tp', [(i, i ^ 1) for i in range(tp_size)])  12.6 us
    ppermute x3, waiting for transfers between devices, across_z(): return lax.ppermute(array, 'tp', [(i, i ^ 1) for i in range(tp_size)])  10.2 us
    pallas_call x7, Pallas kernels, call(): pl.pallas_call(kernel, out_shape=out_shape, in_specs=specs, out_specs=VME...  7.77 us
    ppermute x3, starting transfers between devices, along_z(): return lax.ppermute(array, 'req', [(i, i ^ 2 * k) for i in range(req_size)])  5.37 us
    ppermute x3, starting transfers between devices, along_y(): lax.ppermute(array, 'req', [(i, i ^ 2 * z_size * k) for i in range(req_si...  4.18 us
    pallas_call x1, Pallas kernels, shards(): pl.pallas_call(functools.partial(mixer_weights_kernel, y_size, z_size), o...  3.24 us
  transfers between devices with their start and end apart: 22, of which 12 were waited for; matrix products, arithmetic and copies ran while one was open for 2% of the time, Pallas kernels for 10%

profile of v12, /device:TPU:8, one launch (start us, length us, event | category | flops | bytes accessed | tf_op | source)
XLA Modules:
  0.0 82.7 jit_solution(9126181688023062097)
XLA Ops:
  0.0 1.6 %fold.1 = (bf16[2,160,128]{2,1,0:T(8,128)(2,1)S(1)}, bf16[224,128]{1,0:T(8,128)(2,1)S(1)}) custom-call(bf16[160,273]{1,0:T(8,128)(2,1)} %constant.5.clone.fold_hbm, bf16[273,2,112]{2,1,0:T(2,128)(2,1)} %bitcast.37, bf16[2,273]{1,0:T(2,128)(2,1)} %bitcast.47, bf16[2,224]{1,0:T(2,128)(2,1)} %bitcast.48, bf16[224,128]{1,0:T(8,128)(2,1)} %bitcast.43), custom_call_target="tpu_custom_call" | custom-call | tf_op jit(solution)/shard_map/fold/pallas_call | solution.py:368
  1.6 4.7 %collective-permute-start.3 = (bf16[2,160,128]{2,1,0:T(8,128)(2,1)S(1)}, bf16[2,160,128]{2,1,0:T(8,128)(2,1)S(1)}, u32[]{:S(2)}, u32[]{:S(2)}) collective-permute-start(bf16[2,160,128]{2,1,0:T(8,128)(2,1)S(1)} %get-tuple-element.48), channel_id=1, source_target_pairs={{0,48},{8,56},{16,32},{24,40},{32,16},{40,24},{48,0},{56,8},{64,11... | collective-permute-start | bytes 245768 | tf_op jit(solution)/shard_map/ppermute | solution.py:350
  7.0 6.3 %collective-permute-start = (bf16[224,128]{1,0:T(8,128)(2,1)}, bf16[224,128]{1,0:T(8,128)(2,1)S(1)}, u32[]{:S(2)}, u32[]{:S(2)}) collective-permute-start(bf16[224,128]{1,0:T(8,128)(2,1)} %bitcast.44), channel_id=1, source_target_pairs={{0,1},{1,0},{2,3},{3,2},{4,5},{5,4},{6,7},{7,6},{8,9},{9,8},{10,11... | collective-permute-start | bytes 172040 | tf_op jit(solution)/shard_map/ppermute | solution.py:347
  13.3 1.3 %pad.7.refs_8_ = f32[16,128]{1,0:T(8,128)} pad(f32[14,128]{1,0:T(8,128)} %bitcast.45, f32[]{:T(128)} %constant.4.clone.1), padding=0_2x0_0 | pad | bytes 15364 | tf_op jit(solution)/shard_map/jit(_pad)/pad | solution.py:380
  14.6 3.2 %mixer_weights.1 = (bf16[1792,224]{1,0:T(8,128)(2,1)S(1)}, s32[24]{0:T(128)S(1)}, bf16[512,1792]{1,0:T(8,128)(2,1)S(1)}) custom-call(bf16[224,1792]{1,0:T(8,128)(2,1)} %refs_0_.1, s32[64]{0:T(128)} %refs_1_.1, s32[32]{0:T(128)} %refs_2_.1, s32[32]{0:T(128)} %refs_3_.1, bf16[32,1792]{1,0:T(8,128)(2,1)} %bitcast.38, bf16[32,1792]{1,0:T(8,128)(2,1)} %bitcast.39, ...), custom_call_target="tpu_custom_call" | custom-call | tf_op jit(solution)/shard_map/mixer_weights/pallas_call | solution.py:384
  18.7 3.1 %collective-permute-start.6 = (bf16[2,224,128]{2,1,0:T(8,128)(2,1)S(1)}, bf16[2,224,128]{2,1,0:T(8,128)(2,1)S(1)}, u32[]{:S(2)}, u32[]{:S(2)}) collective-permute-start(bf16[2,224,128]{2,1,0:T(8,128)(2,1)S(1)} %stack_pair.1.own_ref), channel_id=1, source_target_pairs={{0,4},{1,5},{2,6},{3,7},{4,0},{5,1},{6,2},{7,3},{8,10},{9,11},{10,... | collective-permute-start | bytes 344072 | tf_op jit(solution)/shard_map/ppermute | solution.py:344
  21.8 1.0 %select_sent.1 = (bf16[2,2,160,128]{3,2,1,0:T(8,128)(2,1)S(1)}, bf16[2,2,160,128]{3,2,1,0:T(8,128)(2,1)S(1)}, bf16[2,2,160,128]{3,2,1,0:T(8,128)(2,1)S(1)}) custom-call(s32[24]{0:T(128)S(1)} %get-tuple-element.51.slot_ref, bf16[4,2,160,128]{3,2,1,0:T(8,128)(2,1)S(1)} %pad_maximum_fusion.mine_ref, bf16[4,2,160,128]{3,2,1,0:T(8,128)(2,1)S(1)} %collective-permute-done.7.other_ref), custom_call_target="tpu_custom_call" | custom-call | tf_op jit(solution)/shard_map/select_sent/pallas_call | solution.py:25
  22.8 2.4 %collective-permute-start.8 = (bf16[2,2,160,128]{3,2,1,0:T(8,128)(2,1)S(1)}, bf16[2,2,160,128]{3,2,1,0:T(8,128)(2,1)S(1)}, u32[]{:S(2)}, u32[]{:S(2)}) collective-permute-start(bf16[2,2,160,128]{3,2,1,0:T(8,128)(2,1)S(1)} %get-tuple-element.66), channel_id=1, source_target_pairs={{0,128},{8,136},{16,144},{24,152},{32,160},{40,168},{48,176},{56,1... | collective-permute-start | bytes 491528 | tf_op jit(solution)/shard_map/ppermute | solution.py:356
  25.2 1.3 %collective-permute-start.9 = (bf16[2,2,160,128]{3,2,1,0:T(8,128)(2,1)S(1)}, bf16[2,2,160,128]{3,2,1,0:T(8,128)(2,1)S(1)}, u32[]{:S(2)}, u32[]{:S(2)}) collective-permute-start(bf16[2,2,160,128]{3,2,1,0:T(8,128)(2,1)S(1)} %get-tuple-element.67), channel_id=1, source_target_pairs={{0,64},{8,72},{16,80},{24,88},{32,96},{40,104},{48,112},{56,120},{... | collective-permute-start | bytes 491528 | tf_op jit(solution)/shard_map/ppermute | solution.py:356
  27.0 1.3 %collective-permute-start.5 = (bf16[2,224,128]{2,1,0:T(8,128)(2,1)S(1)}, bf16[2,224,128]{2,1,0:T(8,128)(2,1)S(1)}, u32[]{:S(2)}, u32[]{:S(2)}) collective-permute-start(bf16[2,224,128]{2,1,0:T(8,128)(2,1)S(1)} %stack_pair.1.own_ref), channel_id=1, source_target_pairs={{0,6},{1,7},{2,4},{3,5},{4,2},{5,3},{6,0},{7,1},{8,12},{9,13},{10,... | collective-permute-start | bytes 344072 | tf_op jit(solution)/shard_map/ppermute | solution.py:344
  29.2 4.6 %collective-permute-done.5.r3_ref = bf16[2,224,128]{2,1,0:T(8,128)(2,1)S(1)} collective-permute-done((bf16[2,224,128]{2,1,0:T(8,128)(2,1)S(1)}, bf16[2,224,128]{2,1,0:T(8,128)(2,1)S(1)}, u32[]{:S(2)}, u32[]{:S(2)}) %collective-permute-start.5) | collective-permute-done | bytes 114720 | tf_op jit(solution)/shard_map/ppermute | solution.py:344
  33.8 1.1 %local.1 = (f32[224,128]{1,0:T(8,128)S(1)}, f32[224,128]{1,0:T(8,128)S(1)}, bf16[2,128,128]{2,1,0:T(8,128)(2,1)S(1)}, f32[2,1,128]{2,1,0:T(1,128)S(1)}, bf16[2,3...) custom-call(bf16[2,224,128]{2,1,0:T(8,128)(2,1)S(1)} %stack_pair.1.own_ref, ...), custom_call_target="tpu_custom_call" | custom-call | tf_op jit(solution)/shard_map/local/pallas_call | solution.py:25
  35.0 1.1 %mix.1 = (f32[2,224,128]{2,1,0:T(8,128)S(1)}, bf16[2,224,128]{2,1,0:T(8,128)(2,1)S(1)}, bf16[2,224,128]{2,1,0:T(8,128)(2,1)S(1)}, bf16[2,224,128]{2,1,0:T(8,128)(2,1)S(1)}) custom-call(f32[224,128]{1,0:T(8,128)S(1)} %get-tuple-element.60.conv_ref, f32[224,128]{1,0:T(8,128)S(1)} %get-tuple-element.61.silu_ref, ...), custom_call_target="tpu_custom_call" | custom-call | tf_op jit(solution)/shard_map/mix/pallas_call | solution.py:25
  36.1 1.0 %collective-permute-start.11 = (bf16[2,224,128]{2,1,0:T(8,128)(2,1)S(1)}, bf16[2,224,128]{2,1,0:T(8,128)(2,1)S(1)}, u32[]{:S(2)}, u32[]{:S(2)}) collective-permute-start(bf16[2,224,128]{2,1,0:T(8,128)(2,1)S(1)} %get-tuple-element.71), channel_id=1, source_target_pairs={{0,4},{1,5},{2,6},{3,7},{4,0},{5,1},{6,2},{7,3},{8,10},{9,11},{10,... | collective-permute-start | bytes 344072 | tf_op jit(solution)/shard_map/ppermute | solution.py:344
  37.1 1.4 %collective-permute-start.12 = (bf16[2,224,128]{2,1,0:T(8,128)(2,1)S(1)}, bf16[2,224,128]{2,1,0:T(8,128)(2,1)S(1)}, u32[]{:S(2)}, u32[]{:S(2)}) collective-permute-start(bf16[2,224,128]{2,1,0:T(8,128)(2,1)S(1)} %get-tuple-element.72), channel_id=1, source_target_pairs={{0,2},{1,3},{2,0},{3,1},{4,6},{5,7},{6,4},{7,5},{8,14},{9,15},{10,... | collective-permute-start | bytes 344072 | tf_op jit(solution)/shard_map/ppermute | solution.py:344
  38.5 1.7 %collective-permute-start.13 = (bf16[2,224,128]{2,1,0:T(8,128)(2,1)S(1)}, bf16[2,224,128]{2,1,0:T(8,128)(2,1)S(1)}, u32[]{:S(2)}, u32[]{:S(2)}) collective-permute-start(bf16[2,224,128]{2,1,0:T(8,128)(2,1)S(1)} %get-tuple-element.73), channel_id=1, source_target_pairs={{0,6},{1,7},{2,4},{3,5},{4,2},{5,3},{6,0},{7,1},{8,12},{9,13},{10,... | collective-permute-start | bytes 344072 | tf_op jit(solution)/shard_map/ppermute | solution.py:344
  40.3 3.1 %collective-permute-done.11 = bf16[2,224,128]{2,1,0:T(8,128)(2,1)S(1)} collective-permute-done((bf16[2,224,128]{2,1,0:T(8,128)(2,1)S(1)}, bf16[2,224,128]{2,1,0:T(8,128)(2,1)S(1)}, u32[]{:S(2)}, u32[]{:S(2)}) %collective-permute-start.11) | collective-permute-done | bytes 114720 | tf_op jit(solution)/shard_map/ppermute | solution.py:344
  43.8 1.1 %collective-permute-done.13 = bf16[2,224,128]{2,1,0:T(8,128)(2,1)S(1)} collective-permute-done((bf16[2,224,128]{2,1,0:T(8,128)(2,1)S(1)}, bf16[2,224,128]{2,1,0:T(8,128)(2,1)S(1)}, u32[]{:S(2)}, u32[]{:S(2)}) %collective-permute-start.13) | collective-permute-done | bytes 114720 | tf_op jit(solution)/shard_map/ppermute | solution.py:344
  45.0 3.5 %collective-permute-start.14 = (bf16[2,224,128]{2,1,0:T(8,128)(2,1)S(1)}, bf16[2,224,128]{2,1,0:T(8,128)(2,1)S(1)}, u32[]{:S(2)}, u32[]{:S(2)}) collective-permute-start(bf16[2,224,128]{2,1,0:T(8,128)(2,1)S(1)} %pad_maximum_fusion.1), channel_id=1, source_target_pairs={{0,1},{1,0},{2,3},{3,2},{4,5},{5,4},{6,7},{7,6},{8,9},{9,8},{10,11... | collective-permute-start | bytes 344072 | tf_op jit(solution)/shard_map/ppermute | solution.py:347
  48.5 1.8 %ffn_weights.1 = (bf16[1792,608]{1,0:T(8,128)(2,1)S(1)}, bf16[608,1792]{1,0:T(8,128)(2,1)S(1)}, bf16[608,1792]{1,0:T(8,128)(2,1)S(1)}) custom-call(bf16[608,1792]{1,0:T(8,128)(2,1)S(1)} %copy-done, bf16[608,1792]{1,0:T(8,128)(2,1)S(1)} %bitcast.31, bf16[608,1792]{1,0:T(8,128)(2,1)S(1)} %bitcast.32, f32[16,128]{1,0:T(8,128)S(1)} %pad.8.gain_ref), custom_call_target="tpu_custom_call" | custom-call | tf_op jit(solution)/shard_map/ffn_weights/pallas_call | solution.py:25
  50.3 4.2 %collective-permute-done.14 = bf16[2,224,128]{2,1,0:T(8,128)(2,1)S(1)} collective-permute-done((bf16[2,224,128]{2,1,0:T(8,128)(2,1)S(1)}, bf16[2,224,128]{2,1,0:T(8,128)(2,1)S(1)}, u32[]{:S(2)}, u32[]{:S(2)}) %collective-permute-start.14) | collective-permute-done | bytes 114720 | tf_op jit(solution)/shard_map/ppermute | solution.py:347
  54.6 2.0 %collective-permute-start.17 = (bf16[2,224,128]{2,1,0:T(8,128)(2,1)S(1)}, bf16[2,224,128]{2,1,0:T(8,128)(2,1)S(1)}, u32[]{:S(2)}, u32[]{:S(2)}) collective-permute-start(bf16[2,224,128]{2,1,0:T(8,128)(2,1)S(1)} %add_convert_fusion.own_ref), channel_id=1, source_target_pairs={{0,4},{1,5},{2,6},{3,7},{4,0},{5,1},{6,2},{7,3},{8,10},{9,11},{10,... | collective-permute-start | bytes 344072 | tf_op jit(solution)/shard_map/ppermute | solution.py:344
  56.7 2.1 %collective-permute-start.16 = (bf16[2,224,128]{2,1,0:T(8,128)(2,1)S(1)}, bf16[2,224,128]{2,1,0:T(8,128)(2,1)S(1)}, u32[]{:S(2)}, u32[]{:S(2)}) collective-permute-start(bf16[2,224,128]{2,1,0:T(8,128)(2,1)S(1)} %add_convert_fusion.own_ref), channel_id=1, source_target_pairs={{0,6},{1,7},{2,4},{3,5},{4,2},{5,3},{6,0},{7,1},{8,12},{9,13},{10,... | collective-permute-start | bytes 344072 | tf_op jit(solution)/shard_map/ppermute | solution.py:344
  58.8 2.3 %collective-permute-done.17.r2_ref = bf16[2,224,128]{2,1,0:T(8,128)(2,1)S(1)} collective-permute-done((bf16[2,224,128]{2,1,0:T(8,128)(2,1)S(1)}, bf16[2,224,128]{2,1,0:T(8,128)(2,1)S(1)}, u32[]{:S(2)}, u32[]{:S(2)}) %collective-permute-start.17) | collective-permute-done | bytes 114720 | tf_op jit(solution)/shard_map/ppermute | solution.py:344
  61.1 1.5 %collective-permute-done.16.r3_ref = bf16[2,224,128]{2,1,0:T(8,128)(2,1)S(1)} collective-permute-done((bf16[2,224,128]{2,1,0:T(8,128)(2,1)S(1)}, bf16[2,224,128]{2,1,0:T(8,128)(2,1)S(1)}, u32[]{:S(2)}, u32[]{:S(2)}) %collective-permute-start.16) | collective-permute-done | bytes 114720 | tf_op jit(solution)/shard_map/ppermute | solution.py:344
  63.6 2.1 %ffn.1 = (f32[2,224,128]{2,1,0:T(8,128)S(1)}, bf16[2,224,128]{2,1,0:T(8,128)(2,1)S(1)}, bf16[2,224,128]{2,1,0:T(8,128)(2,1)S(1)}, bf16[2,224,128]{2,1,0:T(8,128)(2,1)S(1)}) custom-call(bf16[2,224,128]{2,1,0:T(8,128)(2,1)S(1)} %add_convert_fusion.own_ref, bf16[2,224,128]{2,1,0:T(8,128)(2,1)S(1)} %collective-permute-done.15.r1_ref, ...), custom_call_target="tpu_custom_call" | custom-call | tf_op jit(solution)/shard_map/ffn/pallas_call | solution.py:25
  66.4 1.4 %collective-permute-start.19 = (bf16[2,224,128]{2,1,0:T(8,128)(2,1)S(1)}, bf16[2,224,128]{2,1,0:T(8,128)(2,1)S(1)}, u32[]{:S(2)}, u32[]{:S(2)}) collective-permute-start(bf16[2,224,128]{2,1,0:T(8,128)(2,1)S(1)} %get-tuple-element.85), channel_id=1, source_target_pairs={{0,2},{1,3},{2,0},{3,1},{4,6},{5,7},{6,4},{7,5},{8,14},{9,15},{10,... | collective-permute-start | bytes 344072 | tf_op jit(solution)/shard_map/ppermute | solution.py:344
  67.8 2.0 %collective-permute-start.20 = (bf16[2,224,128]{2,1,0:T(8,128)(2,1)S(1)}, bf16[2,224,128]{2,1,0:T(8,128)(2,1)S(1)}, u32[]{:S(2)}, u32[]{:S(2)}) collective-permute-start(bf16[2,224,128]{2,1,0:T(8,128)(2,1)S(1)} %get-tuple-element.86), channel_id=1, source_target_pairs={{0,6},{1,7},{2,4},{3,5},{4,2},{5,3},{6,0},{7,1},{8,12},{9,13},{10,... | collective-permute-start | bytes 344072 | tf_op jit(solution)/shard_map/ppermute | solution.py:344
  69.8 2.2 %collective-permute-done.18 = bf16[2,224,128]{2,1,0:T(8,128)(2,1)S(1)} collective-permute-done((bf16[2,224,128]{2,1,0:T(8,128)(2,1)S(1)}, bf16[2,224,128]{2,1,0:T(8,128)(2,1)S(1)}, u32[]{:S(2)}, u32[]{:S(2)}) %collective-permute-start.18) | collective-permute-done | bytes 114720 | tf_op jit(solution)/shard_map/ppermute | solution.py:344
  72.0 1.8 %collective-permute-done.20 = bf16[2,224,128]{2,1,0:T(8,128)(2,1)S(1)} collective-permute-done((bf16[2,224,128]{2,1,0:T(8,128)(2,1)S(1)}, bf16[2,224,128]{2,1,0:T(8,128)(2,1)S(1)}, u32[]{:S(2)}, u32[]{:S(2)}) %collective-permute-start.20) | collective-permute-done | bytes 114720 | tf_op jit(solution)/shard_map/ppermute | solution.py:344
  73.9 2.9 %collective-permute-start.21 = (bf16[224,128]{1,0:T(8,128)(2,1)S(1)}, bf16[224,128]{1,0:T(8,128)(2,1)S(1)}, u32[]{:S(2)}, u32[]{:S(2)}) collective-permute-start(bf16[224,128]{1,0:T(8,128)(2,1)S(1)} %fusion.4), channel_id=1, source_target_pairs={{0,1},{1,0},{2,3},{3,2},{4,5},{5,4},{6,7},{7,6},{8,9},{9,8},{10,11... | collective-permute-start | bytes 172040 | tf_op jit(solution)/shard_map/ppermute | solution.py:347
  76.7 5.3 %collective-permute-done.21 = bf16[224,128]{1,0:T(8,128)(2,1)S(1)} collective-permute-done((bf16[224,128]{1,0:T(8,128)(2,1)S(1)}, bf16[224,128]{1,0:T(8,128)(2,1)S(1)}, u32[]{:S(2)}, u32[]{:S(2)}) %collective-permute-start.21) | collective-permute-done | bytes 57376 | tf_op jit(solution)/shard_map/ppermute | solution.py:347
  (43 shorter events, 6.0 us)
Async XLA Ops:
  1.6 16.9 %collective-permute-start.3 = (bf16[2,160,128]{2,1,0:T(8,128)(2,1)S(1)}, bf16[2,160,128]{2,1,0:T(8,128)(2,1)S(1)}, u32[]{:S(2)}, u32[]{:S(2)}) collective-permute-start(bf16[2,160,128]{2,1,0:T(8,128)(2,1)S(1)} %get-tuple-element.48), channel_id=1, source_target_pairs={{0,48},{8,56},{16,32},{24,40},{32,16},{40,24},{48,0},{56,8},{64,11... | collective-permute-start | bytes 245768 | tf_op jit(solution)/shard_map/ppermute | solution.py:350
  6.3 12.2 %collective-permute-start.2 = (bf16[2,160,128]{2,1,0:T(8,128)(2,1)S(1)}, bf16[2,160,128]{2,1,0:T(8,128)(2,1)S(1)}, u32[]{:S(2)}, u32[]{:S(2)}) collective-permute-start(bf16[2,160,128]{2,1,0:T(8,128)(2,1)S(1)} %get-tuple-element.48), channel_id=1, source_target_pairs={{0,32},{8,40},{16,48},{24,56},{32,0},{40,8},{48,16},{56,24},{64,96... | collective-permute-start | bytes 245768 | tf_op jit(solution)/shard_map/ppermute | solution.py:350
  6.3 12.2 %collective-permute-start.1 = (bf16[2,160,128]{2,1,0:T(8,128)(2,1)S(1)}, bf16[2,160,128]{2,1,0:T(8,128)(2,1)S(1)}, u32[]{:S(2)}, u32[]{:S(2)}) collective-permute-start(bf16[2,160,128]{2,1,0:T(8,128)(2,1)S(1)} %get-tuple-element.48), channel_id=1, source_target_pairs={{0,16},{8,24},{16,0},{24,8},{32,48},{40,56},{48,32},{56,40},{64,80... | collective-permute-start | bytes 245768 | tf_op jit(solution)/shard_map/ppermute | solution.py:350
  7.0 11.5 %collective-permute-start = (bf16[224,128]{1,0:T(8,128)(2,1)}, bf16[224,128]{1,0:T(8,128)(2,1)S(1)}, u32[]{:S(2)}, u32[]{:S(2)}) collective-permute-start(bf16[224,128]{1,0:T(8,128)(2,1)} %bitcast.44), channel_id=1, source_target_pairs={{0,1},{1,0},{2,3},{3,2},{4,5},{5,4},{6,7},{7,6},{8,9},{9,8},{10,11... | collective-permute-start | bytes 172040 | tf_op jit(solution)/shard_map/ppermute | solution.py:347
  14.6 19.2 %copy-start.3 = (f32[3,224]{1,0:T(4,128)S(1)}, f32[3,224]{1,0:T(4,128)}, u32[]{:S(2)}) copy-start(f32[3,224]{1,0:T(4,128)} %taps_ref.1) | copy-start | bytes 8068
  14.6 19.2 %copy-start.4 = (s32[128]{0:T(128)S(1)}, s32[128]{0:T(128)}, u32[]{:S(2)}) copy-start(s32[128]{0:T(128)} %param.21) | copy-start | bytes 1540
  18.6 3.2 %collective-permute-start.7 = (bf16[4,2,160,128]{3,2,1,0:T(8,128)(2,1)S(1)}, bf16[4,2,160,128]{3,2,1,0:T(8,128)(2,1)S(1)}, u32[]{:S(2)}, u32[]{:S(2)}) collective-permute-start(bf16[4,2,160,128]{3,2,1,0:T(8,128)(2,1)S(1)} %pad_maximum_fusion.mine_ref), channel_id=1, source_target_pairs={{0,8},{8,0},{16,24},{24,16},{32,40},{40,32},{48,56},{56,48},{64,72... | collective-permute-start | bytes 983048 | tf_op jit(solution)/shard_map/ppermute | solution.py:353
  18.7 9.5 %collective-permute-start.6 = (bf16[2,224,128]{2,1,0:T(8,128)(2,1)S(1)}, bf16[2,224,128]{2,1,0:T(8,128)(2,1)S(1)}, u32[]{:S(2)}, u32[]{:S(2)}) collective-permute-start(bf16[2,224,128]{2,1,0:T(8,128)(2,1)S(1)} %stack_pair.1.own_ref), channel_id=1, source_target_pairs={{0,4},{1,5},{2,6},{3,7},{4,0},{5,1},{6,2},{7,3},{8,10},{9,11},{10,... | collective-permute-start | bytes 344072 | tf_op jit(solution)/shard_map/ppermute | solution.py:344
  22.8 12.2 %collective-permute-start.8 = (bf16[2,2,160,128]{3,2,1,0:T(8,128)(2,1)S(1)}, bf16[2,2,160,128]{3,2,1,0:T(8,128)(2,1)S(1)}, u32[]{:S(2)}, u32[]{:S(2)}) collective-permute-start(bf16[2,2,160,128]{3,2,1,0:T(8,128)(2,1)S(1)} %get-tuple-element.66), channel_id=1, source_target_pairs={{0,128},{8,136},{16,144},{24,152},{32,160},{40,168},{48,176},{56,1... | collective-permute-start | bytes 491528 | tf_op jit(solution)/shard_map/ppermute | solution.py:356
  25.2 9.8 %collective-permute-start.9 = (bf16[2,2,160,128]{3,2,1,0:T(8,128)(2,1)S(1)}, bf16[2,2,160,128]{3,2,1,0:T(8,128)(2,1)S(1)}, u32[]{:S(2)}, u32[]{:S(2)}) collective-permute-start(bf16[2,2,160,128]{3,2,1,0:T(8,128)(2,1)S(1)} %get-tuple-element.67), channel_id=1, source_target_pairs={{0,64},{8,72},{16,80},{24,88},{32,96},{40,104},{48,112},{56,120},{... | collective-permute-start | bytes 491528 | tf_op jit(solution)/shard_map/ppermute | solution.py:356
  26.5 8.5 %collective-permute-start.10 = (bf16[2,2,160,128]{3,2,1,0:T(8,128)(2,1)S(1)}, bf16[2,2,160,128]{3,2,1,0:T(8,128)(2,1)S(1)}, u32[]{:S(2)}, u32[]{:S(2)}) collective-permute-start(bf16[2,2,160,128]{3,2,1,0:T(8,128)(2,1)S(1)} %get-tuple-element.68), channel_id=1, source_target_pairs={{0,192},{8,200},{16,208},{24,216},{32,224},{40,232},{48,240},{56,2... | collective-permute-start | bytes 491528 | tf_op jit(solution)/shard_map/ppermute | solution.py:356
  27.0 6.8 %collective-permute-start.5 = (bf16[2,224,128]{2,1,0:T(8,128)(2,1)S(1)}, bf16[2,224,128]{2,1,0:T(8,128)(2,1)S(1)}, u32[]{:S(2)}, u32[]{:S(2)}) collective-permute-start(bf16[2,224,128]{2,1,0:T(8,128)(2,1)S(1)} %stack_pair.1.own_ref), channel_id=1, source_target_pairs={{0,6},{1,7},{2,4},{3,5},{4,2},{5,3},{6,0},{7,1},{8,12},{9,13},{10,... | collective-permute-start | bytes 344072 | tf_op jit(solution)/shard_map/ppermute | solution.py:344
  28.2 5.5 %collective-permute-start.4 = (bf16[2,224,128]{2,1,0:T(8,128)(2,1)S(1)}, bf16[2,224,128]{2,1,0:T(8,128)(2,1)S(1)}, u32[]{:S(2)}, u32[]{:S(2)}) collective-permute-start(bf16[2,224,128]{2,1,0:T(8,128)(2,1)S(1)} %stack_pair.1.own_ref), channel_id=1, source_target_pairs={{0,2},{1,3},{2,0},{3,1},{4,6},{5,7},{6,4},{7,5},{8,14},{9,15},{10,... | collective-permute-start | bytes 344072 | tf_op jit(solution)/shard_map/ppermute | solution.py:344
  28.5 20.0 %copy-start.2 = (bf16[1792,608]{0,1:T(8,128)(2,1)S(1)}, bf16[1792,608]{0,1:T(8,128)(2,1)}, u32[]{:S(2)}) copy-start(bf16[1792,608]{0,1:T(8,128)(2,1)} %param.37) | copy-start | bytes 6537220
  33.8 14.7 %copy-start.1 = (bf16[1792,608]{0,1:T(8,128)(2,1)S(1)}, bf16[1792,608]{0,1:T(8,128)(2,1)}, u32[]{:S(2)}) copy-start(bf16[1792,608]{0,1:T(8,128)(2,1)} %param.36) | copy-start | bytes 6537220
  34.9 13.5 %copy-start.5 = (f32[1792]{0:T(1024)S(1)}, f32[1792]{0:T(1024)}, u32[]{:S(2)}) copy-start(f32[1792]{0:T(1024)} %param.29) | copy-start | bytes 21508
  35.0 13.6 %copy-start = (bf16[608,1792]{1,0:T(8,128)(2,1)S(1)}, bf16[608,1792]{1,0:T(8,128)(2,1)}, u32[]{:S(2)}) copy-start(bf16[608,1792]{1,0:T(8,128)(2,1)} %down_ref) | copy-start | bytes 6537220
  36.1 7.3 %collective-permute-start.11 = (bf16[2,224,128]{2,1,0:T(8,128)(2,1)S(1)}, bf16[2,224,128]{2,1,0:T(8,128)(2,1)S(1)}, u32[]{:S(2)}, u32[]{:S(2)}) collective-permute-start(bf16[2,224,128]{2,1,0:T(8,128)(2,1)S(1)} %get-tuple-element.71), channel_id=1, source_target_pairs={{0,4},{1,5},{2,6},{3,7},{4,0},{5,1},{6,2},{7,3},{8,10},{9,11},{10,... | collective-permute-start | bytes 344072 | tf_op jit(solution)/shard_map/ppermute | solution.py:344
  37.1 6.7 %collective-permute-start.12 = (bf16[2,224,128]{2,1,0:T(8,128)(2,1)S(1)}, bf16[2,224,128]{2,1,0:T(8,128)(2,1)S(1)}, u32[]{:S(2)}, u32[]{:S(2)}) collective-permute-start(bf16[2,224,128]{2,1,0:T(8,128)(2,1)S(1)} %get-tuple-element.72), channel_id=1, source_target_pairs={{0,2},{1,3},{2,0},{3,1},{4,6},{5,7},{6,4},{7,5},{8,14},{9,15},{10,... | collective-permute-start | bytes 344072 | tf_op jit(solution)/shard_map/ppermute | solution.py:344
  38.5 6.4 %collective-permute-start.13 = (bf16[2,224,128]{2,1,0:T(8,128)(2,1)S(1)}, bf16[2,224,128]{2,1,0:T(8,128)(2,1)S(1)}, u32[]{:S(2)}, u32[]{:S(2)}) collective-permute-start(bf16[2,224,128]{2,1,0:T(8,128)(2,1)S(1)} %get-tuple-element.73), channel_id=1, source_target_pairs={{0,6},{1,7},{2,4},{3,5},{4,2},{5,3},{6,0},{7,1},{8,12},{9,13},{10,... | collective-permute-start | bytes 344072 | tf_op jit(solution)/shard_map/ppermute | solution.py:344
  45.0 9.5 %collective-permute-start.14 = (bf16[2,224,128]{2,1,0:T(8,128)(2,1)S(1)}, bf16[2,224,128]{2,1,0:T(8,128)(2,1)S(1)}, u32[]{:S(2)}, u32[]{:S(2)}) collective-permute-start(bf16[2,224,128]{2,1,0:T(8,128)(2,1)S(1)} %pad_maximum_fusion.1), channel_id=1, source_target_pairs={{0,1},{1,0},{2,3},{3,2},{4,5},{5,4},{6,7},{7,6},{8,9},{9,8},{10,11... | collective-permute-start | bytes 344072 | tf_op jit(solution)/shard_map/ppermute | solution.py:347
  54.6 6.5 %collective-permute-start.17 = (bf16[2,224,128]{2,1,0:T(8,128)(2,1)S(1)}, bf16[2,224,128]{2,1,0:T(8,128)(2,1)S(1)}, u32[]{:S(2)}, u32[]{:S(2)}) collective-permute-start(bf16[2,224,128]{2,1,0:T(8,128)(2,1)S(1)} %add_convert_fusion.own_ref), channel_id=1, source_target_pairs={{0,4},{1,5},{2,6},{3,7},{4,0},{5,1},{6,2},{7,3},{8,10},{9,11},{10,... | collective-permute-start | bytes 344072 | tf_op jit(solution)/shard_map/ppermute | solution.py:344
  56.7 6.0 %collective-permute-start.16 = (bf16[2,224,128]{2,1,0:T(8,128)(2,1)S(1)}, bf16[2,224,128]{2,1,0:T(8,128)(2,1)S(1)}, u32[]{:S(2)}, u32[]{:S(2)}) collective-permute-start(bf16[2,224,128]{2,1,0:T(8,128)(2,1)S(1)} %add_convert_fusion.own_ref), channel_id=1, source_target_pairs={{0,6},{1,7},{2,4},{3,5},{4,2},{5,3},{6,0},{7,1},{8,12},{9,13},{10,... | collective-permute-start | bytes 344072 | tf_op jit(solution)/shard_map/ppermute | solution.py:344
  58.8 4.8 %collective-permute-start.15 = (bf16[2,224,128]{2,1,0:T(8,128)(2,1)S(1)}, bf16[2,224,128]{2,1,0:T(8,128)(2,1)S(1)}, u32[]{:S(2)}, u32[]{:S(2)}) collective-permute-start(bf16[2,224,128]{2,1,0:T(8,128)(2,1)S(1)} %add_convert_fusion.own_ref), channel_id=1, source_target_pairs={{0,2},{1,3},{2,0},{3,1},{4,6},{5,7},{6,4},{7,5},{8,14},{9,15},{10,... | collective-permute-start | bytes 344072 | tf_op jit(solution)/shard_map/ppermute | solution.py:344
  65.6 6.4 %collective-permute-start.18 = (bf16[2,224,128]{2,1,0:T(8,128)(2,1)S(1)}, bf16[2,224,128]{2,1,0:T(8,128)(2,1)S(1)}, u32[]{:S(2)}, u32[]{:S(2)}) collective-permute-start(bf16[2,224,128]{2,1,0:T(8,128)(2,1)S(1)} %get-tuple-element.84), channel_id=1, source_target_pairs={{0,4},{1,5},{2,6},{3,7},{4,0},{5,1},{6,2},{7,3},{8,10},{9,11},{10,... | collective-permute-start | bytes 344072 | tf_op jit(solution)/shard_map/ppermute | solution.py:344
  66.4 5.6 %collective-permute-start.19 = (bf16[2,224,128]{2,1,0:T(8,128)(2,1)S(1)}, bf16[2,224,128]{2,1,0:T(8,128)(2,1)S(1)}, u32[]{:S(2)}, u32[]{:S(2)}) collective-permute-start(bf16[2,224,128]{2,1,0:T(8,128)(2,1)S(1)} %get-tuple-element.85), channel_id=1, source_target_pairs={{0,2},{1,3},{2,0},{3,1},{4,6},{5,7},{6,4},{7,5},{8,14},{9,15},{10,... | collective-permute-start | bytes 344072 | tf_op jit(solution)/shard_map/ppermute | solution.py:344
  67.8 6.0 %collective-permute-start.20 = (bf16[2,224,128]{2,1,0:T(8,128)(2,1)S(1)}, bf16[2,224,128]{2,1,0:T(8,128)(2,1)S(1)}, u32[]{:S(2)}, u32[]{:S(2)}) collective-permute-start(bf16[2,224,128]{2,1,0:T(8,128)(2,1)S(1)} %get-tuple-element.86), channel_id=1, source_target_pairs={{0,6},{1,7},{2,4},{3,5},{4,2},{5,3},{6,0},{7,1},{8,12},{9,13},{10,... | collective-permute-start | bytes 344072 | tf_op jit(solution)/shard_map/ppermute | solution.py:344
  73.9 8.2 %collective-permute-start.21 = (bf16[224,128]{1,0:T(8,128)(2,1)S(1)}, bf16[224,128]{1,0:T(8,128)(2,1)S(1)}, u32[]{:S(2)}, u32[]{:S(2)}) collective-permute-start(bf16[224,128]{1,0:T(8,128)(2,1)S(1)} %fusion.4), channel_id=1, source_target_pairs={{0,1},{1,0},{2,3},{3,2},{4,5},{5,4},{6,7},{7,6},{8,9},{9,8},{10,11... | collective-permute-start | bytes 172040 | tf_op jit(solution)/shard_map/ppermute | solution.py:347
